TPU v7x, 32 devices: a whole 2x2x4 slice. The times are simulated.
32 devices in a mesh: ctx: 8 (over y, x, core), fsdp: 4 (over z).
Axes of the slice: x: 2, y: 2, z: 4, core: 2. Of those that a mesh axis runs over, the one named last changes fastest.
Arguments:
- hidden_in: bfloat16 [4, 1024, 768], P('fsdp', 'ctx'), may hold values from -6 to 6
- out_grad: bfloat16 [4, 1024, 768], P('fsdp', 'ctx'), may hold values from -6 to 6
- block_ids: int32 [4, 1024], P('fsdp'), may hold values from 0 to 7, never falling along the last dimension, each value on 1 to 256 neighbouring positions
- clusters: int32 [4, 12, 1024], P('fsdp'), may hold values from 0 to 1023, as said below
- w_query: bfloat16 [768, 768], P('fsdp'), may hold values from -0.21875 to 0.21875
- w_key: bfloat16 [768, 768], P('fsdp'), may hold values from -0.21875 to 0.21875
- w_value: bfloat16 [768, 768], P('fsdp'), may hold values from -0.21875 to 0.21875
- w_out: bfloat16 [768, 768], P('fsdp'), may hold values from -1.25 to 1.25
- b_query: bfloat16 [768], P('fsdp'), may hold values from -3 to 3
- b_value: bfloat16 [768], P('fsdp'), may hold values from -3 to 3
- b_out: bfloat16 [768], P('fsdp'), may hold values from -3 to 3
- ln1_gain: bfloat16 [768], P('fsdp'), may hold values from 0.5 to 1.5
- ln1_bias: bfloat16 [768], P('fsdp'), may hold values from -3 to 3
- w_in: bfloat16 [768, 3072], P('fsdp'), may hold values from -0.21875 to 0.21875
- b_in: bfloat16 [3072], P('fsdp'), may hold values from -3 to 3
- w_down: bfloat16 [3072, 768], P('fsdp'), may hold values from -0.109375 to 0.109375
- b_down: bfloat16 [768], P('fsdp'), may hold values from -3 to 3
- ln2_gain: bfloat16 [768], P('fsdp'), may hold values from 0.5 to 1.5
- ln2_bias: bfloat16 [768], P('fsdp'), may hold values from -3 to 3
Outputs:
- layer_out: bfloat16 [4, 1024, 768], P('fsdp', 'ctx')
- input_grad: bfloat16 [4, 1024, 768], P('fsdp', 'ctx')
- grad_w_query: float32 [768, 768], P('fsdp')
- grad_w_key: float32 [768, 768], P('fsdp')
- grad_w_value: float32 [768, 768], P('fsdp')
- grad_w_out: float32 [768, 768], P('fsdp')
- grad_b_query: float32 [768], P('fsdp')
- grad_b_value: float32 [768], P('fsdp')
- grad_b_out: float32 [768], P('fsdp')
- grad_ln1_gain: float32 [768], P('fsdp')
- grad_ln1_bias: float32 [768], P('fsdp')
- grad_w_in: float32 [768, 3072], P('fsdp')
- grad_b_in: float32 [3072], P('fsdp')
- grad_w_down: float32 [3072, 768], P('fsdp')
- grad_b_down: float32 [768], P('fsdp')
- grad_ln2_gain: float32 [768], P('fsdp')
- grad_ln2_bias: float32 [768], P('fsdp')
Inputs may be any that keep to these rules, and one draw needn't show every extreme that they name: `clusters`: each head's row is an order of all 1024 stored rows of its sequence; every cluster (128 consecutive entries) holds exactly 16 stored rows of each aligned range of 128 stored rows. `block_ids`: never falls along the positions; each block holds 1 to 256 positions.
All inputs are finite; a program needn't handle non-finite values.
Results may differ from a plain program's by a relative error of at most 0.022.
Values may be sent and summed in bfloat16 or wider, within the bound.
No kernel may reach another device: no remote copies, remote signals or barrier semaphores. Data moves between devices by JAX's collectives and lax.ppermute only.
A program may use at most 192 MiB of HBM per device.

v0:
```python
import jax
import jax.numpy as jnp
from jax import lax
from jax.sharding import PartitionSpec as P

H = 12
DH = 64
CLUSTER = 128


EPSILON = 1e-12
FLOOR = -1e30


def layer_norm(values, gain, shift):
    centre = values - jnp.mean(values, axis=-1, keepdims=True)
    spread = jnp.mean(centre * centre, axis=-1, keepdims=True)
    return centre * lax.rsqrt(spread + EPSILON) * gain + shift


def exact_gelu(values):
    return jax.nn.gelu(values, approximate=False)


def positions(length, per_device, parts):
    stored = jnp.arange(length, dtype=jnp.int32)
    device = stored // per_device
    within = stored % per_device
    half = per_device // 2
    return jnp.where(
        within < half, device * half + within, (2 * parts - 1 - device) * half + within - half
    )


def contract(left, right):
    return lax.dot_general(
        left, right, (((0,), (0,)), ((), ())), preferred_element_type=jnp.float32
    )


def back_product(grad, weight):
    return lax.dot_general(
        grad, weight, (((1,), (1,)), ((), ())), preferred_element_type=jnp.float32
    )


def column_sum(values):
    return jnp.sum(values.astype(jnp.float32), axis=0)


def per_head_rows(rows, index):
    split = rows.reshape(rows.shape[0], H, DH)
    return jnp.take_along_axis(split, index.T[:, :, None], axis=0)


def cluster_tables(order, device, per_device, parts):
    heads, length = order.shape
    groups = length // CLUSTER
    members = CLUSTER // parts
    mine = (order // per_device == device).astype(jnp.int32)
    rank = jnp.cumsum(mine.reshape(heads, groups, CLUSTER), axis=-1).reshape(heads, length) - 1
    entry = jnp.arange(length, dtype=jnp.int32)[None, :]
    slot = jnp.where(mine == 1, entry // CLUSTER * members + rank, per_device)
    head_index = jnp.arange(heads, dtype=jnp.int32)[:, None]
    picked = (
        jnp.zeros((heads, per_device), jnp.int32)
        .at[head_index, slot]
        .set(order - device * per_device, mode="drop")
    )
    counter = jnp.broadcast_to(
        jnp.arange(per_device, dtype=jnp.int32)[None, :], (heads, per_device)
    )
    placed = jnp.zeros((heads, per_device), jnp.int32).at[head_index, picked].set(counter)
    inverse = (
        jnp.zeros((heads, length), jnp.int32)
        .at[head_index, order]
        .set(jnp.broadcast_to(jnp.arange(length, dtype=jnp.int32)[None, :], (heads, length)))
    )
    return (picked, placed, inverse)


def score_blocks(query, key_rows, query_blocks, key_blocks, scale):
    scores = (
        jnp.einsum("cqhd,ckhd->hcqk", query, key_rows, preferred_element_type=jnp.float32) * scale
    )
    allowed = key_blocks[:, :, None, :] <= query_blocks[:, :, :, None]
    return (scores, allowed)


def attend(query, key_rows, value_rows, query_blocks, key_blocks, scale):
    scores, allowed = score_blocks(query, key_rows, query_blocks, key_blocks, scale)
    masked = jnp.where(allowed, scores, FLOOR)
    top = jnp.max(masked, axis=-1, keepdims=True)
    weights = jnp.where(allowed, jnp.exp(masked - top), 0.0)
    total = jnp.sum(weights, axis=-1, keepdims=True)
    probs = (weights / total).astype(jnp.bfloat16)
    mixed = jnp.einsum("hcqk,ckhd->cqhd", probs, value_rows, preferred_element_type=jnp.float32)
    return (mixed.astype(jnp.bfloat16), top + jnp.log(total))


def attend_back(query, key_rows, value_rows, query_blocks, key_blocks, logsum, d_mixed, scale):
    scores, allowed = score_blocks(query, key_rows, query_blocks, key_blocks, scale)
    probs = jnp.where(allowed, jnp.exp(jnp.where(allowed, scores, FLOOR) - logsum), 0.0)
    rounded = probs.astype(jnp.bfloat16)
    d_probs = jnp.einsum("cqhd,ckhd->hcqk", d_mixed, value_rows, preferred_element_type=jnp.float32)
    centred = jnp.sum(probs * d_probs, axis=-1, keepdims=True)
    d_scores = (probs * (d_probs - centred)).astype(jnp.bfloat16)
    d_query = (
        jnp.einsum("hcqk,ckhd->cqhd", d_scores, key_rows, preferred_element_type=jnp.float32)
        * scale
    )
    d_key = (
        jnp.einsum("hcqk,cqhd->ckhd", d_scores, query, preferred_element_type=jnp.float32) * scale
    )
    d_value = jnp.einsum("hcqk,cqhd->ckhd", rounded, d_mixed, preferred_element_type=jnp.float32)
    return (d_query, d_key, d_value)


def body(
    hidden_in,
    out_grad,
    block_ids,
    clusters,
    w_query,
    w_key,
    w_value,
    w_out,
    b_query,
    b_value,
    b_out,
    ln1_gain,
    ln1_bias,
    w_in,
    b_in,
    w_down,
    b_down,
    ln2_gain,
    ln2_bias,
):
    parts = lax.axis_size("ctx")
    device = lax.axis_index("ctx")
    sequences, per_device, width = hidden_in.shape
    length = per_device * parts
    members = CLUSTER // parts
    groups = length // CLUSTER
    scale = DH ** (-0.5)
    (
        full_query,
        full_key,
        full_value,
        full_out,
        bias_query,
        bias_value,
        bias_out,
        gain_one,
        shift_one,
    ) = (
        lax.all_gather(w_query, "fsdp", axis=0, tiled=True),
        lax.all_gather(w_key, "fsdp", axis=0, tiled=True),
        lax.all_gather(w_value, "fsdp", axis=0, tiled=True),
        lax.all_gather(w_out, "fsdp", axis=0, tiled=True),
        lax.all_gather(b_query, "fsdp", axis=0, tiled=True),
        lax.all_gather(b_value, "fsdp", axis=0, tiled=True),
        lax.all_gather(b_out, "fsdp", axis=0, tiled=True),
        lax.all_gather(ln1_gain, "fsdp", axis=0, tiled=True),
        lax.all_gather(ln1_bias, "fsdp", axis=0, tiled=True),
    )
    full_in, full_down, bias_in, bias_down, gain_two, shift_two = (
        lax.all_gather(w_in, "fsdp", axis=0, tiled=True),
        lax.all_gather(w_down, "fsdp", axis=0, tiled=True),
        lax.all_gather(b_in, "fsdp", axis=0, tiled=True),
        lax.all_gather(b_down, "fsdp", axis=0, tiled=True),
        lax.all_gather(ln2_gain, "fsdp", axis=0, tiled=True),
        lax.all_gather(ln2_bias, "fsdp", axis=0, tiled=True),
    )
    hidden = hidden_in.reshape(sequences * per_device, width)
    query_rows = (
        jnp.dot(hidden, full_query, preferred_element_type=jnp.float32) + bias_query
    ).astype(jnp.bfloat16)
    key_rows = jnp.dot(hidden, full_key, preferred_element_type=jnp.float32).astype(jnp.bfloat16)
    value_rows = (
        jnp.dot(hidden, full_value, preferred_element_type=jnp.float32) + bias_value
    ).astype(jnp.bfloat16)
    place = positions(length, per_device, parts)
    index = 0
    order = clusters[index]
    stored_blocks = block_ids[index][place]
    picked, placed, inverse = cluster_tables(order, device, per_device, parts)
    q_local = per_head_rows(query_rows, picked).reshape(groups, members, H, DH)
    query_blocks = stored_blocks[device * per_device + picked].reshape(H, groups, members)
    key_all = lax.all_gather(key_rows, "ctx", axis=0, tiled=True)
    value_all = lax.all_gather(value_rows, "ctx", axis=0, tiled=True)
    key_cluster = per_head_rows(key_all, order).reshape(groups, CLUSTER, H, DH)
    value_cluster = per_head_rows(value_all, order).reshape(groups, CLUSTER, H, DH)
    key_blocks = stored_blocks[order].reshape(H, groups, CLUSTER)
    mixed, logsum = attend(q_local, key_cluster, value_cluster, query_blocks, key_blocks, scale)
    contexts = per_head_rows(mixed.reshape(per_device, width), placed).reshape(per_device, width)
    kept = [
        (
            q_local,
            key_cluster,
            value_cluster,
            query_blocks,
            key_blocks,
            logsum,
            picked,
            placed,
            inverse,
        )
    ]
    attended = jnp.dot(contexts, full_out, preferred_element_type=jnp.float32) + bias_out
    first_sum = hidden.astype(jnp.float32) + attended
    first, first_pull = jax.vjp(
        layer_norm, first_sum, gain_one.astype(jnp.float32), shift_one.astype(jnp.float32)
    )
    first_low = first.astype(jnp.bfloat16)
    inner = jnp.dot(first_low, full_in, preferred_element_type=jnp.float32) + bias_in
    active_full, gelu_pull = jax.vjp(exact_gelu, inner)
    active = active_full.astype(jnp.bfloat16)
    second_sum = first + jnp.dot(active, full_down, preferred_element_type=jnp.float32) + bias_down
    second, second_pull = jax.vjp(
        layer_norm, second_sum, gain_two.astype(jnp.float32), shift_two.astype(jnp.float32)
    )
    layer_out = second.astype(jnp.bfloat16).reshape(sequences, per_device, width)
    d_out = out_grad.reshape(sequences * per_device, width).astype(jnp.float32)
    d_second, g_gain_two, g_shift_two = second_pull(d_out)
    d_branch = d_second.astype(jnp.bfloat16)
    g_w_down = contract(active, d_branch)
    g_b_down = column_sum(d_branch)
    d_active = back_product(d_branch, full_down)
    d_inner = gelu_pull(d_active)[0].astype(jnp.bfloat16)
    g_w_in = contract(first_low, d_inner)
    g_b_in = column_sum(d_inner)
    d_first = d_second + back_product(d_inner, full_in)
    d_sum, g_gain_one, g_shift_one = first_pull(d_first)
    d_attended = d_sum.astype(jnp.bfloat16)
    g_w_out = contract(contexts, d_attended)
    g_b_out = column_sum(d_attended)
    d_context = back_product(d_attended, full_out).astype(jnp.bfloat16)
    index = 0
    q_kept, k_kept, v_kept, blocks_q, blocks_k, logsum, picked, placed, inverse = kept[index]
    d_cluster = per_head_rows(d_context, picked).reshape(groups, members, H, DH)
    d_query, d_key, d_value = attend_back(
        q_kept, k_kept, v_kept, blocks_q, blocks_k, logsum, d_cluster, scale
    )
    key_full = per_head_rows(d_key.reshape(length, width), inverse).reshape(length, width)
    value_full = per_head_rows(d_value.reshape(length, width), inverse).reshape(length, width)
    key_part = lax.psum_scatter(
        key_full.astype(jnp.bfloat16), "ctx", scatter_dimension=0, tiled=True
    )
    value_part = lax.psum_scatter(
        value_full.astype(jnp.bfloat16), "ctx", scatter_dimension=0, tiled=True
    )
    query_local = d_query.astype(jnp.bfloat16).reshape(per_device, width)
    query_grads = per_head_rows(query_local, placed).reshape(per_device, width)
    g_w_query = contract(hidden, query_grads)
    g_b_query = column_sum(query_grads)
    g_w_key = contract(hidden, key_part)
    g_w_value = contract(hidden, value_part)
    g_b_value = column_sum(value_part)
    input_total = (
        d_sum
        + back_product(query_grads, full_query)
        + back_product(key_part, full_key)
        + back_product(value_part, full_value)
    )
    input_grad = input_total.astype(jnp.bfloat16).reshape(sequences, per_device, width)
    shares = (
        lax.psum_scatter(
            g_w_query.astype(jnp.bfloat16), "fsdp", scatter_dimension=0, tiled=True
        ).astype(jnp.float32),
        lax.psum_scatter(
            g_w_key.astype(jnp.bfloat16), "fsdp", scatter_dimension=0, tiled=True
        ).astype(jnp.float32),
        lax.psum_scatter(
            g_w_value.astype(jnp.bfloat16), "fsdp", scatter_dimension=0, tiled=True
        ).astype(jnp.float32),
        lax.psum_scatter(
            g_w_out.astype(jnp.bfloat16), "fsdp", scatter_dimension=0, tiled=True
        ).astype(jnp.float32),
        lax.psum_scatter(
            g_b_query.astype(jnp.bfloat16), "fsdp", scatter_dimension=0, tiled=True
        ).astype(jnp.float32),
        lax.psum_scatter(
            g_b_value.astype(jnp.bfloat16), "fsdp", scatter_dimension=0, tiled=True
        ).astype(jnp.float32),
        lax.psum_scatter(
            g_b_out.astype(jnp.bfloat16), "fsdp", scatter_dimension=0, tiled=True
        ).astype(jnp.float32),
        lax.psum_scatter(
            g_gain_one.astype(jnp.bfloat16), "fsdp", scatter_dimension=0, tiled=True
        ).astype(jnp.float32),
        lax.psum_scatter(
            g_shift_one.astype(jnp.bfloat16), "fsdp", scatter_dimension=0, tiled=True
        ).astype(jnp.float32),
        lax.psum_scatter(
            g_w_in.astype(jnp.bfloat16), "fsdp", scatter_dimension=0, tiled=True
        ).astype(jnp.float32),
        lax.psum_scatter(
            g_b_in.astype(jnp.bfloat16), "fsdp", scatter_dimension=0, tiled=True
        ).astype(jnp.float32),
        lax.psum_scatter(
            g_w_down.astype(jnp.bfloat16), "fsdp", scatter_dimension=0, tiled=True
        ).astype(jnp.float32),
        lax.psum_scatter(
            g_b_down.astype(jnp.bfloat16), "fsdp", scatter_dimension=0, tiled=True
        ).astype(jnp.float32),
        lax.psum_scatter(
            g_gain_two.astype(jnp.bfloat16), "fsdp", scatter_dimension=0, tiled=True
        ).astype(jnp.float32),
        lax.psum_scatter(
            g_shift_two.astype(jnp.bfloat16), "fsdp", scatter_dimension=0, tiled=True
        ).astype(jnp.float32),
    )
    totals = (
        lax.psum(shares[0].astype(jnp.bfloat16), "ctx").astype(jnp.float32),
        lax.psum(shares[1].astype(jnp.bfloat16), "ctx").astype(jnp.float32),
        lax.psum(shares[2].astype(jnp.bfloat16), "ctx").astype(jnp.float32),
        lax.psum(shares[3].astype(jnp.bfloat16), "ctx").astype(jnp.float32),
        lax.psum(shares[4].astype(jnp.bfloat16), "ctx").astype(jnp.float32),
        lax.psum(shares[5].astype(jnp.bfloat16), "ctx").astype(jnp.float32),
        lax.psum(shares[6].astype(jnp.bfloat16), "ctx").astype(jnp.float32),
        lax.psum(shares[7].astype(jnp.bfloat16), "ctx").astype(jnp.float32),
        lax.psum(shares[8].astype(jnp.bfloat16), "ctx").astype(jnp.float32),
        lax.psum(shares[9].astype(jnp.bfloat16), "ctx").astype(jnp.float32),
        lax.psum(shares[10].astype(jnp.bfloat16), "ctx").astype(jnp.float32),
        lax.psum(shares[11].astype(jnp.bfloat16), "ctx").astype(jnp.float32),
        lax.psum(shares[12].astype(jnp.bfloat16), "ctx").astype(jnp.float32),
        lax.psum(shares[13].astype(jnp.bfloat16), "ctx").astype(jnp.float32),
        lax.psum(shares[14].astype(jnp.bfloat16), "ctx").astype(jnp.float32),
    )
    return (
        layer_out,
        input_grad,
        totals[0],
        totals[1],
        totals[2],
        totals[3],
        totals[4],
        totals[5],
        totals[6],
        totals[7],
        totals[8],
        totals[9],
        totals[10],
        totals[11],
        totals[12],
        totals[13],
        totals[14],
    )


def solution(mesh):
    in_specs = (
        P("fsdp", "ctx", None),
        P("fsdp", "ctx", None),
        P("fsdp", None),
        P("fsdp", None, None),
        P("fsdp", None),
        P("fsdp", None),
        P("fsdp", None),
        P("fsdp", None),
        P("fsdp"),
        P("fsdp"),
        P("fsdp"),
        P("fsdp"),
        P("fsdp"),
        P("fsdp", None),
        P("fsdp"),
        P("fsdp", None),
        P("fsdp"),
        P("fsdp"),
        P("fsdp"),
    )
    out_specs = (
        P("fsdp", "ctx", None),
        P("fsdp", "ctx", None),
        P("fsdp", None),
        P("fsdp", None),
        P("fsdp", None),
        P("fsdp", None),
        P("fsdp"),
        P("fsdp"),
        P("fsdp"),
        P("fsdp"),
        P("fsdp"),
        P("fsdp", None),
        P("fsdp"),
        P("fsdp", None),
        P("fsdp"),
        P("fsdp"),
        P("fsdp"),
    )
    return jax.shard_map(body, mesh=mesh, in_specs=in_specs, out_specs=out_specs, check_vma=False)
```

profile of v0, /device:TPU:0, one launch (start us, length us, event | category | flops | bytes accessed | tf_op | source)
XLA Modules:
  0.0 1362.1 jit_solution(14786672146078861802)
XLA Ops:
  17.3 21.1 %all-reduce.20 = (bf16[768]{0:T(1024)(128)(2,1)S(1)}, bf16[768]{0:T(1024)(128)(2,1)S(1)}, bf16[768]{0:T(1024)(128)(2,1)S(1)}, bf16[768]{0:T(1024)(128)(2,1)S(1)}...) all-reduce(bf16[768]{0:T(1024)(128)(2,1)S(1)} %dynamic-update-slice, ...), channel_id=1, replica_groups=mesh['ctx'=8,'fsdp'=4] {'fsdp'}, use_global_device_ids=true, to_apply=%add | all-reduce | flops 5376 | bytes 21504
  38.4 4.9 all-gather.10.cloned.1.call-done
  45.8 28.7 %all-gather.16.cloned.1.call-done = bf16[768,768]{1,0:T(8,128)(2,1)} async-done(((bf16[192,768]{1,0:T(8,128)(2,1)}), bf16[768,768]{1,0:T(8,128)(2,1)}) %all-gather.16.cloned.1.call-update) | async-done | bytes 1179664 | tf_op jit(solution)/shard_map/all_gather | solution.py:159
  79.0 3.4 reduce_window_sum.11
  83.7 45.4 %scatter_custom_fusion = s32[1536]{0:T(1024)S(1)} fusion(s32[12288]{0:T(1024)S(1)} %reshape.537, s32[12288]{0:T(1024)S(1)} %reshape.539, s32[]{:T(128)} %constant.79.clone.1), kind=kCustom, calls=%fused_computation.202 | custom fusion | bytes 6148
  129.6 4.5 gather_fusion
  134.2 5.9 gather_fusion.2
  142.3 49.1 %gather_fusion.1 = s32[12288]{0:T(1024)S(1)} fusion(s32[1024]{0:T(1024)S(1)} %gather_fusion, s32[12288]{0:T(1024)S(1)} %broadcast_clamp_fusion), kind=kCustom, calls=%fused_computation.9 | custom fusion | bytes 147456 | tf_op jit(solution)/shard_map/gather | solution.py:195
  191.5 6.2 scatter_custom_fusion.1
  198.2 13.3 all-gather
  212.7 45.9 %scatter_custom_fusion.2 = s32[12288]{0:T(1024)S(1)} fusion(s32[12288]{0:T(1024)S(1)} %reshape.549, s32[12288]{0:T(1024)S(1)} %reshape.551, s32[]{:T(128)} %constant.79.clone.1), kind=kCustom, calls=%fused_computation.165 | custom fusion | bytes 49156
  261.9 8.5 gather_fusion.4
  274.4 3.1 copy.214
  277.4 119.4 %gather_fusion.3 = bf16[12288,64]{1,0:T(8,128)(2,1)} fusion(bf16[1024,12,64]{2,0,1:T(8,128)(2,1)S(1)} %copy.214, s32[12288]{0:T(1024)S(1)} %reshape.603), kind=kCustom, calls=%fused_computation.clone | custom fusion | bytes 3244032 | tf_op jit(solution)/shard_map/jit(take_along_axis)/gather | solution.py:53
  396.8 6.6 reshape.606
  406.0 3.1 copy.224
  409.0 119.3 %gather_fusion.5 = bf16[12288,64]{1,0:T(8,128)(2,1)} fusion(bf16[1024,12,64]{2,0,1:T(8,128)(2,1)S(1)} %copy.224, s32[12288]{0:T(1024)S(1)} %reshape.603), kind=kCustom, calls=%fused_computation.3.clone | custom fusion | bytes 3244032 | tf_op jit(solution)/shard_map/jit(take_along_axis)/gather | solution.py:53
  528.4 6.6 reshape.614
  535.0 10.9 broadcast_select_fusion
  551.1 8.5 gather_fusion.6
  562.6 8.6 multiply_convert_fusion
  571.2 3.6 fusion.105
  585.0 8.5 gather_fusion.7
  596.6 3.1 copy.268
  599.7 119.4 %gather_fusion.10 = bf16[12288,64]{1,0:T(8,128)(2,1)} fusion(bf16[1024,12,64]{2,0,1:T(8,128)(2,1)S(1)} %bitcast.190, s32[12288]{0:T(1024)S(1)} %reshape.627), kind=kCustom, calls=%fused_computation.7.clone | custom fusion | bytes 3244032 | tf_op jit(solution)/shard_map/jit(take_along_axis)/gather | solution.py:53
  719.0 6.6 reshape.634
  725.6 5.5 copy.255
  731.1 4.0 fusion.1
  735.2 8.4 fusion.32
  746.1 3.1 copy.266
  749.1 119.4 %gather_fusion.9 = bf16[12288,64]{1,0:T(8,128)(2,1)} fusion(bf16[1024,12,64]{2,0,1:T(8,128)(2,1)S(1)} %bitcast.189, s32[12288]{0:T(1024)S(1)} %reshape.627), kind=kCustom, calls=%fused_computation.2.clone | custom fusion | bytes 3244032 | tf_op jit(solution)/shard_map/jit(take_along_axis)/gather | solution.py:53
  868.5 6.6 reshape.630
  875.1 5.3 copy.249
  887.4 3.1 fusion.36
  890.5 8.5 gather_fusion.8
  901.9 20.9 %reduce-scatter.25.cloned.1.call-done = bf16[128,768]{1,0:T(8,128)(2,1)} async-done(((bf16[1024,768]{1,0:T(8,128)(2,1)}), bf16[128,768]{1,0:T(8,128)(2,1)}) %reduce-scatter.25.cloned.1.call-update) | async-done | bytes 196624
  925.8 39.2 %reduce-scatter.27.cloned.1.call-done = bf16[128,768]{1,0:T(8,128)(2,1)} async-done(((bf16[1024,768]{1,0:T(8,128)(2,1)}), bf16[128,768]{1,0:T(8,128)(2,1)}) %reduce-scatter.27.cloned.1.call-update) | async-done | bytes 196624
  969.9 3.7 convolution_convert_fusion.1
  974.7 3.6 convolution_convert_fusion
  978.4 18.2 %reduce-scatter.29.cloned.1.call-done = bf16[192,768]{1,0:T(8,128)(2,1)} async-done(((bf16[768,768]{1,0:T(8,128)(2,1)}), bf16[192,768]{1,0:T(8,128)(2,1)}) %reduce-scatter.29.cloned.1.call-update) | async-done | bytes 294928
  998.4 28.8 %reduce-scatter.31.cloned.1.call-done = bf16[192,768]{1,0:T(8,128)(2,1)} async-done(((bf16[768,768]{1,0:T(8,128)(2,1)}), bf16[192,768]{1,0:T(8,128)(2,1)}) %reduce-scatter.31.cloned.1.call-update) | async-done | bytes 294928
  1029.1 28.9 %reduce-scatter.33.cloned.1.call-done = bf16[192,768]{1,0:T(8,128)(2,1)} async-done(((bf16[768,768]{1,0:T(8,128)(2,1)}), bf16[192,768]{1,0:T(8,128)(2,1)}) %reduce-scatter.33.cloned.1.call-update) | async-done | bytes 294928
  1059.9 28.2 %reduce-scatter.19.cloned.1.call-done = bf16[192,768]{1,0:T(8,128)(2,1)} async-done(((bf16[768,768]{1,0:T(8,128)(2,1)}), bf16[192,768]{1,0:T(8,128)(2,1)}) %reduce-scatter.19.cloned.1.call-update) | async-done | bytes 294928 | tf_op jit(solution)/shard_map/reduce_scatter | solution.py:278
  1088.1 86.1 %reduce-scatter.21.cloned.1.call-done = bf16[192,3072]{1,0:T(8,128)(2,1)} async-done(((bf16[768,3072]{1,0:T(8,128)(2,1)}), bf16[192,3072]{1,0:T(8,128)(2,1)}) %reduce-scatter.21.cloned.1.call-update) | async-done | bytes 1179664 | tf_op jit(solution)/shard_map/reduce_scatter | solution.py:296
  1174.3 88.0 %reduce-scatter.23.cloned.1.call-done = bf16[768,768]{1,0:T(8,128)(2,1)} async-done(((bf16[3072,768]{1,0:T(8,128)(2,1)}), bf16[768,768]{1,0:T(8,128)(2,1)}) %reduce-scatter.23.cloned.1.call-update) | async-done | bytes 1179664 | tf_op jit(solution)/shard_map/reduce_scatter | solution.py:302
  1268.2 18.3 %all-reduce.19 = (bf16[768]{0:T(1024)(128)(2,1)S(1)}, bf16[768]{0:T(1024)(128)(2,1)S(1)}, bf16[768]{0:T(1024)(128)(2,1)S(1)}, bf16[768]{0:T(1024)(128)(2,1)S(1)}...) all-reduce(bf16[768]{0:T(1024)(128)(2,1)S(1)} %dynamic-update-slice, ...), channel_id=1, replica_groups=mesh['ctx'=8,'fsdp'=4] {'fsdp'}, use_global_device_ids=true, to_apply=%add.7 | all-reduce | flops 9984 | bytes 39936
  1287.2 12.0 all-reduce.17
  1308.0 38.7 %all-reduce.23.cloned.1.call-done = (bf16[192,768]{0,1:T(8,128)(2,1)}, bf16[192,768]{0,1:T(8,128)(2,1)}, bf16[192,768]{0,1:T(8,128)(2,1)}, bf16[192,768]{1,0:T(8...) async-done(((bf16[192,768]{0,1:T(8,128)(2,1)}, bf16[192,768]{0,1:T(8,128)(2,1)}, bf16[192,768]{0,1:T(8,128)(2,1)}, bf16[192,768]{1,0:T(8,128)(2,1)}, ...) | async-done | bytes 3538960 | tf_op jit(solution)/shard_map/psum | solution.py:316
  (357 shorter events, 102.1 us)
Async XLA Ops:
  7.2 122.4 %copy-start = (s32[1,1024]{1,0:T(1,128)S(1)}, s32[1,1024]{1,0:T(1,128)}, u32[]{:S(2)}) copy-start(s32[1,1024]{1,0:T(1,128)} %param.27) | copy-start | bytes 12292
  7.2 67.3 %copy-start.8 = (bf16[1,128,768]{2,1,0:T(8,128)(2,1)S(1)}, bf16[1,128,768]{2,1,0:T(8,128)(2,1)}, u32[]{:S(2)}) copy-start(bf16[1,128,768]{2,1,0:T(8,128)(2,1)} %param.25) | copy-start | bytes 589828
  7.2 36.1 %all-gather.10.cloned.1.call-start = ((), (), s32[]{:S(2)}) async-start(), calls=%async_computation.8 | async-start | bytes 1474560 | tf_op jit(solution)/shard_map/all_gather | solution.py:160
  8.0 66.5 %all-gather.16.cloned.1.call-start = ((), (), s32[]{:S(2)}) async-start(), calls=%async_computation.11 | async-start | bytes 1474560 | tf_op jit(solution)/shard_map/all_gather | solution.py:159
  8.7 251.2 %all-gather.14.cloned.1.call-start = ((), (), s32[]{:S(2)}) async-start(), calls=%async_computation.10 | async-start | bytes 1474560 | tf_op jit(solution)/shard_map/all_gather | solution.py:158
  9.4 262.3 %all-gather.12.cloned.1.call-start = ((), (), s32[]{:S(2)}) async-start(), calls=%async_computation.9 | async-start | bytes 1769472 | tf_op jit(solution)/shard_map/all_gather | solution.py:192
  45.7 357.6 %all-gather.18.cloned.1.call-start = ((), (), s32[]{:S(2)}) async-start(), calls=%async_computation.12 | async-start | bytes 1769472 | tf_op jit(solution)/shard_map/all_gather | solution.py:191
  76.8 6.0 copy-start.63
  76.8 6.0 copy-start.68
  76.8 483.7 %all-gather.20.cloned.1.call-start = ((), (), s32[]{:S(2)}) async-start(), calls=%async_computation.13 | async-start | bytes 1474560 | tf_op jit(solution)/shard_map/all_gather | solution.py:161
  77.4 5.8 copy-start.64
  77.4 5.8 copy-start.67
  77.4 485.1 %all-gather.22.cloned.1.call-start = ((), (), s32[]{:S(2)}) async-start(), calls=%async_computation.14 | async-start | bytes 5898240 | tf_op jit(solution)/shard_map/all_gather | solution.py:169
  78.2 493.0 %all-gather.24.cloned.1.call-start = ((), (), s32[]{:S(2)}) async-start(), calls=%async_computation.15 | async-start | bytes 5898240 | tf_op jit(solution)/shard_map/all_gather | solution.py:170
  78.9 843.9 %reduce-scatter.25.cloned.1.call-start = ((), (), s32[]{:S(2)}) async-start(), calls=%async_computation.19 | async-start | bytes 1769472
  142.3 55.9 %copy-start.65 = (bf16[768]{0:T(1024)(128)(2,1)S(1)}, bf16[768]{0:T(1024)(128)(2,1)}, u32[]{:S(2)}) copy-start(bf16[768]{0:T(1024)(128)(2,1)} %param.39) | copy-start | bytes 4612
  528.4 6.6 copy-start.40
  535.0 11.0 copy-start.30
  535.0 11.0 copy-start.36
  546.0 5.1 copy-start.3
  562.3 20.3 %copy-start.4 = (f32[128,768]{1,0:T(8,128)}, f32[128,768]{1,0:T(8,128)S(1)}, u32[]{:S(2)}) copy-start(f32[128,768]{1,0:T(8,128)S(1)} %get-tuple-element.175) | copy-start | bytes 1179652
  562.5 20.1 %copy-start.49 = (f32[128]{0:T(128)}, f32[128]{0:T(128)S(1)}, u32[]{:S(2)}) copy-start(f32[128]{0:T(128)S(1)} %fusion.91) | copy-start | bytes 1540
  562.6 8.6 copy-start.48
  571.2 5.7 slice-start.2
  571.2 5.6 slice-start.3
  571.2 5.6 copy-start.70
  574.9 4.4 copy-start.58
  725.6 5.5 copy-start.31
  735.1 9.1 copy-start.18
  875.1 5.3 copy-start.47
  884.7 80.3 %reduce-scatter.27.cloned.1.call-start = ((), (), s32[]{:S(2)}) async-start(), calls=%async_computation.20 | async-start | bytes 1769472
  886.4 110.1 %reduce-scatter.29.cloned.1.call-start = ((), (), s32[]{:S(2)}) async-start(), calls=%async_computation.21 | async-start | bytes 1474560
  901.9 125.3 %reduce-scatter.31.cloned.1.call-start = ((), (), s32[]{:S(2)}) async-start(), calls=%async_computation.22 | async-start | bytes 1474560
  925.7 132.3 %reduce-scatter.33.cloned.1.call-start = ((), (), s32[]{:S(2)}) async-start(), calls=%async_computation.23 | async-start | bytes 1474560
  968.0 120.2 %reduce-scatter.19.cloned.1.call-start = ((), (), s32[]{:S(2)}) async-start(), calls=%async_computation.16 | async-start | bytes 1474560 | tf_op jit(solution)/shard_map/reduce_scatter | solution.py:278
  969.5 204.7 %reduce-scatter.21.cloned.1.call-start = ((), (), s32[]{:S(2)}) async-start(), calls=%async_computation.17 | async-start | bytes 5898240 | tf_op jit(solution)/shard_map/reduce_scatter | solution.py:296
  973.5 288.7 %reduce-scatter.23.cloned.1.call-start = ((), (), s32[]{:S(2)}) async-start(), calls=%async_computation.18 | async-start | bytes 5898240 | tf_op jit(solution)/shard_map/reduce_scatter | solution.py:302
  978.3 368.4 %all-reduce.23.cloned.1.call-start = ((), (), s32[]{:S(2)}) async-start(), calls=%async_computation.24 | async-start | bytes 7667712 | tf_op jit(solution)/shard_map/psum | solution.py:316
  1263.2 4.9 copy-start.29
  1263.2 4.9 copy-start.52
  1263.2 4.9 copy-start.53
  1263.2 41.2 %copy-start.13 = (bf16[768,768]{1,0:T(8,128)(2,1)S(1)}, bf16[768,768]{1,0:T(8,128)(2,1)}, u32[]{:S(2)}) copy-start(bf16[768,768]{1,0:T(8,128)(2,1)} %all-gather.16.cloned.1.call-done) | copy-start | bytes 3538948
  1263.2 41.2 %copy-start.37 = (bf16[128,768]{1,0:T(8,128)(2,1)S(1)}, bf16[128,768]{1,0:T(8,128)(2,1)}, u32[]{:S(2)}) copy-start(bf16[128,768]{1,0:T(8,128)(2,1)} %reduce-scatter.25.cloned.1.call-done) | copy-start | bytes 589828
  1263.8 4.3 copy-start.55
  1263.8 4.3 copy-start.56
  1263.8 4.3 copy-start.57
  1263.8 4.3 copy-start.60
  1268.0 37.9 %copy-start.16 = (bf16[768,768]{1,0:T(8,128)(2,1)S(1)}, bf16[768,768]{1,0:T(8,128)(2,1)}, u32[]{:S(2)}) copy-start(bf16[768,768]{1,0:T(8,128)(2,1)} %all-gather.10.cloned.1.call-done) | copy-start | bytes 3538948
  (44 other events, 104.6 us)
Sparse Core Ops, SparseCore 0:
  9.6 33.6 all-gather.9
  44.9 29.5 all-gather.15
  76.1 29.5 all-gather.13
  108.0 24.7 all-gather.11
  135.1 25.6 all-gather.17
  162.3 30.4 all-gather.19
  194.3 88.6 all-gather.21
  284.5 87.8 all-gather.23
  884.9 37.9 reduce-scatter.24
  926.5 38.4 reduce-scatter.26
  967.3 29.1 reduce-scatter.28
  999.3 27.8 reduce-scatter.30
  1030.1 27.8 reduce-scatter.32
  1060.2 27.8 reduce-scatter.18
  1090.3 83.9 reduce-scatter.20
  1176.4 85.7 reduce-scatter.22
  1267.3 79.3 all-reduce.22
where the time goes:
time: 1370 us; the launch traced here: 1360 us
  local copies, waits for them, and re-layouts  761 us (56%)
  waiting for transfers between devices  415 us (30%)
  blocking collectives  64.7 us (5%)
  matrix products  55.8 us (4%)
  other arithmetic  47.3 us (3%)
  between operations  17.7 us (1%)
    gather x26, local copies, waits for them, and re-layouts, per_head_rows(): return jnp.take_along_axis(split, index.T[:, :, None], axis=0)  551 us
    unnamed x22, waiting for transfers between devices  140 us
    unnamed x193, local copies, waits for them, and re-layouts  128 us
    reduce_scatter x1, waiting for transfers between devices, body(): lax.psum_scatter(g_w_down.astype(jnp.bfloat16), 'fsdp', scatter_dimension...  88 us
    reduce_scatter x1, waiting for transfers between devices, body(): lax.psum_scatter(g_w_in.astype(jnp.bfloat16), 'fsdp', scatter_dimension=0...  86.1 us
    gather x1, local copies, waits for them, and re-layouts, body(): key_blocks = stored_blocks[order].reshape(H, groups, CLUSTER)  49.1 us
    unnamed x2, blocking collectives  39.4 us
    psum x1, waiting for transfers between devices, body(): lax.psum(shares[0].astype(jnp.bfloat16), 'ctx').astype(jnp.float32)  38.7 us
  transfers between devices with their start and end apart: 17, of which 11 were waited for; matrix products, arithmetic and copies ran while one was open for 40% of the time, Pallas kernels for 0%

commit v1 on v0

--- a/solution.py
+++ b/solution.py
@@ -1,6 +1,10 @@
+import functools
+
 import jax
 import jax.numpy as jnp
 from jax import lax
+from jax.experimental import pallas as pl
+from jax.experimental.pallas import tpu as pltpu
 from jax.sharding import PartitionSpec as P
 
 H = 12
@@ -116,7 +120,7 @@
     return (d_query, d_key, d_value)
 
 
-def body(
+def general_body(
     hidden_in,
     out_grad,
     block_ids,
@@ -350,6 +354,882 @@
     )
 
 
+BF = jnp.bfloat16
+F32 = jnp.float32
+LANES = 256
+VMEM = pl.BlockSpec(memory_space=pltpu.VMEM)
+HBM = pl.BlockSpec(memory_space=pl.ANY)
+SMEM = pl.BlockSpec(memory_space=pltpu.SMEM)
+VEC = 16
+
+
+def shaped(shape, dtype):
+    return jax.ShapeDtypeStruct(shape, dtype)
+
+
+def call(kernel, outs, ins, args, scratch=(), flops=0, name=None):
+    moved = sum(a.size * a.dtype.itemsize for a in args)
+    moved += sum(o.size * o.dtype.itemsize for o in outs)
+    return pl.pallas_call(
+        kernel,
+        out_shape=outs,
+        in_specs=ins,
+        out_specs=[VMEM] * len(outs),
+        scratch_shapes=list(scratch),
+        name=name,
+        cost_estimate=pl.CostEstimate(flops=flops, transcendentals=0, bytes_accessed=moved),
+        compiler_params=pltpu.CompilerParams(vmem_limit_bytes=60000 * 1024),
+    )(*args)
+
+
+def dot(left, right):
+    return jnp.dot(left, right, preferred_element_type=F32)
+
+
+def dot_nt(left, right):
+    return lax.dot_general(left, right, (((1,), (1,)), ((), ())), preferred_element_type=F32)
+
+
+def dot_tn(left, right):
+    return lax.dot_general(left, right, (((0,), (0,)), ((), ())), preferred_element_type=F32)
+
+
+def turned(ring, f, s):
+    return lax.rem(f - s + ring, ring)
+
+
+class Plan:
+    def __init__(self, chips, ring, width, hidden, per_device):
+        self.chips, self.ring, self.width, self.hidden = chips, ring, width, hidden
+        self.rows = per_device
+        self.tokens = chips * per_device
+        self.shard = width // ring
+        self.half = self.shard // 2
+        self.share = hidden // chips
+        self.hshard = hidden // ring
+        self.block = self.hshard // chips
+        self.bhalf = self.block // 2
+        self.heads = H // chips
+        self.cols = self.heads * DH
+        self.qkv = 3 * self.cols
+        self.padded = self.heads * LANES
+        self.clusters = chips
+        self.entries = chips * CLUSTER
+
+
+def prep_kernel(g, sc, wq, wk, wv, wi, wd, wo, vec, qall, qsend, iall, msend, osend, sem):
+    p, k = sc[0], sc[1]
+    at = pl.multiple_of(g.block * p + g.bhalf * k, 16)
+    one = pltpu.make_async_copy(wd.at[pl.ds(at, g.bhalf)], msend.at[pl.ds(g.half, g.bhalf)], sem.at[0])
+    one.start()
+    two = pltpu.make_async_copy(
+        wo.at[pl.ds(pl.multiple_of(g.half * k, 16), g.half)], osend, sem.at[1]
+    )
+    two.start()
+    for q in range(g.chips):
+
+        @pl.when(p == q)
+        def _(q=q):
+            for h in range(g.heads):
+                for i, w in enumerate((wq, wk, wv)):
+                    src = g.cols * q + DH * h
+                    qall[:, 3 * DH * h + DH * i : 3 * DH * h + DH * (i + 1)] = w[:, src : src + DH]
+            for r in range(g.ring):
+                src = g.hshard * r + g.block * q
+                iall[:, g.block * r : g.block * (r + 1)] = wi[:, src : src + g.block]
+
+    mine = pl.ds(pl.multiple_of(g.half * k, 16), g.half)
+    qsend[0 : g.half] = qall[mine]
+    qsend[g.half : g.half + VEC, 0:LANES] = vec[...]
+    qsend[g.half : g.half + VEC, LANES:] = jnp.zeros((VEC, g.qkv - LANES), BF)
+    msend[0 : g.half] = iall[mine]
+    one.wait()
+    two.wait()
+
+
+def gathers(g, sc, own, own_at, mine, theirs, at, piece, dst, sem):
+    k, f = sc[1], sc[2]
+    size = piece
+    out = [
+        pltpu.make_async_copy(
+            own.at[pl.ds(own_at, 2 * size)],
+            dst.at[pl.ds(pl.multiple_of(2 * size * f, 16), 2 * size)],
+            sem.at[0],
+        )
+    ]
+    for s in range(1, g.ring):
+        base = 2 * size * turned(g.ring, f, s)
+        for i, (src, core) in enumerate(((mine[s - 1], k), (theirs[s - 1], 1 - k))):
+            out.append(
+                pltpu.make_async_copy(
+                    src.at[pl.ds(at, size)],
+                    dst.at[pl.ds(pl.multiple_of(base + size * core, 16), size)],
+                    sem.at[2 * s - 1 + i],
+                )
+            )
+    return out
+
+
+def start(copies):
+    for copy in copies:
+        copy.start()
+
+
+def finish(copies):
+    for copy in copies:
+        copy.wait()
+
+
+def qkv_kernel(g, sc, *refs):
+    n = g.ring - 1
+    xs = refs[: g.chips]
+    vec, own = refs[g.chips : g.chips + 2]
+    mine = refs[g.chips + 2 : g.chips + 2 + n]
+    theirs = refs[g.chips + 2 + n : g.chips + 2 + 2 * n]
+    out, wpad, full, w, vs, sem, vsem = refs[g.chips + 2 + 2 * n :]
+    p, f = sc[0], sc[2]
+    copies = gathers(g, sc, own, 0, mine, theirs, 0, g.half, w, sem)
+    start(copies)
+    vcopies = [
+        pltpu.make_async_copy(
+            mine[s].at[pl.ds(g.half, VEC), pl.ds(0, LANES)], vs.at[s], vsem.at[s]
+        )
+        for s in range(n)
+    ]
+    start(vcopies)
+    finish(vcopies)
+    rest = jnp.zeros((VEC, g.width - LANES), F32)
+    total = jnp.zeros((VEC, g.width), F32)
+    for s in range(g.ring):
+        piece = (vec[...] if s == 0 else vs[s - 1]).astype(F32)
+        wide = jnp.concatenate([piece, rest], axis=1)
+        total = total + pltpu.roll(wide, g.shard * turned(g.ring, f, s), 1)
+    full[...] = total
+    back = pltpu.roll(total, lax.rem(g.width - g.cols * p, g.width), 1)
+    gap = jnp.zeros((1, DH), F32)
+    parts = []
+    for h in range(g.heads):
+        parts += [back[0:1, DH * h : DH * (h + 1)], gap, back[1:2, DH * h : DH * (h + 1)], gap]
+    bias = jnp.concatenate(parts, axis=1)
+    finish(copies)
+    for h in range(g.heads):
+        wpad[:, LANES * h : LANES * h + 3 * DH] = w[:, 3 * DH * h : 3 * DH * (h + 1)]
+        wpad[:, LANES * h + 3 * DH : LANES * (h + 1)] = jnp.zeros((g.width, DH), BF)
+    rows = jnp.concatenate([x[...] for x in xs], axis=0)
+    out[...] = (dot(rows, wpad[...]) + bias).astype(BF)
+
+
+def select(index, size, axis_size, lanes):
+    if lanes:
+        ids = lax.broadcasted_iota(jnp.int32, (size, axis_size), 1)
+    else:
+        ids = lax.broadcasted_iota(jnp.int32, (axis_size, size), 0)
+    return jnp.where(ids == index, 1.0, 0.0).astype(BF)
+
+
+def attend_kernel(g, own, other, posr, posc, blocks, ctx_own, ctx_other, kept, probs):
+    both = 2 * g.tokens
+    for h in range(g.heads):
+        pick = select(posc[:, h : h + 1], g.entries, both, True)
+        place = select(posr[h : h + 1, :], g.entries, both, False)
+        lanes = slice(LANES * h, LANES * (h + 1))
+        rows = jnp.concatenate([own[:, lanes], other[:, lanes]], axis=0)
+        picked = dot(pick, rows).astype(BF)
+        kept[h] = picked
+        ids = dot(blocks[...], place)
+        mixed = []
+        for c in range(g.clusters):
+            at = slice(CLUSTER * c, CLUSTER * (c + 1))
+            q, key, v = picked[at, 0:DH], picked[at, DH : 2 * DH], picked[at, 2 * DH : 3 * DH]
+            scores = dot_nt(q, key) * (DH ** (-0.5))
+            row_ids = ids[:, at]
+            col_ids = jnp.transpose(row_ids)[:, 0:1]
+            allowed = row_ids[0:1, :] <= col_ids
+            masked = jnp.where(allowed, scores, FLOOR)
+            top = jnp.max(masked, axis=-1, keepdims=True)
+            weights = jnp.where(allowed, jnp.exp(masked - top), 0.0)
+            share = weights / jnp.sum(weights, axis=-1, keepdims=True)
+            probs[h * g.clusters + c] = share
+            mixed.append(dot(share.astype(BF), v).astype(BF))
+        back = dot(place, jnp.concatenate(mixed, axis=0)).astype(BF)
+        ctx_own[:, DH * h : DH * (h + 1)] = back[: g.tokens]
+        ctx_other[:, DH * h : DH * (h + 1)] = back[g.tokens :]
+
+
+def attend_back_kernel(g, own, other, posr, posc, kept, probs, grad_own, grad_other):
+    both = 2 * g.tokens
+    rows = jnp.concatenate([own[...], other[...]], axis=0)
+    for h in range(g.heads):
+        pick = select(posc[:, h : h + 1], g.entries, both, True)
+        place = select(posr[h : h + 1, :], g.entries, both, False)
+        d_mixed = dot(pick, rows[:, DH * h : DH * (h + 1)]).astype(BF)
+        picked = kept[h]
+        found = []
+        for c in range(g.clusters):
+            at = slice(CLUSTER * c, CLUSTER * (c + 1))
+            q, key, v = picked[at, 0:DH], picked[at, DH : 2 * DH], picked[at, 2 * DH : 3 * DH]
+            d_m = d_mixed[at]
+            share = probs[h * g.clusters + c]
+            d_share = dot_nt(d_m, v)
+            delta = jnp.sum(share * d_share, axis=-1, keepdims=True)
+            d_s = (share * (d_share - delta)).astype(BF)
+            scale = DH ** (-0.5)
+            d_q = dot(d_s, key) * scale
+            d_k = dot_tn(d_s, q) * scale
+            d_v = dot_tn(share.astype(BF), d_m)
+            zero = jnp.zeros((CLUSTER, DH), F32)
+            found.append(jnp.concatenate([d_q, d_k, d_v, zero], axis=1).astype(BF))
+        back = dot(place, jnp.concatenate(found, axis=0)).astype(BF)
+        grad_own[:, LANES * h : LANES * (h + 1)] = back[: g.tokens]
+        grad_other[:, LANES * h : LANES * (h + 1)] = back[g.tokens :]
+
+
+def norm_parts(values):
+    centre = values - jnp.mean(values, axis=-1, keepdims=True)
+    spread = jnp.mean(centre * centre, axis=-1, keepdims=True)
+    scale = lax.rsqrt(spread + EPSILON)
+    return centre * scale, scale
+
+
+def norm_back(grad, z, scale):
+    return scale * (
+        grad
+        - jnp.mean(grad, axis=-1, keepdims=True)
+        - z * jnp.mean(grad * z, axis=-1, keepdims=True)
+    )
+
+
+def seen(g, ref, j):
+    return jnp.concatenate(
+        [ref[g.rows * (i ^ j) : g.rows * ((i ^ j) + 1)] for i in range(g.chips)], axis=0
+    )
+
+
+def up_kernel(g, sc, *refs):
+    n, c = g.ring - 1, g.chips
+    ctxs, xs, full = refs[:c], refs[c : 2 * c], refs[2 * c]
+    refs = refs[2 * c + 1 :]
+    wo_own, wi_own = refs[:2]
+    wo_mine, wo_theirs = refs[2 : 2 + n], refs[2 + n : 2 + 2 * n]
+    m_mine, m_theirs = refs[2 + 2 * n : 2 + 3 * n], refs[2 + 3 * n : 2 + 4 * n]
+    inner, low, first_own, z_own, s_own, wo, wi, sem_o, sem_i = refs[2 + 4 * n :]
+    p = sc[0]
+    copies_o = gathers(g, sc, wo_own, 0, wo_mine, wo_theirs, 0, g.half, wo, sem_o)
+    copies_i = gathers(g, sc, wi_own, 0, m_mine, m_theirs, 0, g.half, wi, sem_i)
+    start(copies_o)
+    start(copies_i)
+    rows = jnp.concatenate([x[...] for x in xs], axis=0).astype(F32)
+    total = rows + full[2:3, :]
+    finish(copies_o)
+    for j in range(c):
+        q = jnp.bitwise_xor(p, j)
+        total = total + dot(seen(g, ctxs[j], j), wo[pl.ds(pl.multiple_of(g.cols * q, 64), g.cols), :])
+    z, scale = norm_parts(total)
+    first = z * full[3:4, :] + full[4:5, :]
+    first_own[...] = first[: g.rows]
+    z_own[...] = z[: g.rows]
+    s_own[...] = jnp.broadcast_to(scale[: g.rows], (g.rows, 128))
+    low[...] = first.astype(BF)
+    finish(copies_i)
+    bias = full[pl.ds(8 + p, 1), :]
+    inner[...] = dot(low[...], wi[...]) + bias
+
+
+def down_kernel(g, sc, *refs):
+    n, c = g.ring - 1, g.chips
+    inner, first_own, full, wd_own = refs[:4]
+    mine, theirs = refs[4 : 4 + n], refs[4 + n : 4 + 2 * n]
+    refs = refs[4 + 2 * n :]
+    parts, active = refs[:c], refs[c]
+    wd, sem = refs[c + 1 :]
+    p = sc[0]
+    at = pl.multiple_of(g.block * p, 16)
+    copies = gathers(g, sc, wd_own, at, mine, theirs, g.half, g.bhalf, wd, sem)
+    start(copies)
+    u = inner[...]
+    active[...] = (u * (1.0 + lax.erf(u * (0.5**0.5))) * 0.5).astype(BF)
+    finish(copies)
+    second = dot(active[...], wd[...])
+    parts[0][...] = second[: g.rows] + first_own[...] + full[5:6, :]
+    for j in range(1, c):
+        parts[j][...] = second[g.rows * j : g.rows * (j + 1)].astype(BF)
+
+
+def turn_kernel(g, *refs):
+    c = g.chips
+    parts, full, cotangent = refs[:c], refs[c], refs[c + 1]
+    out, d_second, branch = refs[c + 2 :]
+    second = parts[0][...]
+    for j in range(1, c):
+        second = second + parts[j][...].astype(F32)
+    z, scale = norm_parts(second)
+    gain = full[6:7, :]
+    out[...] = (z * gain + full[7:8, :]).astype(BF)
+    dy = cotangent[...].astype(F32)
+    grad = norm_back(dy * gain, z, scale)
+    d_second[...] = grad
+    branch[0 : g.rows] = grad.astype(BF)
+    one = jnp.sum(dy * z, axis=0, keepdims=True)
+    two = jnp.sum(dy, axis=0, keepdims=True)
+    rest = jnp.zeros((VEC - 2, g.width), F32)
+    branch[g.rows : g.rows + VEC] = jnp.concatenate([one, two, rest], axis=0).astype(BF)
+
+
+def back_kernel(g, sc, *refs):
+    n, c = g.ring - 1, g.chips
+    branches, slope, wd_own, wi_own = refs[:c], refs[c], refs[c + 1], refs[c + 2]
+    mine, theirs = refs[c + 3 : c + 3 + n], refs[c + 3 + n : c + 3 + 2 * n]
+    refs = refs[c + 3 + 2 * n :]
+    parts, d_inner, wd, wi, sem_d, sem_i = refs[:c], *refs[c:]
+    p = sc[0]
+    at = pl.multiple_of(g.block * p, 16)
+    copies_d = gathers(g, sc, wd_own, at, mine, theirs, g.half, g.bhalf, wd, sem_d)
+    copies_i = gathers(g, sc, wi_own, 0, mine, theirs, 0, g.half, wi, sem_i)
+    start(copies_d)
+    start(copies_i)
+    rows = jnp.concatenate([b[0 : g.rows] for b in branches], axis=0)
+    finish(copies_d)
+    d_active = dot_nt(rows, wd[...])
+    d_inner[...] = (d_active * slope[...]).astype(BF)
+    finish(copies_i)
+    total = dot_nt(d_inner[...], wi[...])
+    parts[0][...] = total[: g.rows]
+    for j in range(1, c):
+        parts[j][...] = total[g.rows * j : g.rows * (j + 1)].astype(BF)
+
+
+def split_rows(g, sc, total, size, own, other, at):
+    k, f = sc[1], sc[2]
+    for s in range(g.ring):
+        base = 2 * size * lax.rem(f + s, g.ring)
+        own[s, at : at + size] = total[pl.ds(pl.multiple_of(base + size * k, 8), size), :]
+        other[s, at : at + size] = total[
+            pl.ds(pl.multiple_of(base + size * (1 - k), 8), size), :
+        ].astype(BF)
+
+
+def mlp_grads_kernel(g, sc, *refs):
+    c = g.chips
+    branches, active, low, d_inner = refs[:c], refs[c], refs[c + 1], refs[c + 2]
+    own, other, sums, total = refs[c + 3 :]
+    rows = jnp.concatenate([b[0 : g.rows] for b in branches], axis=0)
+    total[...] = dot_tn(active[...], rows)
+    split_rows(g, sc, total, g.bhalf, own, other, g.half)
+    total[...] = dot_tn(low[...], d_inner[...])
+    split_rows(g, sc, total, g.half, own, other, 0)
+    stats = branches[0][g.rows : g.rows + VEC].astype(F32)
+    for j in range(1, c):
+        stats = stats + branches[j][g.rows : g.rows + VEC].astype(F32)
+    down = jnp.sum(rows.astype(F32), axis=0, keepdims=True)
+    up = jnp.sum(d_inner[...].astype(F32), axis=0, keepdims=True)
+    sums[...] = jnp.concatenate([stats[0:2], down, up, jnp.zeros((4, g.width), F32)], axis=0)
+
+
+def first_kernel(g, *refs):
+    c = g.chips
+    parts, d_second, z_own, s_own, full = refs[:c], *refs[c : c + 4]
+    d_sum, attended = refs[c + 4 :]
+    d_first = d_second[...] + parts[0][...]
+    for j in range(1, c):
+        d_first = d_first + parts[j][...].astype(F32)
+    z = z_own[...]
+    grad = norm_back(d_first * full[3:4, :], z, s_own[:, 0:1])
+    d_sum[...] = grad
+    attended[0 : g.rows] = grad.astype(BF)
+    one = jnp.sum(d_first * z, axis=0, keepdims=True)
+    two = jnp.sum(d_first, axis=0, keepdims=True)
+    rest = jnp.zeros((VEC - 2, g.width), F32)
+    attended[g.rows : g.rows + VEC] = jnp.concatenate([one, two, rest], axis=0).astype(BF)
+
+
+def context_kernel(g, sc, *refs):
+    n, c = g.ring - 1, g.chips
+    grads, own = refs[:c], refs[c]
+    mine, theirs = refs[c + 1 : c + 1 + n], refs[c + 1 + n : c + 1 + 2 * n]
+    out, wo, sem = refs[c + 1 + 2 * n :]
+    p = sc[0]
+    copies = gathers(g, sc, own, 0, mine, theirs, 0, g.half, wo, sem)
+    start(copies)
+    rows = jnp.concatenate([b[0 : g.rows] for b in grads], axis=0)
+    finish(copies)
+    out[...] = dot_nt(rows, wo[pl.ds(pl.multiple_of(g.cols * p, 64), g.cols), :]).astype(BF)
+
+
+def out_grads_kernel(g, sc, *refs):
+    c = g.chips
+    grads, ctxs, sums = refs[:c], refs[c : 2 * c], refs[2 * c]
+    own, other, total = refs[2 * c + 1 :]
+    p, k, f = sc[0], sc[1], sc[2]
+    rows = jnp.concatenate([b[0 : g.rows] for b in grads], axis=0)
+    for j in range(c):
+        q = jnp.bitwise_xor(p, j)
+        total[pl.ds(pl.multiple_of(g.cols * q, 64), g.cols), :] = dot_tn(seen(g, ctxs[j], j), rows)
+    size = g.half // c
+    for s in range(g.ring):
+        base = g.shard * lax.rem(f + s, g.ring) + 2 * size * p
+        own[s, 0:size] = total[pl.ds(pl.multiple_of(base + size * k, 8), size), :]
+        other[s, 0:size] = total[
+            pl.ds(pl.multiple_of(base + size * (1 - k), 8), size), :
+        ].astype(BF)
+    stats = grads[0][g.rows : g.rows + VEC].astype(F32)
+    for j in range(1, c):
+        stats = stats + grads[j][g.rows : g.rows + VEC].astype(F32)
+    out = jnp.sum(rows.astype(F32), axis=0, keepdims=True)
+    rest = jnp.zeros((VEC - 7, g.width), F32)
+    block = jnp.concatenate([sums[0:4], stats[0:2], out, rest], axis=0)
+    spare = own.shape[1] - size - VEC
+    if spare:
+        block = jnp.concatenate([block, jnp.zeros((spare, g.width), F32)], axis=0)
+    for s in range(g.ring):
+        own[s, size:] = block
+        other[s, size:] = block.astype(BF)
+
+
+def input_kernel(g, *refs):
+    c = g.chips
+    own, other, wpad = refs[:3]
+    parts, d_qkv = refs[3 : 3 + c], refs[3 + c]
+    d_qkv[...] = (own[...].astype(F32) + other[...].astype(F32)).astype(BF)
+    total = dot_nt(d_qkv[...], wpad[...])
+    parts[0][...] = total[: g.rows]
+    for j in range(1, c):
+        parts[j][...] = total[g.rows * j : g.rows * (j + 1)].astype(BF)
+
+
+def qkv_grads_kernel(g, sc, *refs):
+    c = g.chips
+    xs, d_qkv = refs[:c], refs[c]
+    own, other, wide, total = refs[c + 1 :]
+    rows = jnp.concatenate([x[...] for x in xs], axis=0)
+    wide[...] = dot_tn(rows, d_qkv[...])
+    sums = jnp.sum(d_qkv[...].astype(F32), axis=0, keepdims=True)
+    for h in range(g.heads):
+        total[:, 3 * DH * h : 3 * DH * (h + 1)] = wide[:, LANES * h : LANES * h + 3 * DH]
+    split_rows(g, sc, total, g.half, own, other, 0)
+    row = jnp.concatenate(
+        [sums[:, LANES * h : LANES * h + 3 * DH] for h in range(g.heads)], axis=1
+    )
+    block = jnp.concatenate([row, jnp.zeros((VEC - 1, g.qkv), F32)], axis=0)
+    for s in range(g.ring):
+        own[s, g.half :] = block
+        other[s, g.half :] = block.astype(BF)
+
+
+def sources(g, sc, refs):
+    p, k = sc[0], sc[1]
+    out = []
+    for j in range(g.chips):
+        q = jnp.bitwise_xor(p, j)
+        out.append((q, k, refs[j]))
+        out.append((q, 1 - k, refs[g.chips + j]))
+    return out
+
+
+def mlp_final_kernel(g, sc, *refs):
+    found, (g_in, g_down) = refs[: 2 * g.chips], refs[2 * g.chips :]
+    for q, core, ref in sources(g, sc, found):
+        at = pl.multiple_of(g.block * q + g.bhalf * core, 8)
+        g_down[pl.ds(at, g.bhalf), :] = ref[g.half :, :].astype(F32)
+        mine = pl.ds(pl.multiple_of(g.half * core, 8), g.half)
+        for chip in range(g.chips):
+
+            @pl.when(q == chip)
+            def _(chip=chip, ref=ref, mine=mine):
+                for r in range(g.ring):
+                    lane = g.hshard * r + g.block * chip
+                    g_in[mine, lane : lane + g.block] = ref[
+                        0 : g.half, g.block * r : g.block * (r + 1)
+                    ].astype(F32)
+
+
+def out_final_kernel(g, sc, *refs):
+    found, (g_out, vec, wide) = refs[: 2 * g.chips], refs[2 * g.chips :]
+    f = sc[2]
+    size = g.half // g.chips
+    for q, core, ref in sources(g, sc, found):
+        at = pl.multiple_of(2 * size * q + size * core, 8)
+        g_out[pl.ds(at, size), :] = ref[0:size, :].astype(F32)
+
+        @pl.when(core == 0)
+        def _(q=q, ref=ref):
+            for chip in range(g.chips):
+
+                @pl.when(q == chip)
+                def _(chip=chip):
+                    block = ref[size : size + VEC, :].astype(F32)
+                    back = pltpu.roll(block, lax.rem(g.width - g.shard * f, g.width), 1)
+                    if chip == 0:
+                        wide[:, :] = back[:, : g.shard]
+                    vec[3 + chip : 4 + chip, :] = back[3:4, : g.shard]
+
+    vec[0:3, :] = wide[0:3, :]
+    vec[3 + g.chips : 6 + g.chips, :] = wide[4:7, :]
+
+
+def qkv_final_kernel(g, sc, *refs):
+    found, (gq, gk, gv, vec) = refs[: 2 * g.chips], refs[2 * g.chips :]
+    f = sc[2]
+    for q, core, ref in sources(g, sc, found):
+        mine = pl.ds(pl.multiple_of(g.half * core, 8), g.half)
+
+        @pl.when((q == f) & (core == 0))
+        def _(ref=ref):
+            row = ref[g.half : g.half + VEC, :].astype(F32)[0:1]
+            for i, at in ((0, 0), (1, 2)):
+                vec[i : i + 1, :] = jnp.concatenate(
+                    [
+                        row[:, 3 * DH * h + DH * at : 3 * DH * h + DH * (at + 1)]
+                        for h in range(g.heads)
+                    ],
+                    axis=1,
+                )
+
+        for chip in range(g.chips):
+
+            @pl.when(q == chip)
+            def _(chip=chip, ref=ref, mine=mine):
+                for i, dst in enumerate((gq, gk, gv)):
+                    for h in range(g.heads):
+                        lane, src = g.cols * chip + DH * h, 3 * DH * h + DH * i
+                        dst[mine, lane : lane + DH] = ref[0 : g.half, src : src + DH].astype(F32)
+
+
+def to_core(x):
+    n = lax.axis_size("ctx")
+    return lax.ppermute(x, "ctx", [(i, i ^ 1) for i in range(n)])
+
+
+def to_chip(x, j):
+    n = lax.axis_size("ctx")
+    return lax.ppermute(x, "ctx", [(i, i ^ (2 * j)) for i in range(n)])
+
+
+def along(x, s):
+    n = lax.axis_size("fsdp")
+    return lax.ppermute(x, "fsdp", [(i, (i + s) % n) for i in range(n)])
+
+
+def spread(x, chips):
+    far = {j: to_chip(x, j) for j in sorted(range(1, chips), key=lambda j: -bin(j).count("1"))}
+    return [x] + [far[j] for j in range(1, chips)]
+
+
+def swap(parts):
+    far = {j: to_chip(parts[j], j) for j in sorted(range(1, len(parts)), key=lambda j: -bin(j).count("1"))}
+    return [parts[0]] + [far[j] for j in range(1, len(parts))]
+
+
+def ring_sum(own, other, ring):
+    got = to_core(other)
+    mine = [own[s] + got[s].astype(F32) for s in range(ring)]
+    far = [along(mine[s].astype(BF), s) for s in range(1, ring)]
+    total = mine[0]
+    for part in far:
+        total = total + part.astype(F32)
+    return total.astype(BF)
+
+
+def plane_pieces(piece, chips):
+    near = spread(piece, chips)
+    return near + [to_core(part) for part in near]
+
+
+def chip_body(
+    hidden_in,
+    out_grad,
+    block_ids,
+    clusters,
+    w_query,
+    w_key,
+    w_value,
+    w_out,
+    b_query,
+    b_value,
+    b_out,
+    ln1_gain,
+    ln1_bias,
+    w_in,
+    b_in,
+    w_down,
+    b_down,
+    ln2_gain,
+    ln2_bias,
+):
+    n, ring = lax.axis_size("ctx"), lax.axis_size("fsdp")
+    chips = n // 2
+    rows, width = hidden_in.shape[1:]
+    hidden = w_in.shape[1]
+    g = Plan(chips, ring, width, hidden, rows)
+    c, f = lax.axis_index("ctx"), lax.axis_index("fsdp")
+    p, k = c // 2, c % 2
+    sc = jnp.stack([p, k, f]).astype(jnp.int32)
+    bind = functools.partial
+
+    x_own = hidden_in.reshape(rows, width)
+    xs = spread(x_own, chips)
+
+    small = jnp.concatenate(
+        [
+            v.reshape(-1, g.shard)
+            for v in (b_query, b_value, b_out, ln1_gain, ln1_bias, b_down, ln2_gain, ln2_bias)
+        ]
+        + [b_in.reshape(chips, g.block)],
+        axis=0,
+    )
+    vec = jnp.pad(small, ((0, VEC - small.shape[0]), (0, LANES - g.shard)))
+    qall, qsend, iall, msend, osend = call(
+        bind(prep_kernel, g),
+        [
+            shaped((g.shard, g.qkv), BF),
+            shaped((g.half + VEC, g.qkv), BF),
+            shaped((g.shard, g.share), BF),
+            shaped((g.half + g.bhalf, width), BF),
+            shaped((g.half, width), BF),
+        ],
+        [SMEM] + [VMEM] * 4 + [HBM] * 2 + [VMEM],
+        [sc, w_query, w_key, w_value, w_in, w_down, w_out, vec],
+        [pltpu.SemaphoreType.DMA((2,))],
+        name="pick_weights",
+    )
+    q_mine = [along(qsend, s) for s in range(1, ring)]
+    q_theirs = [to_core(part) for part in q_mine]
+    o_mine = [along(osend, s) for s in range(1, ring)]
+    o_theirs = [to_core(part) for part in o_mine]
+    m_mine = [along(msend, s) for s in range(1, ring)]
+    m_theirs = [to_core(part) for part in m_mine]
+
+    order = lax.dynamic_slice(
+        clusters[0], (g.heads * p, g.entries * k), (g.heads, g.entries)
+    )
+    chip, core, within = order // (2 * rows), (order // rows) % 2, order % rows
+    pos = (core ^ k) * g.tokens + (chip ^ p) * rows + within
+    posr = jnp.pad(pos, ((0, 8 - g.heads), (0, 0)))
+    posc = posr.T
+    half_rows = rows // 2
+    devices = 2 * (p ^ jnp.arange(chips)[None, :]) + (k ^ jnp.arange(2)[:, None])
+    pieces = jnp.stack([devices, 2 * n - 1 - devices], axis=-1).reshape(-1)
+    hot = (pieces[:, None] == jnp.arange(2 * n)[None, :]).astype(BF)
+    blk = dot(hot, block_ids[0].reshape(2 * n, half_rows).astype(BF)).astype(BF)
+    blk = jnp.broadcast_to(blk.reshape(1, 2 * g.tokens), (8, 2 * g.tokens))
+
+    gate = pltpu.SemaphoreType.DMA((2 * ring - 1,))
+    qkv, wpad, full = call(
+        bind(qkv_kernel, g),
+        [
+            shaped((g.tokens, g.padded), BF),
+            shaped((width, g.padded), BF),
+            shaped((VEC, width), F32),
+        ],
+        [SMEM] + [VMEM] * (chips + 1) + [HBM] * (2 * ring - 1),
+        [sc, *xs, vec, qall, *q_mine, *q_theirs],
+        [
+            pltpu.VMEM((width, g.qkv), BF),
+            pltpu.VMEM((ring - 1, VEC, LANES), BF),
+            gate,
+            pltpu.SemaphoreType.DMA((ring - 1,)),
+        ],
+        flops=2 * g.tokens * width * g.padded,
+        name="project",
+    )
+    qkv_other = to_core(qkv)
+    ctx_own, ctx_other, kept, probs = call(
+        bind(attend_kernel, g),
+        [
+            shaped((g.tokens, g.cols), BF),
+            shaped((g.tokens, g.cols), BF),
+            shaped((g.heads, g.entries, LANES), BF),
+            shaped((g.heads * g.clusters, CLUSTER, CLUSTER), F32),
+        ],
+        [VMEM] * 5,
+        [qkv, qkv_other, posr, posc, blk],
+        flops=8 * g.entries * g.tokens * LANES * g.heads,
+        name="attend",
+    )
+    ctx = ctx_own + to_core(ctx_other)
+    ctxs = spread(ctx, chips)
+
+    inner, low, first_own, z_own, s_own = call(
+        bind(up_kernel, g),
+        [
+            shaped((g.tokens, g.share), F32),
+            shaped((g.tokens, width), BF),
+            shaped((rows, width), F32),
+            shaped((rows, width), F32),
+            shaped((rows, 128), F32),
+        ],
+        [SMEM] + [VMEM] * (2 * chips + 1) + [HBM] * (4 * ring - 2),
+        [sc, *ctxs, *xs, full, w_out, iall, *o_mine, *o_theirs, *m_mine, *m_theirs],
+        [pltpu.VMEM((width, width), BF), pltpu.VMEM((width, g.share), BF), gate, gate],
+        flops=4 * g.tokens * width * g.share,
+        name="mlp_up",
+    )
+    *second, active = call(
+        bind(down_kernel, g),
+        [shaped((rows, width), F32)]
+        + [shaped((rows, width), BF)] * (chips - 1)
+        + [shaped((g.tokens, g.share), BF)],
+        [SMEM] + [VMEM] * 3 + [HBM] * (2 * ring - 1),
+        [sc, inner, first_own, full, w_down, *m_mine, *m_theirs],
+        [pltpu.VMEM((g.share, width), BF), gate],
+        flops=2 * g.tokens * width * g.share,
+        name="mlp_down",
+    )
+    slope = 0.5 * (1.0 + lax.erf(inner * (0.5**0.5))) + inner * jnp.exp(
+        -0.5 * inner * inner
+    ) * (1.0 / (2.0 * jnp.pi) ** 0.5)
+    second = swap(second)
+    layer_out, d_second, branch = call(
+        bind(turn_kernel, g),
+        [
+            shaped((rows, width), BF),
+            shaped((rows, width), F32),
+            shaped((rows + VEC, width), BF),
+        ],
+        [VMEM] * (chips + 2),
+        [*second, full, out_grad.reshape(rows, width)],
+        name="norm_two",
+    )
+    branches = spread(branch, chips)
+    *d_first, d_inner = call(
+        bind(back_kernel, g),
+        [shaped((rows, width), F32)]
+        + [shaped((rows, width), BF)] * (chips - 1)
+        + [shaped((g.tokens, g.share), BF)],
+        [SMEM] + [VMEM] * (chips + 1) + [HBM] * (2 * ring),
+        [sc, *branches, slope, w_down, iall, *m_mine, *m_theirs],
+        [pltpu.VMEM((g.share, width), BF), pltpu.VMEM((width, g.share), BF), gate, gate],
+        flops=4 * g.tokens * width * g.share,
+        name="mlp_back",
+    )
+    d_first = swap(d_first)
+    m_own, m_other, sums = call(
+        bind(mlp_grads_kernel, g),
+        [
+            shaped((ring, g.half + g.bhalf, width), F32),
+            shaped((ring, g.half + g.bhalf, width), BF),
+            shaped((8, width), F32),
+        ],
+        [SMEM] + [VMEM] * (chips + 3),
+        [sc, *branches, active, low, d_inner],
+        [pltpu.VMEM((width, g.share), F32)],
+        flops=4 * g.tokens * width * g.share,
+        name="mlp_grads",
+    )
+    m_piece = ring_sum(m_own, m_other, ring)
+    d_sum, attended = call(
+        bind(first_kernel, g),
+        [shaped((rows, width), F32), shaped((rows + VEC, width), BF)],
+        [VMEM] * (chips + 4),
+        [*d_first, d_second, z_own, s_own, full],
+        name="norm_one",
+    )
+    grads = spread(attended, chips)
+    (d_ctx,) = call(
+        bind(context_kernel, g),
+        [shaped((g.tokens, g.cols), BF)],
+        [SMEM] + [VMEM] * chips + [HBM] * (2 * ring - 1),
+        [sc, *grads, w_out, *o_mine, *o_theirs],
+        [pltpu.VMEM((width, width), BF), gate],
+        flops=2 * g.tokens * width * g.cols,
+        name="context_back",
+    )
+    d_ctx_other = to_core(d_ctx)
+    size = g.half // chips
+    o_rows = -(-(size + VEC) // 16) * 16
+    o_own, o_other = call(
+        bind(out_grads_kernel, g),
+        [shaped((ring, o_rows, width), F32), shaped((ring, o_rows, width), BF)],
+        [SMEM] + [VMEM] * (2 * chips + 1),
+        [sc, *grads, *ctxs, sums],
+        [pltpu.VMEM((width, width), F32)],
+        flops=2 * g.tokens * width * width,
+        name="out_grads",
+    )
+    o_piece = ring_sum(o_own, o_other, ring)
+    dq_own, dq_other = call(
+        bind(attend_back_kernel, g),
+        [shaped((g.tokens, g.padded), BF)] * 2,
+        [VMEM] * 6,
+        [d_ctx, d_ctx_other, posr, posc, kept, probs],
+        flops=8 * g.entries * g.tokens * LANES * g.heads,
+        name="attend_back",
+    )
+    *d_in, d_qkv = call(
+        bind(input_kernel, g),
+        [shaped((rows, width), F32)]
+        + [shaped((rows, width), BF)] * (chips - 1)
+        + [shaped((g.tokens, g.padded), BF)],
+        [VMEM] * 3,
+        [dq_own, to_core(dq_other), wpad],
+        flops=2 * g.tokens * width * g.padded,
+        name="project_back",
+    )
+    q_own, q_other = call(
+        bind(qkv_grads_kernel, g),
+        [shaped((ring, g.half + VEC, g.qkv), F32), shaped((ring, g.half + VEC, g.qkv), BF)],
+        [SMEM] + [VMEM] * (chips + 1),
+        [sc, *xs, d_qkv],
+        [pltpu.VMEM((width, g.padded), F32), pltpu.VMEM((width, g.qkv), F32)],
+        flops=2 * g.tokens * width * g.padded,
+        name="project_grads",
+    )
+    d_in = swap(d_in)
+    q_piece = ring_sum(q_own, q_other, ring)
+    total = d_sum
+    for part in d_in:
+        total = total + part.astype(F32)
+    input_grad = total.astype(BF)
+
+    g_in, g_down = call(
+        bind(mlp_final_kernel, g),
+        [shaped((g.shard, hidden), F32), shaped((g.hshard, width), F32)],
+        [SMEM] + [VMEM] * (2 * chips),
+        [sc, *plane_pieces(m_piece, chips)],
+        name="mlp_lay",
+    )
+    g_out, vec_two = call(
+        bind(out_final_kernel, g),
+        [shaped((g.shard, width), F32), shaped((VEC, g.shard), F32)],
+        [SMEM] + [VMEM] * (2 * chips),
+        [sc, *plane_pieces(o_piece, chips)],
+        [pltpu.VMEM((VEC, g.shard), F32)],
+        name="out_lay",
+    )
+    gq, gk, gv, vec_one = call(
+        bind(qkv_final_kernel, g),
+        [shaped((g.shard, width), F32)] * 3 + [shaped((8, g.shard), F32)],
+        [SMEM] + [VMEM] * (2 * chips),
+        [sc, *plane_pieces(q_piece, chips)],
+        name="project_lay",
+    )
+    last = 3 + chips
+    return (
+        layer_out.reshape(1, rows, width),
+        input_grad.reshape(1, rows, width),
+        gq,
+        gk,
+        gv,
+        g_out,
+        vec_one[0],
+        vec_one[1],
+        vec_two[last + 2],
+        vec_two[last],
+        vec_two[last + 1],
+        g_in,
+        vec_two[3:last].reshape(-1),
+        g_down,
+        vec_two[2],
+        vec_two[0],
+        vec_two[1],
+    )
+
+
+def fits(mesh):
+    n, ring = mesh.shape["ctx"], mesh.shape["fsdp"]
+    chips = n // 2
+    return n % 2 == 0 and chips & (chips - 1) == 0 and H % chips == 0 and ring * chips <= 16
+
+
 def solution(mesh):
     in_specs = (
         P("fsdp", "ctx", None),
@@ -391,4 +1271,5 @@
         P("fsdp"),
         P("fsdp"),
     )
+    body = chip_body if fits(mesh) else general_body
     return jax.shard_map(body, mesh=mesh, in_specs=in_specs, out_specs=out_specs, check_vma=False)

time: 1370 us -> 277 us (0.20)
  local copies, waits for them, and re-layouts: 761 us -> 20.4 us
  waiting for transfers between devices: 415 us -> 98.8 us
  Pallas kernels: 0 us -> 80.5 us
  blocking collectives: 64.7 us -> 0 us
  starting transfers between devices: 0.94 us -> 64 us
  matrix products: 55.8 us -> 0.19 us
  other arithmetic: 47.3 us -> 10.1 us
  between operations: 17.7 us -> 1.5 us
    gather x29 -> x0, local copies, waits for them, and re-layouts: 610 us -> none  [the longest x26 551 us: per_head_rows(): return jnp.take_along_axis(split, index.T[:, :, None], axis=0)]
    reduce_scatter x3 -> x0, waiting for transfers between devices: 202 us -> none  [the longest x1 88 us: body(): lax.psum_scatter(g_w_down.astype(jnp.bfloat16), 'fsdp', scatter_dimension...]
    unnamed x22 -> x0, waiting for transfers between devices: 140 us -> none
    unnamed x193 -> x155, local copies, waits for them, and re-layouts: 128 us -> 7.24 us
    ppermute x0 -> x76, waiting for transfers between devices: none -> 98.8 us  [the longest x30 70 us: to_chip(): return lax.ppermute(x, 'ctx', [(i, i ^ 2 * j) for i in range(n)])]
    pallas_call x0 -> x17, Pallas kernels: none -> 80.5 us  [call(): pl.pallas_call(kernel, out_shape=outs, in_specs=ins, out_specs=[VMEM] * l...]
    ppermute x0 -> x76, starting transfers between devices: none -> 64 us  [the longest x30 36.5 us: to_chip(): return lax.ppermute(x, 'ctx', [(i, i ^ 2 * j) for i in range(n)])]
    dot_general x24 -> x1, matrix products: 55.8 us -> 0.19 us  [dot(): return jnp.dot(left, right, preferred_element_type=F32)]
  transfers between devices with their start and end apart: 17 -> 76, of which waited for: 11 -> 27; matrix products, arithmetic and copies ran while one was open for 40% -> 8% of each run, Pallas kernels for 0% -> 20%
where the time goes in v1:
time: 277 us; the launch traced here: 276 us
  waiting for transfers between devices  98.8 us (36%)
  Pallas kernels  80.5 us (29%)
  starting transfers between devices  64 us (23%)
  local copies, waits for them, and re-layouts  20.4 us (7%)
  other arithmetic  10.1 us (4%)
    pallas_call x17, Pallas kernels, call(): pl.pallas_call(kernel, out_shape=outs, in_specs=ins, out_specs=[VMEM] * l...  80.5 us
    ppermute x30, waiting for transfers between devices, to_chip(): return lax.ppermute(x, 'ctx', [(i, i ^ 2 * j) for i in range(n)])  70 us
    ppermute x30, starting transfers between devices, to_chip(): return lax.ppermute(x, 'ctx', [(i, i ^ 2 * j) for i in range(n)])  36.5 us
    ppermute x18, waiting for transfers between devices, along(): return lax.ppermute(x, 'fsdp', [(i, (i + s) % n) for i in range(n)])  28 us
    ppermute x18, starting transfers between devices, along(): return lax.ppermute(x, 'fsdp', [(i, (i + s) % n) for i in range(n)])  22.6 us
    unnamed x155, local copies, waits for them, and re-layouts  7.24 us
  transfers between devices with their start and end apart: 76, of which 27 were waited for; matrix products, arithmetic and copies ran while one was open for 8% of the time, Pallas kernels for 20%

profile of v1, /device:TPU:0, one launch (start us, length us, event | category | flops | bytes accessed | tf_op | source)
XLA Modules:
  0.0 275.5 jit_solution(6595320094886021764)
XLA Ops:
  0.7 4.0 %collective-permute-start.2 = (bf16[128,768]{1,0:T(8,128)(2,1)}, bf16[128,768]{1,0:T(8,128)(2,1)S(1)}, u32[]{:S(2)}, u32[]{:S(2)}) collective-permute-start(bf16[128,768]{1,0:T(8,128)(2,1)} %bitcast.80), channel_id=1, source_target_pairs={{0,24},{4,28},{8,16},{12,20},{16,8},{20,12},{24,0},{28,4},{1,25},{... | collective-permute-start | bytes 589832 | tf_op jit(solution)/shard_map/ppermute | solution.py:904
  12.4 3.5 %pick_weights.1 = (bf16[192,576]{1,0:T(8,128)(2,1)}, bf16[112,576]{1,0:T(8,128)(2,1)}, bf16[192,768]{1,0:T(8,128)(2,1)}, bf16[192,768]{1,0:T(8,128)(2,1)}, bf16[96,768]{1,0:T(8,128)(2,1)}) custom-call(s32[3]{0:T(128)} %pad_add_fusion.1.sc, bf16[192,768]{1,0:T(8,128)(2,1)} %wq.1, bf16[192,768]{1,0:T(8,128)(2,1)} %wk.1, bf16[192,768]{1,0:T(8,128)(2,1)} %wv.1, ...), custom_call_target="tpu_custom_call" | custom-call | bytes 4634636 | tf_op jit(solution)/shard_map/pick_weights/pallas_call | solution.py:373
  15.9 3.7 %collective-permute-start.5 = (bf16[112,576]{1,0:T(8,128)(2,1)}, bf16[112,576]{1,0:T(8,128)(2,1)S(1)}, u32[]{:S(2)}, u32[]{:S(2)}) collective-permute-start(bf16[112,576]{1,0:T(8,128)(2,1)} %get-tuple-element.72), channel_id=1, source_target_pairs={{0,3},{1,0},{2,1},{3,2},{4,7},{5,4},{6,5},{7,6},{8,11},{9,8},{10,9... | collective-permute-start | bytes 387080 | tf_op jit(solution)/shard_map/ppermute | solution.py:909
  20.7 3.4 %collective-permute-done.5.refs_8_ = bf16[112,576]{1,0:T(8,128)(2,1)S(1)} collective-permute-done((bf16[112,576]{1,0:T(8,128)(2,1)}, bf16[112,576]{1,0:T(8,128)(2,1)S(1)}, u32[]{:S(2)}, u32[]{:S(2)}) %collective-permute-start.5) | collective-permute-done | bytes 129056 | tf_op jit(solution)/shard_map/ppermute | solution.py:909
  24.7 6.9 %collective-permute-done.4.refs_7_ = bf16[112,576]{1,0:T(8,128)(2,1)S(1)} collective-permute-done((bf16[112,576]{1,0:T(8,128)(2,1)}, bf16[112,576]{1,0:T(8,128)(2,1)S(1)}, u32[]{:S(2)}, u32[]{:S(2)}) %collective-permute-start.4) | collective-permute-done | bytes 129056 | tf_op jit(solution)/shard_map/ppermute | solution.py:909
  34.9 1.9 collective-permute-start.14
  36.8 1.9 collective-permute-start.22
  39.4 4.5 %project.1 = (bf16[512,768]{1,0:T(8,128)(2,1)}, bf16[768,768]{1,0:T(8,128)(2,1)}, f32[16,768]{1,0:T(8,128)}) custom-call(s32[3]{0:T(128)} %pad_add_fusion.1.sc, bf16[128,768]{1,0:T(8,128)(2,1)} %bitcast.82, bf16[128,768]{1,0:T(8,128)(2,1)} %copy-done.50, bf16[128,768]{1,0:T(8,128)(2,1)} %copy-done.49, bf16[128,768]{1,0:T(8,128)(2,1)} %copy-done.48, ...), custom_call_target="tpu_custom_call" | custom-call | flops 603979776 | bytes 3805196 | tf_op jit(solution)/shard_map/project/pallas_call | solution.py:373
  47.9 9.5 %attend.1 = (bf16[512,192]{1,0:T(8,128)(2,1)}, bf16[512,192]{1,0:T(8,128)(2,1)}, bf16[3,512,256]{2,1,0:T(8,128)(2,1)}, f32[12,128,128]{2,1,0:T(8,128)}) custom-call(bf16[512,768]{1,0:T(8,128)(2,1)} %get-tuple-element.73.own, bf16[512,768]{1,0:T(8,128)(2,1)} %copy-done.65, s32[8,512]{1,0:T(8,128)} %pad.9.clone.posr, s32[512,8]{1,0:T(8,128)} %pad_bitcast_fusion.posc, ...), custom_call_target="tpu_custom_call" | custom-call | flops 1610612736 | bytes 3588096 | tf_op jit(solution)/shard_map/attend/pallas_call | solution.py:373
  59.0 14.9 %collective-permute-done.21.refs_18_.refs_5_.refs_8_ = bf16[192,768]{1,0:T(8,128)(2,1)S(1)} collective-permute-done((bf16[192,768]{1,0:T(8,128)(2,1)S(1)}, bf16[192,768]{1,0:T(8,128)(2,1)S(1)}, u32[]{:S(2)}, u32[]{:S(2)}) %collective-permute-start.21) | collective-permute-done | bytes 294944 | tf_op jit(solution)/shard_map/ppermute | solution.py:909
  79.1 6.5 %collective-permute-done.13.refs_3_.refs_7_ = bf16[512,192]{1,0:T(8,128)(2,1)S(1)} collective-permute-done((bf16[512,192]{1,0:T(8,128)(2,1)S(1)}, bf16[512,192]{1,0:T(8,128)(2,1)S(1)}, u32[]{:S(2)}, u32[]{:S(2)}) %collective-permute-start.13) | collective-permute-done | bytes 196640 | tf_op jit(solution)/shard_map/ppermute | solution.py:904
  85.7 5.1 %collective-permute-done.12.refs_2_.refs_6_ = bf16[512,192]{1,0:T(8,128)(2,1)S(1)} collective-permute-done((bf16[512,192]{1,0:T(8,128)(2,1)S(1)}, bf16[512,192]{1,0:T(8,128)(2,1)S(1)}, u32[]{:S(2)}, u32[]{:S(2)}) %collective-permute-start.12) | collective-permute-done | bytes 196640 | tf_op jit(solution)/shard_map/ppermute | solution.py:904
  91.6 6.8 %mlp_up.1 = (f32[512,768]{1,0:T(8,128)}, bf16[512,768]{1,0:T(8,128)(2,1)}, f32[128,768]{1,0:T(8,128)}, f32[128,768]{1,0:T(8,128)}, f32[128,128]{1,0:T(8,128)}) custom-call(s32[3]{0:T(128)} %pad_add_fusion.1.sc, bf16[512,192]{1,0:T(8,128)(2,1)} %copy-done.11, bf16[512,192]{1,0:T(8,128)(2,1)} %copy-done.33, bf16[512,192]{1,0:T(8,128)(2,1)} %copy-done.32, ...), custom_call_target="tpu_custom_call" | custom-call | flops 1207959552 | bytes 8077324 | tf_op jit(solution)/shard_map/mlp_up/pallas_call | solution.py:373
  98.5 4.9 %mlp_down.1 = (f32[128,768]{1,0:T(8,128)}, bf16[128,768]{1,0:T(8,128)(2,1)}, bf16[128,768]{1,0:T(8,128)(2,1)}, bf16[128,768]{1,0:T(8,128)(2,1)}, bf16[512,768]{1,0:T(8,128)(2,1)}) custom-call(s32[3]{0:T(128)} %pad_add_fusion.1.sc, f32[512,768]{1,0:T(8,128)} %get-tuple-element.80.refs_0_, f32[128,768]{1,0:T(8,128)} %get-tuple-element.81.refs_1_, ...), custom_call_target="tpu_custom_call" | custom-call | flops 603979776 | bytes 6733836 | tf_op jit(solution)/shard_map/mlp_down/pallas_call | solution.py:373
  106.9 4.5 %collective-permute-done.26.refs_1_ = bf16[128,768]{1,0:T(8,128)(2,1)S(1)} collective-permute-done((bf16[128,768]{1,0:T(8,128)(2,1)}, bf16[128,768]{1,0:T(8,128)(2,1)S(1)}, u32[]{:S(2)}, u32[]{:S(2)}) %collective-permute-start.26) | collective-permute-done | bytes 196640 | tf_op jit(solution)/shard_map/ppermute | solution.py:904
  111.4 3.6 %collective-permute-done.27.refs_2_ = bf16[128,768]{1,0:T(8,128)(2,1)S(1)} collective-permute-done((bf16[128,768]{1,0:T(8,128)(2,1)}, bf16[128,768]{1,0:T(8,128)(2,1)S(1)}, u32[]{:S(2)}, u32[]{:S(2)}) %collective-permute-start.27) | collective-permute-done | bytes 196640 | tf_op jit(solution)/shard_map/ppermute | solution.py:904
  115.7 2.5 norm_two.1
  121.7 1.7 fusion.3.refs_4_
  123.4 3.8 %collective-permute-done.31.refs_3_ = bf16[144,768]{1,0:T(8,128)(2,1)S(1)} collective-permute-done((bf16[144,768]{1,0:T(8,128)(2,1)}, bf16[144,768]{1,0:T(8,128)(2,1)S(1)}, u32[]{:S(2)}, u32[]{:S(2)}) %collective-permute-start.31) | collective-permute-done | bytes 221216 | tf_op jit(solution)/shard_map/ppermute | solution.py:904
  127.2 2.3 collective-permute-done.30.refs_2_
  131.1 6.6 %mlp_back.1 = (f32[128,768]{1,0:T(8,128)}, bf16[128,768]{1,0:T(8,128)(2,1)}, bf16[128,768]{1,0:T(8,128)(2,1)}, bf16[128,768]{1,0:T(8,128)(2,1)}, bf16[512,768]{1,0:T(8,128)(2,1)}) custom-call(s32[3]{0:T(128)} %pad_add_fusion.1.sc, bf16[144,768]{1,0:T(8,128)(2,1)} %get-tuple-element.87.refs_0_, bf16[144,768]{1,0:T(8,128)(2,1)} %copy-done.39, ...), custom_call_target="tpu_custom_call" | custom-call | flops 1207959552 | bytes 7471116 | tf_op jit(solution)/shard_map/mlp_back/pallas_call | solution.py:373
  137.7 2.2 collective-permute-start.32
  141.4 5.6 %mlp_grads.1 = (f32[4,192,768]{2,1,0:T(8,128)}, bf16[4,192,768]{2,1,0:T(8,128)(2,1)}, f32[8,768]{1,0:T(8,128)}) custom-call(s32[3]{0:T(128)} %pad_add_fusion.1.sc, bf16[144,768]{1,0:T(8,128)(2,1)} %get-tuple-element.87.refs_0_, bf16[144,768]{1,0:T(8,128)(2,1)} %copy-done.39, bf16[144,768]{1,0:T(8,128)(2,1)} %copy-done.38, bf16[144,768]{1,0:T(8,128)(2,1)} %copy-done.37, ...), custom_call_target="tpu_custom_call" | custom-call | flops 1207959552 | bytes 6807564 | tf_op jit(solution)/shard_map/mlp_grads/pallas_call | solution.py:373
  147.0 3.8 %collective-permute-done.33.refs_2_ = bf16[128,768]{1,0:T(8,128)(2,1)S(1)} collective-permute-done((bf16[128,768]{1,0:T(8,128)(2,1)}, bf16[128,768]{1,0:T(8,128)(2,1)S(1)}, u32[]{:S(2)}, u32[]{:S(2)}) %collective-permute-start.33) | collective-permute-done | bytes 196640 | tf_op jit(solution)/shard_map/ppermute | solution.py:904
  151.6 2.6 norm_one.1
  156.0 1.7 collective-permute-start.35
  157.7 6.0 %collective-permute-done.37.refs_3_ = bf16[144,768]{1,0:T(8,128)(2,1)S(1)} collective-permute-done((bf16[144,768]{1,0:T(8,128)(2,1)}, bf16[144,768]{1,0:T(8,128)(2,1)S(1)}, u32[]{:S(2)}, u32[]{:S(2)}) %collective-permute-start.37) | collective-permute-done | bytes 221216 | tf_op jit(solution)/shard_map/ppermute | solution.py:904
  163.7 2.5 collective-permute-done.36.refs_2_
  167.6 3.7 %context_back.1.own = bf16[512,192]{1,0:T(8,128)(2,1)} custom-call(s32[3]{0:T(128)} %pad_add_fusion.1.sc, bf16[144,768]{1,0:T(8,128)(2,1)} %get-tuple-element.96.refs_0_, bf16[144,768]{1,0:T(8,128)(2,1)} %copy-done.36, bf16[144,768]{1,0:T(8,128)(2,1)} %copy-done.35, bf16[144,768]{1,0:T(8,128)(2,1)} %copy-done.34, bf16[192,768]{1,0:T(8,128)(2,1)} %refs_4_.1, ...), custom_call_target="tpu_custom_call" | custom-call | flops 150994944 | bytes 2261004 | tf_op jit(solution)/shard_map/context_back/pallas_call | solution.py:373
  171.4 3.3 %out_grads.1 = (f32[4,48,768]{2,1,0:T(8,128)}, bf16[4,48,768]{2,1,0:T(8,128)(2,1)}) custom-call(s32[3]{0:T(128)} %pad_add_fusion.1.sc, bf16[144,768]{1,0:T(8,128)(2,1)} %get-tuple-element.96.refs_0_, bf16[144,768]{1,0:T(8,128)(2,1)} %copy-done.36, bf16[144,768]{1,0:T(8,128)(2,1)} %copy-done.35, bf16[144,768]{1,0:T(8,128)(2,1)} %copy-done.34, ...), custom_call_target="tpu_custom_call" | custom-call | flops 603979776 | bytes 2580492 | tf_op jit(solution)/shard_map/out_grads/pallas_call | solution.py:373
  175.9 8.8 %attend_back.1 = (bf16[512,768]{1,0:T(8,128)(2,1)}, bf16[512,768]{1,0:T(8,128)(2,1)}) custom-call(bf16[512,192]{1,0:T(8,128)(2,1)} %context_back.1.own, bf16[512,192]{1,0:T(8,128)(2,1)} %copy-done.67, s32[8,512]{1,0:T(8,128)} %pad.9.clone.posr, s32[512,8]{1,0:T(8,128)} %pad_bitcast_fusion.posc, bf16[3,512,256]{2,1,0:T(8,128)(2,1)} %get-tuple-element.97.kept, ...), custom_call_target="tpu_custom_call" | custom-call | flops 1610612736 | bytes 3571712 | tf_op jit(solution)/shard_map/attend_back/pallas_call | solution.py:373
  184.9 3.8 %collective-permute-start.57 = (bf16[48,768]{1,0:T(8,128)(2,1)S(1)}, bf16[48,768]{1,0:T(8,128)(2,1)}, u32[]{:S(2)}, u32[]{:S(2)}) collective-permute-start(bf16[48,768]{1,0:T(8,128)(2,1)S(1)} %get-tuple-element.132), channel_id=1, source_target_pairs={{0,3},{1,0},{2,1},{3,2},{4,7},{5,4},{6,5},{7,6},{8,11},{9,8},{10,9... | collective-permute-start | bytes 221192 | tf_op jit(solution)/shard_map/ppermute | solution.py:909
  190.3 3.3 %collective-permute-start.68 = (bf16[192,768]{1,0:T(8,128)(2,1)}, bf16[192,768]{1,0:T(8,128)(2,1)}, u32[]{:S(2)}, u32[]{:S(2)}) collective-permute-start(bf16[192,768]{1,0:T(8,128)(2,1)} %get-tuple-element.126), channel_id=1, source_target_pairs={{0,3},{1,0},{2,1},{3,2},{4,7},{5,4},{6,5},{7,6},{8,11},{9,8},{10,9... | collective-permute-start | bytes 884744 | tf_op jit(solution)/shard_map/ppermute | solution.py:909
  193.6 3.7 %project_back.1 = (f32[128,768]{1,0:T(8,128)}, bf16[128,768]{1,0:T(8,128)(2,1)}, bf16[128,768]{1,0:T(8,128)(2,1)}, bf16[128,768]{1,0:T(8,128)(2,1)}, bf16[512,768]{1,0:T(8,128)(2,1)}) custom-call(bf16[512,768]{1,0:T(8,128)(2,1)} %get-tuple-element.99.refs_0_, bf16[512,768]{1,0:T(8,128)(2,1)} %copy-done.12, bf16[768,768]{1,0:T(8,128)(2,1)} %get-tuple-element.101.refs_2_), custom_call_target="tpu_custom_call" | custom-call | flops 603979776 | bytes 4521984 | tf_op jit(solution)/shard_map/project_back/pallas_call | solution.py:373
  197.3 3.6 %project_grads.1 = (f32[4,112,576]{2,1,0:T(8,128)}, bf16[4,112,576]{2,1,0:T(8,128)(2,1)}) custom-call(s32[3]{0:T(128)} %pad_add_fusion.1.sc, bf16[128,768]{1,0:T(8,128)(2,1)} %bitcast.84, bf16[128,768]{1,0:T(8,128)(2,1)} %copy-done.50, bf16[128,768]{1,0:T(8,128)(2,1)} %copy-done.49, bf16[128,768]{1,0:T(8,128)(2,1)} %copy-done.48, ...), custom_call_target="tpu_custom_call" | custom-call | flops 603979776 | bytes 3121164 | tf_op jit(solution)/shard_map/project_grads/pallas_call | solution.py:373
  205.0 3.8 %collective-permute-done.60.refs_3_ = bf16[48,768]{1,0:T(8,128)(2,1)S(1)} collective-permute-done((bf16[48,768]{1,0:T(8,128)(2,1)S(1)}, bf16[48,768]{1,0:T(8,128)(2,1)S(1)}, u32[]{:S(2)}, u32[]{:S(2)}) %collective-permute-start.60) | collective-permute-done | bytes 73760 | tf_op jit(solution)/shard_map/ppermute | solution.py:904
  209.4 3.7 %collective-permute-done.59.refs_2_ = bf16[48,768]{1,0:T(8,128)(2,1)S(1)} collective-permute-done((bf16[48,768]{1,0:T(8,128)(2,1)S(1)}, bf16[48,768]{1,0:T(8,128)(2,1)S(1)}, u32[]{:S(2)}, u32[]{:S(2)}) %collective-permute-start.59) | collective-permute-done | bytes 73760 | tf_op jit(solution)/shard_map/ppermute | solution.py:904
  213.7 3.8 %collective-permute-done.58.refs_1_ = bf16[48,768]{1,0:T(8,128)(2,1)S(1)} collective-permute-done((bf16[48,768]{1,0:T(8,128)(2,1)S(1)}, bf16[48,768]{1,0:T(8,128)(2,1)S(1)}, u32[]{:S(2)}, u32[]{:S(2)}) %collective-permute-start.58) | collective-permute-done | bytes 73760 | tf_op jit(solution)/shard_map/ppermute | solution.py:904
  218.1 2.6 collective-permute-done.67
  226.4 3.3 %collective-permute-done.40 = bf16[128,768]{1,0:T(8,128)(2,1)S(1)} collective-permute-done((bf16[128,768]{1,0:T(8,128)(2,1)S(1)}, bf16[128,768]{1,0:T(8,128)(2,1)S(1)}, u32[]{:S(2)}, u32[]{:S(2)}) %collective-permute-start.40) | collective-permute-done | bytes 196640 | tf_op jit(solution)/shard_map/ppermute | solution.py:904
  229.7 1.8 collective-permute-start.46
  231.5 5.2 %collective-permute-done.41 = bf16[128,768]{1,0:T(8,128)(2,1)S(1)} collective-permute-done((bf16[128,768]{1,0:T(8,128)(2,1)S(1)}, bf16[128,768]{1,0:T(8,128)(2,1)S(1)}, u32[]{:S(2)}, u32[]{:S(2)}) %collective-permute-start.41) | collective-permute-done | bytes 196640 | tf_op jit(solution)/shard_map/ppermute | solution.py:904
  238.2 4.0 %collective-permute-done.70.refs_2_ = bf16[192,768]{1,0:T(8,128)(2,1)S(1)} collective-permute-done((bf16[192,768]{1,0:T(8,128)(2,1)S(1)}, bf16[192,768]{1,0:T(8,128)(2,1)S(1)}, u32[]{:S(2)}, u32[]{:S(2)}) %collective-permute-start.70) | collective-permute-done | bytes 294944 | tf_op jit(solution)/shard_map/ppermute | solution.py:904
  242.8 2.6 out_lay.1
  248.8 4.6 %collective-permute-done.42 = bf16[128,768]{1,0:T(8,128)(2,1)S(1)} collective-permute-done((bf16[128,768]{1,0:T(8,128)(2,1)S(1)}, bf16[128,768]{1,0:T(8,128)(2,1)S(1)}, u32[]{:S(2)}, u32[]{:S(2)}) %collective-permute-start.42) | collective-permute-done | bytes 196640 | tf_op jit(solution)/shard_map/ppermute | solution.py:904
  262.7 1.7 fusion.26
  264.5 4.8 %mlp_lay.1 = (f32[192,3072]{1,0:T(8,128)}, f32[768,768]{1,0:T(8,128)}) custom-call(s32[3]{0:T(128)} %pad_add_fusion.1.sc, bf16[192,768]{1,0:T(8,128)(2,1)} %copy-done.9, bf16[192,768]{1,0:T(8,128)(2,1)} %copy-done.25, bf16[192,768]{1,0:T(8,128)(2,1)} %copy-done.24, bf16[192,768]{1,0:T(8,128)(2,1)} %copy-done.23, bf16[192,768]{1,0:T(8,128)(2,1)} %copy-done.26, ...), custom_call_target="tpu_custom_call" | custom-call | bytes 7077900 | tf_op jit(solution)/shard_map/mlp_lay/pallas_call | solution.py:373
  270.7 3.5 %project_lay.1 = (f32[192,768]{1,0:T(8,128)}, f32[192,768]{1,0:T(8,128)}, f32[192,768]{1,0:T(8,128)}, f32[8,192]{1,0:T(8,128)}) custom-call(s32[3]{0:T(128)} %pad_add_fusion.1.sc, bf16[112,576]{1,0:T(8,128)(2,1)} %copy-done.20, bf16[112,576]{1,0:T(8,128)(2,1)} %copy-done.52, bf16[112,576]{1,0:T(8,128)(2,1)} %copy-done.51, ...), custom_call_target="tpu_custom_call" | custom-call | bytes 2807820 | tf_op jit(solution)/shard_map/project_lay/pallas_call | solution.py:373
  (316 shorter events, 71.8 us)
Async XLA Ops:
  0.7 31.4 %collective-permute-start.2 = (bf16[128,768]{1,0:T(8,128)(2,1)}, bf16[128,768]{1,0:T(8,128)(2,1)S(1)}, u32[]{:S(2)}, u32[]{:S(2)}) collective-permute-start(bf16[128,768]{1,0:T(8,128)(2,1)} %bitcast.80), channel_id=1, source_target_pairs={{0,24},{4,28},{8,16},{12,20},{16,8},{20,12},{24,0},{28,4},{1,25},{... | collective-permute-start | bytes 589832 | tf_op jit(solution)/shard_map/ppermute | solution.py:904
  4.6 27.6 %collective-permute-start.1 = (bf16[128,768]{1,0:T(8,128)(2,1)}, bf16[128,768]{1,0:T(8,128)(2,1)S(1)}, u32[]{:S(2)}, u32[]{:S(2)}) collective-permute-start(bf16[128,768]{1,0:T(8,128)(2,1)} %bitcast.81), channel_id=1, source_target_pairs={{0,16},{4,20},{8,24},{12,28},{16,0},{20,4},{24,8},{28,12},{1,17},{... | collective-permute-start | bytes 589832 | tf_op jit(solution)/shard_map/ppermute | solution.py:904
  19.6 11.9 %collective-permute-start.4 = (bf16[112,576]{1,0:T(8,128)(2,1)}, bf16[112,576]{1,0:T(8,128)(2,1)S(1)}, u32[]{:S(2)}, u32[]{:S(2)}) collective-permute-start(bf16[112,576]{1,0:T(8,128)(2,1)} %get-tuple-element.72), channel_id=1, source_target_pairs={{0,2},{1,3},{2,0},{3,1},{4,6},{5,7},{6,4},{7,5},{8,10},{9,11},{10,... | collective-permute-start | bytes 387080 | tf_op jit(solution)/shard_map/ppermute | solution.py:909
  19.6 11.9 %collective-permute-start.3 = (bf16[112,576]{1,0:T(8,128)(2,1)}, bf16[112,576]{1,0:T(8,128)(2,1)S(1)}, u32[]{:S(2)}, u32[]{:S(2)}) collective-permute-start(bf16[112,576]{1,0:T(8,128)(2,1)} %get-tuple-element.72), channel_id=1, source_target_pairs={{0,1},{1,2},{2,3},{3,0},{4,5},{5,6},{6,7},{7,4},{8,9},{9,10},{10,1... | collective-permute-start | bytes 387080 | tf_op jit(solution)/shard_map/ppermute | solution.py:909
  24.1 9.5 %collective-permute-start = (bf16[128,768]{1,0:T(8,128)(2,1)S(1)}, bf16[128,768]{1,0:T(8,128)(2,1)S(1)}, u32[]{:S(2)}, u32[]{:S(2)}) collective-permute-start(bf16[128,768]{1,0:T(8,128)(2,1)S(1)} %bitcast.85), channel_id=1, source_target_pairs={{0,8},{4,12},{8,0},{12,4},{16,24},{20,28},{24,16},{28,20},{1,9},{5... | collective-permute-start | bytes 589832 | tf_op jit(solution)/shard_map/ppermute | solution.py:904
  32.2 14.3 %collective-permute-start.16 = (bf16[96,768]{1,0:T(8,128)(2,1)}, bf16[96,768]{1,0:T(8,128)(2,1)S(1)}, u32[]{:S(2)}, u32[]{:S(2)}) collective-permute-start(bf16[96,768]{1,0:T(8,128)(2,1)} %get-tuple-element.78), channel_id=1, source_target_pairs={{0,3},{1,0},{2,1},{3,2},{4,7},{5,4},{6,5},{7,6},{8,11},{9,8},{10,9... | collective-permute-start | bytes 442376 | tf_op jit(solution)/shard_map/ppermute | solution.py:909
  33.6 23.8 %collective-permute-start.15 = (bf16[96,768]{1,0:T(8,128)(2,1)}, bf16[96,768]{1,0:T(8,128)(2,1)S(1)}, u32[]{:S(2)}, u32[]{:S(2)}) collective-permute-start(bf16[96,768]{1,0:T(8,128)(2,1)} %get-tuple-element.78), channel_id=1, source_target_pairs={{0,2},{1,3},{2,0},{3,1},{4,6},{5,7},{6,4},{7,5},{8,10},{9,11},{10,... | collective-permute-start | bytes 442376 | tf_op jit(solution)/shard_map/ppermute | solution.py:909
  34.9 22.8 %collective-permute-start.14 = (bf16[96,768]{1,0:T(8,128)(2,1)}, bf16[96,768]{1,0:T(8,128)(2,1)S(1)}, u32[]{:S(2)}, u32[]{:S(2)}) collective-permute-start(bf16[96,768]{1,0:T(8,128)(2,1)} %get-tuple-element.78), channel_id=1, source_target_pairs={{0,1},{1,2},{2,3},{3,0},{4,5},{5,6},{6,7},{7,4},{8,9},{9,10},{10,1... | collective-permute-start | bytes 442376 | tf_op jit(solution)/shard_map/ppermute | solution.py:909
  36.8 21.2 %collective-permute-start.22 = (bf16[192,768]{1,0:T(8,128)(2,1)}, bf16[192,768]{1,0:T(8,128)(2,1)S(1)}, u32[]{:S(2)}, u32[]{:S(2)}) collective-permute-start(bf16[192,768]{1,0:T(8,128)(2,1)} %get-tuple-element.79), channel_id=1, source_target_pairs={{0,3},{1,0},{2,1},{3,2},{4,7},{5,4},{6,5},{7,6},{8,11},{9,8},{10,9... | collective-permute-start | bytes 884744 | tf_op jit(solution)/shard_map/ppermute | solution.py:909
  46.6 27.3 %collective-permute-start.21 = (bf16[192,768]{1,0:T(8,128)(2,1)S(1)}, bf16[192,768]{1,0:T(8,128)(2,1)S(1)}, u32[]{:S(2)}, u32[]{:S(2)}) collective-permute-start(bf16[192,768]{1,0:T(8,128)(2,1)S(1)} %copy-done.66), channel_id=1, source_target_pairs={{0,2},{1,3},{2,0},{3,1},{4,6},{5,7},{6,4},{7,5},{8,10},{9,11},{10,... | collective-permute-start | bytes 884744 | tf_op jit(solution)/shard_map/ppermute | solution.py:909
  46.7 27.2 %collective-permute-start.20 = (bf16[192,768]{1,0:T(8,128)(2,1)S(1)}, bf16[192,768]{1,0:T(8,128)(2,1)S(1)}, u32[]{:S(2)}, u32[]{:S(2)}) collective-permute-start(bf16[192,768]{1,0:T(8,128)(2,1)S(1)} %copy-done.66), channel_id=1, source_target_pairs={{0,1},{1,2},{2,3},{3,0},{4,5},{5,6},{6,7},{7,4},{8,9},{9,10},{10,1... | collective-permute-start | bytes 884744 | tf_op jit(solution)/shard_map/ppermute | solution.py:909
  57.7 16.8 %collective-permute-start.10 = (bf16[512,192]{1,0:T(8,128)(2,1)}, bf16[512,192]{1,0:T(8,128)(2,1)S(1)}, u32[]{:S(2)}, u32[]{:S(2)}) collective-permute-start(bf16[512,192]{1,0:T(8,128)(2,1)} %get-tuple-element.75), channel_id=1, source_target_pairs={{0,4},{4,0},{8,12},{12,8},{16,20},{20,16},{24,28},{28,24},{1,5},{5... | collective-permute-start | bytes 589832 | tf_op jit(solution)/shard_map/ppermute | solution.py:899
  58.0 19.6 %collective-permute-start.25 = (bf16[192,768]{1,0:T(8,128)(2,1)S(1)}, bf16[192,768]{1,0:T(8,128)(2,1)S(1)}, u32[]{:S(2)}, u32[]{:S(2)}) collective-permute-start(bf16[192,768]{1,0:T(8,128)(2,1)S(1)} %collective-permute-done.22.refs_19_.refs_6_.refs_9_), channel_id=1, source_target_pairs={{0,4},{4,0},{8,12},{12,8},{16,20},{20,16},{24,28},{28,24},{1,5},{5... | collective-permute-start | bytes 884744 | tf_op jit(solution)/shard_map/ppermute | solution.py:899
  58.9 16.7 %collective-permute-start.18 = (bf16[96,768]{1,0:T(8,128)(2,1)S(1)}, bf16[96,768]{1,0:T(8,128)(2,1)S(1)}, u32[]{:S(2)}, u32[]{:S(2)}) collective-permute-start(bf16[96,768]{1,0:T(8,128)(2,1)S(1)} %collective-permute-done.15.refs_12_.refs_6_), channel_id=1, source_target_pairs={{0,4},{4,0},{8,12},{12,8},{16,20},{20,16},{24,28},{28,24},{1,5},{5... | collective-permute-start | bytes 442376 | tf_op jit(solution)/shard_map/ppermute | solution.py:899
  75.5 10.1 %collective-permute-start.13 = (bf16[512,192]{1,0:T(8,128)(2,1)S(1)}, bf16[512,192]{1,0:T(8,128)(2,1)S(1)}, u32[]{:S(2)}, u32[]{:S(2)}) collective-permute-start(bf16[512,192]{1,0:T(8,128)(2,1)S(1)} %add.172.refs_0_.refs_4_), channel_id=1, source_target_pairs={{0,24},{4,28},{8,16},{12,20},{16,8},{20,12},{24,0},{28,4},{1,25},{... | collective-permute-start | bytes 589832 | tf_op jit(solution)/shard_map/ppermute | solution.py:904
  77.1 13.7 %collective-permute-start.12 = (bf16[512,192]{1,0:T(8,128)(2,1)S(1)}, bf16[512,192]{1,0:T(8,128)(2,1)S(1)}, u32[]{:S(2)}, u32[]{:S(2)}) collective-permute-start(bf16[512,192]{1,0:T(8,128)(2,1)S(1)} %add.172.refs_0_.refs_4_), channel_id=1, source_target_pairs={{0,16},{4,20},{8,24},{12,28},{16,0},{20,4},{24,8},{28,12},{1,17},{... | collective-permute-start | bytes 589832 | tf_op jit(solution)/shard_map/ppermute | solution.py:904
  77.6 13.3 %collective-permute-start.11 = (bf16[512,192]{1,0:T(8,128)(2,1)S(1)}, bf16[512,192]{1,0:T(8,128)(2,1)S(1)}, u32[]{:S(2)}, u32[]{:S(2)}) collective-permute-start(bf16[512,192]{1,0:T(8,128)(2,1)S(1)} %add.172.refs_0_.refs_4_), channel_id=1, source_target_pairs={{0,8},{4,12},{8,0},{12,4},{16,24},{20,28},{24,16},{28,20},{1,9},{5... | collective-permute-start | bytes 589832 | tf_op jit(solution)/shard_map/ppermute | solution.py:904
  104.0 11.0 %collective-permute-start.27 = (bf16[128,768]{1,0:T(8,128)(2,1)}, bf16[128,768]{1,0:T(8,128)(2,1)S(1)}, u32[]{:S(2)}, u32[]{:S(2)}) collective-permute-start(bf16[128,768]{1,0:T(8,128)(2,1)} %get-tuple-element.84), channel_id=1, source_target_pairs={{0,16},{4,20},{8,24},{12,28},{16,0},{20,4},{24,8},{28,12},{1,17},{... | collective-permute-start | bytes 589832 | tf_op jit(solution)/shard_map/ppermute | solution.py:904
  105.5 9.5 %collective-permute-start.28 = (bf16[128,768]{1,0:T(8,128)(2,1)}, bf16[128,768]{1,0:T(8,128)(2,1)S(1)}, u32[]{:S(2)}, u32[]{:S(2)}) collective-permute-start(bf16[128,768]{1,0:T(8,128)(2,1)} %get-tuple-element.85), channel_id=1, source_target_pairs={{0,24},{4,28},{8,16},{12,20},{16,8},{20,12},{24,0},{28,4},{1,25},{... | collective-permute-start | bytes 589832 | tf_op jit(solution)/shard_map/ppermute | solution.py:904
  119.5 10.0 %collective-permute-start.30 = (bf16[144,768]{1,0:T(8,128)(2,1)}, bf16[144,768]{1,0:T(8,128)(2,1)S(1)}, u32[]{:S(2)}, u32[]{:S(2)}) collective-permute-start(bf16[144,768]{1,0:T(8,128)(2,1)} %get-tuple-element.87.refs_0_), channel_id=1, source_target_pairs={{0,16},{4,20},{8,24},{12,28},{16,0},{20,4},{24,8},{28,12},{1,17},{... | collective-permute-start | bytes 663560 | tf_op jit(solution)/shard_map/ppermute | solution.py:904
  121.2 9.2 %collective-permute-start.29 = (bf16[144,768]{1,0:T(8,128)(2,1)}, bf16[144,768]{1,0:T(8,128)(2,1)S(1)}, u32[]{:S(2)}, u32[]{:S(2)}) collective-permute-start(bf16[144,768]{1,0:T(8,128)(2,1)} %get-tuple-element.87.refs_0_), channel_id=1, source_target_pairs={{0,8},{4,12},{8,0},{12,4},{16,24},{20,28},{24,16},{28,20},{1,9},{5... | collective-permute-start | bytes 663560 | tf_op jit(solution)/shard_map/ppermute | solution.py:904
  137.7 9.3 %collective-permute-start.32 = (bf16[128,768]{1,0:T(8,128)(2,1)}, bf16[128,768]{1,0:T(8,128)(2,1)S(1)}, u32[]{:S(2)}, u32[]{:S(2)}) collective-permute-start(bf16[128,768]{1,0:T(8,128)(2,1)} %get-tuple-element.89), channel_id=1, source_target_pairs={{0,8},{4,12},{8,0},{12,4},{16,24},{20,28},{24,16},{28,20},{1,9},{5... | collective-permute-start | bytes 589832 | tf_op jit(solution)/shard_map/ppermute | solution.py:904
  139.8 11.0 %collective-permute-start.33 = (bf16[128,768]{1,0:T(8,128)(2,1)}, bf16[128,768]{1,0:T(8,128)(2,1)S(1)}, u32[]{:S(2)}, u32[]{:S(2)}) collective-permute-start(bf16[128,768]{1,0:T(8,128)(2,1)} %get-tuple-element.90), channel_id=1, source_target_pairs={{0,16},{4,20},{8,24},{12,28},{16,0},{20,4},{24,8},{28,12},{1,17},{... | collective-permute-start | bytes 589832 | tf_op jit(solution)/shard_map/ppermute | solution.py:904
  140.4 10.5 %collective-permute-start.34 = (bf16[128,768]{1,0:T(8,128)(2,1)}, bf16[128,768]{1,0:T(8,128)(2,1)S(1)}, u32[]{:S(2)}, u32[]{:S(2)}) collective-permute-start(bf16[128,768]{1,0:T(8,128)(2,1)} %get-tuple-element.91), channel_id=1, source_target_pairs={{0,24},{4,28},{8,16},{12,20},{16,8},{20,12},{24,0},{28,4},{1,25},{... | collective-permute-start | bytes 589832 | tf_op jit(solution)/shard_map/ppermute | solution.py:904
  146.9 41.8 %collective-permute-start.65 = (bf16[4,192,768]{2,1,0:T(8,128)(2,1)}, bf16[4,192,768]{2,1,0:T(8,128)(2,1)S(1)}, u32[]{:S(2)}, u32[]{:S(2)}) collective-permute-start(bf16[4,192,768]{2,1,0:T(8,128)(2,1)} %get-tuple-element.122), channel_id=1, source_target_pairs={{0,4},{4,0},{8,12},{12,8},{16,20},{20,16},{24,28},{28,24},{1,5},{5... | collective-permute-start | bytes 3538952 | tf_op jit(solution)/shard_map/ppermute | solution.py:899
  154.2 9.5 %collective-permute-start.37 = (bf16[144,768]{1,0:T(8,128)(2,1)}, bf16[144,768]{1,0:T(8,128)(2,1)S(1)}, u32[]{:S(2)}, u32[]{:S(2)}) collective-permute-start(bf16[144,768]{1,0:T(8,128)(2,1)} %get-tuple-element.96.refs_0_), channel_id=1, source_target_pairs={{0,24},{4,28},{8,16},{12,20},{16,8},{20,12},{24,0},{28,4},{1,25},{... | collective-permute-start | bytes 663560 | tf_op jit(solution)/shard_map/ppermute | solution.py:904
  155.6 10.6 %collective-permute-start.36 = (bf16[144,768]{1,0:T(8,128)(2,1)}, bf16[144,768]{1,0:T(8,128)(2,1)S(1)}, u32[]{:S(2)}, u32[]{:S(2)}) collective-permute-start(bf16[144,768]{1,0:T(8,128)(2,1)} %get-tuple-element.96.refs_0_), channel_id=1, source_target_pairs={{0,16},{4,20},{8,24},{12,28},{16,0},{20,4},{24,8},{28,12},{1,17},{... | collective-permute-start | bytes 663560 | tf_op jit(solution)/shard_map/ppermute | solution.py:904
  156.0 10.2 %collective-permute-start.35 = (bf16[144,768]{1,0:T(8,128)(2,1)}, bf16[144,768]{1,0:T(8,128)(2,1)S(1)}, u32[]{:S(2)}, u32[]{:S(2)}) collective-permute-start(bf16[144,768]{1,0:T(8,128)(2,1)} %get-tuple-element.96.refs_0_), channel_id=1, source_target_pairs={{0,8},{4,12},{8,0},{12,4},{16,24},{20,28},{24,16},{28,20},{1,9},{5... | collective-permute-start | bytes 663560 | tf_op jit(solution)/shard_map/ppermute | solution.py:904
  174.7 10.1 %collective-permute-start.54 = (bf16[4,48,768]{2,1,0:T(8,128)(2,1)}, bf16[4,48,768]{2,1,0:T(8,128)(2,1)S(1)}, u32[]{:S(2)}, u32[]{:S(2)}) collective-permute-start(bf16[4,48,768]{2,1,0:T(8,128)(2,1)} %get-tuple-element.117), channel_id=1, source_target_pairs={{0,4},{4,0},{8,12},{12,8},{16,20},{20,16},{24,28},{28,24},{1,5},{5... | collective-permute-start | bytes 884744 | tf_op jit(solution)/shard_map/ppermute | solution.py:899
  184.8 16.1 %collective-permute-start.55 = (bf16[48,768]{1,0:T(8,128)(2,1)S(1)}, bf16[48,768]{1,0:T(8,128)(2,1)S(1)}, u32[]{:S(2)}, u32[]{:S(2)}) collective-permute-start(bf16[48,768]{1,0:T(8,128)(2,1)S(1)} %get-tuple-element.131), channel_id=1, source_target_pairs={{0,1},{1,2},{2,3},{3,0},{4,5},{5,6},{6,7},{7,4},{8,9},{9,10},{10,1... | collective-permute-start | bytes 221192 | tf_op jit(solution)/shard_map/ppermute | solution.py:909
  184.9 17.2 %collective-permute-start.57 = (bf16[48,768]{1,0:T(8,128)(2,1)S(1)}, bf16[48,768]{1,0:T(8,128)(2,1)}, u32[]{:S(2)}, u32[]{:S(2)}) collective-permute-start(bf16[48,768]{1,0:T(8,128)(2,1)S(1)} %get-tuple-element.132), channel_id=1, source_target_pairs={{0,3},{1,0},{2,1},{3,2},{4,7},{5,4},{6,5},{7,6},{8,11},{9,8},{10,9... | collective-permute-start | bytes 221192 | tf_op jit(solution)/shard_map/ppermute | solution.py:909
  188.7 13.7 %collective-permute-start.56 = (bf16[48,768]{1,0:T(8,128)(2,1)S(1)}, bf16[48,768]{1,0:T(8,128)(2,1)}, u32[]{:S(2)}, u32[]{:S(2)}) collective-permute-start(bf16[48,768]{1,0:T(8,128)(2,1)S(1)} %get-tuple-element.133), channel_id=1, source_target_pairs={{0,2},{1,3},{2,0},{3,1},{4,6},{5,7},{6,4},{7,5},{8,10},{9,11},{10,... | collective-permute-start | bytes 221192 | tf_op jit(solution)/shard_map/ppermute | solution.py:909
  189.7 27.7 %collective-permute-start.66 = (bf16[192,768]{1,0:T(8,128)(2,1)}, bf16[192,768]{1,0:T(8,128)(2,1)}, u32[]{:S(2)}, u32[]{:S(2)}) collective-permute-start(bf16[192,768]{1,0:T(8,128)(2,1)} %get-tuple-element.125), channel_id=1, source_target_pairs={{0,1},{1,2},{2,3},{3,0},{4,5},{5,6},{6,7},{7,4},{8,9},{9,10},{10,1... | collective-permute-start | bytes 884744 | tf_op jit(solution)/shard_map/ppermute | solution.py:909
  190.3 27.7 %collective-permute-start.68 = (bf16[192,768]{1,0:T(8,128)(2,1)}, bf16[192,768]{1,0:T(8,128)(2,1)}, u32[]{:S(2)}, u32[]{:S(2)}) collective-permute-start(bf16[192,768]{1,0:T(8,128)(2,1)} %get-tuple-element.126), channel_id=1, source_target_pairs={{0,3},{1,0},{2,1},{3,2},{4,7},{5,4},{6,5},{7,6},{8,11},{9,8},{10,9... | collective-permute-start | bytes 884744 | tf_op jit(solution)/shard_map/ppermute | solution.py:909
  200.9 19.7 %collective-permute-start.67 = (bf16[192,768]{1,0:T(8,128)(2,1)S(1)}, bf16[192,768]{1,0:T(8,128)(2,1)S(1)}, u32[]{:S(2)}, u32[]{:S(2)}) collective-permute-start(bf16[192,768]{1,0:T(8,128)(2,1)S(1)} %get-tuple-element.127), channel_id=1, source_target_pairs={{0,2},{1,3},{2,0},{3,1},{4,6},{5,7},{6,4},{7,5},{8,10},{9,11},{10,... | collective-permute-start | bytes 884744 | tf_op jit(solution)/shard_map/ppermute | solution.py:909
  202.1 23.4 %collective-permute-start.43 = (bf16[4,112,576]{2,1,0:T(8,128)(2,1)}, bf16[4,112,576]{2,1,0:T(8,128)(2,1)S(1)}, u32[]{:S(2)}, u32[]{:S(2)}) collective-permute-start(bf16[4,112,576]{2,1,0:T(8,128)(2,1)} %get-tuple-element.108), channel_id=1, source_target_pairs={{0,4},{4,0},{8,12},{12,8},{16,20},{20,16},{24,28},{28,24},{1,5},{5... | collective-permute-start | bytes 1548296 | tf_op jit(solution)/shard_map/ppermute | solution.py:899
  222.5 14.1 %collective-permute-start.41 = (bf16[128,768]{1,0:T(8,128)(2,1)S(1)}, bf16[128,768]{1,0:T(8,128)(2,1)S(1)}, u32[]{:S(2)}, u32[]{:S(2)}) collective-permute-start(bf16[128,768]{1,0:T(8,128)(2,1)S(1)} %copy-done.69), channel_id=1, source_target_pairs={{0,16},{4,20},{8,24},{12,28},{16,0},{20,4},{24,8},{28,12},{1,17},{... | collective-permute-start | bytes 589832 | tf_op jit(solution)/shard_map/ppermute | solution.py:904
  224.1 12.5 %collective-permute-start.71 = (bf16[192,768]{1,0:T(8,128)(2,1)S(1)}, bf16[192,768]{1,0:T(8,128)(2,1)S(1)}, u32[]{:S(2)}, u32[]{:S(2)}) collective-permute-start(bf16[192,768]{1,0:T(8,128)(2,1)S(1)} %fusion.6.refs_0_), channel_id=1, source_target_pairs={{0,24},{4,28},{8,16},{12,20},{16,8},{20,12},{24,0},{28,4},{1,25},{... | collective-permute-start | bytes 884744 | tf_op jit(solution)/shard_map/ppermute | solution.py:904
  225.5 16.7 %collective-permute-start.70 = (bf16[192,768]{1,0:T(8,128)(2,1)S(1)}, bf16[192,768]{1,0:T(8,128)(2,1)S(1)}, u32[]{:S(2)}, u32[]{:S(2)}) collective-permute-start(bf16[192,768]{1,0:T(8,128)(2,1)S(1)} %fusion.6.refs_0_), channel_id=1, source_target_pairs={{0,16},{4,20},{8,24},{12,28},{16,0},{20,4},{24,8},{28,12},{1,17},{... | collective-permute-start | bytes 884744 | tf_op jit(solution)/shard_map/ppermute | solution.py:904
  226.3 16.0 %collective-permute-start.44 = (bf16[112,576]{1,0:T(8,128)(2,1)S(1)}, bf16[112,576]{1,0:T(8,128)(2,1)S(1)}, u32[]{:S(2)}, u32[]{:S(2)}) collective-permute-start(bf16[112,576]{1,0:T(8,128)(2,1)S(1)} %get-tuple-element.128), channel_id=1, source_target_pairs={{0,1},{1,2},{2,3},{3,0},{4,5},{5,6},{6,7},{7,4},{8,9},{9,10},{10,1... | collective-permute-start | bytes 387080 | tf_op jit(solution)/shard_map/ppermute | solution.py:909
  229.7 15.8 %collective-permute-start.46 = (bf16[112,576]{1,0:T(8,128)(2,1)S(1)}, bf16[112,576]{1,0:T(8,128)(2,1)S(1)}, u32[]{:S(2)}, u32[]{:S(2)}) collective-permute-start(bf16[112,576]{1,0:T(8,128)(2,1)S(1)} %get-tuple-element.129), channel_id=1, source_target_pairs={{0,3},{1,0},{2,1},{3,2},{4,7},{5,4},{6,5},{7,6},{8,11},{9,8},{10,9... | collective-permute-start | bytes 387080 | tf_op jit(solution)/shard_map/ppermute | solution.py:909
  236.6 10.5 %collective-permute-start.45 = (bf16[112,576]{1,0:T(8,128)(2,1)S(1)}, bf16[112,576]{1,0:T(8,128)(2,1)S(1)}, u32[]{:S(2)}, u32[]{:S(2)}) collective-permute-start(bf16[112,576]{1,0:T(8,128)(2,1)S(1)} %get-tuple-element.130), channel_id=1, source_target_pairs={{0,2},{1,3},{2,0},{3,1},{4,6},{5,7},{6,4},{7,5},{8,10},{9,11},{10,... | collective-permute-start | bytes 387080 | tf_op jit(solution)/shard_map/ppermute | solution.py:909
  236.6 11.5 %collective-permute-start.69 = (bf16[192,768]{1,0:T(8,128)(2,1)S(1)}, bf16[192,768]{1,0:T(8,128)(2,1)S(1)}, u32[]{:S(2)}, u32[]{:S(2)}) collective-permute-start(bf16[192,768]{1,0:T(8,128)(2,1)S(1)} %fusion.6.refs_0_), channel_id=1, source_target_pairs={{0,8},{4,12},{8,0},{12,4},{16,24},{20,28},{24,16},{28,20},{1,9},{5... | collective-permute-start | bytes 884744 | tf_op jit(solution)/shard_map/ppermute | solution.py:904
  242.2 12.6 %collective-permute-start.72 = (bf16[192,768]{1,0:T(8,128)(2,1)S(1)}, bf16[192,768]{1,0:T(8,128)(2,1)S(1)}, u32[]{:S(2)}, u32[]{:S(2)}) collective-permute-start(bf16[192,768]{1,0:T(8,128)(2,1)S(1)} %fusion.6.refs_0_), channel_id=1, source_target_pairs={{0,4},{4,0},{8,12},{12,8},{16,20},{20,16},{24,28},{28,24},{1,5},{5... | collective-permute-start | bytes 884744 | tf_op jit(solution)/shard_map/ppermute | solution.py:899
  242.3 14.0 %collective-permute-start.75 = (bf16[192,768]{1,0:T(8,128)(2,1)S(1)}, bf16[192,768]{1,0:T(8,128)(2,1)S(1)}, u32[]{:S(2)}, u32[]{:S(2)}) collective-permute-start(bf16[192,768]{1,0:T(8,128)(2,1)S(1)} %collective-permute-done.71.refs_3_), channel_id=1, source_target_pairs={{0,4},{4,0},{8,12},{12,8},{16,20},{20,16},{24,28},{28,24},{1,5},{5... | collective-permute-start | bytes 884744 | tf_op jit(solution)/shard_map/ppermute | solution.py:899
  247.1 12.6 %collective-permute-start.74 = (bf16[192,768]{1,0:T(8,128)(2,1)S(1)}, bf16[192,768]{1,0:T(8,128)(2,1)S(1)}, u32[]{:S(2)}, u32[]{:S(2)}) collective-permute-start(bf16[192,768]{1,0:T(8,128)(2,1)S(1)} %collective-permute-done.70.refs_2_), channel_id=1, source_target_pairs={{0,4},{4,0},{8,12},{12,8},{16,20},{20,16},{24,28},{28,24},{1,5},{5... | collective-permute-start | bytes 884744 | tf_op jit(solution)/shard_map/ppermute | solution.py:899
  248.2 16.3 %collective-permute-start.73 = (bf16[192,768]{1,0:T(8,128)(2,1)S(1)}, bf16[192,768]{1,0:T(8,128)(2,1)}, u32[]{:S(2)}, u32[]{:S(2)}) collective-permute-start(bf16[192,768]{1,0:T(8,128)(2,1)S(1)} %collective-permute-done.69.refs_1_), channel_id=1, source_target_pairs={{0,4},{4,0},{8,12},{12,8},{16,20},{20,16},{24,28},{28,24},{1,5},{5... | collective-permute-start | bytes 884744 | tf_op jit(solution)/shard_map/ppermute | solution.py:899
  259.7 9.6 %collective-permute-start.50 = (bf16[112,576]{1,0:T(8,128)(2,1)S(1)}, bf16[112,576]{1,0:T(8,128)(2,1)S(1)}, u32[]{:S(2)}, u32[]{:S(2)}) collective-permute-start(bf16[112,576]{1,0:T(8,128)(2,1)S(1)} %fusion.12.refs_0_), channel_id=1, source_target_pairs={{0,4},{4,0},{8,12},{12,8},{16,20},{20,16},{24,28},{28,24},{1,5},{5... | collective-permute-start | bytes 387080 | tf_op jit(solution)/shard_map/ppermute | solution.py:899
  (105 other events, 1098.2 us)

commit v2 on v1

--- a/solution.py
+++ b/solution.py
@@ -1,4 +1,5 @@
 import functools
+import math
 
 import jax
 import jax.numpy as jnp
@@ -359,6 +360,7 @@
 LANES = 256
 VMEM = pl.BlockSpec(memory_space=pltpu.VMEM)
 HBM = pl.BlockSpec(memory_space=pl.ANY)
+FAR = pl.BlockSpec(memory_space=pltpu.HBM)
 SMEM = pl.BlockSpec(memory_space=pltpu.SMEM)
 VEC = 16
 
@@ -370,6 +372,11 @@
 def call(kernel, outs, ins, args, scratch=(), flops=0, name=None):
     moved = sum(a.size * a.dtype.itemsize for a in args)
     moved += sum(o.size * o.dtype.itemsize for o in outs)
+    held = sum(
+        math.prod(r.shape) * jnp.dtype(r.dtype).itemsize
+        for r in scratch
+        if jnp.issubdtype(r.dtype, jnp.number)
+    )
     return pl.pallas_call(
         kernel,
         out_shape=outs,
@@ -377,8 +384,8 @@
         out_specs=[VMEM] * len(outs),
         scratch_shapes=list(scratch),
         name=name,
-        cost_estimate=pl.CostEstimate(flops=flops, transcendentals=0, bytes_accessed=moved),
-        compiler_params=pltpu.CompilerParams(vmem_limit_bytes=60000 * 1024),
+        cost_estimate=pl.CostEstimate(flops=1, transcendentals=0, bytes_accessed=1),
+        compiler_params=pltpu.CompilerParams(vmem_limit_bytes=moved + held + (4 << 20)),
     )(*args)
 
 
@@ -413,38 +420,72 @@
         self.cols = self.heads * DH
         self.qkv = 3 * self.cols
         self.padded = self.heads * LANES
+        self.wide = -(-self.qkv // 128) * 128
+        self.packed = self.half * self.qkv // width
         self.clusters = chips
         self.entries = chips * CLUSTER
 
 
-def prep_kernel(g, sc, wq, wk, wv, wi, wd, wo, vec, qall, qsend, iall, msend, osend, sem):
+def pick_kernel(g, sc, *refs):
+    weights, small = refs[:3], refs[3:12]
+    qall, qsend, vec, here, *lines, sem = refs[12:]
     p, k = sc[0], sc[1]
-    at = pl.multiple_of(g.block * p + g.bhalf * k, 16)
-    one = pltpu.make_async_copy(wd.at[pl.ds(at, g.bhalf)], msend.at[pl.ds(g.half, g.bhalf)], sem.at[0])
-    one.start()
-    two = pltpu.make_async_copy(
-        wo.at[pl.ds(pl.multiple_of(g.half * k, 16), g.half)], osend, sem.at[1]
-    )
-    two.start()
+    copies = [
+        pltpu.make_async_copy(w, here.at[i], sem.at[i]) for i, w in enumerate(weights)
+    ]
+    copies += [
+        pltpu.make_async_copy(ref, lines[i], sem.at[3 + i])
+        for i, ref in enumerate(small)
+    ]
+    start(copies)
+    finish(copies)
     for q in range(g.chips):
 
         @pl.when(p == q)
         def _(q=q):
             for h in range(g.heads):
-                for i, w in enumerate((wq, wk, wv)):
+                for i in range(3):
                     src = g.cols * q + DH * h
-                    qall[:, 3 * DH * h + DH * i : 3 * DH * h + DH * (i + 1)] = w[:, src : src + DH]
-            for r in range(g.ring):
-                src = g.hshard * r + g.block * q
-                iall[:, g.block * r : g.block * (r + 1)] = wi[:, src : src + g.block]
-
+                    qall[:, 3 * DH * h + DH * i : 3 * DH * h + DH * (i + 1)] = here[
+                        i, :, src : src + DH
+                    ]
+
+    vec[...] = jnp.zeros((VEC, LANES), BF)
+    for i in range(8):
+        vec[i : i + 1, 0 : g.shard] = lines[i][...].reshape(1, g.shard)
+    for q in range(g.chips):
+        vec[8 + q : 9 + q, 0 : g.block] = lines[8][g.block * q : g.block * (q + 1)].reshape(
+            1, g.block
+        )
     mine = pl.ds(pl.multiple_of(g.half * k, 16), g.half)
     qsend[0 : g.half] = qall[mine]
     qsend[g.half : g.half + VEC, 0:LANES] = vec[...]
     qsend[g.half : g.half + VEC, LANES:] = jnp.zeros((VEC, g.qkv - LANES), BF)
-    msend[0 : g.half] = iall[mine]
-    one.wait()
-    two.wait()
+
+
+def prep_kernel(g, sc, _, wi, wd, wo, iall, send, here, sem):
+    p, k = sc[0], sc[1]
+    at = pl.multiple_of(g.block * p + g.bhalf * k, 16)
+    mine = pl.ds(pl.multiple_of(g.half * k, 16), g.half)
+    copies = [
+        pltpu.make_async_copy(wi, here, sem.at[0]),
+        pltpu.make_async_copy(wo.at[mine], send.at[pl.ds(g.half, g.half)], sem.at[1]),
+        pltpu.make_async_copy(
+            wd.at[pl.ds(at, g.bhalf)], send.at[pl.ds(2 * g.half, g.bhalf)], sem.at[2]
+        ),
+    ]
+    start(copies)
+    finish(copies[:1])
+    for q in range(g.chips):
+
+        @pl.when(p == q)
+        def _(q=q):
+            for r in range(g.ring):
+                src = g.hshard * r + g.block * q
+                iall[:, g.block * r : g.block * (r + 1)] = here[:, src : src + g.block]
+
+    send[0 : g.half] = iall[mine]
+    finish(copies[1:])
 
 
 def gathers(g, sc, own, own_at, mine, theirs, at, piece, dst, sem):
@@ -486,7 +527,7 @@
     vec, own = refs[g.chips : g.chips + 2]
     mine = refs[g.chips + 2 : g.chips + 2 + n]
     theirs = refs[g.chips + 2 + n : g.chips + 2 + 2 * n]
-    out, wpad, full, w, vs, sem, vsem = refs[g.chips + 2 + 2 * n :]
+    out, w, full, vs, sem, vsem = refs[g.chips + 2 + 2 * n :]
     p, f = sc[0], sc[2]
     copies = gathers(g, sc, own, 0, mine, theirs, 0, g.half, w, sem)
     start(copies)
@@ -509,14 +550,14 @@
     gap = jnp.zeros((1, DH), F32)
     parts = []
     for h in range(g.heads):
-        parts += [back[0:1, DH * h : DH * (h + 1)], gap, back[1:2, DH * h : DH * (h + 1)], gap]
+        parts += [back[0:1, DH * h : DH * (h + 1)], gap, back[1:2, DH * h : DH * (h + 1)]]
     bias = jnp.concatenate(parts, axis=1)
     finish(copies)
+    rows = jnp.concatenate([x[...] for x in xs], axis=0)
+    found = (dot(rows, w[...]) + bias).astype(BF)
     for h in range(g.heads):
-        wpad[:, LANES * h : LANES * h + 3 * DH] = w[:, 3 * DH * h : 3 * DH * (h + 1)]
-        wpad[:, LANES * h + 3 * DH : LANES * (h + 1)] = jnp.zeros((g.width, DH), BF)
-    rows = jnp.concatenate([x[...] for x in xs], axis=0)
-    out[...] = (dot(rows, wpad[...]) + bias).astype(BF)
+        out[:, LANES * h : LANES * h + 3 * DH] = found[:, 3 * DH * h : 3 * DH * (h + 1)]
+        out[:, LANES * h + 3 * DH : LANES * (h + 1)] = jnp.zeros((g.tokens, DH), BF)
 
 
 def select(index, size, axis_size, lanes):
@@ -556,7 +597,7 @@
         ctx_other[:, DH * h : DH * (h + 1)] = back[g.tokens :]
 
 
-def attend_back_kernel(g, own, other, posr, posc, kept, probs, grad_own, grad_other):
+def attend_back_kernel(g, own, other, posr, posc, kept, probs, grads):
     both = 2 * g.tokens
     rows = jnp.concatenate([own[...], other[...]], axis=0)
     for h in range(g.heads):
@@ -577,11 +618,10 @@
             d_q = dot(d_s, key) * scale
             d_k = dot_tn(d_s, q) * scale
             d_v = dot_tn(share.astype(BF), d_m)
-            zero = jnp.zeros((CLUSTER, DH), F32)
-            found.append(jnp.concatenate([d_q, d_k, d_v, zero], axis=1).astype(BF))
+            found.append(jnp.concatenate([d_q, d_k, d_v], axis=1).astype(BF))
         back = dot(place, jnp.concatenate(found, axis=0)).astype(BF)
-        grad_own[:, LANES * h : LANES * (h + 1)] = back[: g.tokens]
-        grad_other[:, LANES * h : LANES * (h + 1)] = back[g.tokens :]
+        grads[:, 3 * DH * h : 3 * DH * (h + 1)] = back
+    grads[:, g.qkv :] = jnp.zeros((both, g.wide - g.qkv), BF)
 
 
 def norm_parts(values):
@@ -605,53 +645,51 @@
     )
 
 
-def up_kernel(g, sc, *refs):
-    n, c = g.ring - 1, g.chips
-    ctxs, xs, full = refs[:c], refs[c : 2 * c], refs[2 * c]
-    refs = refs[2 * c + 1 :]
-    wo_own, wi_own = refs[:2]
-    wo_mine, wo_theirs = refs[2 : 2 + n], refs[2 + n : 2 + 2 * n]
-    m_mine, m_theirs = refs[2 + 2 * n : 2 + 3 * n], refs[2 + 3 * n : 2 + 4 * n]
-    inner, low, first_own, z_own, s_own, wo, wi, sem_o, sem_i = refs[2 + 4 * n :]
+def lay_kernel(g, sc, *refs):
+    n = g.ring - 1
+    wo_own, wi_own, wd_own = refs[:3]
+    mine, theirs = refs[3 : 3 + n], refs[3 + n : 3 + 2 * n]
+    wo, wi, wd, *sems = refs[3 + 2 * n :]
+    at = pl.multiple_of(g.block * sc[0], 16)
+    copies = gathers(g, sc, wo_own, 0, mine, theirs, g.half, g.half, wo, sems[0])
+    copies += gathers(g, sc, wi_own, 0, mine, theirs, 0, g.half, wi, sems[1])
+    copies += gathers(g, sc, wd_own, at, mine, theirs, 2 * g.half, g.bhalf, wd, sems[2])
+    start(copies)
+    finish(copies)
+
+
+def first_norm_kernel(g, sc, *refs):
+    c = g.chips
+    ctxs, xs, full, wo = refs[:c], refs[c : 2 * c], refs[2 * c], refs[2 * c + 1]
+    low, first_own, z_own, s_own, wo_rows = refs[2 * c + 2 :]
     p = sc[0]
-    copies_o = gathers(g, sc, wo_own, 0, wo_mine, wo_theirs, 0, g.half, wo, sem_o)
-    copies_i = gathers(g, sc, wi_own, 0, m_mine, m_theirs, 0, g.half, wi, sem_i)
-    start(copies_o)
-    start(copies_i)
     rows = jnp.concatenate([x[...] for x in xs], axis=0).astype(F32)
     total = rows + full[2:3, :]
-    finish(copies_o)
     for j in range(c):
         q = jnp.bitwise_xor(p, j)
-        total = total + dot(seen(g, ctxs[j], j), wo[pl.ds(pl.multiple_of(g.cols * q, 64), g.cols), :])
+        part = wo[pl.ds(pl.multiple_of(g.cols * q, 64), g.cols), :]
+        total = total + dot(seen(g, ctxs[j], j), part)
+        if j == 0:
+            wo_rows[...] = part
     z, scale = norm_parts(total)
     first = z * full[3:4, :] + full[4:5, :]
     first_own[...] = first[: g.rows]
     z_own[...] = z[: g.rows]
     s_own[...] = jnp.broadcast_to(scale[: g.rows], (g.rows, 128))
     low[...] = first.astype(BF)
-    finish(copies_i)
-    bias = full[pl.ds(8 + p, 1), :]
-    inner[...] = dot(low[...], wi[...]) + bias
-
-
-def down_kernel(g, sc, *refs):
-    n, c = g.ring - 1, g.chips
-    inner, first_own, full, wd_own = refs[:4]
-    mine, theirs = refs[4 : 4 + n], refs[4 + n : 4 + 2 * n]
-    refs = refs[4 + 2 * n :]
-    parts, active = refs[:c], refs[c]
-    wd, sem = refs[c + 1 :]
-    p = sc[0]
-    at = pl.multiple_of(g.block * p, 16)
-    copies = gathers(g, sc, wd_own, at, mine, theirs, g.half, g.bhalf, wd, sem)
-    start(copies)
+
+
+def up_kernel(g, sc, low, wi, full, inner):
+    inner[...] = dot(low[...], wi[...]) + full[pl.ds(8 + sc[0], 1), :]
+
+
+def down_kernel(g, inner, first_own, full, wd, *refs):
+    parts, active = refs[: g.chips], refs[g.chips]
     u = inner[...]
     active[...] = (u * (1.0 + lax.erf(u * (0.5**0.5))) * 0.5).astype(BF)
-    finish(copies)
     second = dot(active[...], wd[...])
     parts[0][...] = second[: g.rows] + first_own[...] + full[5:6, :]
-    for j in range(1, c):
+    for j in range(1, g.chips):
         parts[j][...] = second[g.rows * j : g.rows * (j + 1)].astype(BF)
 
 
@@ -675,23 +713,13 @@
     branch[g.rows : g.rows + VEC] = jnp.concatenate([one, two, rest], axis=0).astype(BF)
 
 
-def back_kernel(g, sc, *refs):
-    n, c = g.ring - 1, g.chips
-    branches, slope, wd_own, wi_own = refs[:c], refs[c], refs[c + 1], refs[c + 2]
-    mine, theirs = refs[c + 3 : c + 3 + n], refs[c + 3 + n : c + 3 + 2 * n]
-    refs = refs[c + 3 + 2 * n :]
-    parts, d_inner, wd, wi, sem_d, sem_i = refs[:c], *refs[c:]
-    p = sc[0]
-    at = pl.multiple_of(g.block * p, 16)
-    copies_d = gathers(g, sc, wd_own, at, mine, theirs, g.half, g.bhalf, wd, sem_d)
-    copies_i = gathers(g, sc, wi_own, 0, mine, theirs, 0, g.half, wi, sem_i)
-    start(copies_d)
-    start(copies_i)
+def back_kernel(g, *refs):
+    c = g.chips
+    branches, slope, wd, wi = refs[:c], refs[c], refs[c + 1], refs[c + 2]
+    parts, d_inner = refs[c + 3 : 2 * c + 3], refs[2 * c + 3]
     rows = jnp.concatenate([b[0 : g.rows] for b in branches], axis=0)
-    finish(copies_d)
     d_active = dot_nt(rows, wd[...])
     d_inner[...] = (d_active * slope[...]).astype(BF)
-    finish(copies_i)
     total = dot_nt(d_inner[...], wi[...])
     parts[0][...] = total[: g.rows]
     for j in range(1, c):
@@ -742,77 +770,92 @@
     attended[g.rows : g.rows + VEC] = jnp.concatenate([one, two, rest], axis=0).astype(BF)
 
 
-def context_kernel(g, sc, *refs):
-    n, c = g.ring - 1, g.chips
-    grads, own = refs[:c], refs[c]
-    mine, theirs = refs[c + 1 : c + 1 + n], refs[c + 1 + n : c + 1 + 2 * n]
-    out, wo, sem = refs[c + 1 + 2 * n :]
-    p = sc[0]
-    copies = gathers(g, sc, own, 0, mine, theirs, 0, g.half, wo, sem)
-    start(copies)
+def context_kernel(g, *refs):
+    grads, wo_rows, out = refs[: g.chips], refs[g.chips], refs[g.chips + 1]
     rows = jnp.concatenate([b[0 : g.rows] for b in grads], axis=0)
-    finish(copies)
-    out[...] = dot_nt(rows, wo[pl.ds(pl.multiple_of(g.cols * p, 64), g.cols), :]).astype(BF)
+    out[...] = dot_nt(rows, wo_rows[...]).astype(BF)
 
 
 def out_grads_kernel(g, sc, *refs):
     c = g.chips
     grads, ctxs, sums = refs[:c], refs[c : 2 * c], refs[2 * c]
-    own, other, total = refs[2 * c + 1 :]
-    p, k, f = sc[0], sc[1], sc[2]
+    own, total = refs[2 * c + 1], refs[-1]
+    away = refs[2 * c + 2 : -1]
+    p, f = sc[0], sc[2]
     rows = jnp.concatenate([b[0 : g.rows] for b in grads], axis=0)
     for j in range(c):
         q = jnp.bitwise_xor(p, j)
         total[pl.ds(pl.multiple_of(g.cols * q, 64), g.cols), :] = dot_tn(seen(g, ctxs[j], j), rows)
-    size = g.half // c
-    for s in range(g.ring):
-        base = g.shard * lax.rem(f + s, g.ring) + 2 * size * p
-        own[s, 0:size] = total[pl.ds(pl.multiple_of(base + size * k, 8), size), :]
-        other[s, 0:size] = total[
-            pl.ds(pl.multiple_of(base + size * (1 - k), 8), size), :
-        ].astype(BF)
     stats = grads[0][g.rows : g.rows + VEC].astype(F32)
     for j in range(1, c):
         stats = stats + grads[j][g.rows : g.rows + VEC].astype(F32)
     out = jnp.sum(rows.astype(F32), axis=0, keepdims=True)
     rest = jnp.zeros((VEC - 7, g.width), F32)
     block = jnp.concatenate([sums[0:4], stats[0:2], out, rest], axis=0)
-    spare = own.shape[1] - size - VEC
-    if spare:
-        block = jnp.concatenate([block, jnp.zeros((spare, g.width), F32)], axis=0)
+    size = g.shard // c
     for s in range(g.ring):
-        own[s, size:] = block
-        other[s, size:] = block.astype(BF)
-
-
-def input_kernel(g, *refs):
-    c = g.chips
-    own, other, wpad = refs[:3]
-    parts, d_qkv = refs[3 : 3 + c], refs[3 + c]
-    d_qkv[...] = (own[...].astype(F32) + other[...].astype(F32)).astype(BF)
-    total = dot_nt(d_qkv[...], wpad[...])
+        base = g.shard * lax.rem(f + s, g.ring) + size * p
+        part = total[pl.ds(pl.multiple_of(base, 8), size), :]
+        if s == 0:
+            own[0:size] = part
+            own[size:] = block
+        else:
+            away[s - 1][0:size] = part.astype(BF)
+            away[s - 1][size:] = block.astype(BF)
+
+
+def summed(g, mine, theirs, at):
+    one = mine[g.tokens * at : g.tokens * (at + 1), : g.qkv].astype(F32)
+    two = theirs[g.tokens * (1 - at) : g.tokens * (2 - at), : g.qkv].astype(F32)
+    return (one + two).astype(BF)
+
+
+def input_kernel(g, mine, theirs, w, *parts):
+    total = dot_nt(summed(g, mine, theirs, 0), w[...])
     parts[0][...] = total[: g.rows]
-    for j in range(1, c):
+    for j in range(1, g.chips):
         parts[j][...] = total[g.rows * j : g.rows * (j + 1)].astype(BF)
 
 
-def qkv_grads_kernel(g, sc, *refs):
-    c = g.chips
-    xs, d_qkv = refs[:c], refs[c]
-    own, other, wide, total = refs[c + 1 :]
+def turn_rows_kernel(g, sc, *refs):
+    xs, out = refs[: 2 * g.chips], refs[2 * g.chips]
     rows = jnp.concatenate([x[...] for x in xs], axis=0)
-    wide[...] = dot_tn(rows, d_qkv[...])
-    sums = jnp.sum(d_qkv[...].astype(F32), axis=0, keepdims=True)
-    for h in range(g.heads):
-        total[:, 3 * DH * h : 3 * DH * (h + 1)] = wide[:, LANES * h : LANES * h + 3 * DH]
-    split_rows(g, sc, total, g.half, own, other, 0)
-    row = jnp.concatenate(
-        [sums[:, LANES * h : LANES * h + 3 * DH] for h in range(g.heads)], axis=1
-    )
-    block = jnp.concatenate([row, jnp.zeros((VEC - 1, g.qkv), F32)], axis=0)
+    for core in range(2):
+
+        @pl.when(sc[1] == core)
+        def _(core=core):
+            for r in range(g.ring):
+                lane = g.shard * r + g.half * core
+                out[g.half * r : g.half * (r + 1), :] = jnp.transpose(rows[:, lane : lane + g.half])
+
+
+def qkv_grads_kernel(g, sc, mine, theirs, turned_x, own, *refs):
+    away, total = refs[:-1], refs[-1]
+    f = sc[2]
+    rows = jnp.concatenate([summed(g, mine, theirs, 0), summed(g, mine, theirs, 1)], axis=0)
+    total[...] = dot(turned_x[...], rows)
+    sums = jnp.sum(rows.astype(F32), axis=0, keepdims=True)
+    gap = jnp.zeros((8, g.width - g.qkv), F32)
+    block = jnp.concatenate(
+        [jnp.concatenate([sums, jnp.zeros((7, g.qkv), F32)], axis=0), gap], axis=1
+    )
     for s in range(g.ring):
-        own[s, g.half :] = block
-        other[s, g.half :] = block.astype(BF)
+        part = total[pl.ds(pl.multiple_of(g.half * lax.rem(f + s, g.ring), 8), g.half), :]
+        dst = own if s == 0 else away[s - 1]
+        packed = pack(g, part)
+        dst[0 : g.packed] = packed if s == 0 else packed.astype(BF)
+        dst[g.packed :] = block if s == 0 else block.astype(BF)
+
+
+def pack(g, part):
+    step = g.half - g.packed
+    beside = [
+        part[g.packed :, step_lanes : step_lanes + g.width - g.qkv]
+        for step_lanes in range(0, g.qkv, g.width - g.qkv)
+    ]
+    return jnp.concatenate(
+        [part[0 : g.packed], jnp.concatenate(beside, axis=0)], axis=1
+    )
 
 
 def sources(g, sc, refs):
@@ -826,7 +869,8 @@
 
 
 def mlp_final_kernel(g, sc, *refs):
-    found, (g_in, g_down) = refs[: 2 * g.chips], refs[2 * g.chips :]
+    found = refs[: 2 * g.chips]
+    g_in, g_down = refs[2 * g.chips :]
     for q, core, ref in sources(g, sc, found):
         at = pl.multiple_of(g.block * q + g.bhalf * core, 8)
         g_down[pl.ds(at, g.bhalf), :] = ref[g.half :, :].astype(F32)
@@ -842,56 +886,55 @@
                     ].astype(F32)
 
 
-def out_final_kernel(g, sc, *refs):
-    found, (g_out, vec, wide) = refs[: 2 * g.chips], refs[2 * g.chips :]
-    f = sc[2]
-    size = g.half // g.chips
+def last_kernel(g, sc, *refs):
+    found = refs[: 2 * g.chips]
+    gq, gk, gv, g_bq, g_bv, g_out, g_bin, *small = refs[2 * g.chips :]
+    p, f = sc[0], sc[2]
+    size, side, step = g.shard // g.chips, g.width - g.qkv, g.half - g.packed
+    top = g.packed + 8
     for q, core, ref in sources(g, sc, found):
-        at = pl.multiple_of(2 * size * q + size * core, 8)
-        g_out[pl.ds(at, size), :] = ref[0:size, :].astype(F32)
-
-        @pl.when(core == 0)
-        def _(q=q, ref=ref):
-            for chip in range(g.chips):
-
-                @pl.when(q == chip)
-                def _(chip=chip):
-                    block = ref[size : size + VEC, :].astype(F32)
-                    back = pltpu.roll(block, lax.rem(g.width - g.shard * f, g.width), 1)
-                    if chip == 0:
-                        wide[:, :] = back[:, : g.shard]
-                    vec[3 + chip : 4 + chip, :] = back[3:4, : g.shard]
-
-    vec[0:3, :] = wide[0:3, :]
-    vec[3 + g.chips : 6 + g.chips, :] = wide[4:7, :]
-
-
-def qkv_final_kernel(g, sc, *refs):
-    found, (gq, gk, gv, vec) = refs[: 2 * g.chips], refs[2 * g.chips :]
-    f = sc[2]
-    for q, core, ref in sources(g, sc, found):
-        mine = pl.ds(pl.multiple_of(g.half * core, 8), g.half)
 
         @pl.when((q == f) & (core == 0))
         def _(ref=ref):
-            row = ref[g.half : g.half + VEC, :].astype(F32)[0:1]
-            for i, at in ((0, 0), (1, 2)):
-                vec[i : i + 1, :] = jnp.concatenate(
+            row = ref[g.packed : top, :].astype(F32)[0:1]
+            for dst, at in zip((g_bq, g_bv), (0, 2)):
+                dst[...] = jnp.concatenate(
                     [
                         row[:, 3 * DH * h + DH * at : 3 * DH * h + DH * (at + 1)]
                         for h in range(g.heads)
                     ],
                     axis=1,
-                )
-
+                ).reshape(g.shard)
+
+        base = pl.multiple_of(g.half * core, 8)
         for chip in range(g.chips):
 
             @pl.when(q == chip)
-            def _(chip=chip, ref=ref, mine=mine):
+            def _(chip=chip, ref=ref, base=base):
+                part = ref[0 : g.packed, :].astype(F32)
                 for i, dst in enumerate((gq, gk, gv)):
                     for h in range(g.heads):
                         lane, src = g.cols * chip + DH * h, 3 * DH * h + DH * i
-                        dst[mine, lane : lane + DH] = ref[0 : g.half, src : src + DH].astype(F32)
+                        dst[pl.ds(base, g.packed), lane : lane + DH] = part[:, src : src + DH]
+                        third, at = src // side, g.qkv + src % side
+                        dst[pl.ds(base + g.packed, step), lane : lane + DH] = part[
+                            step * third : step * (third + 1), at : at + DH
+                        ]
+
+    for j in range(g.chips):
+        q = jnp.bitwise_xor(p, j)
+        one, two = found[j], found[g.chips + j]
+        both = one[top:, :].astype(F32) + two[top:, :].astype(F32)
+        g_out[pl.ds(pl.multiple_of(size * q, 8), size), :] = both[0:size]
+        back = pltpu.roll(both[size : size + VEC], lax.rem(g.width - g.shard * f, g.width), 1)
+        for chip in range(g.chips):
+
+            @pl.when(q == chip)
+            def _(chip=chip, back=back):
+                g_bin[g.block * chip : g.block * (chip + 1)] = back[3:4, : g.shard].reshape(g.shard)
+                if chip == 0:
+                    for i, dst in zip((0, 1, 2, 4, 5, 6), small):
+                        dst[...] = back[i : i + 1, : g.shard].reshape(g.shard)
 
 
 def to_core(x):
@@ -919,14 +962,19 @@
     return [parts[0]] + [far[j] for j in range(1, len(parts))]
 
 
-def ring_sum(own, other, ring):
-    got = to_core(other)
-    mine = [own[s] + got[s].astype(F32) for s in range(ring)]
-    far = [along(mine[s].astype(BF), s) for s in range(1, ring)]
-    total = mine[0]
+def ring_sum(own, far):
+    total = own
     for part in far:
         total = total + part.astype(F32)
     return total.astype(BF)
+
+
+def kept_far(x):
+    return pltpu.with_memory_space_constraint(x, pltpu.HBM)
+
+
+def after(x, *first):
+    return lax.optimization_barrier((x, *first))[0]
 
 
 def plane_pieces(piece, chips):
@@ -965,38 +1013,59 @@
     sc = jnp.stack([p, k, f]).astype(jnp.int32)
     bind = functools.partial
 
-    x_own = hidden_in.reshape(rows, width)
-    xs = spread(x_own, chips)
-
-    small = jnp.concatenate(
-        [
-            v.reshape(-1, g.shard)
-            for v in (b_query, b_value, b_out, ln1_gain, ln1_bias, b_down, ln2_gain, ln2_bias)
-        ]
-        + [b_in.reshape(chips, g.block)],
-        axis=0,
-    )
-    vec = jnp.pad(small, ((0, VEC - small.shape[0]), (0, LANES - g.shard)))
-    qall, qsend, iall, msend, osend = call(
-        bind(prep_kernel, g),
+    gate = pltpu.SemaphoreType.DMA((2 * ring - 1,))
+
+    qall, qsend, vec = call(
+        bind(pick_kernel, g),
         [
             shaped((g.shard, g.qkv), BF),
             shaped((g.half + VEC, g.qkv), BF),
+            shaped((VEC, LANES), BF),
+        ],
+        [SMEM] + [FAR] * 12,
+        [
+            sc,
+            *map(
+                kept_far,
+                (
+                    w_query,
+                    w_key,
+                    w_value,
+                    b_query,
+                    b_value,
+                    b_out,
+                    ln1_gain,
+                    ln1_bias,
+                    b_down,
+                    ln2_gain,
+                    ln2_bias,
+                    b_in,
+                ),
+            ),
+        ],
+        [
+            pltpu.VMEM((3, g.shard, width), BF),
+        ]
+        + [pltpu.VMEM((g.shard,), BF)] * 8
+        + [pltpu.VMEM((g.hshard,), BF), pltpu.SemaphoreType.DMA((12,))],
+        name="pick_weights",
+    )
+    q_mine = [along(qsend, s) for s in range(1, ring)]
+    x_own = after(hidden_in.reshape(rows, width), qsend)
+    xs = spread(x_own, chips)
+    iall, send = call(
+        bind(prep_kernel, g),
+        [
             shaped((g.shard, g.share), BF),
-            shaped((g.half + g.bhalf, width), BF),
-            shaped((g.half, width), BF),
+            shaped((2 * g.half + g.bhalf, width), BF),
         ],
-        [SMEM] + [VMEM] * 4 + [HBM] * 2 + [VMEM],
-        [sc, w_query, w_key, w_value, w_in, w_down, w_out, vec],
-        [pltpu.SemaphoreType.DMA((2,))],
-        name="pick_weights",
-    )
-    q_mine = [along(qsend, s) for s in range(1, ring)]
+        [SMEM, HBM, FAR, FAR, FAR],
+        [sc, qsend, kept_far(w_in), kept_far(w_down), kept_far(w_out)],
+        [pltpu.VMEM((g.shard, hidden), BF), pltpu.SemaphoreType.DMA((3,))],
+        name="prepare_weights",
+    )
+    w_mine = [along(send, s) for s in range(1, ring)]
     q_theirs = [to_core(part) for part in q_mine]
-    o_mine = [along(osend, s) for s in range(1, ring)]
-    o_theirs = [to_core(part) for part in o_mine]
-    m_mine = [along(msend, s) for s in range(1, ring)]
-    m_theirs = [to_core(part) for part in m_mine]
 
     order = lax.dynamic_slice(
         clusters[0], (g.heads * p, g.entries * k), (g.heads, g.entries)
@@ -1012,26 +1081,23 @@
     blk = dot(hot, block_ids[0].reshape(2 * n, half_rows).astype(BF)).astype(BF)
     blk = jnp.broadcast_to(blk.reshape(1, 2 * g.tokens), (8, 2 * g.tokens))
 
-    gate = pltpu.SemaphoreType.DMA((2 * ring - 1,))
-    qkv, wpad, full = call(
+    qkv, w_qkv, full = call(
         bind(qkv_kernel, g),
         [
             shaped((g.tokens, g.padded), BF),
-            shaped((width, g.padded), BF),
+            shaped((width, g.qkv), BF),
             shaped((VEC, width), F32),
         ],
         [SMEM] + [VMEM] * (chips + 1) + [HBM] * (2 * ring - 1),
         [sc, *xs, vec, qall, *q_mine, *q_theirs],
         [
-            pltpu.VMEM((width, g.qkv), BF),
             pltpu.VMEM((ring - 1, VEC, LANES), BF),
             gate,
             pltpu.SemaphoreType.DMA((ring - 1,)),
         ],
-        flops=2 * g.tokens * width * g.padded,
+        flops=2 * g.tokens * width * g.qkv,
         name="project",
     )
-    qkv_other = to_core(qkv)
     ctx_own, ctx_other, kept, probs = call(
         bind(attend_kernel, g),
         [
@@ -1041,26 +1107,42 @@
             shaped((g.heads * g.clusters, CLUSTER, CLUSTER), F32),
         ],
         [VMEM] * 5,
-        [qkv, qkv_other, posr, posc, blk],
+        [qkv, to_core(qkv), posr, posc, blk],
         flops=8 * g.entries * g.tokens * LANES * g.heads,
         name="attend",
     )
     ctx = ctx_own + to_core(ctx_other)
     ctxs = spread(ctx, chips)
 
-    inner, low, first_own, z_own, s_own = call(
-        bind(up_kernel, g),
+    w_theirs = [to_core(after(part, *ctxs[1:])) for part in w_mine]
+    wo, wi, wd = call(
+        bind(lay_kernel, g),
+        [shaped((width, width), BF), shaped((width, g.share), BF), shaped((g.share, width), BF)],
+        [SMEM] + [FAR, HBM, FAR] + [HBM] * (2 * ring - 2),
+        [sc, kept_far(w_out), iall, kept_far(w_down), *w_mine, *w_theirs],
+        [gate, gate, gate],
+        name="lay_weights",
+    )
+    low, first_own, z_own, s_own, wo_rows = call(
+        bind(first_norm_kernel, g),
         [
-            shaped((g.tokens, g.share), F32),
             shaped((g.tokens, width), BF),
             shaped((rows, width), F32),
             shaped((rows, width), F32),
             shaped((rows, 128), F32),
+            shaped((g.cols, width), BF),
         ],
-        [SMEM] + [VMEM] * (2 * chips + 1) + [HBM] * (4 * ring - 2),
-        [sc, *ctxs, *xs, full, w_out, iall, *o_mine, *o_theirs, *m_mine, *m_theirs],
-        [pltpu.VMEM((width, width), BF), pltpu.VMEM((width, g.share), BF), gate, gate],
-        flops=4 * g.tokens * width * g.share,
+        [SMEM] + [VMEM] * (2 * chips + 2),
+        [sc, *ctxs, *xs, full, wo],
+        flops=2 * g.tokens * width * width,
+        name="out_project",
+    )
+    (inner,) = call(
+        bind(up_kernel, g),
+        [shaped((g.tokens, g.share), F32)],
+        [SMEM] + [VMEM] * 3,
+        [sc, low, wi, full],
+        flops=2 * g.tokens * width * g.share,
         name="mlp_up",
     )
     *second, active = call(
@@ -1068,15 +1150,23 @@
         [shaped((rows, width), F32)]
         + [shaped((rows, width), BF)] * (chips - 1)
         + [shaped((g.tokens, g.share), BF)],
-        [SMEM] + [VMEM] * 3 + [HBM] * (2 * ring - 1),
-        [sc, inner, first_own, full, w_down, *m_mine, *m_theirs],
-        [pltpu.VMEM((g.share, width), BF), gate],
+        [VMEM] * 4,
+        [inner, first_own, full, wd],
         flops=2 * g.tokens * width * g.share,
         name="mlp_down",
     )
+    inner = after(inner, active)
     slope = 0.5 * (1.0 + lax.erf(inner * (0.5**0.5))) + inner * jnp.exp(
         -0.5 * inner * inner
     ) * (1.0 / (2.0 * jnp.pi) ** 0.5)
+    x_other = [to_core(after(x, inner)) for x in xs]
+    (turned_x,) = call(
+        bind(turn_rows_kernel, g),
+        [shaped((ring * g.half, 2 * g.tokens), BF)],
+        [SMEM] + [VMEM] * (2 * chips),
+        [sc, *xs, *x_other],
+        name="turn_rows",
+    )
     second = swap(second)
     layer_out, d_second, branch = call(
         bind(turn_kernel, g),
@@ -1086,7 +1176,7 @@
             shaped((rows + VEC, width), BF),
         ],
         [VMEM] * (chips + 2),
-        [*second, full, out_grad.reshape(rows, width)],
+        [*second, after(full, turned_x), out_grad.reshape(rows, width)],
         name="norm_two",
     )
     branches = spread(branch, chips)
@@ -1095,9 +1185,8 @@
         [shaped((rows, width), F32)]
         + [shaped((rows, width), BF)] * (chips - 1)
         + [shaped((g.tokens, g.share), BF)],
-        [SMEM] + [VMEM] * (chips + 1) + [HBM] * (2 * ring),
-        [sc, *branches, slope, w_down, iall, *m_mine, *m_theirs],
-        [pltpu.VMEM((g.share, width), BF), pltpu.VMEM((width, g.share), BF), gate, gate],
+        [VMEM] * (chips + 3),
+        [*branches, slope, wd, wi],
         flops=4 * g.tokens * width * g.share,
         name="mlp_back",
     )
@@ -1115,94 +1204,93 @@
         flops=4 * g.tokens * width * g.share,
         name="mlp_grads",
     )
-    m_piece = ring_sum(m_own, m_other, ring)
+    m_got = to_core(m_other)
+    m_mine = [m_own[s] + m_got[s].astype(F32) for s in range(ring)]
+    m_away = [m_mine[s].astype(BF) for s in range(1, ring)]
+    m_far = [along(part, s) for s, part in enumerate(m_away, 1)]
+    m_piece = ring_sum(m_mine[0], m_far)
     d_sum, attended = call(
         bind(first_kernel, g),
         [shaped((rows, width), F32), shaped((rows + VEC, width), BF)],
         [VMEM] * (chips + 4),
-        [*d_first, d_second, z_own, s_own, full],
+        [*d_first, after(d_second, *m_away), z_own, s_own, full],
         name="norm_one",
     )
     grads = spread(attended, chips)
     (d_ctx,) = call(
         bind(context_kernel, g),
         [shaped((g.tokens, g.cols), BF)],
-        [SMEM] + [VMEM] * chips + [HBM] * (2 * ring - 1),
-        [sc, *grads, w_out, *o_mine, *o_theirs],
-        [pltpu.VMEM((width, width), BF), gate],
+        [VMEM] * (chips + 1),
+        [*grads, after(wo_rows, m_piece)],
         flops=2 * g.tokens * width * g.cols,
         name="context_back",
     )
     d_ctx_other = to_core(d_ctx)
-    size = g.half // chips
-    o_rows = -(-(size + VEC) // 16) * 16
-    o_own, o_other = call(
+    o_rows = g.shard // chips + VEC
+    o_own, *o_away = call(
         bind(out_grads_kernel, g),
-        [shaped((ring, o_rows, width), F32), shaped((ring, o_rows, width), BF)],
+        [shaped((o_rows, width), F32)] + [shaped((o_rows, width), BF)] * (ring - 1),
         [SMEM] + [VMEM] * (2 * chips + 1),
         [sc, *grads, *ctxs, sums],
         [pltpu.VMEM((width, width), F32)],
         flops=2 * g.tokens * width * width,
         name="out_grads",
     )
-    o_piece = ring_sum(o_own, o_other, ring)
-    dq_own, dq_other = call(
+    (dq_mine,) = call(
         bind(attend_back_kernel, g),
-        [shaped((g.tokens, g.padded), BF)] * 2,
+        [shaped((2 * g.tokens, g.wide), BF)],
         [VMEM] * 6,
-        [d_ctx, d_ctx_other, posr, posc, kept, probs],
+        [d_ctx, d_ctx_other, posr, posc, after(kept, o_own), probs],
         flops=8 * g.entries * g.tokens * LANES * g.heads,
         name="attend_back",
     )
-    *d_in, d_qkv = call(
+    o_far = [along(after(part, dq_mine), s) for s, part in enumerate(o_away, 1)]
+    dq_theirs = to_core(dq_mine)
+    q_rows = g.packed + 8
+    q_own, *q_away = call(
+        bind(qkv_grads_kernel, g),
+        [shaped((q_rows, width), F32)] + [shaped((q_rows, width), BF)] * (ring - 1),
+        [SMEM] + [VMEM] * 3,
+        [sc, dq_mine, dq_theirs, turned_x],
+        [pltpu.VMEM((ring * g.half, g.qkv), F32)],
+        flops=2 * g.tokens * width * g.qkv,
+        name="project_grads",
+    )
+    q_far = [along(part, s) for s, part in enumerate(q_away, 1)]
+    d_in = call(
         bind(input_kernel, g),
-        [shaped((rows, width), F32)]
-        + [shaped((rows, width), BF)] * (chips - 1)
-        + [shaped((g.tokens, g.padded), BF)],
+        [shaped((rows, width), F32)] + [shaped((rows, width), BF)] * (chips - 1),
         [VMEM] * 3,
-        [dq_own, to_core(dq_other), wpad],
-        flops=2 * g.tokens * width * g.padded,
+        [after(dq_mine, *q_away), dq_theirs, w_qkv],
+        flops=2 * g.tokens * width * g.qkv,
         name="project_back",
     )
-    q_own, q_other = call(
-        bind(qkv_grads_kernel, g),
-        [shaped((ring, g.half + VEC, g.qkv), F32), shaped((ring, g.half + VEC, g.qkv), BF)],
-        [SMEM] + [VMEM] * (chips + 1),
-        [sc, *xs, d_qkv],
-        [pltpu.VMEM((width, g.padded), F32), pltpu.VMEM((width, g.qkv), F32)],
-        flops=2 * g.tokens * width * g.padded,
-        name="project_grads",
-    )
     d_in = swap(d_in)
-    q_piece = ring_sum(q_own, q_other, ring)
+    m_pieces = plane_pieces(m_piece, chips)
+    g_in, g_down = call(
+        bind(mlp_final_kernel, g),
+        [shaped((g.shard, hidden), F32), shaped((g.hshard, width), F32)],
+        [SMEM] + [VMEM] * (2 * chips),
+        [sc, *m_pieces],
+        name="mlp_lay",
+    )
     total = d_sum
     for part in d_in:
         total = total + part.astype(F32)
     input_grad = total.astype(BF)
-
-    g_in, g_down = call(
-        bind(mlp_final_kernel, g),
-        [shaped((g.shard, hidden), F32), shaped((g.hshard, width), F32)],
+    vector = shaped((g.shard,), F32)
+    piece = jnp.concatenate([ring_sum(q_own, q_far), ring_sum(o_own, o_far)], axis=0)
+    found = call(
+        bind(last_kernel, g),
+        [shaped((g.shard, width), F32)] * 3
+        + [vector] * 2
+        + [shaped((g.shard, width), F32), shaped((g.hshard,), F32)]
+        + [vector] * 6,
         [SMEM] + [VMEM] * (2 * chips),
-        [sc, *plane_pieces(m_piece, chips)],
-        name="mlp_lay",
-    )
-    g_out, vec_two = call(
-        bind(out_final_kernel, g),
-        [shaped((g.shard, width), F32), shaped((VEC, g.shard), F32)],
-        [SMEM] + [VMEM] * (2 * chips),
-        [sc, *plane_pieces(o_piece, chips)],
-        [pltpu.VMEM((VEC, g.shard), F32)],
-        name="out_lay",
-    )
-    gq, gk, gv, vec_one = call(
-        bind(qkv_final_kernel, g),
-        [shaped((g.shard, width), F32)] * 3 + [shaped((8, g.shard), F32)],
-        [SMEM] + [VMEM] * (2 * chips),
-        [sc, *plane_pieces(q_piece, chips)],
-        name="project_lay",
-    )
-    last = 3 + chips
+        [after(sc, g_down), *plane_pieces(piece, chips)],
+        name="last_lay",
+    )
+    gq, gk, gv, g_bq, g_bv, g_out, g_bin, g_gain2, g_bias2, g_bdown, g_gain1, g_bias1, g_bout = found
     return (
         layer_out.reshape(1, rows, width),
         input_grad.reshape(1, rows, width),
@@ -1210,17 +1298,17 @@
         gk,
         gv,
         g_out,
-        vec_one[0],
-        vec_one[1],
-        vec_two[last + 2],
-        vec_two[last],
-        vec_two[last + 1],
+        g_bq,
+        g_bv,
+        g_bout,
+        g_gain1,
+        g_bias1,
         g_in,
-        vec_two[3:last].reshape(-1),
+        g_bin,
         g_down,
-        vec_two[2],
-        vec_two[0],
-        vec_two[1],
+        g_bdown,
+        g_gain2,
+        g_bias2,
     )
 
 

time: 277 us -> 199 us (0.72)
  Pallas kernels: 80.5 us -> 47.9 us
  waiting for transfers between devices: 98.8 us -> 77.5 us
  local copies, waits for them, and re-layouts: 20.4 us -> 5.86 us
  other arithmetic: 10.1 us -> 3.43 us
    pallas_call x17 -> x20, Pallas kernels: 80.5 us -> 47.9 us  [call(): pl.pallas_call(kernel, out_shape=outs, in_specs=ins, out_specs=[VMEM] * l...]
    ppermute x30 -> x27, waiting for transfers between devices: 70 us -> 47.2 us  [to_chip(): return lax.ppermute(x, 'ctx', [(i, i ^ 2 * j) for i in range(n)])]
    reshape x10 -> x0, local copies, waits for them, and re-layouts: 6.7 us -> none  [the longest x8 5.26 us: chip_body(): v.reshape(-1, g.shard)]
    ppermute x28 -> x23, waiting for transfers between devices: 0.75 us -> 5.99 us  [to_core(): return lax.ppermute(x, 'ctx', [(i, i ^ 1) for i in range(n)])]
    ppermute x30 -> x27, starting transfers between devices: 36.5 us -> 32.6 us  [to_chip(): return lax.ppermute(x, 'ctx', [(i, i ^ 2 * j) for i in range(n)])]
    ppermute x18 -> x15, waiting for transfers between devices: 28 us -> 24.3 us  [along(): return lax.ppermute(x, 'fsdp', [(i, (i + s) % n) for i in range(n)])]
    slice x3 -> x0, local copies, waits for them, and re-layouts: 3.47 us -> none  [the longest x1 1.43 us: chip_body(): vec_two[1]]
    convert_element_type x3, other arithmetic: 3.28 us -> 0.32 us  [ring_sum(): return total.astype(BF)]
  transfers between devices with their start and end apart: 76 -> 65, of which waited for: 27 -> 25; matrix products, arithmetic and copies ran while one was open for 8% -> 3% of each run, Pallas kernels for 20% -> 12%
where the time goes in v2:
time: 199 us; the launch traced here: 198 us
  waiting for transfers between devices  77.5 us (39%)
  starting transfers between devices  62.2 us (31%)
  Pallas kernels  47.9 us (24%)
  local copies, waits for them, and re-layouts  5.86 us (3%)
  other arithmetic  3.43 us (2%)
    pallas_call x20, Pallas kernels, call(): pl.pallas_call(kernel, out_shape=outs, in_specs=ins, out_specs=[VMEM] * l...  47.9 us
    ppermute x27, waiting for transfers between devices, to_chip(): return lax.ppermute(x, 'ctx', [(i, i ^ 2 * j) for i in range(n)])  47.2 us
    ppermute x27, starting transfers between devices, to_chip(): return lax.ppermute(x, 'ctx', [(i, i ^ 2 * j) for i in range(n)])  32.6 us
    ppermute x15, starting transfers between devices, along(): return lax.ppermute(x, 'fsdp', [(i, (i + s) % n) for i in range(n)])  24.7 us
    ppermute x15, waiting for transfers between devices, along(): return lax.ppermute(x, 'fsdp', [(i, (i + s) % n) for i in range(n)])  24.3 us
    ppermute x23, waiting for transfers between devices, to_core(): return lax.ppermute(x, 'ctx', [(i, i ^ 1) for i in range(n)])  5.99 us
    unnamed x21, local copies, waits for them, and re-layouts  5.43 us
    ppermute x23, starting transfers between devices, to_core(): return lax.ppermute(x, 'ctx', [(i, i ^ 1) for i in range(n)])  4.93 us
  transfers between devices with their start and end apart: 65, of which 25 were waited for; matrix products, arithmetic and copies ran while one was open for 3% of the time, Pallas kernels for 12%

profile of v2, /device:TPU:0, one launch (start us, length us, event | category | flops | bytes accessed | tf_op | source)
XLA Modules:
  0.0 198.3 jit_solution(15071347011095769681)
XLA Ops:
  0.8 2.0 %pick_weights.1 = (bf16[192,576]{1,0:T(8,128)(2,1)S(1)}, bf16[112,576]{1,0:T(8,128)(2,1)S(1)}, bf16[16,256]{1,0:T(8,128)(2,1)S(1)}) custom-call(s32[3]{0:T(128)S(1)} %pad_add_fusion.1.sc, bf16[192,768]{1,0:T(8,128)(2,1)} %refs_0_.2, bf16[192,768]{1,0:T(8,128)(2,1)} %refs_1_.1, bf16[192,768]{1,0:T(8,128)(2,1)} %refs_2_.2, bf16[192]{0:T(256)(128)(2,1)} %refs_3_.1, ...), custom_call_target="tpu_custom_call" | custom-call | flops 1 | bytes 1 | tf_op jit(solution)/shard_map/pick_weights/pallas_call | solution.py:380
  2.8 5.1 %collective-permute-start.5 = (bf16[112,576]{1,0:T(8,128)(2,1)S(1)}, bf16[112,576]{1,0:T(8,128)(2,1)S(1)}, u32[]{:S(2)}, u32[]{:S(2)}) collective-permute-start(bf16[112,576]{1,0:T(8,128)(2,1)S(1)} %get-tuple-element.100._), channel_id=1, source_target_pairs={{0,3},{1,0},{2,1},{3,2},{4,7},{5,4},{6,5},{7,6},{8,11},{9,8},{10,9... | collective-permute-start | bytes 387080 | tf_op jit(solution)/shard_map/ppermute | solution.py:952
  8.9 2.5 %collective-permute-start.2 = (bf16[128,768]{1,0:T(8,128)(2,1)}, bf16[128,768]{1,0:T(8,128)(2,1)S(1)}, u32[]{:S(2)}, u32[]{:S(2)}) collective-permute-start(bf16[128,768]{1,0:T(8,128)(2,1)} %bitcast.43), channel_id=1, source_target_pairs={{0,24},{4,28},{8,16},{12,20},{16,8},{20,12},{24,0},{28,4},{1,25},{... | collective-permute-start | bytes 589832 | tf_op jit(solution)/shard_map/ppermute | solution.py:947
  12.7 2.7 %prepare_weights.1 = (bf16[192,768]{1,0:T(8,128)(2,1)S(1)}, bf16[288,768]{1,0:T(8,128)(2,1)}) custom-call(s32[3]{0:T(128)S(1)} %pad_add_fusion.1.sc, bf16[112,576]{1,0:T(8,128)(2,1)S(1)} %get-tuple-element.100._, bf16[192,3072]{1,0:T(8,128)(2,1)} %wi.1, bf16[768,768]{1,0:T(8,128)(2,1)} %refs_2_.3, bf16[192,768]{1,0:T(8,128)(2,1)} %refs_0_.3), custom_call_target="tpu_custom_call" | custom-call | flops 1 | bytes 1 | tf_op jit(solution)/shard_map/prepare_weights/pallas_call | solution.py:380
  16.8 3.3 %collective-permute-done.4.refs_7_ = bf16[112,576]{1,0:T(8,128)(2,1)S(1)} collective-permute-done((bf16[112,576]{1,0:T(8,128)(2,1)S(1)}, bf16[112,576]{1,0:T(8,128)(2,1)S(1)}, u32[]{:S(2)}, u32[]{:S(2)}) %collective-permute-start.4) | collective-permute-done | bytes 129056 | tf_op jit(solution)/shard_map/ppermute | solution.py:952
  22.0 1.5 collective-permute-start.16
  24.8 1.9 collective-permute-start.14
  28.6 3.0 %project.1 = (bf16[512,768]{1,0:T(8,128)(2,1)S(1)}, bf16[768,576]{1,0:T(8,128)(2,1)S(1)}, f32[16,768]{1,0:T(8,128)S(1)}) custom-call(s32[3]{0:T(128)S(1)} %pad_add_fusion.1.sc, bf16[128,768]{1,0:T(8,128)(2,1)S(1)} %bitcast.46, bf16[128,768]{1,0:T(8,128)(2,1)S(1)} %collective-permute-done.refs_1_.refs_5_, ...), custom_call_target="tpu_custom_call" | custom-call | flops 1 | bytes 1 | tf_op jit(solution)/shard_map/project/pallas_call | solution.py:380
  34.4 8.3 %attend.1 = (bf16[512,192]{1,0:T(8,128)(2,1)S(1)}, bf16[512,192]{1,0:T(8,128)(2,1)S(1)}, bf16[3,512,256]{2,1,0:T(8,128)(2,1)S(1)}, f32[12,128,128]{2,1,0:T(8,128)S(1)}) custom-call(bf16[512,768]{1,0:T(8,128)(2,1)S(1)} %get-tuple-element.104.own, bf16[512,768]{1,0:T(8,128)(2,1)} %collective-permute-done.9.other, s32[8,512]{1,0:T(8,128)S(1)} %pad.4.clone.posr, ...), custom_call_target="tpu_custom_call" | custom-call | flops 1 | bytes 1 | tf_op jit(solution)/shard_map/attend/pallas_call | solution.py:380
  44.4 2.6 %collective-permute-start.13 = (bf16[512,192]{1,0:T(8,128)(2,1)S(1)}, bf16[512,192]{1,0:T(8,128)(2,1)S(1)}, u32[]{:S(2)}, u32[]{:S(2)}) collective-permute-start(bf16[512,192]{1,0:T(8,128)(2,1)S(1)} %add.134.refs_0_.refs_4_), channel_id=1, source_target_pairs={{0,24},{4,28},{8,16},{12,20},{16,8},{20,12},{24,0},{28,4},{1,25},{... | collective-permute-start | bytes 589832 | tf_op jit(solution)/shard_map/ppermute | solution.py:947
  48.0 6.6 %collective-permute-done.13.refs_3_.refs_7_ = bf16[512,192]{1,0:T(8,128)(2,1)S(1)} collective-permute-done((bf16[512,192]{1,0:T(8,128)(2,1)S(1)}, bf16[512,192]{1,0:T(8,128)(2,1)S(1)}, u32[]{:S(2)}, u32[]{:S(2)}) %collective-permute-start.13) | collective-permute-done | bytes 196640 | tf_op jit(solution)/shard_map/ppermute | solution.py:947
  54.6 5.0 %collective-permute-done.12.refs_2_.refs_6_ = bf16[512,192]{1,0:T(8,128)(2,1)S(1)} collective-permute-done((bf16[512,192]{1,0:T(8,128)(2,1)S(1)}, bf16[512,192]{1,0:T(8,128)(2,1)S(1)}, u32[]{:S(2)}, u32[]{:S(2)}) %collective-permute-start.12) | collective-permute-done | bytes 196640 | tf_op jit(solution)/shard_map/ppermute | solution.py:947
  59.7 4.1 %collective-permute-done.15.refs_4_ = bf16[288,768]{1,0:T(8,128)(2,1)} collective-permute-done((bf16[288,768]{1,0:T(8,128)(2,1)}, bf16[288,768]{1,0:T(8,128)(2,1)}, u32[]{:S(2)}, u32[]{:S(2)}) %collective-permute-start.15) | collective-permute-done | bytes 442400 | tf_op jit(solution)/shard_map/ppermute | solution.py:952
  64.4 1.5 collective-permute-done.17.refs_6_
  67.1 3.5 %lay_weights.1 = (bf16[768,768]{1,0:T(8,128)(2,1)S(1)}, bf16[768,768]{1,0:T(8,128)(2,1)S(1)}, bf16[768,768]{1,0:T(8,128)(2,1)S(1)}) custom-call(s32[3]{0:T(128)S(1)} %pad_add_fusion.1.sc, bf16[192,768]{1,0:T(8,128)(2,1)} %refs_0_.3, bf16[192,768]{1,0:T(8,128)(2,1)S(1)} %copy-done.3, bf16[768,768]{1,0:T(8,128)(2,1)} %refs_2_.3, ...), custom_call_target="tpu_custom_call" | custom-call | flops 1 | bytes 1 | tf_op jit(solution)/shard_map/lay_weights/pallas_call | solution.py:380
  70.6 2.0 %out_project.1 = (bf16[512,768]{1,0:T(8,128)(2,1)S(1)}, f32[128,768]{1,0:T(8,128)S(1)}, f32[128,768]{1,0:T(8,128)S(1)}, f32[128,128]{1,0:T(8,128)S(1)}, bf16[192,768]{1,0:T(8,128)(2,1)S(1)}) custom-call(s32[3]{0:T(128)S(1)} %pad_add_fusion.1.sc, bf16[512,192]{1,0:T(8,128)(2,1)S(1)} %add.134.refs_0_.refs_4_, ...), custom_call_target="tpu_custom_call" | custom-call | flops 1 | bytes 1 | tf_op jit(solution)/shard_map/out_project/pallas_call | solution.py:380
  76.0 1.6 collective-permute-start.20
  77.6 1.5 collective-permute-start.21
  79.5 1.4 turn_rows.1.turned_x
  81.0 2.8 %collective-permute-done.20.refs_1_ = bf16[128,768]{1,0:T(8,128)(2,1)S(1)} collective-permute-done((bf16[128,768]{1,0:T(8,128)(2,1)S(1)}, bf16[128,768]{1,0:T(8,128)(2,1)S(1)}, u32[]{:S(2)}, u32[]{:S(2)}) %collective-permute-start.20) | collective-permute-done | bytes 196640 | tf_op jit(solution)/shard_map/ppermute | solution.py:947
  83.8 4.7 %collective-permute-done.21.refs_2_ = bf16[128,768]{1,0:T(8,128)(2,1)S(1)} collective-permute-done((bf16[128,768]{1,0:T(8,128)(2,1)S(1)}, bf16[128,768]{1,0:T(8,128)(2,1)S(1)}, u32[]{:S(2)}, u32[]{:S(2)}) %collective-permute-start.21) | collective-permute-done | bytes 196640 | tf_op jit(solution)/shard_map/ppermute | solution.py:947
  89.5 1.7 collective-permute-start.29
  93.5 5.2 %collective-permute-done.29.refs_3_ = bf16[144,768]{1,0:T(8,128)(2,1)S(1)} collective-permute-done((bf16[144,768]{1,0:T(8,128)(2,1)S(1)}, bf16[144,768]{1,0:T(8,128)(2,1)S(1)}, u32[]{:S(2)}, u32[]{:S(2)}) %collective-permute-start.29) | collective-permute-done | bytes 221216 | tf_op jit(solution)/shard_map/ppermute | solution.py:947
  98.8 2.7 %collective-permute-done.28.refs_2_ = bf16[144,768]{1,0:T(8,128)(2,1)S(1)} collective-permute-done((bf16[144,768]{1,0:T(8,128)(2,1)S(1)}, bf16[144,768]{1,0:T(8,128)(2,1)S(1)}, u32[]{:S(2)}, u32[]{:S(2)}) %collective-permute-start.28) | collective-permute-done | bytes 221216 | tf_op jit(solution)/shard_map/ppermute | solution.py:947
  101.5 1.6 mlp_back.1
  103.1 2.2 %mlp_grads.1 = (f32[4,192,768]{2,1,0:T(8,128)S(1)}, bf16[4,192,768]{2,1,0:T(8,128)(2,1)S(1)}, f32[8,768]{1,0:T(8,128)S(1)}) custom-call(s32[3]{0:T(128)S(1)} %pad_add_fusion.1.sc, bf16[144,768]{1,0:T(8,128)(2,1)S(1)} %get-tuple-element.130.refs_0_, bf16[144,768]{1,0:T(8,128)(2,1)S(1)} %collective-permute-done.27.refs_1_, ...), custom_call_target="tpu_custom_call" | custom-call | flops 1 | bytes 1 | tf_op jit(solution)/shard_map/mlp_grads/pallas_call | solution.py:380
  105.4 1.5 collective-permute-start.30
  108.6 1.9 collective-permute-start.38
  110.5 1.9 collective-permute-start.37
  112.5 1.4 collective-permute-start.31
  113.9 1.5 collective-permute-start.32
  115.4 7.4 %collective-permute-done.31.refs_2_ = bf16[128,768]{1,0:T(8,128)(2,1)S(1)} collective-permute-done((bf16[128,768]{1,0:T(8,128)(2,1)S(1)}, bf16[128,768]{1,0:T(8,128)(2,1)S(1)}, u32[]{:S(2)}, u32[]{:S(2)}) %collective-permute-start.31) | collective-permute-done | bytes 196640 | tf_op jit(solution)/shard_map/ppermute | solution.py:947
  123.1 1.6 collective-permute-start.36
  126.7 10.0 %collective-permute-done.38 = bf16[192,768]{1,0:T(8,128)(2,1)S(1)} collective-permute-done((bf16[192,768]{1,0:T(8,128)(2,1)S(1)}, bf16[192,768]{1,0:T(8,128)(2,1)S(1)}, u32[]{:S(2)}, u32[]{:S(2)}) %collective-permute-start.38) | collective-permute-done | bytes 294944 | tf_op jit(solution)/shard_map/ppermute | solution.py:952
  139.0 6.1 %attend_back.1.mine = bf16[1024,640]{1,0:T(8,128)(2,1)S(1)} custom-call(bf16[512,192]{1,0:T(8,128)(2,1)S(1)} %context_back.1.own, bf16[512,192]{1,0:T(8,128)(2,1)S(1)} %collective-permute-done.40.other, s32[8,512]{1,0:T(8,128)S(1)} %pad.4.clone.posr, s32[512,8]{1,0:T(8,128)S(1)} %pad_bitcast_fusion.posc, bf16[3,512,256]{2,1,0:T(8,128)(2,1)S(1)} %get-tuple-element.149.kept, ...), custom_call_target="tpu_custom_call" | custom-call | flops 1 | bytes 1 | tf_op jit(solution)/shard_map/attend_back/pallas_call | solution.py:380
  145.5 1.5 collective-permute-start.47
  148.1 2.9 %collective-permute-start.57 = (bf16[64,768]{1,0:T(8,128)(2,1)S(1)}, bf16[64,768]{1,0:T(8,128)(2,1)S(1)}, u32[]{:S(2)}, u32[]{:S(2)}) collective-permute-start(bf16[64,768]{1,0:T(8,128)(2,1)S(1)} %get-tuple-element.168), channel_id=1, source_target_pairs={{0,3},{1,0},{2,1},{3,2},{4,7},{5,4},{6,5},{7,6},{8,11},{9,8},{10,9... | collective-permute-start | bytes 294920 | tf_op jit(solution)/shard_map/ppermute | solution.py:952
  151.0 3.5 %collective-permute-done.55 = bf16[64,768]{1,0:T(8,128)(2,1)S(1)} collective-permute-done((bf16[64,768]{1,0:T(8,128)(2,1)S(1)}, bf16[64,768]{1,0:T(8,128)(2,1)S(1)}, u32[]{:S(2)}, u32[]{:S(2)}) %collective-permute-start.55) | collective-permute-done | bytes 98336 | tf_op jit(solution)/shard_map/ppermute | solution.py:952
  156.5 1.7 project_grads.1
  158.5 2.7 %collective-permute-start.53 = (bf16[80,768]{1,0:T(8,128)(2,1)S(1)}, bf16[80,768]{1,0:T(8,128)(2,1)S(1)}, u32[]{:S(2)}, u32[]{:S(2)}) collective-permute-start(bf16[80,768]{1,0:T(8,128)(2,1)S(1)} %get-tuple-element.152), channel_id=1, source_target_pairs={{0,2},{1,3},{2,0},{3,1},{4,6},{5,7},{6,4},{7,5},{8,10},{9,11},{10,... | collective-permute-start | bytes 368648 | tf_op jit(solution)/shard_map/ppermute | solution.py:952
  161.2 2.8 %collective-permute-start.54 = (bf16[80,768]{1,0:T(8,128)(2,1)S(1)}, bf16[80,768]{1,0:T(8,128)(2,1)S(1)}, u32[]{:S(2)}, u32[]{:S(2)}) collective-permute-start(bf16[80,768]{1,0:T(8,128)(2,1)S(1)} %get-tuple-element.153), channel_id=1, source_target_pairs={{0,3},{1,0},{2,1},{3,2},{4,7},{5,4},{6,5},{7,6},{8,11},{9,8},{10,9... | collective-permute-start | bytes 368648 | tf_op jit(solution)/shard_map/ppermute | solution.py:952
  166.1 2.7 %collective-permute-done.53 = bf16[80,768]{1,0:T(8,128)(2,1)S(1)} collective-permute-done((bf16[80,768]{1,0:T(8,128)(2,1)S(1)}, bf16[80,768]{1,0:T(8,128)(2,1)S(1)}, u32[]{:S(2)}, u32[]{:S(2)}) %collective-permute-start.53) | collective-permute-done | bytes 122912 | tf_op jit(solution)/shard_map/ppermute | solution.py:952
  170.4 1.6 collective-permute-start.60
  174.6 2.1 %collective-permute-done.42 = bf16[128,768]{1,0:T(8,128)(2,1)S(1)} collective-permute-done((bf16[128,768]{1,0:T(8,128)(2,1)S(1)}, bf16[128,768]{1,0:T(8,128)(2,1)S(1)}, u32[]{:S(2)}, u32[]{:S(2)}) %collective-permute-start.42) | collective-permute-done | bytes 196640 | tf_op jit(solution)/shard_map/ppermute | solution.py:947
  176.7 1.4 collective-permute-start.44
  178.1 3.7 %mlp_lay.1 = (f32[192,3072]{1,0:T(8,128)}, f32[768,768]{1,0:T(8,128)}) custom-call(s32[3]{0:T(128)S(1)} %pad_add_fusion.1.sc, bf16[192,768]{1,0:T(8,128)(2,1)S(1)} %fusion.6.refs_0_, bf16[192,768]{1,0:T(8,128)(2,1)S(1)} %collective-permute-done.45.refs_1_, bf16[192,768]{1,0:T(8,128)(2,1)S(1)} %collective-permute-done.46.refs_2_, ...), custom_call_target="tpu_custom_call" | custom-call | flops 1 | bytes 1 | tf_op jit(solution)/shard_map/mlp_lay/pallas_call | solution.py:380
  181.8 10.5 %collective-permute-done.43 = bf16[128,768]{1,0:T(8,128)(2,1)S(1)} collective-permute-done((bf16[128,768]{1,0:T(8,128)(2,1)S(1)}, bf16[128,768]{1,0:T(8,128)(2,1)S(1)}, u32[]{:S(2)}, u32[]{:S(2)}) %collective-permute-start.43) | collective-permute-done | bytes 196640 | tf_op jit(solution)/shard_map/ppermute | solution.py:947
  194.7 3.4 %last_lay.1 = (f32[192,768]{1,0:T(8,128)}, f32[192,768]{1,0:T(8,128)}, f32[192,768]{1,0:T(8,128)}, f32[192]{0:T(256)}, f32[192]{0:T(256)}, /*index=5*/f32[192,76...) custom-call(s32[3]{0:T(128)S(1)} %pad_add_fusion.1.sc, ...), custom_call_target="tpu_custom_call" | custom-call | flops 1 | bytes 1 | tf_op jit(solution)/shard_map/last_lay/pallas_call | solution.py:380
  (147 shorter events, 42.0 us)
Async XLA Ops:
  2.8 13.4 %collective-permute-start.5 = (bf16[112,576]{1,0:T(8,128)(2,1)S(1)}, bf16[112,576]{1,0:T(8,128)(2,1)S(1)}, u32[]{:S(2)}, u32[]{:S(2)}) collective-permute-start(bf16[112,576]{1,0:T(8,128)(2,1)S(1)} %get-tuple-element.100._), channel_id=1, source_target_pairs={{0,3},{1,0},{2,1},{3,2},{4,7},{5,4},{6,5},{7,6},{8,11},{9,8},{10,9... | collective-permute-start | bytes 387080 | tf_op jit(solution)/shard_map/ppermute | solution.py:952
  7.9 12.1 %collective-permute-start.4 = (bf16[112,576]{1,0:T(8,128)(2,1)S(1)}, bf16[112,576]{1,0:T(8,128)(2,1)S(1)}, u32[]{:S(2)}, u32[]{:S(2)}) collective-permute-start(bf16[112,576]{1,0:T(8,128)(2,1)S(1)} %get-tuple-element.100._), channel_id=1, source_target_pairs={{0,2},{1,3},{2,0},{3,1},{4,6},{5,7},{6,4},{7,5},{8,10},{9,11},{10,... | collective-permute-start | bytes 387080 | tf_op jit(solution)/shard_map/ppermute | solution.py:952
  7.9 12.1 %collective-permute-start.3 = (bf16[112,576]{1,0:T(8,128)(2,1)S(1)}, bf16[112,576]{1,0:T(8,128)(2,1)S(1)}, u32[]{:S(2)}, u32[]{:S(2)}) collective-permute-start(bf16[112,576]{1,0:T(8,128)(2,1)S(1)} %get-tuple-element.100._), channel_id=1, source_target_pairs={{0,1},{1,2},{2,3},{3,0},{4,5},{5,6},{6,7},{7,4},{8,9},{9,10},{10,1... | collective-permute-start | bytes 387080 | tf_op jit(solution)/shard_map/ppermute | solution.py:952
  8.9 12.3 %collective-permute-start.2 = (bf16[128,768]{1,0:T(8,128)(2,1)}, bf16[128,768]{1,0:T(8,128)(2,1)S(1)}, u32[]{:S(2)}, u32[]{:S(2)}) collective-permute-start(bf16[128,768]{1,0:T(8,128)(2,1)} %bitcast.43), channel_id=1, source_target_pairs={{0,24},{4,28},{8,16},{12,20},{16,8},{20,12},{24,0},{28,4},{1,25},{... | collective-permute-start | bytes 589832 | tf_op jit(solution)/shard_map/ppermute | solution.py:947
  11.5 10.5 %collective-permute-start.1 = (bf16[128,768]{1,0:T(8,128)(2,1)}, bf16[128,768]{1,0:T(8,128)(2,1)S(1)}, u32[]{:S(2)}, u32[]{:S(2)}) collective-permute-start(bf16[128,768]{1,0:T(8,128)(2,1)} %bitcast.44), channel_id=1, source_target_pairs={{0,16},{4,20},{8,24},{12,28},{16,0},{20,4},{24,8},{28,12},{1,17},{... | collective-permute-start | bytes 589832 | tf_op jit(solution)/shard_map/ppermute | solution.py:947
  16.2 7.2 %collective-permute-start = (bf16[128,768]{1,0:T(8,128)(2,1)S(1)}, bf16[128,768]{1,0:T(8,128)(2,1)S(1)}, u32[]{:S(2)}, u32[]{:S(2)}) collective-permute-start(bf16[128,768]{1,0:T(8,128)(2,1)S(1)} %bitcast.45), channel_id=1, source_target_pairs={{0,8},{4,12},{8,0},{12,4},{16,24},{20,28},{24,16},{28,20},{1,9},{5... | collective-permute-start | bytes 589832 | tf_op jit(solution)/shard_map/ppermute | solution.py:947
  20.1 6.7 %collective-permute-start.7 = (bf16[112,576]{1,0:T(8,128)(2,1)S(1)}, bf16[112,576]{1,0:T(8,128)(2,1)S(1)}, u32[]{:S(2)}, u32[]{:S(2)}) collective-permute-start(bf16[112,576]{1,0:T(8,128)(2,1)S(1)} %collective-permute-done.4.refs_7_), channel_id=1, source_target_pairs={{0,4},{4,0},{8,12},{12,8},{16,20},{20,16},{24,28},{28,24},{1,5},{5... | collective-permute-start | bytes 387080 | tf_op jit(solution)/shard_map/ppermute | solution.py:942
  21.2 5.6 %collective-permute-start.6 = (bf16[112,576]{1,0:T(8,128)(2,1)S(1)}, bf16[112,576]{1,0:T(8,128)(2,1)S(1)}, u32[]{:S(2)}, u32[]{:S(2)}) collective-permute-start(bf16[112,576]{1,0:T(8,128)(2,1)S(1)} %collective-permute-done.3.refs_6_), channel_id=1, source_target_pairs={{0,4},{4,0},{8,12},{12,8},{16,20},{20,16},{24,28},{28,24},{1,5},{5... | collective-permute-start | bytes 387080 | tf_op jit(solution)/shard_map/ppermute | solution.py:942
  22.0 25.6 %collective-permute-start.16 = (bf16[288,768]{1,0:T(8,128)(2,1)}, bf16[288,768]{1,0:T(8,128)(2,1)S(1)}, u32[]{:S(2)}, u32[]{:S(2)}) collective-permute-start(bf16[288,768]{1,0:T(8,128)(2,1)} %get-tuple-element.109), channel_id=1, source_target_pairs={{0,3},{1,0},{2,1},{3,2},{4,7},{5,4},{6,5},{7,6},{8,11},{9,8},{10,9... | collective-permute-start | bytes 1327112 | tf_op jit(solution)/shard_map/ppermute | solution.py:952
  23.5 40.4 %collective-permute-start.15 = (bf16[288,768]{1,0:T(8,128)(2,1)}, bf16[288,768]{1,0:T(8,128)(2,1)}, u32[]{:S(2)}, u32[]{:S(2)}) collective-permute-start(bf16[288,768]{1,0:T(8,128)(2,1)} %get-tuple-element.109), channel_id=1, source_target_pairs={{0,2},{1,3},{2,0},{3,1},{4,6},{5,7},{6,4},{7,5},{8,10},{9,11},{10,... | collective-permute-start | bytes 1327112 | tf_op jit(solution)/shard_map/ppermute | solution.py:952
  24.8 39.0 %collective-permute-start.14 = (bf16[288,768]{1,0:T(8,128)(2,1)}, bf16[288,768]{1,0:T(8,128)(2,1)}, u32[]{:S(2)}, u32[]{:S(2)}) collective-permute-start(bf16[288,768]{1,0:T(8,128)(2,1)} %get-tuple-element.109), channel_id=1, source_target_pairs={{0,1},{1,2},{2,3},{3,0},{4,5},{5,6},{6,7},{7,4},{8,9},{9,10},{10,1... | collective-permute-start | bytes 1327112 | tf_op jit(solution)/shard_map/ppermute | solution.py:952
  44.4 10.1 %collective-permute-start.13 = (bf16[512,192]{1,0:T(8,128)(2,1)S(1)}, bf16[512,192]{1,0:T(8,128)(2,1)S(1)}, u32[]{:S(2)}, u32[]{:S(2)}) collective-permute-start(bf16[512,192]{1,0:T(8,128)(2,1)S(1)} %add.134.refs_0_.refs_4_), channel_id=1, source_target_pairs={{0,24},{4,28},{8,16},{12,20},{16,8},{20,12},{24,0},{28,4},{1,25},{... | collective-permute-start | bytes 589832 | tf_op jit(solution)/shard_map/ppermute | solution.py:947
  47.1 12.6 %collective-permute-start.12 = (bf16[512,192]{1,0:T(8,128)(2,1)S(1)}, bf16[512,192]{1,0:T(8,128)(2,1)S(1)}, u32[]{:S(2)}, u32[]{:S(2)}) collective-permute-start(bf16[512,192]{1,0:T(8,128)(2,1)S(1)} %add.134.refs_0_.refs_4_), channel_id=1, source_target_pairs={{0,16},{4,20},{8,24},{12,28},{16,0},{20,4},{24,8},{28,12},{1,17},{... | collective-permute-start | bytes 589832 | tf_op jit(solution)/shard_map/ppermute | solution.py:947
  47.6 12.2 %collective-permute-start.11 = (bf16[512,192]{1,0:T(8,128)(2,1)S(1)}, bf16[512,192]{1,0:T(8,128)(2,1)S(1)}, u32[]{:S(2)}, u32[]{:S(2)}) collective-permute-start(bf16[512,192]{1,0:T(8,128)(2,1)S(1)} %add.134.refs_0_.refs_4_), channel_id=1, source_target_pairs={{0,8},{4,12},{8,0},{12,4},{16,24},{20,28},{24,16},{28,20},{1,9},{5... | collective-permute-start | bytes 589832 | tf_op jit(solution)/shard_map/ppermute | solution.py:947
  76.0 7.7 %collective-permute-start.20 = (bf16[128,768]{1,0:T(8,128)(2,1)S(1)}, bf16[128,768]{1,0:T(8,128)(2,1)S(1)}, u32[]{:S(2)}, u32[]{:S(2)}) collective-permute-start(bf16[128,768]{1,0:T(8,128)(2,1)S(1)} %get-tuple-element.119), channel_id=1, source_target_pairs={{0,8},{4,12},{8,0},{12,4},{16,24},{20,28},{24,16},{28,20},{1,9},{5... | collective-permute-start | bytes 589832 | tf_op jit(solution)/shard_map/ppermute | solution.py:947
  77.6 10.9 %collective-permute-start.21 = (bf16[128,768]{1,0:T(8,128)(2,1)S(1)}, bf16[128,768]{1,0:T(8,128)(2,1)S(1)}, u32[]{:S(2)}, u32[]{:S(2)}) collective-permute-start(bf16[128,768]{1,0:T(8,128)(2,1)S(1)} %get-tuple-element.120), channel_id=1, source_target_pairs={{0,16},{4,20},{8,24},{12,28},{16,0},{20,4},{24,8},{28,12},{1,17},{... | collective-permute-start | bytes 589832 | tf_op jit(solution)/shard_map/ppermute | solution.py:947
  79.1 9.4 %collective-permute-start.22 = (bf16[128,768]{1,0:T(8,128)(2,1)S(1)}, bf16[128,768]{1,0:T(8,128)(2,1)S(1)}, u32[]{:S(2)}, u32[]{:S(2)}) collective-permute-start(bf16[128,768]{1,0:T(8,128)(2,1)S(1)} %get-tuple-element.121), channel_id=1, source_target_pairs={{0,24},{4,28},{8,16},{12,20},{16,8},{20,12},{24,0},{28,4},{1,25},{... | collective-permute-start | bytes 589832 | tf_op jit(solution)/shard_map/ppermute | solution.py:947
  89.5 9.3 %collective-permute-start.29 = (bf16[144,768]{1,0:T(8,128)(2,1)S(1)}, bf16[144,768]{1,0:T(8,128)(2,1)S(1)}, u32[]{:S(2)}, u32[]{:S(2)}) collective-permute-start(bf16[144,768]{1,0:T(8,128)(2,1)S(1)} %get-tuple-element.130.refs_0_), channel_id=1, source_target_pairs={{0,24},{4,28},{8,16},{12,20},{16,8},{20,12},{24,0},{28,4},{1,25},{... | collective-permute-start | bytes 663560 | tf_op jit(solution)/shard_map/ppermute | solution.py:947
  91.1 10.3 %collective-permute-start.28 = (bf16[144,768]{1,0:T(8,128)(2,1)S(1)}, bf16[144,768]{1,0:T(8,128)(2,1)S(1)}, u32[]{:S(2)}, u32[]{:S(2)}) collective-permute-start(bf16[144,768]{1,0:T(8,128)(2,1)S(1)} %get-tuple-element.130.refs_0_), channel_id=1, source_target_pairs={{0,16},{4,20},{8,24},{12,28},{16,0},{20,4},{24,8},{28,12},{1,17},{... | collective-permute-start | bytes 663560 | tf_op jit(solution)/shard_map/ppermute | solution.py:947
  92.2 9.4 %collective-permute-start.27 = (bf16[144,768]{1,0:T(8,128)(2,1)S(1)}, bf16[144,768]{1,0:T(8,128)(2,1)S(1)}, u32[]{:S(2)}, u32[]{:S(2)}) collective-permute-start(bf16[144,768]{1,0:T(8,128)(2,1)S(1)} %get-tuple-element.130.refs_0_), channel_id=1, source_target_pairs={{0,8},{4,12},{8,0},{12,4},{16,24},{20,28},{24,16},{28,20},{1,9},{5... | collective-permute-start | bytes 663560 | tf_op jit(solution)/shard_map/ppermute | solution.py:947
  105.4 8.5 %collective-permute-start.30 = (bf16[128,768]{1,0:T(8,128)(2,1)S(1)}, bf16[128,768]{1,0:T(8,128)(2,1)S(1)}, u32[]{:S(2)}, u32[]{:S(2)}) collective-permute-start(bf16[128,768]{1,0:T(8,128)(2,1)S(1)} %get-tuple-element.132), channel_id=1, source_target_pairs={{0,8},{4,12},{8,0},{12,4},{16,24},{20,28},{24,16},{28,20},{1,9},{5... | collective-permute-start | bytes 589832 | tf_op jit(solution)/shard_map/ppermute | solution.py:947
  108.5 17.6 %collective-permute-start.39 = (bf16[192,768]{1,0:T(8,128)(2,1)S(1)}, bf16[192,768]{1,0:T(8,128)(2,1)S(1)}, u32[]{:S(2)}, u32[]{:S(2)}) collective-permute-start(bf16[192,768]{1,0:T(8,128)(2,1)S(1)} %get-tuple-element.183), channel_id=1, source_target_pairs={{0,3},{1,0},{2,1},{3,2},{4,7},{5,4},{6,5},{7,6},{8,11},{9,8},{10,9... | collective-permute-start | bytes 884744 | tf_op jit(solution)/shard_map/ppermute | solution.py:952
  108.6 28.1 %collective-permute-start.38 = (bf16[192,768]{1,0:T(8,128)(2,1)S(1)}, bf16[192,768]{1,0:T(8,128)(2,1)S(1)}, u32[]{:S(2)}, u32[]{:S(2)}) collective-permute-start(bf16[192,768]{1,0:T(8,128)(2,1)S(1)} %get-tuple-element.184), channel_id=1, source_target_pairs={{0,2},{1,3},{2,0},{3,1},{4,6},{5,7},{6,4},{7,5},{8,10},{9,11},{10,... | collective-permute-start | bytes 884744 | tf_op jit(solution)/shard_map/ppermute | solution.py:952
  110.5 26.2 %collective-permute-start.37 = (bf16[192,768]{1,0:T(8,128)(2,1)S(1)}, bf16[192,768]{1,0:T(8,128)(2,1)S(1)}, u32[]{:S(2)}, u32[]{:S(2)}) collective-permute-start(bf16[192,768]{1,0:T(8,128)(2,1)S(1)} %get-tuple-element.185), channel_id=1, source_target_pairs={{0,1},{1,2},{2,3},{3,0},{4,5},{5,6},{6,7},{7,4},{8,9},{9,10},{10,1... | collective-permute-start | bytes 884744 | tf_op jit(solution)/shard_map/ppermute | solution.py:952
  112.5 10.3 %collective-permute-start.31 = (bf16[128,768]{1,0:T(8,128)(2,1)S(1)}, bf16[128,768]{1,0:T(8,128)(2,1)S(1)}, u32[]{:S(2)}, u32[]{:S(2)}) collective-permute-start(bf16[128,768]{1,0:T(8,128)(2,1)S(1)} %get-tuple-element.133), channel_id=1, source_target_pairs={{0,16},{4,20},{8,24},{12,28},{16,0},{20,4},{24,8},{28,12},{1,17},{... | collective-permute-start | bytes 589832 | tf_op jit(solution)/shard_map/ppermute | solution.py:947
  113.9 8.9 %collective-permute-start.32 = (bf16[128,768]{1,0:T(8,128)(2,1)S(1)}, bf16[128,768]{1,0:T(8,128)(2,1)S(1)}, u32[]{:S(2)}, u32[]{:S(2)}) collective-permute-start(bf16[128,768]{1,0:T(8,128)(2,1)S(1)} %get-tuple-element.134), channel_id=1, source_target_pairs={{0,24},{4,28},{8,16},{12,20},{16,8},{20,12},{24,0},{28,4},{1,25},{... | collective-permute-start | bytes 589832 | tf_op jit(solution)/shard_map/ppermute | solution.py:947
  123.1 13.8 %collective-permute-start.36 = (bf16[144,768]{1,0:T(8,128)(2,1)S(1)}, bf16[144,768]{1,0:T(8,128)(2,1)S(1)}, u32[]{:S(2)}, u32[]{:S(2)}) collective-permute-start(bf16[144,768]{1,0:T(8,128)(2,1)S(1)} %get-tuple-element.143.refs_0_), channel_id=1, source_target_pairs={{0,24},{4,28},{8,16},{12,20},{16,8},{20,12},{24,0},{28,4},{1,25},{... | collective-permute-start | bytes 663560 | tf_op jit(solution)/shard_map/ppermute | solution.py:947
  124.7 12.3 %collective-permute-start.35 = (bf16[144,768]{1,0:T(8,128)(2,1)S(1)}, bf16[144,768]{1,0:T(8,128)(2,1)S(1)}, u32[]{:S(2)}, u32[]{:S(2)}) collective-permute-start(bf16[144,768]{1,0:T(8,128)(2,1)S(1)} %get-tuple-element.143.refs_0_), channel_id=1, source_target_pairs={{0,16},{4,20},{8,24},{12,28},{16,0},{20,4},{24,8},{28,12},{1,17},{... | collective-permute-start | bytes 663560 | tf_op jit(solution)/shard_map/ppermute | solution.py:947
  126.1 10.8 %collective-permute-start.34 = (bf16[144,768]{1,0:T(8,128)(2,1)S(1)}, bf16[144,768]{1,0:T(8,128)(2,1)S(1)}, u32[]{:S(2)}, u32[]{:S(2)}) collective-permute-start(bf16[144,768]{1,0:T(8,128)(2,1)S(1)} %get-tuple-element.143.refs_0_), channel_id=1, source_target_pairs={{0,8},{4,12},{8,0},{12,4},{16,24},{20,28},{24,16},{28,20},{1,9},{5... | collective-permute-start | bytes 663560 | tf_op jit(solution)/shard_map/ppermute | solution.py:947
  145.1 10.9 %collective-permute-start.41 = (bf16[1024,640]{1,0:T(8,128)(2,1)S(1)}, bf16[1024,640]{1,0:T(8,128)(2,1)S(1)}, u32[]{:S(2)}, u32[]{:S(2)}) collective-permute-start(bf16[1024,640]{1,0:T(8,128)(2,1)S(1)} %attend_back.1.mine), channel_id=1, source_target_pairs={{0,4},{4,0},{8,12},{12,8},{16,20},{20,16},{24,28},{28,24},{1,5},{5... | collective-permute-start | bytes 3932168 | tf_op jit(solution)/shard_map/ppermute | solution.py:942
  145.5 15.7 %collective-permute-start.47 = (bf16[192,768]{1,0:T(8,128)(2,1)S(1)}, bf16[192,768]{1,0:T(8,128)(2,1)S(1)}, u32[]{:S(2)}, u32[]{:S(2)}) collective-permute-start(bf16[192,768]{1,0:T(8,128)(2,1)S(1)} %fusion.6.refs_0_), channel_id=1, source_target_pairs={{0,24},{4,28},{8,16},{12,20},{16,8},{20,12},{24,0},{28,4},{1,25},{... | collective-permute-start | bytes 884744 | tf_op jit(solution)/shard_map/ppermute | solution.py:947
  147.0 7.5 %collective-permute-start.55 = (bf16[64,768]{1,0:T(8,128)(2,1)S(1)}, bf16[64,768]{1,0:T(8,128)(2,1)S(1)}, u32[]{:S(2)}, u32[]{:S(2)}) collective-permute-start(bf16[64,768]{1,0:T(8,128)(2,1)S(1)} %get-tuple-element.164), channel_id=1, source_target_pairs={{0,1},{1,2},{2,3},{3,0},{4,5},{5,6},{6,7},{7,4},{8,9},{9,10},{10,1... | collective-permute-start | bytes 294920 | tf_op jit(solution)/shard_map/ppermute | solution.py:952
  147.0 11.2 %collective-permute-start.56 = (bf16[64,768]{1,0:T(8,128)(2,1)S(1)}, bf16[64,768]{1,0:T(8,128)(2,1)S(1)}, u32[]{:S(2)}, u32[]{:S(2)}) collective-permute-start(bf16[64,768]{1,0:T(8,128)(2,1)S(1)} %get-tuple-element.166), channel_id=1, source_target_pairs={{0,2},{1,3},{2,0},{3,1},{4,6},{5,7},{6,4},{7,5},{8,10},{9,11},{10,... | collective-permute-start | bytes 294920 | tf_op jit(solution)/shard_map/ppermute | solution.py:952
  148.1 10.4 %collective-permute-start.57 = (bf16[64,768]{1,0:T(8,128)(2,1)S(1)}, bf16[64,768]{1,0:T(8,128)(2,1)S(1)}, u32[]{:S(2)}, u32[]{:S(2)}) collective-permute-start(bf16[64,768]{1,0:T(8,128)(2,1)S(1)} %get-tuple-element.168), channel_id=1, source_target_pairs={{0,3},{1,0},{2,1},{3,2},{4,7},{5,4},{6,5},{7,6},{8,11},{9,8},{10,9... | collective-permute-start | bytes 294920 | tf_op jit(solution)/shard_map/ppermute | solution.py:952
  154.5 10.5 %collective-permute-start.46 = (bf16[192,768]{1,0:T(8,128)(2,1)S(1)}, bf16[192,768]{1,0:T(8,128)(2,1)S(1)}, u32[]{:S(2)}, u32[]{:S(2)}) collective-permute-start(bf16[192,768]{1,0:T(8,128)(2,1)S(1)} %fusion.6.refs_0_), channel_id=1, source_target_pairs={{0,16},{4,20},{8,24},{12,28},{16,0},{20,4},{24,8},{28,12},{1,17},{... | collective-permute-start | bytes 884744 | tf_op jit(solution)/shard_map/ppermute | solution.py:947
  155.9 9.2 %collective-permute-start.45 = (bf16[192,768]{1,0:T(8,128)(2,1)S(1)}, bf16[192,768]{1,0:T(8,128)(2,1)S(1)}, u32[]{:S(2)}, u32[]{:S(2)}) collective-permute-start(bf16[192,768]{1,0:T(8,128)(2,1)S(1)} %fusion.6.refs_0_), channel_id=1, source_target_pairs={{0,8},{4,12},{8,0},{12,4},{16,24},{20,28},{24,16},{28,20},{1,9},{5... | collective-permute-start | bytes 884744 | tf_op jit(solution)/shard_map/ppermute | solution.py:947
  158.2 7.8 %collective-permute-start.52 = (bf16[80,768]{1,0:T(8,128)(2,1)S(1)}, bf16[80,768]{1,0:T(8,128)(2,1)S(1)}, u32[]{:S(2)}, u32[]{:S(2)}) collective-permute-start(bf16[80,768]{1,0:T(8,128)(2,1)S(1)} %get-tuple-element.151), channel_id=1, source_target_pairs={{0,1},{1,2},{2,3},{3,0},{4,5},{5,6},{6,7},{7,4},{8,9},{9,10},{10,1... | collective-permute-start | bytes 368648 | tf_op jit(solution)/shard_map/ppermute | solution.py:952
  158.5 10.2 %collective-permute-start.53 = (bf16[80,768]{1,0:T(8,128)(2,1)S(1)}, bf16[80,768]{1,0:T(8,128)(2,1)S(1)}, u32[]{:S(2)}, u32[]{:S(2)}) collective-permute-start(bf16[80,768]{1,0:T(8,128)(2,1)S(1)} %get-tuple-element.152), channel_id=1, source_target_pairs={{0,2},{1,3},{2,0},{3,1},{4,6},{5,7},{6,4},{7,5},{8,10},{9,11},{10,... | collective-permute-start | bytes 368648 | tf_op jit(solution)/shard_map/ppermute | solution.py:952
  161.2 7.7 %collective-permute-start.54 = (bf16[80,768]{1,0:T(8,128)(2,1)S(1)}, bf16[80,768]{1,0:T(8,128)(2,1)S(1)}, u32[]{:S(2)}, u32[]{:S(2)}) collective-permute-start(bf16[80,768]{1,0:T(8,128)(2,1)S(1)} %get-tuple-element.153), channel_id=1, source_target_pairs={{0,3},{1,0},{2,1},{3,2},{4,7},{5,4},{6,5},{7,6},{8,11},{9,8},{10,9... | collective-permute-start | bytes 368648 | tf_op jit(solution)/shard_map/ppermute | solution.py:952
  165.0 5.4 %collective-permute-start.48 = (bf16[192,768]{1,0:T(8,128)(2,1)S(1)}, bf16[192,768]{1,0:T(8,128)(2,1)S(1)}, u32[]{:S(2)}, u32[]{:S(2)}) collective-permute-start(bf16[192,768]{1,0:T(8,128)(2,1)S(1)} %fusion.6.refs_0_), channel_id=1, source_target_pairs={{0,4},{4,0},{8,12},{12,8},{16,20},{20,16},{24,28},{28,24},{1,5},{5... | collective-permute-start | bytes 884744 | tf_op jit(solution)/shard_map/ppermute | solution.py:942
  165.1 6.9 %collective-permute-start.51 = (bf16[192,768]{1,0:T(8,128)(2,1)S(1)}, bf16[192,768]{1,0:T(8,128)(2,1)S(1)}, u32[]{:S(2)}, u32[]{:S(2)}) collective-permute-start(bf16[192,768]{1,0:T(8,128)(2,1)S(1)} %collective-permute-done.47.refs_3_), channel_id=1, source_target_pairs={{0,4},{4,0},{8,12},{12,8},{16,20},{20,16},{24,28},{28,24},{1,5},{5... | collective-permute-start | bytes 884744 | tf_op jit(solution)/shard_map/ppermute | solution.py:942
  166.1 6.5 %collective-permute-start.50 = (bf16[192,768]{1,0:T(8,128)(2,1)S(1)}, bf16[192,768]{1,0:T(8,128)(2,1)S(1)}, u32[]{:S(2)}, u32[]{:S(2)}) collective-permute-start(bf16[192,768]{1,0:T(8,128)(2,1)S(1)} %collective-permute-done.46.refs_2_), channel_id=1, source_target_pairs={{0,4},{4,0},{8,12},{12,8},{16,20},{20,16},{24,28},{28,24},{1,5},{5... | collective-permute-start | bytes 884744 | tf_op jit(solution)/shard_map/ppermute | solution.py:942
  168.9 7.7 %collective-permute-start.42 = (bf16[128,768]{1,0:T(8,128)(2,1)S(1)}, bf16[128,768]{1,0:T(8,128)(2,1)S(1)}, u32[]{:S(2)}, u32[]{:S(2)}) collective-permute-start(bf16[128,768]{1,0:T(8,128)(2,1)S(1)} %get-tuple-element.157), channel_id=1, source_target_pairs={{0,8},{4,12},{8,0},{12,4},{16,24},{20,28},{24,16},{28,20},{1,9},{5... | collective-permute-start | bytes 589832 | tf_op jit(solution)/shard_map/ppermute | solution.py:947
  170.4 21.9 %collective-permute-start.60 = (bf16[144,768]{1,0:T(8,128)(2,1)S(1)}, bf16[144,768]{1,0:T(8,128)(2,1)S(1)}, u32[]{:S(2)}, u32[]{:S(2)}) collective-permute-start(bf16[144,768]{1,0:T(8,128)(2,1)S(1)} %pad_maximum_fusion.refs_0_), channel_id=1, source_target_pairs={{0,24},{4,28},{8,16},{12,20},{16,8},{20,12},{24,0},{28,4},{1,25},{... | collective-permute-start | bytes 663560 | tf_op jit(solution)/shard_map/ppermute | solution.py:947
  172.0 20.8 %collective-permute-start.59 = (bf16[144,768]{1,0:T(8,128)(2,1)S(1)}, bf16[144,768]{1,0:T(8,128)(2,1)S(1)}, u32[]{:S(2)}, u32[]{:S(2)}) collective-permute-start(bf16[144,768]{1,0:T(8,128)(2,1)S(1)} %pad_maximum_fusion.refs_0_), channel_id=1, source_target_pairs={{0,16},{4,20},{8,24},{12,28},{16,0},{20,4},{24,8},{28,12},{1,17},{... | collective-permute-start | bytes 663560 | tf_op jit(solution)/shard_map/ppermute | solution.py:947
  172.6 20.3 %collective-permute-start.58 = (bf16[144,768]{1,0:T(8,128)(2,1)S(1)}, bf16[144,768]{1,0:T(8,128)(2,1)S(1)}, u32[]{:S(2)}, u32[]{:S(2)}) collective-permute-start(bf16[144,768]{1,0:T(8,128)(2,1)S(1)} %pad_maximum_fusion.refs_0_), channel_id=1, source_target_pairs={{0,8},{4,12},{8,0},{12,4},{16,24},{20,28},{24,16},{28,20},{1,9},{5... | collective-permute-start | bytes 663560 | tf_op jit(solution)/shard_map/ppermute | solution.py:947
  174.0 18.3 %collective-permute-start.43 = (bf16[128,768]{1,0:T(8,128)(2,1)S(1)}, bf16[128,768]{1,0:T(8,128)(2,1)S(1)}, u32[]{:S(2)}, u32[]{:S(2)}) collective-permute-start(bf16[128,768]{1,0:T(8,128)(2,1)S(1)} %get-tuple-element.158), channel_id=1, source_target_pairs={{0,16},{4,20},{8,24},{12,28},{16,0},{20,4},{24,8},{28,12},{1,17},{... | collective-permute-start | bytes 589832 | tf_op jit(solution)/shard_map/ppermute | solution.py:947
  176.7 16.7 %collective-permute-start.44 = (bf16[128,768]{1,0:T(8,128)(2,1)S(1)}, bf16[128,768]{1,0:T(8,128)(2,1)S(1)}, u32[]{:S(2)}, u32[]{:S(2)}) collective-permute-start(bf16[128,768]{1,0:T(8,128)(2,1)S(1)} %get-tuple-element.159), channel_id=1, source_target_pairs={{0,24},{4,28},{8,16},{12,20},{16,8},{20,12},{24,0},{28,4},{1,25},{... | collective-permute-start | bytes 589832 | tf_op jit(solution)/shard_map/ppermute | solution.py:947
  (27 other events, 144.2 us)

commit v3 on v2

--- a/solution.py
+++ b/solution.py
@@ -363,13 +363,14 @@
 FAR = pl.BlockSpec(memory_space=pltpu.HBM)
 SMEM = pl.BlockSpec(memory_space=pltpu.SMEM)
 VEC = 16
+SLAB = 64
 
 
 def shaped(shape, dtype):
     return jax.ShapeDtypeStruct(shape, dtype)
 
 
-def call(kernel, outs, ins, args, scratch=(), flops=0, name=None):
+def call(kernel, outs, ins, args, scratch=(), name=None, weight=1):
     moved = sum(a.size * a.dtype.itemsize for a in args)
     moved += sum(o.size * o.dtype.itemsize for o in outs)
     held = sum(
@@ -384,11 +385,20 @@
         out_specs=[VMEM] * len(outs),
         scratch_shapes=list(scratch),
         name=name,
-        cost_estimate=pl.CostEstimate(flops=1, transcendentals=0, bytes_accessed=1),
+        cost_estimate=pl.CostEstimate(flops=weight, transcendentals=0, bytes_accessed=weight),
         compiler_params=pltpu.CompilerParams(vmem_limit_bytes=moved + held + (4 << 20)),
     )(*args)
 
 
+def mix(function, outs, *args, name=None):
+    def kernel(*refs):
+        found = function(*(ref[...] for ref in refs[: len(args)]))
+        for ref, value in zip(refs[len(args) :], found):
+            ref[...] = value
+
+    return call(kernel, outs, [VMEM] * len(args), args, name=name)
+
+
 def dot(left, right):
     return jnp.dot(left, right, preferred_element_type=F32)
 
@@ -399,10 +409,6 @@
 
 def dot_tn(left, right):
     return lax.dot_general(left, right, (((0,), (0,)), ((), ())), preferred_element_type=F32)
-
-
-def turned(ring, f, s):
-    return lax.rem(f - s + ring, ring)
 
 
 class Plan:
@@ -423,6 +429,7 @@
         self.wide = -(-self.qkv // 128) * 128
         self.packed = self.half * self.qkv // width
         self.clusters = chips
+        self.members = CLUSTER // (2 * chips)
         self.entries = chips * CLUSTER
 
 
@@ -443,12 +450,10 @@
 
         @pl.when(p == q)
         def _(q=q):
-            for h in range(g.heads):
-                for i in range(3):
-                    src = g.cols * q + DH * h
-                    qall[:, 3 * DH * h + DH * i : 3 * DH * h + DH * (i + 1)] = here[
-                        i, :, src : src + DH
-                    ]
+            for i in range(3):
+                qall[:, g.cols * i : g.cols * (i + 1)] = here[
+                    i, :, g.cols * q : g.cols * (q + 1)
+                ]
 
     vec[...] = jnp.zeros((VEC, LANES), BF)
     for i in range(8):
@@ -488,8 +493,8 @@
     finish(copies[1:])
 
 
-def gathers(g, sc, own, own_at, mine, theirs, at, piece, dst, sem):
-    k, f = sc[1], sc[2]
+def gathers(g, sc, own, own_at, mine, theirs, at, piece, dst, sem, turn=0):
+    k, f = sc[1], jnp.bitwise_xor(sc[2], turn)
     size = piece
     out = [
         pltpu.make_async_copy(
@@ -499,7 +504,7 @@
         )
     ]
     for s in range(1, g.ring):
-        base = 2 * size * turned(g.ring, f, s)
+        base = 2 * size * jnp.bitwise_xor(f, s)
         for i, (src, core) in enumerate(((mine[s - 1], k), (theirs[s - 1], 1 - k))):
             out.append(
                 pltpu.make_async_copy(
@@ -522,12 +527,12 @@
 
 
 def qkv_kernel(g, sc, *refs):
-    n = g.ring - 1
-    xs = refs[: g.chips]
-    vec, own = refs[g.chips : g.chips + 2]
-    mine = refs[g.chips + 2 : g.chips + 2 + n]
-    theirs = refs[g.chips + 2 + n : g.chips + 2 + 2 * n]
-    out, w, full, vs, sem, vsem = refs[g.chips + 2 + 2 * n :]
+    n, c = g.ring - 1, 2 * g.chips
+    xs = refs[:c]
+    vec, own = refs[c : c + 2]
+    mine = refs[c + 2 : c + 2 + n]
+    theirs = refs[c + 2 + n : c + 2 + 2 * n]
+    out, w, full, vs, sem, vsem = refs[c + 2 + 2 * n :]
     p, f = sc[0], sc[2]
     copies = gathers(g, sc, own, 0, mine, theirs, 0, g.half, w, sem)
     start(copies)
@@ -544,20 +549,21 @@
     for s in range(g.ring):
         piece = (vec[...] if s == 0 else vs[s - 1]).astype(F32)
         wide = jnp.concatenate([piece, rest], axis=1)
-        total = total + pltpu.roll(wide, g.shard * turned(g.ring, f, s), 1)
+        total = total + pltpu.roll(wide, g.shard * jnp.bitwise_xor(f, s), 1)
     full[...] = total
     back = pltpu.roll(total, lax.rem(g.width - g.cols * p, g.width), 1)
-    gap = jnp.zeros((1, DH), F32)
-    parts = []
-    for h in range(g.heads):
-        parts += [back[0:1, DH * h : DH * (h + 1)], gap, back[1:2, DH * h : DH * (h + 1)]]
-    bias = jnp.concatenate(parts, axis=1)
+    bias = jnp.concatenate(
+        [back[0:1, : g.cols], jnp.zeros((1, g.cols), F32), back[1:2, : g.cols]], axis=1
+    )
     finish(copies)
     rows = jnp.concatenate([x[...] for x in xs], axis=0)
     found = (dot(rows, w[...]) + bias).astype(BF)
     for h in range(g.heads):
-        out[:, LANES * h : LANES * h + 3 * DH] = found[:, 3 * DH * h : 3 * DH * (h + 1)]
-        out[:, LANES * h + 3 * DH : LANES * (h + 1)] = jnp.zeros((g.tokens, DH), BF)
+        for i in range(3):
+            out[:, LANES * h + DH * i : LANES * h + DH * (i + 1)] = found[
+                :, g.cols * i + DH * h : g.cols * i + DH * (h + 1)
+            ]
+        out[:, LANES * h + 3 * DH : LANES * (h + 1)] = jnp.zeros((2 * g.tokens, DH), BF)
 
 
 def select(index, size, axis_size, lanes):
@@ -568,60 +574,166 @@
     return jnp.where(ids == index, 1.0, 0.0).astype(BF)
 
 
-def attend_kernel(g, own, other, posr, posc, blocks, ctx_own, ctx_other, kept, probs):
-    both = 2 * g.tokens
+def over(x, size):
+    return lax.shift_right_logical(x, jnp.int32(size.bit_length() - 1))
+
+
+def tables_kernel(g, sc, _, clusters, block_ids, pick, place, blocks):
+    p, k = sc[0], sc[1]
+    ranges, step = 2 * g.chips, g.clusters * g.members
+    shape = (2 * ranges, 2 * ranges)
+    piece, source = (lax.broadcasted_iota(jnp.int32, shape, axis) for axis in (0, 1))
+    device = 2 * jnp.bitwise_xor(p, over(piece, 2) & (g.chips - 1)) + jnp.bitwise_xor(
+        k, over(piece, 2 * g.chips)
+    )
+    found = jnp.where(piece & 1 == 0, device, 2 * ranges - 1 - device)
+    hot = jnp.where(found == source, 1.0, 0.0).astype(BF)
+    half = g.rows // 2
+    line = block_ids[...].astype(F32)
+    lines = [line[:, half * i : half * (i + 1)] for i in range(2 * ranges)]
+    ids = dot(hot, jnp.concatenate(lines, axis=0).astype(BF))
+    for d in range(ranges):
+        line = jnp.concatenate([ids[2 * d : 2 * d + 1], ids[2 * d + 1 : 2 * d + 2]], axis=1)
+        blocks[:, g.rows * d : g.rows * (d + 1)] = jnp.broadcast_to(line, (8, g.rows)).astype(BF)
+    before = lax.broadcasted_iota(jnp.int32, (CLUSTER, CLUSTER), 1) < lax.broadcasted_iota(
+        jnp.int32, (CLUSTER, CLUSTER), 0
+    )
+    rows, cols, tokens = [], [], []
     for h in range(g.heads):
-        pick = select(posc[:, h : h + 1], g.entries, both, True)
-        place = select(posr[h : h + 1, :], g.entries, both, False)
-        lanes = slice(LANES * h, LANES * (h + 1))
-        rows = jnp.concatenate([own[:, lanes], other[:, lanes]], axis=0)
-        picked = dot(pick, rows).astype(BF)
-        kept[h] = picked
-        ids = dot(blocks[...], place)
-        mixed = []
+        order = clusters[
+            pl.ds(g.heads * p + h, 1), pl.ds(pl.multiple_of(g.entries * k, 128), g.entries)
+        ]
+        chip, core = over(order, 2 * g.rows), over(order, g.rows) & 1
+        within = order & (g.rows - 1)
+        rows.append(
+            jnp.bitwise_xor(core, k) * g.tokens + jnp.bitwise_xor(chip, p) * g.rows + within
+        )
+    units = [(h, c) for h in range(g.heads) for c in range(g.clusters)]
+    for h, c in units:
+        row = rows[h][:, CLUSTER * c : CLUSTER * (c + 1)]
+        tall = jnp.broadcast_to(row.astype(F32), (CLUSTER, CLUSTER))
+        cols.append(over(jnp.transpose(tall)[:, 0:1].astype(jnp.int32), g.rows))
+    spots = []
+    for (h, c), col in zip(units, cols):
+        row = rows[h][:, CLUSTER * c : CLUSTER * (c + 1)]
+        same = (col == over(row, g.rows)) & before
+        rank = jnp.sum(jnp.where(same, 1.0, 0.0), axis=1, keepdims=True).astype(jnp.int32)
+        spots.append(select(col * g.members + rank, CLUSTER, CLUSTER, True))
+    for (h, c), spot in zip(units, spots):
+        row = rows[h][:, CLUSTER * c : CLUSTER * (c + 1)]
+        within = jnp.broadcast_to((row & (g.rows - 1)).astype(F32), (8, CLUSTER)).astype(BF)
+        tokens.append(dot(within, spot))
+    for h in range(g.heads):
+        for d in range(ranges):
+            lanes = slice(g.members * d, g.members * (d + 1))
+            mine = jnp.concatenate(
+                [tokens[h * g.clusters + c][:, lanes] for c in range(g.clusters)], axis=1
+            ).astype(jnp.int32)
+            place[h, g.rows * d : g.rows * (d + 1)] = select(mine[0:1, :], step, g.rows, False)
+            pick[h, step * d : step * (d + 1)] = select(
+                jnp.transpose(mine)[:, 0:1], step, g.rows, True
+            )
+
+
+def mask_kernel(g, blocks, place, mask):
+    ids = [
+        [
+            dot(blocks[:, g.rows * d : g.rows * (d + 1)], place[h, g.rows * d : g.rows * (d + 1)])
+            for d in range(2 * g.chips)
+        ]
+        for h in range(g.heads)
+    ]
+    for h in range(g.heads):
         for c in range(g.clusters):
-            at = slice(CLUSTER * c, CLUSTER * (c + 1))
-            q, key, v = picked[at, 0:DH], picked[at, DH : 2 * DH], picked[at, 2 * DH : 3 * DH]
-            scores = dot_nt(q, key) * (DH ** (-0.5))
-            row_ids = ids[:, at]
-            col_ids = jnp.transpose(row_ids)[:, 0:1]
-            allowed = row_ids[0:1, :] <= col_ids
-            masked = jnp.where(allowed, scores, FLOOR)
-            top = jnp.max(masked, axis=-1, keepdims=True)
-            weights = jnp.where(allowed, jnp.exp(masked - top), 0.0)
-            share = weights / jnp.sum(weights, axis=-1, keepdims=True)
-            probs[h * g.clusters + c] = share
-            mixed.append(dot(share.astype(BF), v).astype(BF))
-        back = dot(place, jnp.concatenate(mixed, axis=0)).astype(BF)
-        ctx_own[:, DH * h : DH * (h + 1)] = back[: g.tokens]
-        ctx_other[:, DH * h : DH * (h + 1)] = back[g.tokens :]
-
-
-def attend_back_kernel(g, own, other, posr, posc, kept, probs, grads):
-    both = 2 * g.tokens
-    rows = jnp.concatenate([own[...], other[...]], axis=0)
+            lanes = slice(g.members * c, g.members * (c + 1))
+            keys = jnp.concatenate([part[:, lanes] for part in ids[h]], axis=1)
+            allowed = keys[0:1, :] <= jnp.transpose(keys)[:, 0:1]
+            mask[h * g.clusters + c] = jnp.where(allowed, 0.0, FLOOR)
+
+
+def cluster_rows(g, ref, c):
+    step = g.clusters * g.members
+    return jnp.concatenate(
+        [
+            ref[step * d + g.members * c : step * d + g.members * (c + 1)]
+            for d in range(2 * g.chips)
+        ],
+        axis=0,
+    )
+
+
+def put_cluster(g, ref, c, values):
+    step = g.clusters * g.members
+    for d in range(2 * g.chips):
+        ref[step * d + g.members * c : step * d + g.members * (c + 1)] = values[
+            g.members * d : g.members * (d + 1)
+        ]
+
+
+def attend_kernel(g, qkv, pick, place, mask, ctx_own, ctx_other, kept, probs, mixed):
+    step, ranges = g.clusters * g.members, 2 * g.chips
+    units = [(h, c) for h in range(g.heads) for c in range(g.clusters)]
     for h in range(g.heads):
-        pick = select(posc[:, h : h + 1], g.entries, both, True)
-        place = select(posr[h : h + 1, :], g.entries, both, False)
-        d_mixed = dot(pick, rows[:, DH * h : DH * (h + 1)]).astype(BF)
-        picked = kept[h]
-        found = []
-        for c in range(g.clusters):
-            at = slice(CLUSTER * c, CLUSTER * (c + 1))
-            q, key, v = picked[at, 0:DH], picked[at, DH : 2 * DH], picked[at, 2 * DH : 3 * DH]
-            d_m = d_mixed[at]
-            share = probs[h * g.clusters + c]
-            d_share = dot_nt(d_m, v)
-            delta = jnp.sum(share * d_share, axis=-1, keepdims=True)
-            d_s = (share * (d_share - delta)).astype(BF)
-            scale = DH ** (-0.5)
-            d_q = dot(d_s, key) * scale
-            d_k = dot_tn(d_s, q) * scale
-            d_v = dot_tn(share.astype(BF), d_m)
-            found.append(jnp.concatenate([d_q, d_k, d_v], axis=1).astype(BF))
-        back = dot(place, jnp.concatenate(found, axis=0)).astype(BF)
-        grads[:, 3 * DH * h : 3 * DH * (h + 1)] = back
-    grads[:, g.qkv :] = jnp.zeros((both, g.wide - g.qkv), BF)
+        for d in range(ranges):
+            rows = qkv[g.rows * d : g.rows * (d + 1), LANES * h : LANES * (h + 1)]
+            slots = slice(step * d, step * (d + 1))
+            kept[h, slots] = dot(pick[h, slots], rows).astype(BF)
+    for h, c in units:
+        rows = cluster_rows(g, kept.at[h], c)
+        q, key = rows[:, 0:DH], rows[:, DH : 2 * DH]
+        at = h * g.clusters + c
+        probs[at] = dot_nt(q, key) * (DH ** (-0.5)) + mask[at]
+    for h, c in units:
+        at = h * g.clusters + c
+        masked = probs[at]
+        weights = jnp.exp(masked - jnp.max(masked, axis=-1, keepdims=True))
+        probs[at] = weights * (1.0 / jnp.sum(weights, axis=-1, keepdims=True))
+    for h, c in units:
+        v = cluster_rows(g, kept.at[h], c)[:, 2 * DH : 3 * DH]
+        put_cluster(
+            g, mixed.at[h], c, dot(probs[h * g.clusters + c].astype(BF), v).astype(BF)
+        )
+    for h in range(g.heads):
+        for d in range(ranges):
+            side, at = (ctx_own, d) if d < g.chips else (ctx_other, d - g.chips)
+            rows = dot(
+                place[h, g.rows * d : g.rows * (d + 1)], mixed[h, step * d : step * (d + 1)]
+            )
+            side[g.rows * at : g.rows * (at + 1), DH * h : DH * (h + 1)] = rows.astype(BF)
+
+
+def attend_back_kernel(g, own, other, pick, place, kept, probs, grads, d_mixed, found, d_scores):
+    step, ranges = g.clusters * g.members, 2 * g.chips
+    scale = DH ** (-0.5)
+    units = [(h, c) for h in range(g.heads) for c in range(g.clusters)]
+    for h in range(g.heads):
+        for d in range(ranges):
+            side, at = (own, d) if d < g.chips else (other, d - g.chips)
+            rows = side[g.rows * at : g.rows * (at + 1), DH * h : DH * (h + 1)]
+            slots = slice(step * d, step * (d + 1))
+            d_mixed[h, slots] = dot(pick[h, slots], rows).astype(BF)
+    for h, c in units:
+        v = cluster_rows(g, kept.at[h], c)[:, 2 * DH : 3 * DH]
+        share = probs[h * g.clusters + c]
+        d_share = dot_nt(cluster_rows(g, d_mixed.at[h], c), v)
+        delta = jnp.sum(share * d_share, axis=-1, keepdims=True)
+        d_scores[h * g.clusters + c] = (share * (d_share - delta)).astype(BF)
+    for h, c in units:
+        rows = cluster_rows(g, kept.at[h], c)
+        d_s, share = d_scores[h * g.clusters + c], probs[h * g.clusters + c].astype(BF)
+        d_q = dot(d_s, rows[:, DH : 2 * DH]) * scale
+        d_k = dot_tn(d_s, rows[:, 0:DH]) * scale
+        d_v = dot_tn(share, cluster_rows(g, d_mixed.at[h], c))
+        put_cluster(g, found.at[h], c, jnp.concatenate([d_q, d_k, d_v], axis=1).astype(BF))
+    for h in range(g.heads):
+        for d in range(ranges):
+            at = slice(g.rows * d, g.rows * (d + 1))
+            rows = dot(place[h, at], found[h, step * d : step * (d + 1)]).astype(BF)
+            for i in range(3):
+                grads[at, g.cols * i + DH * h : g.cols * i + DH * (h + 1)] = rows[
+                    :, DH * i : DH * (i + 1)
+                ]
+    grads[:, g.qkv :] = jnp.zeros((2 * g.tokens, g.wide - g.qkv), BF)
 
 
 def norm_parts(values):
@@ -645,52 +757,70 @@
     )
 
 
-def lay_kernel(g, sc, *refs):
-    n = g.ring - 1
-    wo_own, wi_own, wd_own = refs[:3]
-    mine, theirs = refs[3 : 3 + n], refs[3 + n : 3 + 2 * n]
-    wo, wi, wd, *sems = refs[3 + 2 * n :]
-    at = pl.multiple_of(g.block * sc[0], 16)
-    copies = gathers(g, sc, wo_own, 0, mine, theirs, g.half, g.half, wo, sems[0])
-    copies += gathers(g, sc, wi_own, 0, mine, theirs, 0, g.half, wi, sems[1])
-    copies += gathers(g, sc, wd_own, at, mine, theirs, 2 * g.half, g.bhalf, wd, sems[2])
-    start(copies)
-    finish(copies)
-
-
-def first_norm_kernel(g, sc, *refs):
-    c = g.chips
-    ctxs, xs, full, wo = refs[:c], refs[c : 2 * c], refs[2 * c], refs[2 * c + 1]
-    low, first_own, z_own, s_own, wo_rows = refs[2 * c + 2 :]
+def forward_kernel(g, sc, *refs):
+    c, n = g.chips, g.ring - 1
+    ctxs, xs, full = refs[:c], refs[c : 2 * c], refs[2 * c]
+    wo_own, wi_own, wd_own = refs[2 * c + 1 : 2 * c + 4]
+    refs = refs[2 * c + 4 :]
+    mine, theirs = refs[:n], refs[n : 2 * n]
+    refs = refs[2 * n :]
+    parts, (active, inner, low, z_own, s_own, wo_rows, wi, wd) = refs[:c], refs[c : c + 8]
+    wo, work, sem_o, sem_i, sem_d = refs[c + 8 :]
     p = sc[0]
-    rows = jnp.concatenate([x[...] for x in xs], axis=0).astype(F32)
-    total = rows + full[2:3, :]
-    for j in range(c):
-        q = jnp.bitwise_xor(p, j)
-        part = wo[pl.ds(pl.multiple_of(g.cols * q, 64), g.cols), :]
-        total = total + dot(seen(g, ctxs[j], j), part)
-        if j == 0:
-            wo_rows[...] = part
-    z, scale = norm_parts(total)
-    first = z * full[3:4, :] + full[4:5, :]
-    first_own[...] = first[: g.rows]
-    z_own[...] = z[: g.rows]
-    s_own[...] = jnp.broadcast_to(scale[: g.rows], (g.rows, 128))
-    low[...] = first.astype(BF)
-
-
-def up_kernel(g, sc, low, wi, full, inner):
-    inner[...] = dot(low[...], wi[...]) + full[pl.ds(8 + sc[0], 1), :]
-
-
-def down_kernel(g, inner, first_own, full, wd, *refs):
-    parts, active = refs[: g.chips], refs[g.chips]
-    u = inner[...]
-    active[...] = (u * (1.0 + lax.erf(u * (0.5**0.5))) * 0.5).astype(BF)
-    second = dot(active[...], wd[...])
-    parts[0][...] = second[: g.rows] + first_own[...] + full[5:6, :]
-    for j in range(1, g.chips):
-        parts[j][...] = second[g.rows * j : g.rows * (j + 1)].astype(BF)
+    at = pl.multiple_of(g.block * p, 16)
+    copies_o = gathers(g, sc, wo_own, 0, mine, theirs, g.half, g.half, wo, sem_o, p)
+    copies_i = gathers(g, sc, wi_own, 0, mine, theirs, 0, g.half, wi, sem_i)
+    copies_d = gathers(g, sc, wd_own, at, mine, theirs, 2 * g.half, g.bhalf, wd, sem_d)
+    start(copies_o)
+    rows = jnp.concatenate([seen(g, ctxs[j], j) for j in range(c)], axis=1)
+    finish(copies_o)
+    start(copies_i)
+    start(copies_d)
+    wo_rows[...] = wo[0 : g.cols]
+    halves = [slice(i, i + g.tokens // 2) for i in range(0, g.tokens, g.tokens // 2)]
+    bias = full[pl.ds(8 + p, 1), :]
+
+    def first_norm(half):
+        for i in range(half.start, half.stop, SLAB):
+            at = slice(i, i + SLAB)
+            x = xs[i // g.rows][i % g.rows : i % g.rows + SLAB].astype(F32)
+            z, scale = norm_parts(work[at] + x + full[2:3, :])
+            first = z * full[3:4, :] + full[4:5, :]
+            low[at] = first.astype(BF)
+            if i < g.rows:
+                z_own[at] = z
+                s_own[at] = jnp.broadcast_to(scale, (SLAB, 128))
+                parts[0][at] = first + full[5:6, :]
+
+    def activate(half):
+        for i in range(half.start, half.stop, SLAB):
+            at = slice(i, i + SLAB)
+            u = inner[at] + bias
+            inner[at] = u
+            active[at] = (u * (1.0 + lax.erf(u * (0.5**0.5))) * 0.5).astype(BF)
+
+    def descend(half):
+        second = dot(active[half], wd[...])
+        for i in range(half.start, half.stop, g.rows):
+            block = second[i - half.start : i - half.start + g.rows]
+            if i == 0:
+                parts[0][...] += block
+            else:
+                parts[i // g.rows][...] = block.astype(BF)
+
+    one, two = halves
+    work[one] = dot(rows[one], wo[...])
+    work[two] = dot(rows[two], wo[...])
+    first_norm(one)
+    finish(copies_i)
+    inner[one] = dot(low[one], wi[...])
+    first_norm(two)
+    inner[two] = dot(low[two], wi[...])
+    activate(one)
+    finish(copies_d)
+    descend(one)
+    activate(two)
+    descend(two)
 
 
 def turn_kernel(g, *refs):
@@ -729,7 +859,7 @@
 def split_rows(g, sc, total, size, own, other, at):
     k, f = sc[1], sc[2]
     for s in range(g.ring):
-        base = 2 * size * lax.rem(f + s, g.ring)
+        base = 2 * size * jnp.bitwise_xor(f, s)
         own[s, at : at + size] = total[pl.ds(pl.multiple_of(base + size * k, 8), size), :]
         other[s, at : at + size] = total[
             pl.ds(pl.multiple_of(base + size * (1 - k), 8), size), :
@@ -779,8 +909,7 @@
 def out_grads_kernel(g, sc, *refs):
     c = g.chips
     grads, ctxs, sums = refs[:c], refs[c : 2 * c], refs[2 * c]
-    own, total = refs[2 * c + 1], refs[-1]
-    away = refs[2 * c + 2 : -1]
+    own, away, total = refs[2 * c + 1 :]
     p, f = sc[0], sc[2]
     rows = jnp.concatenate([b[0 : g.rows] for b in grads], axis=0)
     for j in range(c):
@@ -794,14 +923,14 @@
     block = jnp.concatenate([sums[0:4], stats[0:2], out, rest], axis=0)
     size = g.shard // c
     for s in range(g.ring):
-        base = g.shard * lax.rem(f + s, g.ring) + size * p
+        base = g.shard * jnp.bitwise_xor(f, s) + size * p
         part = total[pl.ds(pl.multiple_of(base, 8), size), :]
-        if s == 0:
-            own[0:size] = part
-            own[size:] = block
+        if s % 2:
+            away[s // 2, 0:size] = part.astype(BF)
+            away[s // 2, size:] = block.astype(BF)
         else:
-            away[s - 1][0:size] = part.astype(BF)
-            away[s - 1][size:] = block.astype(BF)
+            own[s // 2, 0:size] = part
+            own[s // 2, size:] = block
 
 
 def summed(g, mine, theirs, at):
@@ -829,8 +958,7 @@
                 out[g.half * r : g.half * (r + 1), :] = jnp.transpose(rows[:, lane : lane + g.half])
 
 
-def qkv_grads_kernel(g, sc, mine, theirs, turned_x, own, *refs):
-    away, total = refs[:-1], refs[-1]
+def qkv_grads_kernel(g, sc, mine, theirs, turned_x, own, away, total):
     f = sc[2]
     rows = jnp.concatenate([summed(g, mine, theirs, 0), summed(g, mine, theirs, 1)], axis=0)
     total[...] = dot(turned_x[...], rows)
@@ -840,11 +968,14 @@
         [jnp.concatenate([sums, jnp.zeros((7, g.qkv), F32)], axis=0), gap], axis=1
     )
     for s in range(g.ring):
-        part = total[pl.ds(pl.multiple_of(g.half * lax.rem(f + s, g.ring), 8), g.half), :]
-        dst = own if s == 0 else away[s - 1]
+        part = total[pl.ds(pl.multiple_of(g.half * jnp.bitwise_xor(f, s), 8), g.half), :]
         packed = pack(g, part)
-        dst[0 : g.packed] = packed if s == 0 else packed.astype(BF)
-        dst[g.packed :] = block if s == 0 else block.astype(BF)
+        if s % 2:
+            away[s // 2, 0 : g.packed] = packed.astype(BF)
+            away[s // 2, g.packed :] = block.astype(BF)
+        else:
+            own[s // 2, 0 : g.packed] = packed
+            own[s // 2, g.packed :] = block
 
 
 def pack(g, part):
@@ -861,16 +992,20 @@
 def sources(g, sc, refs):
     p, k = sc[0], sc[1]
     out = []
-    for j in range(g.chips):
+    for j, (mine, theirs) in enumerate(zip(refs, others(g, refs))):
         q = jnp.bitwise_xor(p, j)
-        out.append((q, k, refs[j]))
-        out.append((q, 1 - k, refs[g.chips + j]))
+        out.append((q, k, mine))
+        out.append((q, 1 - k, theirs))
     return out
 
 
+def others(g, refs):
+    far = refs[g.chips :]
+    return far if len(far) > 1 else [far[0].at[j] for j in range(g.chips)]
+
+
 def mlp_final_kernel(g, sc, *refs):
-    found = refs[: 2 * g.chips]
-    g_in, g_down = refs[2 * g.chips :]
+    found, (g_in, g_down) = refs[:-2], refs[-2:]
     for q, core, ref in sources(g, sc, found):
         at = pl.multiple_of(g.block * q + g.bhalf * core, 8)
         g_down[pl.ds(at, g.bhalf), :] = ref[g.half :, :].astype(F32)
@@ -890,7 +1025,7 @@
     found = refs[: 2 * g.chips]
     gq, gk, gv, g_bq, g_bv, g_out, g_bin, *small = refs[2 * g.chips :]
     p, f = sc[0], sc[2]
-    size, side, step = g.shard // g.chips, g.width - g.qkv, g.half - g.packed
+    size, step = g.shard // g.chips, g.half - g.packed
     top = g.packed + 8
     for q, core, ref in sources(g, sc, found):
 
@@ -898,28 +1033,21 @@
         def _(ref=ref):
             row = ref[g.packed : top, :].astype(F32)[0:1]
             for dst, at in zip((g_bq, g_bv), (0, 2)):
-                dst[...] = jnp.concatenate(
-                    [
-                        row[:, 3 * DH * h + DH * at : 3 * DH * h + DH * (at + 1)]
-                        for h in range(g.heads)
-                    ],
-                    axis=1,
-                ).reshape(g.shard)
+                dst[...] = row[:, g.cols * at : g.cols * (at + 1)].reshape(g.shard)
 
         base = pl.multiple_of(g.half * core, 8)
         for chip in range(g.chips):
 
             @pl.when(q == chip)
             def _(chip=chip, ref=ref, base=base):
-                part = ref[0 : g.packed, :].astype(F32)
+                lane = g.cols * chip
                 for i, dst in enumerate((gq, gk, gv)):
-                    for h in range(g.heads):
-                        lane, src = g.cols * chip + DH * h, 3 * DH * h + DH * i
-                        dst[pl.ds(base, g.packed), lane : lane + DH] = part[:, src : src + DH]
-                        third, at = src // side, g.qkv + src % side
-                        dst[pl.ds(base + g.packed, step), lane : lane + DH] = part[
-                            step * third : step * (third + 1), at : at + DH
-                        ]
+                    dst[pl.ds(base, g.packed), lane : lane + g.cols] = ref[
+                        0 : g.packed, g.cols * i : g.cols * (i + 1)
+                    ].astype(F32)
+                    dst[pl.ds(base + g.packed, step), lane : lane + g.cols] = ref[
+                        step * i : step * (i + 1), g.qkv :
+                    ].astype(F32)
 
     for j in range(g.chips):
         q = jnp.bitwise_xor(p, j)
@@ -947,9 +1075,21 @@
     return lax.ppermute(x, "ctx", [(i, i ^ (2 * j)) for i in range(n)])
 
 
-def along(x, s):
+def along(x, mask):
     n = lax.axis_size("fsdp")
-    return lax.ppermute(x, "fsdp", [(i, (i + s) % n) for i in range(n)])
+    return lax.ppermute(x, "fsdp", [(i, i ^ mask) for i in range(n)])
+
+
+def gather_ring(x, pause=None):
+    n = lax.axis_size("fsdp")
+    found, mask, first = {0: x}, n // 2, ()
+    while mask:
+        for s in sorted(found):
+            first = [found[t] for t in sorted(found) if t]
+            part = found[s] if s == 0 or pause is None else after(found[s], pause, *first)
+            found[s | mask] = along(part, mask)
+        mask //= 2
+    return [found[s] for s in range(1, n)]
 
 
 def spread(x, chips):
@@ -957,16 +1097,71 @@
     return [x] + [far[j] for j in range(1, chips)]
 
 
+def pass_on(x, chips, pause):
+    found = {0: x}
+    mask = 1
+    while mask < chips:
+        for j in sorted(found):
+            found[j | mask] = to_chip(found[j] if j == 0 else after(found[j], pause), mask)
+        mask *= 2
+    return [found[j] for j in range(chips)]
+
+
 def swap(parts):
     far = {j: to_chip(parts[j], j) for j in sorted(range(1, len(parts)), key=lambda j: -bin(j).count("1"))}
     return [parts[0]] + [far[j] for j in range(1, len(parts))]
 
 
-def ring_sum(own, far):
-    total = own
-    for part in far:
-        total = total + part.astype(F32)
-    return total.astype(BF)
+def ring_step(kept, away, mask):
+    count, rows, width = kept.shape
+    half = count // 2
+
+    def step(mine, got):
+        total = mine + got.astype(F32)
+        if not half:
+            return (total.astype(BF),)
+        return total.reshape(half, 2, rows, width)[:, 0], total.reshape(
+            half, 2, rows, width
+        )[:, 1].astype(BF)
+
+    outs = [shaped((half, rows, width), F32), shaped((half, rows, width), BF)]
+    return mix(
+        step,
+        outs if half else [shaped((1, rows, width), BF)],
+        kept,
+        along(away, mask),
+        name="ring_step",
+    )
+
+
+def kept_far(x):
+    return pltpu.with_memory_space_constraint(x, pltpu.HBM)
+
+
+def after(x, *first):
+    return lax.optimization_barrier((x, *first))[0]
+
+
+def ring_step(kept, away, mask):
+    count, rows, width = kept.shape
+    half = count // 2
+
+    def step(mine, got):
+        total = mine + got.astype(F32)
+        if not half:
+            return (total.astype(BF),)
+        return total.reshape(half, 2, rows, width)[:, 0], total.reshape(
+            half, 2, rows, width
+        )[:, 1].astype(BF)
+
+    outs = [shaped((half, rows, width), F32), shaped((half, rows, width), BF)]
+    return mix(
+        step,
+        outs if half else [shaped((1, rows, width), BF)],
+        kept,
+        along(away, mask),
+        name="ring_step",
+    )
 
 
 def kept_far(x):
@@ -1050,7 +1245,7 @@
         + [pltpu.VMEM((g.hshard,), BF), pltpu.SemaphoreType.DMA((12,))],
         name="pick_weights",
     )
-    q_mine = [along(qsend, s) for s in range(1, ring)]
+    q_mine = gather_ring(qsend)
     x_own = after(hidden_in.reshape(rows, width), qsend)
     xs = spread(x_own, chips)
     iall, send = call(
@@ -1064,38 +1259,42 @@
         [pltpu.VMEM((g.shard, hidden), BF), pltpu.SemaphoreType.DMA((3,))],
         name="prepare_weights",
     )
-    w_mine = [along(send, s) for s in range(1, ring)]
-    q_theirs = [to_core(part) for part in q_mine]
-
-    order = lax.dynamic_slice(
-        clusters[0], (g.heads * p, g.entries * k), (g.heads, g.entries)
-    )
-    chip, core, within = order // (2 * rows), (order // rows) % 2, order % rows
-    pos = (core ^ k) * g.tokens + (chip ^ p) * rows + within
-    posr = jnp.pad(pos, ((0, 8 - g.heads), (0, 0)))
-    posc = posr.T
-    half_rows = rows // 2
-    devices = 2 * (p ^ jnp.arange(chips)[None, :]) + (k ^ jnp.arange(2)[:, None])
-    pieces = jnp.stack([devices, 2 * n - 1 - devices], axis=-1).reshape(-1)
-    hot = (pieces[:, None] == jnp.arange(2 * n)[None, :]).astype(BF)
-    blk = dot(hot, block_ids[0].reshape(2 * n, half_rows).astype(BF)).astype(BF)
-    blk = jnp.broadcast_to(blk.reshape(1, 2 * g.tokens), (8, 2 * g.tokens))
-
+
+    step = g.clusters * g.members
+    pick, place, blk = call(
+        bind(tables_kernel, g),
+        [
+            shaped((g.heads, 2 * chips * step, rows), BF),
+            shaped((g.heads, 2 * g.tokens, step), BF),
+            shaped((8, 2 * g.tokens), BF),
+        ],
+        [SMEM, HBM] + [VMEM] * 2,
+        [sc, q_mine[-1], clusters[0], block_ids],
+        name="cluster_tables",
+    )
+    (mask,) = call(
+        bind(mask_kernel, g),
+        [shaped((g.heads * g.clusters, CLUSTER, CLUSTER), F32)],
+        [VMEM] * 2,
+        [blk, place],
+        name="cluster_mask",
+    )
+    x_other = [to_core(after(xs[0], xs[1]))] + [to_core(x) for x in xs[1:]]
+    q_theirs = [to_core(after(part, *xs[1:])) for part in q_mine]
     qkv, w_qkv, full = call(
         bind(qkv_kernel, g),
         [
-            shaped((g.tokens, g.padded), BF),
+            shaped((2 * g.tokens, g.padded), BF),
             shaped((width, g.qkv), BF),
             shaped((VEC, width), F32),
         ],
-        [SMEM] + [VMEM] * (chips + 1) + [HBM] * (2 * ring - 1),
-        [sc, *xs, vec, qall, *q_mine, *q_theirs],
+        [SMEM] + [VMEM] * (2 * chips + 1) + [HBM] * (2 * ring - 1),
+        [sc, *xs, *x_other, after(vec, pick), qall, *q_mine, *q_theirs],
         [
             pltpu.VMEM((ring - 1, VEC, LANES), BF),
             gate,
             pltpu.SemaphoreType.DMA((ring - 1,)),
         ],
-        flops=2 * g.tokens * width * g.qkv,
         name="project",
     )
     ctx_own, ctx_other, kept, probs = call(
@@ -1106,65 +1305,55 @@
             shaped((g.heads, g.entries, LANES), BF),
             shaped((g.heads * g.clusters, CLUSTER, CLUSTER), F32),
         ],
-        [VMEM] * 5,
-        [qkv, to_core(qkv), posr, posc, blk],
-        flops=8 * g.entries * g.tokens * LANES * g.heads,
+        [VMEM] * 4,
+        [qkv, pick, place, mask],
+        [pltpu.VMEM((g.heads, g.entries, DH), BF)],
         name="attend",
     )
-    ctx = ctx_own + to_core(ctx_other)
+    (ctx,) = mix(
+        lambda a, b: (a + b,),
+        [shaped((g.tokens, g.cols), BF)],
+        ctx_own,
+        to_core(ctx_other),
+        name="join_context",
+    )
     ctxs = spread(ctx, chips)
+    w_mine = gather_ring(send, ctx)
 
     w_theirs = [to_core(after(part, *ctxs[1:])) for part in w_mine]
-    wo, wi, wd = call(
-        bind(lay_kernel, g),
-        [shaped((width, width), BF), shaped((width, g.share), BF), shaped((g.share, width), BF)],
-        [SMEM] + [FAR, HBM, FAR] + [HBM] * (2 * ring - 2),
-        [sc, kept_far(w_out), iall, kept_far(w_down), *w_mine, *w_theirs],
-        [gate, gate, gate],
-        name="lay_weights",
-    )
-    low, first_own, z_own, s_own, wo_rows = call(
-        bind(first_norm_kernel, g),
-        [
+    *second, active, inner, low, z_own, s_own, wo_rows, wi, wd = call(
+        bind(forward_kernel, g),
+        [shaped((rows, width), F32)]
+        + [shaped((rows, width), BF)] * (chips - 1)
+        + [
+            shaped((g.tokens, g.share), BF),
+            shaped((g.tokens, g.share), F32),
             shaped((g.tokens, width), BF),
-            shaped((rows, width), F32),
             shaped((rows, width), F32),
             shaped((rows, 128), F32),
             shaped((g.cols, width), BF),
+            shaped((width, g.share), BF),
+            shaped((g.share, width), BF),
         ],
-        [SMEM] + [VMEM] * (2 * chips + 2),
-        [sc, *ctxs, *xs, full, wo],
-        flops=2 * g.tokens * width * width,
-        name="out_project",
-    )
-    (inner,) = call(
-        bind(up_kernel, g),
+        [SMEM] + [VMEM] * (2 * chips + 1) + [FAR, HBM, FAR] + [HBM] * (2 * ring - 2),
+        [sc, *ctxs, *xs, full, kept_far(w_out), iall, kept_far(w_down), *w_mine, *w_theirs],
+        [pltpu.VMEM((width, width), BF), pltpu.VMEM((g.tokens, width), F32), gate, gate, gate],
+        name="mlp_forward",
+    )
+    (slope,) = mix(
+        lambda u: (
+            0.5 * (1.0 + lax.erf(u * (0.5**0.5)))
+            + u * jnp.exp(-0.5 * u * u) * (1.0 / (2.0 * math.pi) ** 0.5),
+        ),
         [shaped((g.tokens, g.share), F32)],
-        [SMEM] + [VMEM] * 3,
-        [sc, low, wi, full],
-        flops=2 * g.tokens * width * g.share,
-        name="mlp_up",
-    )
-    *second, active = call(
-        bind(down_kernel, g),
-        [shaped((rows, width), F32)]
-        + [shaped((rows, width), BF)] * (chips - 1)
-        + [shaped((g.tokens, g.share), BF)],
-        [VMEM] * 4,
-        [inner, first_own, full, wd],
-        flops=2 * g.tokens * width * g.share,
-        name="mlp_down",
-    )
-    inner = after(inner, active)
-    slope = 0.5 * (1.0 + lax.erf(inner * (0.5**0.5))) + inner * jnp.exp(
-        -0.5 * inner * inner
-    ) * (1.0 / (2.0 * jnp.pi) ** 0.5)
-    x_other = [to_core(after(x, inner)) for x in xs]
+        inner,
+        name="gelu_slope",
+    )
     (turned_x,) = call(
         bind(turn_rows_kernel, g),
         [shaped((ring * g.half, 2 * g.tokens), BF)],
         [SMEM] + [VMEM] * (2 * chips),
-        [sc, *xs, *x_other],
+        [sc, after(xs[0], inner), *xs[1:], *x_other],
         name="turn_rows",
     )
     second = swap(second)
@@ -1187,7 +1376,6 @@
         + [shaped((g.tokens, g.share), BF)],
         [VMEM] * (chips + 3),
         [*branches, slope, wd, wi],
-        flops=4 * g.tokens * width * g.share,
         name="mlp_back",
     )
     d_first = swap(d_first)
@@ -1201,14 +1389,29 @@
         [SMEM] + [VMEM] * (chips + 3),
         [sc, *branches, active, low, d_inner],
         [pltpu.VMEM((width, g.share), F32)],
-        flops=4 * g.tokens * width * g.share,
         name="mlp_grads",
     )
     m_got = to_core(m_other)
-    m_mine = [m_own[s] + m_got[s].astype(F32) for s in range(ring)]
-    m_away = [m_mine[s].astype(BF) for s in range(1, ring)]
-    m_far = [along(part, s) for s, part in enumerate(m_away, 1)]
-    m_piece = ring_sum(m_mine[0], m_far)
+    m_rows = g.half + g.bhalf
+
+    def joined(own, got):
+        total = own + got.astype(F32)
+        return (total[0], *(total[s].astype(BF) for s in range(1, ring)))
+
+    m_kept, *m_away = mix(
+        joined,
+        [shaped((m_rows, width), F32)] + [shaped((m_rows, width), BF)] * (ring - 1),
+        m_own,
+        m_got,
+        name="join_grads",
+    )
+    (m_piece,) = mix(
+        lambda kept, *parts: (sum((part.astype(F32) for part in parts), kept).astype(BF),),
+        [shaped((m_rows, width), BF)],
+        m_kept,
+        *(along(part, s) for s, part in enumerate(m_away, 1)),
+        name="mlp_sum",
+    )
     d_sum, attended = call(
         bind(first_kernel, g),
         [shaped((rows, width), F32), shaped((rows + VEC, width), BF)],
@@ -1222,64 +1425,85 @@
         [shaped((g.tokens, g.cols), BF)],
         [VMEM] * (chips + 1),
         [*grads, after(wo_rows, m_piece)],
-        flops=2 * g.tokens * width * g.cols,
         name="context_back",
     )
     d_ctx_other = to_core(d_ctx)
     o_rows = g.shard // chips + VEC
-    o_own, *o_away = call(
+    o_own, o_away = call(
         bind(out_grads_kernel, g),
-        [shaped((o_rows, width), F32)] + [shaped((o_rows, width), BF)] * (ring - 1),
+        [shaped((ring // 2, o_rows, width), F32), shaped((ring // 2, o_rows, width), BF)],
         [SMEM] + [VMEM] * (2 * chips + 1),
         [sc, *grads, *ctxs, sums],
         [pltpu.VMEM((width, width), F32)],
-        flops=2 * g.tokens * width * width,
         name="out_grads",
     )
     (dq_mine,) = call(
         bind(attend_back_kernel, g),
         [shaped((2 * g.tokens, g.wide), BF)],
         [VMEM] * 6,
-        [d_ctx, d_ctx_other, posr, posc, after(kept, o_own), probs],
-        flops=8 * g.entries * g.tokens * LANES * g.heads,
+        [d_ctx, d_ctx_other, pick, place, after(kept, o_own), probs],
+        [
+            pltpu.VMEM((g.heads, g.entries, DH), BF),
+            pltpu.VMEM((g.heads, g.entries, 3 * DH), BF),
+            pltpu.VMEM((g.heads * g.clusters, CLUSTER, CLUSTER), BF),
+        ],
         name="attend_back",
     )
-    o_far = [along(after(part, dq_mine), s) for s, part in enumerate(o_away, 1)]
     dq_theirs = to_core(dq_mine)
     q_rows = g.packed + 8
-    q_own, *q_away = call(
+    q_own, q_away = call(
         bind(qkv_grads_kernel, g),
-        [shaped((q_rows, width), F32)] + [shaped((q_rows, width), BF)] * (ring - 1),
+        [shaped((ring // 2, q_rows, width), F32), shaped((ring // 2, q_rows, width), BF)],
         [SMEM] + [VMEM] * 3,
         [sc, dq_mine, dq_theirs, turned_x],
         [pltpu.VMEM((ring * g.half, g.qkv), F32)],
-        flops=2 * g.tokens * width * g.qkv,
         name="project_grads",
     )
-    q_far = [along(part, s) for s, part in enumerate(q_away, 1)]
     d_in = call(
         bind(input_kernel, g),
         [shaped((rows, width), F32)] + [shaped((rows, width), BF)] * (chips - 1),
         [VMEM] * 3,
-        [after(dq_mine, *q_away), dq_theirs, w_qkv],
-        flops=2 * g.tokens * width * g.qkv,
+        [dq_mine, dq_theirs, w_qkv],
         name="project_back",
     )
     d_in = swap(d_in)
-    m_pieces = plane_pieces(m_piece, chips)
+    mask_at = 2
+    q_away0 = q_away
+    o_away = after(o_away, dq_mine)
+    while q_own.shape[0] > 1:
+        q_own, q_away = ring_step(q_own, q_away, mask_at // 2)
+        o_own, o_away = ring_step(o_own, o_away, mask_at // 2)
+        mask_at *= 2
+    near = spread(m_piece, chips)
+    m_pieces = near + [to_core(after(part, q_away)) for part in near]
+    (input_grad,) = mix(
+        lambda kept, *parts: (sum((part.astype(F32) for part in parts), kept).astype(BF),),
+        [shaped((rows, width), BF)],
+        d_sum,
+        *d_in,
+        name="input_sum",
+    )
     g_in, g_down = call(
         bind(mlp_final_kernel, g),
         [shaped((g.shard, hidden), F32), shaped((g.hshard, width), F32)],
-        [SMEM] + [VMEM] * (2 * chips),
+        [SMEM] + [VMEM] * len(m_pieces),
         [sc, *m_pieces],
         name="mlp_lay",
     )
-    total = d_sum
-    for part in d_in:
-        total = total + part.astype(F32)
-    input_grad = total.astype(BF)
     vector = shaped((g.shard,), F32)
-    piece = jnp.concatenate([ring_sum(q_own, q_far), ring_sum(o_own, o_far)], axis=0)
+    (piece,) = mix(
+        lambda a, b, c, d: (
+            jnp.concatenate([a[0] + b[0].astype(F32), c[0] + d[0].astype(F32)], axis=0).astype(BF),
+        ),
+        [shaped((q_rows + o_rows, width), BF)],
+        q_own,
+        along(q_away, mask_at // 2),
+        o_own,
+        along(o_away, mask_at // 2),
+        name="last_sum",
+    )
+    near = spread(piece, chips)
+    pieces = near + [to_core(after(part, input_grad, g_down)) for part in near]
     found = call(
         bind(last_kernel, g),
         [shaped((g.shard, width), F32)] * 3
@@ -1287,7 +1511,7 @@
         + [shaped((g.shard, width), F32), shaped((g.hshard,), F32)]
         + [vector] * 6,
         [SMEM] + [VMEM] * (2 * chips),
-        [after(sc, g_down), *plane_pieces(piece, chips)],
+        [sc, *pieces],
         name="last_lay",
     )
     gq, gk, gv, g_bq, g_bv, g_out, g_bin, g_gain2, g_bias2, g_bdown, g_gain1, g_bias1, g_bout = found
@@ -1315,7 +1539,7 @@
 def fits(mesh):
     n, ring = mesh.shape["ctx"], mesh.shape["fsdp"]
     chips = n // 2
-    return n % 2 == 0 and chips & (chips - 1) == 0 and H % chips == 0 and ring * chips <= 16
+    return n % 2 == 0 and chips & (chips - 1) == 0 and chips > 1 and ring == chips and H % chips == 0 and ring * chips <= 16
 
 
 def solution(mesh):

time: 199 us -> 189 us (0.950)
  local copies, waits for them, and re-layouts: 5.86 us -> 0.04 us
  Pallas kernels: 47.9 us -> 43.7 us
  other arithmetic: 3.43 us -> 0.08 us
  waiting for transfers between devices: 77.5 us -> 79.5 us
    ppermute x27, waiting for transfers between devices: 47.2 us -> 40.1 us  [to_chip(): return lax.ppermute(x, 'ctx', [(i, i ^ 2 * j) for i in range(n)])]
    ppermute x15 -> x13, waiting for transfers between devices: 24.3 us -> 31.2 us  [along(): return lax.ppermute(x, 'fsdp', [(i, i ^ mask) for i in range(n)])]
    unnamed x21 -> x9, local copies, waits for them, and re-layouts: 5.43 us -> 0.04 us
    pallas_call x20 -> x27, Pallas kernels: 47.9 us -> 43.7 us  [call(): pl.pallas_call(kernel, out_shape=outs, in_specs=ins, out_specs=[VMEM] * l...]
    ppermute x15 -> x13, starting transfers between devices: 24.7 us -> 27.1 us  [along(): return lax.ppermute(x, 'fsdp', [(i, i ^ mask) for i in range(n)])]
    ppermute x23 -> x22, waiting for transfers between devices: 5.99 us -> 8.26 us  [to_core(): return lax.ppermute(x, 'ctx', [(i, i ^ 1) for i in range(n)])]
    ppermute x23 -> x22, starting transfers between devices: 4.93 us -> 3.87 us  [to_core(): return lax.ppermute(x, 'ctx', [(i, i ^ 1) for i in range(n)])]
  transfers between devices with their start and end apart: 65 -> 62, of which waited for: 25 -> 29; matrix products, arithmetic and copies ran while one was open for 3% -> 0% of each run, Pallas kernels for 12% -> 13%
where the time goes in v3:
time: 189 us; the launch traced here: 188 us
  waiting for transfers between devices  79.5 us (42%)
  starting transfers between devices  63.9 us (34%)
  Pallas kernels  43.7 us (23%)
    pallas_call x27, Pallas kernels, call(): pl.pallas_call(kernel, out_shape=outs, in_specs=ins, out_specs=[VMEM] * l...  43.7 us
    ppermute x27, waiting for transfers between devices, to_chip(): return lax.ppermute(x, 'ctx', [(i, i ^ 2 * j) for i in range(n)])  40.1 us
    ppermute x27, starting transfers between devices, to_chip(): return lax.ppermute(x, 'ctx', [(i, i ^ 2 * j) for i in range(n)])  32.9 us
    ppermute x13, waiting for transfers between devices, along(): return lax.ppermute(x, 'fsdp', [(i, i ^ mask) for i in range(n)])  31.2 us
    ppermute x13, starting transfers between devices, along(): return lax.ppermute(x, 'fsdp', [(i, i ^ mask) for i in range(n)])  27.1 us
    ppermute x22, waiting for transfers between devices, to_core(): return lax.ppermute(x, 'ctx', [(i, i ^ 1) for i in range(n)])  8.26 us
    ppermute x22, starting transfers between devices, to_core(): return lax.ppermute(x, 'ctx', [(i, i ^ 1) for i in range(n)])  3.87 us
  transfers between devices with their start and end apart: 62, of which 29 were waited for; matrix products, arithmetic and copies ran while one was open for 0% of the time, Pallas kernels for 13%

profile of v3, /device:TPU:0, one launch (start us, length us, event | category | flops | bytes accessed | tf_op | source)
XLA Modules:
  0.0 188.4 jit_solution(11959313957583803725)
XLA Ops:
  0.7 2.0 %pick_weights.1 = (bf16[192,576]{1,0:T(8,128)(2,1)S(1)}, bf16[112,576]{1,0:T(8,128)(2,1)S(1)}, bf16[16,256]{1,0:T(8,128)(2,1)S(1)}) custom-call(s32[3]{0:T(128)S(1)} %pad_add_fusion.sc, bf16[192,768]{1,0:T(8,128)(2,1)} %refs_0_.1, bf16[192,768]{1,0:T(8,128)(2,1)} %refs_1_.1, bf16[192,768]{1,0:T(8,128)(2,1)} %refs_2_.1, bf16[192]{0:T(256)(128)(2,1)} %refs_3_.1, ...), custom_call_target="tpu_custom_call" | custom-call | flops 1 | bytes 1 | tf_op jit(solution)/shard_map/pick_weights/pallas_call | solution.py:381
  2.8 4.0 %collective-permute-start.2 = (bf16[128,768]{1,0:T(8,128)(2,1)}, bf16[128,768]{1,0:T(8,128)(2,1)S(1)}, u32[]{:S(2)}, u32[]{:S(2)}) collective-permute-start(bf16[128,768]{1,0:T(8,128)(2,1)} %bitcast.10), channel_id=1, source_target_pairs={{0,24},{4,28},{8,16},{12,20},{16,8},{20,12},{24,0},{28,4},{1,25},{... | collective-permute-start | bytes 589832 | tf_op jit(solution)/shard_map/ppermute | solution.py:1075
  6.8 2.6 %collective-permute-start.7 = (bf16[112,576]{1,0:T(8,128)(2,1)S(1)}, bf16[112,576]{1,0:T(8,128)(2,1)S(1)}, u32[]{:S(2)}, u32[]{:S(2)}) collective-permute-start(bf16[112,576]{1,0:T(8,128)(2,1)S(1)} %get-tuple-element.112._), channel_id=1, source_target_pairs={{0,2},{1,3},{2,0},{3,1},{4,6},{5,7},{6,4},{7,5},{8,10},{9,11},{10,... | collective-permute-start | bytes 387080 | tf_op jit(solution)/shard_map/ppermute | solution.py:1080
  10.4 1.6 collective-permute-start.9
  11.9 4.1 %collective-permute-done.7.refs_11_ = bf16[112,576]{1,0:T(8,128)(2,1)S(1)} collective-permute-done((bf16[112,576]{1,0:T(8,128)(2,1)S(1)}, bf16[112,576]{1,0:T(8,128)(2,1)S(1)}, u32[]{:S(2)}, u32[]{:S(2)}) %collective-permute-start.7) | collective-permute-done | bytes 129056 | tf_op jit(solution)/shard_map/ppermute | solution.py:1080
  17.3 3.8 %collective-permute-done.8._.refs_12_ = bf16[112,576]{1,0:T(8,128)(2,1)S(1)} collective-permute-done((bf16[112,576]{1,0:T(8,128)(2,1)S(1)}, bf16[112,576]{1,0:T(8,128)(2,1)S(1)}, u32[]{:S(2)}, u32[]{:S(2)}) %collective-permute-start.8) | collective-permute-done | bytes 129056 | tf_op jit(solution)/shard_map/ppermute | solution.py:1080
  21.2 2.0 %prepare_weights.1 = (bf16[192,768]{1,0:T(8,128)(2,1)S(1)}, bf16[288,768]{1,0:T(8,128)(2,1)S(1)}) custom-call(s32[3]{0:T(128)S(1)} %pad_add_fusion.sc, bf16[112,576]{1,0:T(8,128)(2,1)S(1)} %get-tuple-element.112._, bf16[192,3072]{1,0:T(8,128)(2,1)} %wi.1, bf16[768,768]{1,0:T(8,128)(2,1)} %refs_11_.3, bf16[192,768]{1,0:T(8,128)(2,1)} %refs_9_.3), custom_call_target="tpu_custom_call" | custom-call | flops 1 | bytes 1 | tf_op jit(solution)/shard_map/prepare_weights/pallas_call | solution.py:381
  23.2 2.9 %collective-permute-start.18 = (bf16[288,768]{1,0:T(8,128)(2,1)S(1)}, bf16[288,768]{1,0:T(8,128)(2,1)S(1)}, u32[]{:S(2)}, u32[]{:S(2)}) collective-permute-start(bf16[288,768]{1,0:T(8,128)(2,1)S(1)} %get-tuple-element.129), channel_id=1, source_target_pairs={{0,2},{1,3},{2,0},{3,1},{4,6},{5,7},{6,4},{7,5},{8,10},{9,11},{10,... | collective-permute-start | bytes 1327112 | tf_op jit(solution)/shard_map/ppermute | solution.py:1080
  26.1 1.7 collective-permute-start.17
  28.4 4.9 %cluster_tables.1 = (bf16[3,512,128]{2,1,0:T(8,128)(2,1)S(1)}, bf16[3,1024,64]{2,1,0:T(8,128)(2,1)S(1)}, bf16[8,1024]{1,0:T(8,128)(2,1)S(1)}) custom-call(s32[3]{0:T(128)S(1)} %pad_add_fusion.sc, bf16[112,576]{1,0:T(8,128)(2,1)S(1)} %collective-permute-done.8._.refs_12_, s32[12,1024]{1,0:T(8,128)S(1)} %bitcast.17, s32[1,1024]{1,0:T(1,128)S(1)} %copy-done.2), custom_call_target="tpu_custom_call" | custom-call | flops 1 | bytes 1 | tf_op jit(solution)/shard_map/cluster_tables/pallas_call | solution.py:381
  34.3 3.6 %project.1 = (bf16[1024,768]{1,0:T(8,128)(2,1)S(1)}, bf16[768,576]{1,0:T(8,128)(2,1)S(1)}, f32[16,768]{1,0:T(8,128)S(1)}) custom-call(s32[3]{0:T(128)S(1)} %pad_add_fusion.sc, bf16[128,768]{1,0:T(8,128)(2,1)S(1)} %bitcast.14, bf16[128,768]{1,0:T(8,128)(2,1)S(1)} %collective-permute-done.refs_1_.refs_5_, ...), custom_call_target="tpu_custom_call" | custom-call | flops 1 | bytes 1 | tf_op jit(solution)/shard_map/project/pallas_call | solution.py:381
  41.0 5.5 %collective-permute-done.18.refs_13_ = bf16[288,768]{1,0:T(8,128)(2,1)S(1)} collective-permute-done((bf16[288,768]{1,0:T(8,128)(2,1)S(1)}, bf16[288,768]{1,0:T(8,128)(2,1)S(1)}, u32[]{:S(2)}, u32[]{:S(2)}) %collective-permute-start.18) | collective-permute-done | bytes 442400 | tf_op jit(solution)/shard_map/ppermute | solution.py:1080
  46.6 1.6 collective-permute-start.19
  48.6 1.5 collective-permute-start.15
  50.1 1.5 collective-permute-start.14
  51.6 6.7 %collective-permute-done.16.refs_3_.refs_7_ = bf16[512,192]{1,0:T(8,128)(2,1)S(1)} collective-permute-done((bf16[512,192]{1,0:T(8,128)(2,1)S(1)}, bf16[512,192]{1,0:T(8,128)(2,1)S(1)}, u32[]{:S(2)}, u32[]{:S(2)}) %collective-permute-start.16) | collective-permute-done | bytes 196640 | tf_op jit(solution)/shard_map/ppermute | solution.py:1075
  58.3 3.3 %collective-permute-done.15.refs_2_.refs_6_ = bf16[512,192]{1,0:T(8,128)(2,1)S(1)} collective-permute-done((bf16[512,192]{1,0:T(8,128)(2,1)S(1)}, bf16[512,192]{1,0:T(8,128)(2,1)S(1)}, u32[]{:S(2)}, u32[]{:S(2)}) %collective-permute-start.15) | collective-permute-done | bytes 196640 | tf_op jit(solution)/shard_map/ppermute | solution.py:1075
  64.7 7.2 %mlp_forward.1 = (f32[128,768]{1,0:T(8,128)S(1)}, bf16[128,768]{1,0:T(8,128)(2,1)S(1)}, bf16[128,768]{1,0:T(8,128)(2,1)S(1)}, bf16[128,768]{1,0:T(8,128)(2,1)S(1...) custom-call(s32[3]{0:T(128)S(1)} %pad_add_fusion.sc, ...), custom_call_target="tpu_custom_call" | custom-call | flops 1 | bytes 1 | tf_op jit(solution)/shard_map/mlp_forward/pallas_call | solution.py:381
  73.8 1.6 collective-permute-start.25
  75.5 1.4 turn_rows.1.turned_x
  76.9 2.8 %collective-permute-done.23.refs_1_ = bf16[128,768]{1,0:T(8,128)(2,1)S(1)} collective-permute-done((bf16[128,768]{1,0:T(8,128)(2,1)S(1)}, bf16[128,768]{1,0:T(8,128)(2,1)S(1)}, u32[]{:S(2)}, u32[]{:S(2)}) %collective-permute-start.23) | collective-permute-done | bytes 196640 | tf_op jit(solution)/shard_map/ppermute | solution.py:1075
  79.7 4.4 %collective-permute-done.24.refs_2_ = bf16[128,768]{1,0:T(8,128)(2,1)S(1)} collective-permute-done((bf16[128,768]{1,0:T(8,128)(2,1)S(1)}, bf16[128,768]{1,0:T(8,128)(2,1)S(1)}, u32[]{:S(2)}, u32[]{:S(2)}) %collective-permute-start.24) | collective-permute-done | bytes 196640 | tf_op jit(solution)/shard_map/ppermute | solution.py:1075
  85.1 1.6 collective-permute-start.28
  89.1 5.2 %collective-permute-done.28.refs_3_ = bf16[144,768]{1,0:T(8,128)(2,1)S(1)} collective-permute-done((bf16[144,768]{1,0:T(8,128)(2,1)S(1)}, bf16[144,768]{1,0:T(8,128)(2,1)S(1)}, u32[]{:S(2)}, u32[]{:S(2)}) %collective-permute-start.28) | collective-permute-done | bytes 221216 | tf_op jit(solution)/shard_map/ppermute | solution.py:1075
  94.4 2.9 %collective-permute-done.27.refs_2_ = bf16[144,768]{1,0:T(8,128)(2,1)S(1)} collective-permute-done((bf16[144,768]{1,0:T(8,128)(2,1)S(1)}, bf16[144,768]{1,0:T(8,128)(2,1)S(1)}, u32[]{:S(2)}, u32[]{:S(2)}) %collective-permute-start.27) | collective-permute-done | bytes 221216 | tf_op jit(solution)/shard_map/ppermute | solution.py:1075
  97.2 1.5 mlp_back.1
  98.8 2.2 %mlp_grads.1 = (f32[4,192,768]{2,1,0:T(8,128)S(1)}, bf16[4,192,768]{2,1,0:T(8,128)(2,1)S(1)}, f32[8,768]{1,0:T(8,128)S(1)}) custom-call(s32[3]{0:T(128)S(1)} %pad_add_fusion.sc, bf16[144,768]{1,0:T(8,128)(2,1)S(1)} %get-tuple-element.142.refs_0_, bf16[144,768]{1,0:T(8,128)(2,1)S(1)} %collective-permute-done.26.refs_1_, ...), custom_call_target="tpu_custom_call" | custom-call | flops 1 | bytes 1 | tf_op jit(solution)/shard_map/mlp_grads/pallas_call | solution.py:381
  101.1 2.8 %collective-permute-done.32.refs_1_ = bf16[4,192,768]{2,1,0:T(8,128)(2,1)S(1)} collective-permute-done((bf16[4,192,768]{2,1,0:T(8,128)(2,1)S(1)}, bf16[4,192,768]{2,1,0:T(8,128)(2,1)S(1)}, u32[]{:S(2)}, u32[]{:S(2)}) %collective-permute-start.32) | collective-permute-done | bytes 1179680 | tf_op jit(solution)/shard_map/ppermute | solution.py:1070
  106.5 1.6 collective-permute-start.31
  108.1 2.5 %collective-permute-start.37 = (bf16[192,768]{1,0:T(8,128)(2,1)S(1)}, bf16[192,768]{1,0:T(8,128)(2,1)S(1)}, u32[]{:S(2)}, u32[]{:S(2)}) collective-permute-start(bf16[192,768]{1,0:T(8,128)(2,1)S(1)} %get-tuple-element.156), channel_id=1, source_target_pairs={{0,2},{1,3},{2,0},{3,1},{4,6},{5,7},{6,4},{7,5},{8,10},{9,11},{10,... | collective-permute-start | bytes 884744 | tf_op jit(solution)/shard_map/ppermute | solution.py:1080
  110.6 1.7 collective-permute-done.29.refs_1_
  112.4 3.7 %collective-permute-start.38 = (bf16[192,768]{1,0:T(8,128)(2,1)S(1)}, bf16[192,768]{1,0:T(8,128)(2,1)S(1)}, u32[]{:S(2)}, u32[]{:S(2)}) collective-permute-start(bf16[192,768]{1,0:T(8,128)(2,1)S(1)} %get-tuple-element.157), channel_id=1, source_target_pairs={{0,3},{1,2},{2,1},{3,0},{4,7},{5,6},{6,5},{7,4},{8,11},{9,10},{10,... | collective-permute-start | bytes 884744 | tf_op jit(solution)/shard_map/ppermute | solution.py:1080
  116.5 1.5 collective-permute-start.35
  120.0 11.5 %collective-permute-done.37.refs_2_ = bf16[192,768]{1,0:T(8,128)(2,1)S(1)} collective-permute-done((bf16[192,768]{1,0:T(8,128)(2,1)S(1)}, bf16[192,768]{1,0:T(8,128)(2,1)S(1)}, u32[]{:S(2)}, u32[]{:S(2)}) %collective-permute-start.37) | collective-permute-done | bytes 294944 | tf_op jit(solution)/shard_map/ppermute | solution.py:1080
  132.2 1.4 out_grads.1
  133.7 1.9 attend_back.1.mine
  136.1 5.2 %collective-permute-start.46 = (bf16[2,64,768]{2,1,0:T(8,128)(2,1)S(1)}, bf16[2,64,768]{2,1,0:T(8,128)(2,1)S(1)}, u32[]{:S(2)}, u32[]{:S(2)}) collective-permute-start(bf16[2,64,768]{2,1,0:T(8,128)(2,1)S(1)} %get-tuple-element.181), channel_id=1, source_target_pairs={{0,1},{1,0},{2,3},{3,2},{4,5},{5,4},{6,7},{7,6},{8,9},{9,8},{10,11... | collective-permute-start | bytes 589832 | tf_op jit(solution)/shard_map/ppermute | solution.py:1080
  141.8 1.6 collective-permute-start.53
  144.8 1.6 project_grads.1
  147.9 5.4 %collective-permute-done.44.refs_1_ = bf16[2,80,768]{2,1,0:T(8,128)(2,1)S(1)} collective-permute-done((bf16[2,80,768]{2,1,0:T(8,128)(2,1)S(1)}, bf16[2,80,768]{2,1,0:T(8,128)(2,1)S(1)}, u32[]{:S(2)}, u32[]{:S(2)}) %collective-permute-start.44) | collective-permute-done | bytes 245792 | tf_op jit(solution)/shard_map/ppermute | solution.py:1080
  153.3 2.5 %collective-permute-start.47 = (bf16[1,64,768]{2,1,0:T(8,128)(2,1)S(1)}, bf16[1,64,768]{2,1,0:T(8,128)(2,1)S(1)}, u32[]{:S(2)}, u32[]{:S(2)}) collective-permute-start(bf16[1,64,768]{2,1,0:T(8,128)(2,1)S(1)} %get-tuple-element.183), channel_id=1, source_target_pairs={{0,2},{1,3},{2,0},{3,1},{4,6},{5,7},{6,4},{7,5},{8,10},{9,11},{10,... | collective-permute-start | bytes 294920 | tf_op jit(solution)/shard_map/ppermute | solution.py:1080
  155.9 1.8 collective-permute-done.53.refs_3_
  159.9 1.6 collective-permute-start.45
  162.9 6.3 %collective-permute-done.42.refs_3_ = bf16[128,768]{1,0:T(8,128)(2,1)S(1)} collective-permute-done((bf16[128,768]{1,0:T(8,128)(2,1)S(1)}, bf16[128,768]{1,0:T(8,128)(2,1)S(1)}, u32[]{:S(2)}, u32[]{:S(2)}) %collective-permute-start.42) | collective-permute-done | bytes 196640 | tf_op jit(solution)/shard_map/ppermute | solution.py:1075
  171.1 1.4 collective-permute-start.49
  174.1 3.9 %mlp_lay.1 = (f32[192,3072]{1,0:T(8,128)}, f32[768,768]{1,0:T(8,128)}) custom-call(s32[3]{0:T(128)S(1)} %pad_add_fusion.sc, bf16[192,768]{1,0:T(8,128)(2,1)S(1)} %mlp_sum.1.refs_0_, bf16[192,768]{1,0:T(8,128)(2,1)S(1)} %collective-permute-done.51.refs_1_, bf16[192,768]{1,0:T(8,128)(2,1)S(1)} %collective-permute-done.52.refs_2_, ...), custom_call_target="tpu_custom_call" | custom-call | flops 1 | bytes 1 | tf_op jit(solution)/shard_map/mlp_lay/pallas_call | solution.py:381
  179.1 3.7 %collective-permute-done.49.refs_2_ = bf16[144,768]{1,0:T(8,128)(2,1)S(1)} collective-permute-done((bf16[144,768]{1,0:T(8,128)(2,1)S(1)}, bf16[144,768]{1,0:T(8,128)(2,1)S(1)}, u32[]{:S(2)}, u32[]{:S(2)}) %collective-permute-start.49) | collective-permute-done | bytes 221216 | tf_op jit(solution)/shard_map/ppermute | solution.py:1075
  184.9 3.3 %last_lay.1 = (f32[192,768]{1,0:T(8,128)}, f32[192,768]{1,0:T(8,128)}, f32[192,768]{1,0:T(8,128)}, f32[192]{0:T(256)}, f32[192]{0:T(256)}, /*index=5*/f32[192,76...) custom-call(s32[3]{0:T(128)S(1)} %pad_add_fusion.sc, ...), custom_call_target="tpu_custom_call" | custom-call | flops 1 | bytes 1 | tf_op jit(solution)/shard_map/last_lay/pallas_call | solution.py:381
  (113 shorter events, 36.0 us)
Async XLA Ops:
  2.8 13.9 %collective-permute-start.2 = (bf16[128,768]{1,0:T(8,128)(2,1)}, bf16[128,768]{1,0:T(8,128)(2,1)S(1)}, u32[]{:S(2)}, u32[]{:S(2)}) collective-permute-start(bf16[128,768]{1,0:T(8,128)(2,1)} %bitcast.10), channel_id=1, source_target_pairs={{0,24},{4,28},{8,16},{12,20},{16,8},{20,12},{24,0},{28,4},{1,25},{... | collective-permute-start | bytes 589832 | tf_op jit(solution)/shard_map/ppermute | solution.py:1075
  6.8 9.3 %collective-permute-start.7 = (bf16[112,576]{1,0:T(8,128)(2,1)S(1)}, bf16[112,576]{1,0:T(8,128)(2,1)S(1)}, u32[]{:S(2)}, u32[]{:S(2)}) collective-permute-start(bf16[112,576]{1,0:T(8,128)(2,1)S(1)} %get-tuple-element.112._), channel_id=1, source_target_pairs={{0,2},{1,3},{2,0},{3,1},{4,6},{5,7},{6,4},{7,5},{8,10},{9,11},{10,... | collective-permute-start | bytes 387080 | tf_op jit(solution)/shard_map/ppermute | solution.py:1080
  9.4 7.4 %collective-permute-start.1 = (bf16[128,768]{1,0:T(8,128)(2,1)}, bf16[128,768]{1,0:T(8,128)(2,1)S(1)}, u32[]{:S(2)}, u32[]{:S(2)}) collective-permute-start(bf16[128,768]{1,0:T(8,128)(2,1)} %bitcast.11), channel_id=1, source_target_pairs={{0,16},{4,20},{8,24},{12,28},{16,0},{20,4},{24,8},{28,12},{1,17},{... | collective-permute-start | bytes 589832 | tf_op jit(solution)/shard_map/ppermute | solution.py:1075
  9.9 6.9 %collective-permute-start = (bf16[128,768]{1,0:T(8,128)(2,1)}, bf16[128,768]{1,0:T(8,128)(2,1)S(1)}, u32[]{:S(2)}, u32[]{:S(2)}) collective-permute-start(bf16[128,768]{1,0:T(8,128)(2,1)} %bitcast.12), channel_id=1, source_target_pairs={{0,8},{4,12},{8,0},{12,4},{16,24},{20,28},{24,16},{28,20},{1,9},{5... | collective-permute-start | bytes 589832 | tf_op jit(solution)/shard_map/ppermute | solution.py:1075
  10.4 6.4 %collective-permute-start.9 = (bf16[112,576]{1,0:T(8,128)(2,1)S(1)}, bf16[112,576]{1,0:T(8,128)(2,1)S(1)}, u32[]{:S(2)}, u32[]{:S(2)}) collective-permute-start(bf16[112,576]{1,0:T(8,128)(2,1)S(1)} %get-tuple-element.112._), channel_id=1, source_target_pairs={{0,1},{1,0},{2,3},{3,2},{4,5},{5,4},{6,7},{7,6},{8,9},{9,8},{10,11... | collective-permute-start | bytes 387080 | tf_op jit(solution)/shard_map/ppermute | solution.py:1080
  16.7 11.6 %collective-permute-start.6 = (bf16[128,768]{1,0:T(8,128)(2,1)S(1)}, bf16[128,768]{1,0:T(8,128)(2,1)S(1)}, u32[]{:S(2)}, u32[]{:S(2)}) collective-permute-start(bf16[128,768]{1,0:T(8,128)(2,1)S(1)} %collective-permute-done.2.refs_3_.refs_7_), channel_id=1, source_target_pairs={{0,4},{4,0},{8,12},{12,8},{16,20},{20,16},{24,28},{28,24},{1,5},{5... | collective-permute-start | bytes 589832 | tf_op jit(solution)/shard_map/ppermute | solution.py:1070
  16.8 9.3 %collective-permute-start.10 = (bf16[112,576]{1,0:T(8,128)(2,1)S(1)}, bf16[112,576]{1,0:T(8,128)(2,1)S(1)}, u32[]{:S(2)}, u32[]{:S(2)}) collective-permute-start(bf16[112,576]{1,0:T(8,128)(2,1)S(1)} %collective-permute-done.9.refs_10_), channel_id=1, source_target_pairs={{0,4},{4,0},{8,12},{12,8},{16,20},{20,16},{24,28},{28,24},{1,5},{5... | collective-permute-start | bytes 387080 | tf_op jit(solution)/shard_map/ppermute | solution.py:1070
  17.3 10.5 %collective-permute-start.11 = (bf16[112,576]{1,0:T(8,128)(2,1)S(1)}, bf16[112,576]{1,0:T(8,128)(2,1)S(1)}, u32[]{:S(2)}, u32[]{:S(2)}) collective-permute-start(bf16[112,576]{1,0:T(8,128)(2,1)S(1)} %collective-permute-done.7.refs_11_), channel_id=1, source_target_pairs={{0,4},{4,0},{8,12},{12,8},{16,20},{20,16},{24,28},{28,24},{1,5},{5... | collective-permute-start | bytes 387080 | tf_op jit(solution)/shard_map/ppermute | solution.py:1070
  21.2 6.6 %collective-permute-start.12 = (bf16[112,576]{1,0:T(8,128)(2,1)S(1)}, bf16[112,576]{1,0:T(8,128)(2,1)S(1)}, u32[]{:S(2)}, u32[]{:S(2)}) collective-permute-start(bf16[112,576]{1,0:T(8,128)(2,1)S(1)} %collective-permute-done.8._.refs_12_), channel_id=1, source_target_pairs={{0,4},{4,0},{8,12},{12,8},{16,20},{20,16},{24,28},{28,24},{1,5},{5... | collective-permute-start | bytes 387080 | tf_op jit(solution)/shard_map/ppermute | solution.py:1070
  23.2 23.3 %collective-permute-start.18 = (bf16[288,768]{1,0:T(8,128)(2,1)S(1)}, bf16[288,768]{1,0:T(8,128)(2,1)S(1)}, u32[]{:S(2)}, u32[]{:S(2)}) collective-permute-start(bf16[288,768]{1,0:T(8,128)(2,1)S(1)} %get-tuple-element.129), channel_id=1, source_target_pairs={{0,2},{1,3},{2,0},{3,1},{4,6},{5,7},{6,4},{7,5},{8,10},{9,11},{10,... | collective-permute-start | bytes 1327112 | tf_op jit(solution)/shard_map/ppermute | solution.py:1080
  26.1 20.5 %collective-permute-start.17 = (bf16[288,768]{1,0:T(8,128)(2,1)S(1)}, bf16[288,768]{1,0:T(8,128)(2,1)S(1)}, u32[]{:S(2)}, u32[]{:S(2)}) collective-permute-start(bf16[288,768]{1,0:T(8,128)(2,1)S(1)} %get-tuple-element.129), channel_id=1, source_target_pairs={{0,1},{1,0},{2,3},{3,2},{4,5},{5,4},{6,7},{7,6},{8,9},{9,8},{10,11... | collective-permute-start | bytes 1327112 | tf_op jit(solution)/shard_map/ppermute | solution.py:1080
  27.8 6.5 %collective-permute-start.3 = (bf16[128,768]{1,0:T(8,128)(2,1)S(1)}, bf16[128,768]{1,0:T(8,128)(2,1)S(1)}, u32[]{:S(2)}, u32[]{:S(2)}) collective-permute-start(bf16[128,768]{1,0:T(8,128)(2,1)S(1)} %bitcast.13), channel_id=1, source_target_pairs={{0,4},{4,0},{8,12},{12,8},{16,20},{20,16},{24,28},{28,24},{1,5},{5... | collective-permute-start | bytes 589832 | tf_op jit(solution)/shard_map/ppermute | solution.py:1070
  27.8 6.4 %collective-permute-start.5 = (bf16[128,768]{1,0:T(8,128)(2,1)S(1)}, bf16[128,768]{1,0:T(8,128)(2,1)S(1)}, u32[]{:S(2)}, u32[]{:S(2)}) collective-permute-start(bf16[128,768]{1,0:T(8,128)(2,1)S(1)} %collective-permute-done.1.refs_2_.refs_6_), channel_id=1, source_target_pairs={{0,4},{4,0},{8,12},{12,8},{16,20},{20,16},{24,28},{28,24},{1,5},{5... | collective-permute-start | bytes 589832 | tf_op jit(solution)/shard_map/ppermute | solution.py:1070
  46.6 15.6 %collective-permute-start.19 = (bf16[288,768]{1,0:T(8,128)(2,1)S(1)}, bf16[288,768]{1,0:T(8,128)(2,1)S(1)}, u32[]{:S(2)}, u32[]{:S(2)}) collective-permute-start(bf16[288,768]{1,0:T(8,128)(2,1)S(1)} %collective-permute-done.18.refs_13_), channel_id=1, source_target_pairs={{0,1},{1,0},{2,3},{3,2},{4,5},{5,4},{6,7},{7,6},{8,9},{9,8},{10,11... | collective-permute-start | bytes 1327112 | tf_op jit(solution)/shard_map/ppermute | solution.py:1080
  48.2 10.1 %collective-permute-start.16 = (bf16[512,192]{1,0:T(8,128)(2,1)S(1)}, bf16[512,192]{1,0:T(8,128)(2,1)S(1)}, u32[]{:S(2)}, u32[]{:S(2)}) collective-permute-start(bf16[512,192]{1,0:T(8,128)(2,1)S(1)} %join_context.1.refs_0_.refs_4_), channel_id=1, source_target_pairs={{0,24},{4,28},{8,16},{12,20},{16,8},{20,12},{24,0},{28,4},{1,25},{... | collective-permute-start | bytes 589832 | tf_op jit(solution)/shard_map/ppermute | solution.py:1075
  48.6 13.0 %collective-permute-start.15 = (bf16[512,192]{1,0:T(8,128)(2,1)S(1)}, bf16[512,192]{1,0:T(8,128)(2,1)S(1)}, u32[]{:S(2)}, u32[]{:S(2)}) collective-permute-start(bf16[512,192]{1,0:T(8,128)(2,1)S(1)} %join_context.1.refs_0_.refs_4_), channel_id=1, source_target_pairs={{0,16},{4,20},{8,24},{12,28},{16,0},{20,4},{24,8},{28,12},{1,17},{... | collective-permute-start | bytes 589832 | tf_op jit(solution)/shard_map/ppermute | solution.py:1075
  50.1 11.5 %collective-permute-start.14 = (bf16[512,192]{1,0:T(8,128)(2,1)S(1)}, bf16[512,192]{1,0:T(8,128)(2,1)S(1)}, u32[]{:S(2)}, u32[]{:S(2)}) collective-permute-start(bf16[512,192]{1,0:T(8,128)(2,1)S(1)} %join_context.1.refs_0_.refs_4_), channel_id=1, source_target_pairs={{0,8},{4,12},{8,0},{12,4},{16,24},{20,28},{24,16},{28,20},{1,9},{5... | collective-permute-start | bytes 589832 | tf_op jit(solution)/shard_map/ppermute | solution.py:1075
  71.9 7.8 %collective-permute-start.23 = (bf16[128,768]{1,0:T(8,128)(2,1)S(1)}, bf16[128,768]{1,0:T(8,128)(2,1)S(1)}, u32[]{:S(2)}, u32[]{:S(2)}) collective-permute-start(bf16[128,768]{1,0:T(8,128)(2,1)S(1)} %get-tuple-element.135), channel_id=1, source_target_pairs={{0,8},{4,12},{8,0},{12,4},{16,24},{20,28},{24,16},{28,20},{1,9},{5... | collective-permute-start | bytes 589832 | tf_op jit(solution)/shard_map/ppermute | solution.py:1075
  73.2 10.9 %collective-permute-start.24 = (bf16[128,768]{1,0:T(8,128)(2,1)S(1)}, bf16[128,768]{1,0:T(8,128)(2,1)S(1)}, u32[]{:S(2)}, u32[]{:S(2)}) collective-permute-start(bf16[128,768]{1,0:T(8,128)(2,1)S(1)} %get-tuple-element.136), channel_id=1, source_target_pairs={{0,16},{4,20},{8,24},{12,28},{16,0},{20,4},{24,8},{28,12},{1,17},{... | collective-permute-start | bytes 589832 | tf_op jit(solution)/shard_map/ppermute | solution.py:1075
  73.8 10.3 %collective-permute-start.25 = (bf16[128,768]{1,0:T(8,128)(2,1)S(1)}, bf16[128,768]{1,0:T(8,128)(2,1)S(1)}, u32[]{:S(2)}, u32[]{:S(2)}) collective-permute-start(bf16[128,768]{1,0:T(8,128)(2,1)S(1)} %get-tuple-element.137), channel_id=1, source_target_pairs={{0,24},{4,28},{8,16},{12,20},{16,8},{20,12},{24,0},{28,4},{1,25},{... | collective-permute-start | bytes 589832 | tf_op jit(solution)/shard_map/ppermute | solution.py:1075
  85.1 9.3 %collective-permute-start.28 = (bf16[144,768]{1,0:T(8,128)(2,1)S(1)}, bf16[144,768]{1,0:T(8,128)(2,1)S(1)}, u32[]{:S(2)}, u32[]{:S(2)}) collective-permute-start(bf16[144,768]{1,0:T(8,128)(2,1)S(1)} %get-tuple-element.142.refs_0_), channel_id=1, source_target_pairs={{0,24},{4,28},{8,16},{12,20},{16,8},{20,12},{24,0},{28,4},{1,25},{... | collective-permute-start | bytes 663560 | tf_op jit(solution)/shard_map/ppermute | solution.py:1075
  86.6 10.6 %collective-permute-start.27 = (bf16[144,768]{1,0:T(8,128)(2,1)S(1)}, bf16[144,768]{1,0:T(8,128)(2,1)S(1)}, u32[]{:S(2)}, u32[]{:S(2)}) collective-permute-start(bf16[144,768]{1,0:T(8,128)(2,1)S(1)} %get-tuple-element.142.refs_0_), channel_id=1, source_target_pairs={{0,16},{4,20},{8,24},{12,28},{16,0},{20,4},{24,8},{28,12},{1,17},{... | collective-permute-start | bytes 663560 | tf_op jit(solution)/shard_map/ppermute | solution.py:1075
  87.3 9.9 %collective-permute-start.26 = (bf16[144,768]{1,0:T(8,128)(2,1)S(1)}, bf16[144,768]{1,0:T(8,128)(2,1)S(1)}, u32[]{:S(2)}, u32[]{:S(2)}) collective-permute-start(bf16[144,768]{1,0:T(8,128)(2,1)S(1)} %get-tuple-element.142.refs_0_), channel_id=1, source_target_pairs={{0,8},{4,12},{8,0},{12,4},{16,24},{20,28},{24,16},{28,20},{1,9},{5... | collective-permute-start | bytes 663560 | tf_op jit(solution)/shard_map/ppermute | solution.py:1075
  104.1 15.0 %collective-permute-start.36 = (bf16[192,768]{1,0:T(8,128)(2,1)S(1)}, bf16[192,768]{1,0:T(8,128)(2,1)S(1)}, u32[]{:S(2)}, u32[]{:S(2)}) collective-permute-start(bf16[192,768]{1,0:T(8,128)(2,1)S(1)} %get-tuple-element.155), channel_id=1, source_target_pairs={{0,1},{1,0},{2,3},{3,2},{4,5},{5,4},{6,7},{7,6},{8,9},{9,8},{10,11... | collective-permute-start | bytes 884744 | tf_op jit(solution)/shard_map/ppermute | solution.py:1080
  104.6 7.8 %collective-permute-start.29 = (bf16[128,768]{1,0:T(8,128)(2,1)S(1)}, bf16[128,768]{1,0:T(8,128)(2,1)S(1)}, u32[]{:S(2)}, u32[]{:S(2)}) collective-permute-start(bf16[128,768]{1,0:T(8,128)(2,1)S(1)} %get-tuple-element.146), channel_id=1, source_target_pairs={{0,8},{4,12},{8,0},{12,4},{16,24},{20,28},{24,16},{28,20},{1,9},{5... | collective-permute-start | bytes 589832 | tf_op jit(solution)/shard_map/ppermute | solution.py:1075
  105.2 10.9 %collective-permute-start.30 = (bf16[128,768]{1,0:T(8,128)(2,1)S(1)}, bf16[128,768]{1,0:T(8,128)(2,1)S(1)}, u32[]{:S(2)}, u32[]{:S(2)}) collective-permute-start(bf16[128,768]{1,0:T(8,128)(2,1)S(1)} %get-tuple-element.147), channel_id=1, source_target_pairs={{0,16},{4,20},{8,24},{12,28},{16,0},{20,4},{24,8},{28,12},{1,17},{... | collective-permute-start | bytes 589832 | tf_op jit(solution)/shard_map/ppermute | solution.py:1075
  106.5 9.6 %collective-permute-start.31 = (bf16[128,768]{1,0:T(8,128)(2,1)S(1)}, bf16[128,768]{1,0:T(8,128)(2,1)S(1)}, u32[]{:S(2)}, u32[]{:S(2)}) collective-permute-start(bf16[128,768]{1,0:T(8,128)(2,1)S(1)} %get-tuple-element.148), channel_id=1, source_target_pairs={{0,24},{4,28},{8,16},{12,20},{16,8},{20,12},{24,0},{28,4},{1,25},{... | collective-permute-start | bytes 589832 | tf_op jit(solution)/shard_map/ppermute | solution.py:1075
  108.1 23.5 %collective-permute-start.37 = (bf16[192,768]{1,0:T(8,128)(2,1)S(1)}, bf16[192,768]{1,0:T(8,128)(2,1)S(1)}, u32[]{:S(2)}, u32[]{:S(2)}) collective-permute-start(bf16[192,768]{1,0:T(8,128)(2,1)S(1)} %get-tuple-element.156), channel_id=1, source_target_pairs={{0,2},{1,3},{2,0},{3,1},{4,6},{5,7},{6,4},{7,5},{8,10},{9,11},{10,... | collective-permute-start | bytes 884744 | tf_op jit(solution)/shard_map/ppermute | solution.py:1080
  112.4 19.2 %collective-permute-start.38 = (bf16[192,768]{1,0:T(8,128)(2,1)S(1)}, bf16[192,768]{1,0:T(8,128)(2,1)S(1)}, u32[]{:S(2)}, u32[]{:S(2)}) collective-permute-start(bf16[192,768]{1,0:T(8,128)(2,1)S(1)} %get-tuple-element.157), channel_id=1, source_target_pairs={{0,3},{1,2},{2,1},{3,0},{4,7},{5,6},{6,5},{7,4},{8,11},{9,10},{10,... | collective-permute-start | bytes 884744 | tf_op jit(solution)/shard_map/ppermute | solution.py:1080
  116.5 15.2 %collective-permute-start.35 = (bf16[144,768]{1,0:T(8,128)(2,1)S(1)}, bf16[144,768]{1,0:T(8,128)(2,1)S(1)}, u32[]{:S(2)}, u32[]{:S(2)}) collective-permute-start(bf16[144,768]{1,0:T(8,128)(2,1)S(1)} %get-tuple-element.162.refs_0_), channel_id=1, source_target_pairs={{0,24},{4,28},{8,16},{12,20},{16,8},{20,12},{24,0},{28,4},{1,25},{... | collective-permute-start | bytes 663560 | tf_op jit(solution)/shard_map/ppermute | solution.py:1075
  118.0 13.8 %collective-permute-start.34 = (bf16[144,768]{1,0:T(8,128)(2,1)S(1)}, bf16[144,768]{1,0:T(8,128)(2,1)S(1)}, u32[]{:S(2)}, u32[]{:S(2)}) collective-permute-start(bf16[144,768]{1,0:T(8,128)(2,1)S(1)} %get-tuple-element.162.refs_0_), channel_id=1, source_target_pairs={{0,16},{4,20},{8,24},{12,28},{16,0},{20,4},{24,8},{28,12},{1,17},{... | collective-permute-start | bytes 663560 | tf_op jit(solution)/shard_map/ppermute | solution.py:1075
  119.1 12.6 %collective-permute-start.33 = (bf16[144,768]{1,0:T(8,128)(2,1)S(1)}, bf16[144,768]{1,0:T(8,128)(2,1)S(1)}, u32[]{:S(2)}, u32[]{:S(2)}) collective-permute-start(bf16[144,768]{1,0:T(8,128)(2,1)S(1)} %get-tuple-element.162.refs_0_), channel_id=1, source_target_pairs={{0,8},{4,12},{8,0},{12,4},{16,24},{20,28},{24,16},{28,20},{1,9},{5... | collective-permute-start | bytes 663560 | tf_op jit(solution)/shard_map/ppermute | solution.py:1075
  135.6 9.2 %collective-permute-start.40 = (bf16[1024,640]{1,0:T(8,128)(2,1)S(1)}, bf16[1024,640]{1,0:T(8,128)(2,1)S(1)}, u32[]{:S(2)}, u32[]{:S(2)}) collective-permute-start(bf16[1024,640]{1,0:T(8,128)(2,1)S(1)} %attend_back.1.mine), channel_id=1, source_target_pairs={{0,4},{4,0},{8,12},{12,8},{16,20},{20,16},{24,28},{28,24},{1,5},{5... | collective-permute-start | bytes 3932168 | tf_op jit(solution)/shard_map/ppermute | solution.py:1070
  136.1 11.2 %collective-permute-start.46 = (bf16[2,64,768]{2,1,0:T(8,128)(2,1)S(1)}, bf16[2,64,768]{2,1,0:T(8,128)(2,1)S(1)}, u32[]{:S(2)}, u32[]{:S(2)}) collective-permute-start(bf16[2,64,768]{2,1,0:T(8,128)(2,1)S(1)} %get-tuple-element.181), channel_id=1, source_target_pairs={{0,1},{1,0},{2,3},{3,2},{4,5},{5,4},{6,7},{7,6},{8,9},{9,8},{10,11... | collective-permute-start | bytes 589832 | tf_op jit(solution)/shard_map/ppermute | solution.py:1080
  141.3 14.5 %collective-permute-start.51 = (bf16[192,768]{1,0:T(8,128)(2,1)S(1)}, bf16[192,768]{1,0:T(8,128)(2,1)S(1)}, u32[]{:S(2)}, u32[]{:S(2)}) collective-permute-start(bf16[192,768]{1,0:T(8,128)(2,1)S(1)} %mlp_sum.1.refs_0_), channel_id=1, source_target_pairs={{0,8},{4,12},{8,0},{12,4},{16,24},{20,28},{24,16},{28,20},{1,9},{5... | collective-permute-start | bytes 884744 | tf_op jit(solution)/shard_map/ppermute | solution.py:1075
  141.8 15.9 %collective-permute-start.53 = (bf16[192,768]{1,0:T(8,128)(2,1)S(1)}, bf16[192,768]{1,0:T(8,128)(2,1)S(1)}, u32[]{:S(2)}, u32[]{:S(2)}) collective-permute-start(bf16[192,768]{1,0:T(8,128)(2,1)S(1)} %mlp_sum.1.refs_0_), channel_id=1, source_target_pairs={{0,24},{4,28},{8,16},{12,20},{16,8},{20,12},{24,0},{28,4},{1,25},{... | collective-permute-start | bytes 884744 | tf_op jit(solution)/shard_map/ppermute | solution.py:1075
  143.4 14.5 %collective-permute-start.52 = (bf16[192,768]{1,0:T(8,128)(2,1)S(1)}, bf16[192,768]{1,0:T(8,128)(2,1)S(1)}, u32[]{:S(2)}, u32[]{:S(2)}) collective-permute-start(bf16[192,768]{1,0:T(8,128)(2,1)S(1)} %mlp_sum.1.refs_0_), channel_id=1, source_target_pairs={{0,16},{4,20},{8,24},{12,28},{16,0},{20,4},{24,8},{28,12},{1,17},{... | collective-permute-start | bytes 884744 | tf_op jit(solution)/shard_map/ppermute | solution.py:1075
  146.4 6.9 %collective-permute-start.44 = (bf16[2,80,768]{2,1,0:T(8,128)(2,1)S(1)}, bf16[2,80,768]{2,1,0:T(8,128)(2,1)S(1)}, u32[]{:S(2)}, u32[]{:S(2)}) collective-permute-start(bf16[2,80,768]{2,1,0:T(8,128)(2,1)S(1)} %get-tuple-element.177), channel_id=1, source_target_pairs={{0,1},{1,0},{2,3},{3,2},{4,5},{5,4},{6,7},{7,6},{8,9},{9,8},{10,11... | collective-permute-start | bytes 737288 | tf_op jit(solution)/shard_map/ppermute | solution.py:1080
  147.3 14.2 %collective-permute-start.41 = (bf16[128,768]{1,0:T(8,128)(2,1)S(1)}, bf16[128,768]{1,0:T(8,128)(2,1)S(1)}, u32[]{:S(2)}, u32[]{:S(2)}) collective-permute-start(bf16[128,768]{1,0:T(8,128)(2,1)S(1)} %get-tuple-element.173), channel_id=1, source_target_pairs={{0,8},{4,12},{8,0},{12,4},{16,24},{20,28},{24,16},{28,20},{1,9},{5... | collective-permute-start | bytes 589832 | tf_op jit(solution)/shard_map/ppermute | solution.py:1075
  153.3 6.6 %collective-permute-start.47 = (bf16[1,64,768]{2,1,0:T(8,128)(2,1)S(1)}, bf16[1,64,768]{2,1,0:T(8,128)(2,1)S(1)}, u32[]{:S(2)}, u32[]{:S(2)}) collective-permute-start(bf16[1,64,768]{2,1,0:T(8,128)(2,1)S(1)} %get-tuple-element.183), channel_id=1, source_target_pairs={{0,2},{1,3},{2,0},{3,1},{4,6},{5,7},{6,4},{7,5},{8,10},{9,11},{10,... | collective-permute-start | bytes 294920 | tf_op jit(solution)/shard_map/ppermute | solution.py:1080
  155.8 15.3 %collective-permute-start.54 = (bf16[192,768]{1,0:T(8,128)(2,1)S(1)}, bf16[192,768]{1,0:T(8,128)(2,1)S(1)}, u32[]{:S(2)}, u32[]{:S(2)}) collective-permute-start(bf16[192,768]{1,0:T(8,128)(2,1)S(1)} %mlp_sum.1.refs_0_), channel_id=1, source_target_pairs={{0,4},{4,0},{8,12},{12,8},{16,20},{20,16},{24,28},{28,24},{1,5},{5... | collective-permute-start | bytes 884744 | tf_op jit(solution)/shard_map/ppermute | solution.py:1070
  157.7 14.9 %collective-permute-start.55 = (bf16[192,768]{1,0:T(8,128)(2,1)S(1)}, bf16[192,768]{1,0:T(8,128)(2,1)S(1)}, u32[]{:S(2)}, u32[]{:S(2)}) collective-permute-start(bf16[192,768]{1,0:T(8,128)(2,1)S(1)} %collective-permute-done.51.refs_1_), channel_id=1, source_target_pairs={{0,4},{4,0},{8,12},{12,8},{16,20},{20,16},{24,28},{28,24},{1,5},{5... | collective-permute-start | bytes 884744 | tf_op jit(solution)/shard_map/ppermute | solution.py:1070
  157.9 11.2 %collective-permute-start.42 = (bf16[128,768]{1,0:T(8,128)(2,1)S(1)}, bf16[128,768]{1,0:T(8,128)(2,1)S(1)}, u32[]{:S(2)}, u32[]{:S(2)}) collective-permute-start(bf16[128,768]{1,0:T(8,128)(2,1)S(1)} %get-tuple-element.174), channel_id=1, source_target_pairs={{0,16},{4,20},{8,24},{12,28},{16,0},{20,4},{24,8},{28,12},{1,17},{... | collective-permute-start | bytes 589832 | tf_op jit(solution)/shard_map/ppermute | solution.py:1075
  159.9 9.3 %collective-permute-start.45 = (bf16[1,80,768]{2,1,0:T(8,128)(2,1)S(1)}, bf16[1,80,768]{2,1,0:T(8,128)(2,1)S(1)}, u32[]{:S(2)}, u32[]{:S(2)}) collective-permute-start(bf16[1,80,768]{2,1,0:T(8,128)(2,1)S(1)} %get-tuple-element.179), channel_id=1, source_target_pairs={{0,2},{1,3},{2,0},{3,1},{4,6},{5,7},{6,4},{7,5},{8,10},{9,11},{10,... | collective-permute-start | bytes 368648 | tf_op jit(solution)/shard_map/ppermute | solution.py:1080
  161.5 8.2 %collective-permute-start.43 = (bf16[128,768]{1,0:T(8,128)(2,1)S(1)}, bf16[128,768]{1,0:T(8,128)(2,1)S(1)}, u32[]{:S(2)}, u32[]{:S(2)}) collective-permute-start(bf16[128,768]{1,0:T(8,128)(2,1)S(1)} %get-tuple-element.175), channel_id=1, source_target_pairs={{0,24},{4,28},{8,16},{12,20},{16,8},{20,12},{24,0},{28,4},{1,25},{... | collective-permute-start | bytes 589832 | tf_op jit(solution)/shard_map/ppermute | solution.py:1075
  169.8 9.3 %collective-permute-start.50 = (bf16[144,768]{1,0:T(8,128)(2,1)S(1)}, bf16[144,768]{1,0:T(8,128)(2,1)S(1)}, u32[]{:S(2)}, u32[]{:S(2)}) collective-permute-start(bf16[144,768]{1,0:T(8,128)(2,1)S(1)} %last_sum.1.refs_0_), channel_id=1, source_target_pairs={{0,24},{4,28},{8,16},{12,20},{16,8},{20,12},{24,0},{28,4},{1,25},{... | collective-permute-start | bytes 663560 | tf_op jit(solution)/shard_map/ppermute | solution.py:1075
  171.1 11.7 %collective-permute-start.49 = (bf16[144,768]{1,0:T(8,128)(2,1)S(1)}, bf16[144,768]{1,0:T(8,128)(2,1)S(1)}, u32[]{:S(2)}, u32[]{:S(2)}) collective-permute-start(bf16[144,768]{1,0:T(8,128)(2,1)S(1)} %last_sum.1.refs_0_), channel_id=1, source_target_pairs={{0,16},{4,20},{8,24},{12,28},{16,0},{20,4},{24,8},{28,12},{1,17},{... | collective-permute-start | bytes 663560 | tf_op jit(solution)/shard_map/ppermute | solution.py:1075
  172.6 10.3 %collective-permute-start.48 = (bf16[144,768]{1,0:T(8,128)(2,1)S(1)}, bf16[144,768]{1,0:T(8,128)(2,1)S(1)}, u32[]{:S(2)}, u32[]{:S(2)}) collective-permute-start(bf16[144,768]{1,0:T(8,128)(2,1)S(1)} %last_sum.1.refs_0_), channel_id=1, source_target_pairs={{0,8},{4,12},{8,0},{12,4},{16,24},{20,28},{24,16},{28,20},{1,9},{5... | collective-permute-start | bytes 663560 | tf_op jit(solution)/shard_map/ppermute | solution.py:1075
  (18 other events, 132.6 us)

commit v4 on v3

--- a/solution.py
+++ b/solution.py
@@ -468,16 +468,13 @@
     qsend[g.half : g.half + VEC, LANES:] = jnp.zeros((VEC, g.qkv - LANES), BF)
 
 
-def prep_kernel(g, sc, _, wi, wd, wo, iall, send, here, sem):
+def prep_kernel(g, sc, _, wi, wd, wo, iall, oall, dall, send, here, sem):
     p, k = sc[0], sc[1]
-    at = pl.multiple_of(g.block * p + g.bhalf * k, 16)
-    mine = pl.ds(pl.multiple_of(g.half * k, 16), g.half)
+    at = pl.multiple_of(g.block * p, 16)
     copies = [
         pltpu.make_async_copy(wi, here, sem.at[0]),
-        pltpu.make_async_copy(wo.at[mine], send.at[pl.ds(g.half, g.half)], sem.at[1]),
-        pltpu.make_async_copy(
-            wd.at[pl.ds(at, g.bhalf)], send.at[pl.ds(2 * g.half, g.bhalf)], sem.at[2]
-        ),
+        pltpu.make_async_copy(wo, oall, sem.at[1]),
+        pltpu.make_async_copy(wd.at[pl.ds(at, g.block)], dall, sem.at[2]),
     ]
     start(copies)
     finish(copies[:1])
@@ -489,31 +486,20 @@
                 src = g.hshard * r + g.block * q
                 iall[:, g.block * r : g.block * (r + 1)] = here[:, src : src + g.block]
 
+    mine = pl.ds(pl.multiple_of(g.half * k, 16), g.half)
     send[0 : g.half] = iall[mine]
     finish(copies[1:])
-
-
-def gathers(g, sc, own, own_at, mine, theirs, at, piece, dst, sem, turn=0):
+    send[g.half : 2 * g.half] = oall[mine]
+    send[2 * g.half :] = dall[pl.ds(pl.multiple_of(g.bhalf * k, 16), g.bhalf)]
+
+
+def lay(g, sc, own, mine, theirs, at, size, dst, turn=0):
     k, f = sc[1], jnp.bitwise_xor(sc[2], turn)
-    size = piece
-    out = [
-        pltpu.make_async_copy(
-            own.at[pl.ds(own_at, 2 * size)],
-            dst.at[pl.ds(pl.multiple_of(2 * size * f, 16), 2 * size)],
-            sem.at[0],
-        )
-    ]
+    dst[pl.ds(pl.multiple_of(2 * size * f, 16), 2 * size), :] = own[...]
     for s in range(1, g.ring):
         base = 2 * size * jnp.bitwise_xor(f, s)
-        for i, (src, core) in enumerate(((mine[s - 1], k), (theirs[s - 1], 1 - k))):
-            out.append(
-                pltpu.make_async_copy(
-                    src.at[pl.ds(at, size)],
-                    dst.at[pl.ds(pl.multiple_of(base + size * core, 16), size)],
-                    sem.at[2 * s - 1 + i],
-                )
-            )
-    return out
+        for src, core in ((mine[s - 1], k), (theirs[s - 1], 1 - k)):
+            dst[pl.ds(pl.multiple_of(base + size * core, 16), size), :] = src[at : at + size, :]
 
 
 def start(copies):
@@ -532,22 +518,14 @@
     vec, own = refs[c : c + 2]
     mine = refs[c + 2 : c + 2 + n]
     theirs = refs[c + 2 + n : c + 2 + 2 * n]
-    out, w, full, vs, sem, vsem = refs[c + 2 + 2 * n :]
+    out, w, full = refs[c + 2 + 2 * n :]
     p, f = sc[0], sc[2]
-    copies = gathers(g, sc, own, 0, mine, theirs, 0, g.half, w, sem)
-    start(copies)
-    vcopies = [
-        pltpu.make_async_copy(
-            mine[s].at[pl.ds(g.half, VEC), pl.ds(0, LANES)], vs.at[s], vsem.at[s]
-        )
-        for s in range(n)
-    ]
-    start(vcopies)
-    finish(vcopies)
+    lay(g, sc, own, mine, theirs, 0, g.half, w)
     rest = jnp.zeros((VEC, g.width - LANES), F32)
     total = jnp.zeros((VEC, g.width), F32)
     for s in range(g.ring):
-        piece = (vec[...] if s == 0 else vs[s - 1]).astype(F32)
+        piece = vec[...] if s == 0 else mine[s - 1][g.half : g.half + VEC, 0:LANES]
+        piece = piece.astype(F32)
         wide = jnp.concatenate([piece, rest], axis=1)
         total = total + pltpu.roll(wide, g.shard * jnp.bitwise_xor(f, s), 1)
     full[...] = total
@@ -555,7 +533,6 @@
     bias = jnp.concatenate(
         [back[0:1, : g.cols], jnp.zeros((1, g.cols), F32), back[1:2, : g.cols]], axis=1
     )
-    finish(copies)
     rows = jnp.concatenate([x[...] for x in xs], axis=0)
     found = (dot(rows, w[...]) + bias).astype(BF)
     for h in range(g.heads):
@@ -765,17 +742,10 @@
     mine, theirs = refs[:n], refs[n : 2 * n]
     refs = refs[2 * n :]
     parts, (active, inner, low, z_own, s_own, wo_rows, wi, wd) = refs[:c], refs[c : c + 8]
-    wo, work, sem_o, sem_i, sem_d = refs[c + 8 :]
+    wo, work = refs[c + 8 :]
     p = sc[0]
-    at = pl.multiple_of(g.block * p, 16)
-    copies_o = gathers(g, sc, wo_own, 0, mine, theirs, g.half, g.half, wo, sem_o, p)
-    copies_i = gathers(g, sc, wi_own, 0, mine, theirs, 0, g.half, wi, sem_i)
-    copies_d = gathers(g, sc, wd_own, at, mine, theirs, 2 * g.half, g.bhalf, wd, sem_d)
-    start(copies_o)
+    lay(g, sc, wo_own, mine, theirs, g.half, g.half, wo, p)
     rows = jnp.concatenate([seen(g, ctxs[j], j) for j in range(c)], axis=1)
-    finish(copies_o)
-    start(copies_i)
-    start(copies_d)
     wo_rows[...] = wo[0 : g.cols]
     halves = [slice(i, i + g.tokens // 2) for i in range(0, g.tokens, g.tokens // 2)]
     bias = full[pl.ds(8 + p, 1), :]
@@ -811,13 +781,13 @@
     one, two = halves
     work[one] = dot(rows[one], wo[...])
     work[two] = dot(rows[two], wo[...])
+    lay(g, sc, wi_own, mine, theirs, 0, g.half, wi)
     first_norm(one)
-    finish(copies_i)
     inner[one] = dot(low[one], wi[...])
     first_norm(two)
     inner[two] = dot(low[two], wi[...])
+    lay(g, sc, wd_own, mine, theirs, 2 * g.half, g.bhalf, wd)
     activate(one)
-    finish(copies_d)
     descend(one)
     activate(two)
     descend(two)
@@ -1208,7 +1178,6 @@
     sc = jnp.stack([p, k, f]).astype(jnp.int32)
     bind = functools.partial
 
-    gate = pltpu.SemaphoreType.DMA((2 * ring - 1,))
 
     qall, qsend, vec = call(
         bind(pick_kernel, g),
@@ -1245,13 +1214,14 @@
         + [pltpu.VMEM((g.hshard,), BF), pltpu.SemaphoreType.DMA((12,))],
         name="pick_weights",
     )
-    q_mine = gather_ring(qsend)
     x_own = after(hidden_in.reshape(rows, width), qsend)
     xs = spread(x_own, chips)
-    iall, send = call(
+    iall, oall, dall, send = call(
         bind(prep_kernel, g),
         [
             shaped((g.shard, g.share), BF),
+            shaped((g.shard, width), BF),
+            shaped((g.block, width), BF),
             shaped((2 * g.half + g.bhalf, width), BF),
         ],
         [SMEM, HBM, FAR, FAR, FAR],
@@ -1259,6 +1229,7 @@
         [pltpu.VMEM((g.shard, hidden), BF), pltpu.SemaphoreType.DMA((3,))],
         name="prepare_weights",
     )
+    q_mine = gather_ring(qsend, send)
 
     step = g.clusters * g.members
     pick, place, blk = call(
@@ -1269,7 +1240,7 @@
             shaped((8, 2 * g.tokens), BF),
         ],
         [SMEM, HBM] + [VMEM] * 2,
-        [sc, q_mine[-1], clusters[0], block_ids],
+        [sc, q_mine[0], clusters[0], block_ids],
         name="cluster_tables",
     )
     (mask,) = call(
@@ -1280,7 +1251,7 @@
         name="cluster_mask",
     )
     x_other = [to_core(after(xs[0], xs[1]))] + [to_core(x) for x in xs[1:]]
-    q_theirs = [to_core(after(part, *xs[1:])) for part in q_mine]
+    q_theirs = [to_core(after(part, xs[1])) for part in q_mine]
     qkv, w_qkv, full = call(
         bind(qkv_kernel, g),
         [
@@ -1288,13 +1259,8 @@
             shaped((width, g.qkv), BF),
             shaped((VEC, width), F32),
         ],
-        [SMEM] + [VMEM] * (2 * chips + 1) + [HBM] * (2 * ring - 1),
-        [sc, *xs, *x_other, after(vec, pick), qall, *q_mine, *q_theirs],
-        [
-            pltpu.VMEM((ring - 1, VEC, LANES), BF),
-            gate,
-            pltpu.SemaphoreType.DMA((ring - 1,)),
-        ],
+        [SMEM] + [VMEM] * (2 * chips + 2 * ring),
+        [sc, *xs, *x_other, after(vec, send), qall, *q_mine, *q_theirs],
         name="project",
     )
     ctx_own, ctx_other, kept, probs = call(
@@ -1318,7 +1284,7 @@
         name="join_context",
     )
     ctxs = spread(ctx, chips)
-    w_mine = gather_ring(send, ctx)
+    w_mine = gather_ring(send, ctx_own)
 
     w_theirs = [to_core(after(part, *ctxs[1:])) for part in w_mine]
     *second, active, inner, low, z_own, s_own, wo_rows, wi, wd = call(
@@ -1335,9 +1301,9 @@
             shaped((width, g.share), BF),
             shaped((g.share, width), BF),
         ],
-        [SMEM] + [VMEM] * (2 * chips + 1) + [FAR, HBM, FAR] + [HBM] * (2 * ring - 2),
-        [sc, *ctxs, *xs, full, kept_far(w_out), iall, kept_far(w_down), *w_mine, *w_theirs],
-        [pltpu.VMEM((width, width), BF), pltpu.VMEM((g.tokens, width), F32), gate, gate, gate],
+        [SMEM] + [VMEM] * (2 * chips + 2 * ring + 2),
+        [sc, *ctxs, *xs, full, oall, iall, dall, *w_mine, *w_theirs],
+        [pltpu.VMEM((width, width), BF), pltpu.VMEM((g.tokens, width), F32)],
         name="mlp_forward",
     )
     (slope,) = mix(
@@ -1474,8 +1440,8 @@
         q_own, q_away = ring_step(q_own, q_away, mask_at // 2)
         o_own, o_away = ring_step(o_own, o_away, mask_at // 2)
         mask_at *= 2
-    near = spread(m_piece, chips)
-    m_pieces = near + [to_core(after(part, q_away)) for part in near]
+    near = pass_on(m_piece, chips, dq_theirs)
+    m_pieces = near + [to_core(part) for part in near]
     (input_grad,) = mix(
         lambda kept, *parts: (sum((part.astype(F32) for part in parts), kept).astype(BF),),
         [shaped((rows, width), BF)],
@@ -1502,8 +1468,8 @@
         along(o_away, mask_at // 2),
         name="last_sum",
     )
-    near = spread(piece, chips)
-    pieces = near + [to_core(after(part, input_grad, g_down)) for part in near]
+    near = spread(after(piece, input_grad), chips)
+    pieces = near + [to_core(part) for part in near]
     found = call(
         bind(last_kernel, g),
         [shaped((g.shard, width), F32)] * 3
@@ -1511,7 +1477,7 @@
         + [shaped((g.shard, width), F32), shaped((g.hshard,), F32)]
         + [vector] * 6,
         [SMEM] + [VMEM] * (2 * chips),
-        [sc, *pieces],
+        [after(sc, g_down), *pieces],
         name="last_lay",
     )
     gq, gk, gv, g_bq, g_bv, g_out, g_bin, g_gain2, g_bias2, g_bdown, g_gain1, g_bias1, g_bout = found

time: 189 us -> 180 us (0.952)
  Pallas kernels: 43.7 us -> 38.2 us
  waiting for transfers between devices: 79.5 us -> 74.8 us
    ppermute x13, waiting for transfers between devices: 31.2 us -> 23.7 us  [along(): return lax.ppermute(x, 'fsdp', [(i, i ^ mask) for i in range(n)])]
    pallas_call x27, Pallas kernels: 43.7 us -> 38.2 us  [call(): pl.pallas_call(kernel, out_shape=outs, in_specs=ins, out_specs=[VMEM] * l...]
    ppermute x27, waiting for transfers between devices: 40.1 us -> 43.1 us  [to_chip(): return lax.ppermute(x, 'ctx', [(i, i ^ 2 * j) for i in range(n)])]
  transfers between devices with their start and end apart: 62 -> 62, of which waited for: 29 -> 30; matrix products, arithmetic and copies ran while one was open for 0% -> 0% of each run, Pallas kernels for 13% -> 13%
where the time goes in v4:
time: 180 us; the launch traced here: 179 us
  waiting for transfers between devices  74.8 us (42%)
  starting transfers between devices  64.4 us (36%)
  Pallas kernels  38.2 us (21%)
    ppermute x27, waiting for transfers between devices, to_chip(): return lax.ppermute(x, 'ctx', [(i, i ^ 2 * j) for i in range(n)])  43.1 us
    pallas_call x27, Pallas kernels, call(): pl.pallas_call(kernel, out_shape=outs, in_specs=ins, out_specs=[VMEM] * l...  38.2 us
    ppermute x27, starting transfers between devices, to_chip(): return lax.ppermute(x, 'ctx', [(i, i ^ 2 * j) for i in range(n)])  32.6 us
    ppermute x13, starting transfers between devices, along(): return lax.ppermute(x, 'fsdp', [(i, i ^ mask) for i in range(n)])  28.4 us
    ppermute x13, waiting for transfers between devices, along(): return lax.ppermute(x, 'fsdp', [(i, i ^ mask) for i in range(n)])  23.7 us
    ppermute x22, waiting for transfers between devices, to_core(): return lax.ppermute(x, 'ctx', [(i, i ^ 1) for i in range(n)])  7.97 us
  transfers between devices with their start and end apart: 62, of which 30 were waited for; matrix products, arithmetic and copies ran while one was open for 0% of the time, Pallas kernels for 13%

profile of v4, /device:TPU:0, one launch (start us, length us, event | category | flops | bytes accessed | tf_op | source)
XLA Modules:
  0.0 178.7 jit_solution(433947723556207974)
XLA Ops:
  0.7 2.0 %pick_weights.1 = (bf16[192,576]{1,0:T(8,128)(2,1)S(1)}, bf16[112,576]{1,0:T(8,128)(2,1)S(1)}, bf16[16,256]{1,0:T(8,128)(2,1)S(1)}) custom-call(s32[3]{0:T(128)S(1)} %pad_add_fusion.sc, bf16[192,768]{1,0:T(8,128)(2,1)} %refs_0_.1, bf16[192,768]{1,0:T(8,128)(2,1)} %refs_1_.1, bf16[192,768]{1,0:T(8,128)(2,1)} %refs_2_.1, bf16[192]{0:T(256)(128)(2,1)} %refs_3_.1, ...), custom_call_target="tpu_custom_call" | custom-call | flops 1 | bytes 1 | tf_op jit(solution)/shard_map/pick_weights/pallas_call | solution.py:381
  2.8 3.0 %collective-permute-start = (bf16[128,768]{1,0:T(8,128)(2,1)}, bf16[128,768]{1,0:T(8,128)(2,1)S(1)}, u32[]{:S(2)}, u32[]{:S(2)}) collective-permute-start(bf16[128,768]{1,0:T(8,128)(2,1)} %bitcast.10), channel_id=1, source_target_pairs={{0,8},{4,12},{8,0},{12,4},{16,24},{20,28},{24,16},{28,20},{1,9},{5... | collective-permute-start | bytes 589832 | tf_op jit(solution)/shard_map/ppermute | solution.py:1045
  5.8 2.6 %collective-permute-start.8 = (bf16[112,576]{1,0:T(8,128)(2,1)S(1)}, bf16[112,576]{1,0:T(8,128)(2,1)S(1)}, u32[]{:S(2)}, u32[]{:S(2)}) collective-permute-start(bf16[112,576]{1,0:T(8,128)(2,1)S(1)} %get-tuple-element.110._), channel_id=1, source_target_pairs={{0,2},{1,3},{2,0},{3,1},{4,6},{5,7},{6,4},{7,5},{8,10},{9,11},{10,... | collective-permute-start | bytes 387080 | tf_op jit(solution)/shard_map/ppermute | solution.py:1050
  8.4 1.6 collective-permute-start.7
  10.0 1.5 collective-permute-start.2
  11.9 2.0 %prepare_weights.1 = (bf16[192,768]{1,0:T(8,128)(2,1)S(1)}, bf16[192,768]{1,0:T(8,128)(2,1)S(1)}, bf16[192,768]{1,0:T(8,128)(2,1)S(1)}, bf16[288,768]{1,0:T(8,128)(2,1)S(1)}) custom-call(s32[3]{0:T(128)S(1)} %pad_add_fusion.sc, bf16[112,576]{1,0:T(8,128)(2,1)S(1)} %get-tuple-element.110._, bf16[192,3072]{1,0:T(8,128)(2,1)} %wi.1, bf16[768,768]{1,0:T(8,128)(2,1)} %wd.1, ...), custom_call_target="tpu_custom_call" | custom-call | flops 1 | bytes 1 | tf_op jit(solution)/shard_map/prepare_weights/pallas_call | solution.py:381
  16.7 2.4 %collective-permute-start.18 = (bf16[288,768]{1,0:T(8,128)(2,1)S(1)}, bf16[288,768]{1,0:T(8,128)(2,1)S(1)}, u32[]{:S(2)}, u32[]{:S(2)}) collective-permute-start(bf16[288,768]{1,0:T(8,128)(2,1)S(1)} %get-tuple-element.114), channel_id=1, source_target_pairs={{0,2},{1,3},{2,0},{3,1},{4,6},{5,7},{6,4},{7,5},{8,10},{9,11},{10,... | collective-permute-start | bytes 1327112 | tf_op jit(solution)/shard_map/ppermute | solution.py:1050
  23.2 4.9 %cluster_tables.1 = (bf16[3,512,128]{2,1,0:T(8,128)(2,1)S(1)}, bf16[3,1024,64]{2,1,0:T(8,128)(2,1)S(1)}, bf16[8,1024]{1,0:T(8,128)(2,1)S(1)}) custom-call(s32[3]{0:T(128)S(1)} %pad_add_fusion.sc, bf16[112,576]{1,0:T(8,128)(2,1)S(1)} %collective-permute-done.7.refs_10_._, s32[12,1024]{1,0:T(8,128)S(1)} %bitcast.17, s32[1,1024]{1,0:T(1,128)S(1)} %copy-done.2), custom_call_target="tpu_custom_call" | custom-call | flops 1 | bytes 1 | tf_op jit(solution)/shard_map/cluster_tables/pallas_call | solution.py:381
  29.1 2.1 %project.1 = (bf16[1024,768]{1,0:T(8,128)(2,1)S(1)}, bf16[768,576]{1,0:T(8,128)(2,1)S(1)}, f32[16,768]{1,0:T(8,128)S(1)}) custom-call(s32[3]{0:T(128)S(1)} %pad_add_fusion.sc, bf16[128,768]{1,0:T(8,128)(2,1)S(1)} %bitcast.14, bf16[128,768]{1,0:T(8,128)(2,1)S(1)} %collective-permute-done.refs_1_.refs_5_, ...), custom_call_target="tpu_custom_call" | custom-call | flops 1 | bytes 1 | tf_op jit(solution)/shard_map/project/pallas_call | solution.py:381
  32.6 7.1 %collective-permute-done.18.refs_13_ = bf16[288,768]{1,0:T(8,128)(2,1)S(1)} collective-permute-done((bf16[288,768]{1,0:T(8,128)(2,1)S(1)}, bf16[288,768]{1,0:T(8,128)(2,1)S(1)}, u32[]{:S(2)}, u32[]{:S(2)}) %collective-permute-start.18) | collective-permute-done | bytes 442400 | tf_op jit(solution)/shard_map/ppermute | solution.py:1050
  39.7 1.5 collective-permute-start.19
  41.2 1.5 collective-permute-done.13.refs_1_
  42.7 1.5 collective-permute-start.16
  44.8 1.5 collective-permute-start.14
  46.3 6.6 %collective-permute-done.16.refs_3_.refs_7_ = bf16[512,192]{1,0:T(8,128)(2,1)S(1)} collective-permute-done((bf16[512,192]{1,0:T(8,128)(2,1)S(1)}, bf16[512,192]{1,0:T(8,128)(2,1)S(1)}, u32[]{:S(2)}, u32[]{:S(2)}) %collective-permute-start.16) | collective-permute-done | bytes 196640 | tf_op jit(solution)/shard_map/ppermute | solution.py:1045
  52.9 4.8 %collective-permute-done.15.refs_2_.refs_6_ = bf16[512,192]{1,0:T(8,128)(2,1)S(1)} collective-permute-done((bf16[512,192]{1,0:T(8,128)(2,1)S(1)}, bf16[512,192]{1,0:T(8,128)(2,1)S(1)}, u32[]{:S(2)}, u32[]{:S(2)}) %collective-permute-start.15) | collective-permute-done | bytes 196640 | tf_op jit(solution)/shard_map/ppermute | solution.py:1045
  60.8 3.2 %mlp_forward.1 = (f32[128,768]{1,0:T(8,128)S(1)}, bf16[128,768]{1,0:T(8,128)(2,1)S(1)}, bf16[128,768]{1,0:T(8,128)(2,1)S(1)}, bf16[128,768]{1,0:T(8,128)(2,1)S(1...) custom-call(s32[3]{0:T(128)S(1)} %pad_add_fusion.sc, ...), custom_call_target="tpu_custom_call" | custom-call | flops 1 | bytes 1 | tf_op jit(solution)/shard_map/mlp_forward/pallas_call | solution.py:381
  64.6 1.4 collective-permute-start.24
  66.0 1.6 collective-permute-start.25
  67.6 1.4 turn_rows.1.turned_x
  69.1 2.8 %collective-permute-done.23.refs_1_ = bf16[128,768]{1,0:T(8,128)(2,1)S(1)} collective-permute-done((bf16[128,768]{1,0:T(8,128)(2,1)S(1)}, bf16[128,768]{1,0:T(8,128)(2,1)S(1)}, u32[]{:S(2)}, u32[]{:S(2)}) %collective-permute-start.23) | collective-permute-done | bytes 196640 | tf_op jit(solution)/shard_map/ppermute | solution.py:1045
  72.1 3.4 %collective-permute-done.25.refs_3_ = bf16[128,768]{1,0:T(8,128)(2,1)S(1)} collective-permute-done((bf16[128,768]{1,0:T(8,128)(2,1)S(1)}, bf16[128,768]{1,0:T(8,128)(2,1)S(1)}, u32[]{:S(2)}, u32[]{:S(2)}) %collective-permute-start.25) | collective-permute-done | bytes 196640 | tf_op jit(solution)/shard_map/ppermute | solution.py:1045
  76.5 1.7 collective-permute-start.28
  80.5 5.2 %collective-permute-done.28.refs_3_ = bf16[144,768]{1,0:T(8,128)(2,1)S(1)} collective-permute-done((bf16[144,768]{1,0:T(8,128)(2,1)S(1)}, bf16[144,768]{1,0:T(8,128)(2,1)S(1)}, u32[]{:S(2)}, u32[]{:S(2)}) %collective-permute-start.28) | collective-permute-done | bytes 221216 | tf_op jit(solution)/shard_map/ppermute | solution.py:1045
  85.8 2.9 %collective-permute-done.27.refs_2_ = bf16[144,768]{1,0:T(8,128)(2,1)S(1)} collective-permute-done((bf16[144,768]{1,0:T(8,128)(2,1)S(1)}, bf16[144,768]{1,0:T(8,128)(2,1)S(1)}, u32[]{:S(2)}, u32[]{:S(2)}) %collective-permute-start.27) | collective-permute-done | bytes 221216 | tf_op jit(solution)/shard_map/ppermute | solution.py:1045
  88.7 1.5 mlp_back.1
  90.3 2.2 %mlp_grads.1 = (f32[4,192,768]{2,1,0:T(8,128)S(1)}, bf16[4,192,768]{2,1,0:T(8,128)(2,1)S(1)}, f32[8,768]{1,0:T(8,128)S(1)}) custom-call(s32[3]{0:T(128)S(1)} %pad_add_fusion.sc, bf16[144,768]{1,0:T(8,128)(2,1)S(1)} %get-tuple-element.143.refs_0_, bf16[144,768]{1,0:T(8,128)(2,1)S(1)} %collective-permute-done.26.refs_1_, ...), custom_call_target="tpu_custom_call" | custom-call | flops 1 | bytes 1 | tf_op jit(solution)/shard_map/mlp_grads/pallas_call | solution.py:381
  92.6 2.8 %collective-permute-done.32.refs_1_ = bf16[4,192,768]{2,1,0:T(8,128)(2,1)S(1)} collective-permute-done((bf16[4,192,768]{2,1,0:T(8,128)(2,1)S(1)}, bf16[4,192,768]{2,1,0:T(8,128)(2,1)S(1)}, u32[]{:S(2)}, u32[]{:S(2)}) %collective-permute-start.32) | collective-permute-done | bytes 1179680 | tf_op jit(solution)/shard_map/ppermute | solution.py:1040
  98.1 1.6 collective-permute-start.31
  99.7 2.3 %collective-permute-start.37 = (bf16[192,768]{1,0:T(8,128)(2,1)S(1)}, bf16[192,768]{1,0:T(8,128)(2,1)S(1)}, u32[]{:S(2)}, u32[]{:S(2)}) collective-permute-start(bf16[192,768]{1,0:T(8,128)(2,1)S(1)} %get-tuple-element.157), channel_id=1, source_target_pairs={{0,2},{1,3},{2,0},{3,1},{4,6},{5,7},{6,4},{7,5},{8,10},{9,11},{10,... | collective-permute-start | bytes 884744 | tf_op jit(solution)/shard_map/ppermute | solution.py:1050
  102.0 2.0 %collective-permute-done.29.refs_1_ = bf16[128,768]{1,0:T(8,128)(2,1)S(1)} collective-permute-done((bf16[128,768]{1,0:T(8,128)(2,1)S(1)}, bf16[128,768]{1,0:T(8,128)(2,1)S(1)}, u32[]{:S(2)}, u32[]{:S(2)}) %collective-permute-start.29) | collective-permute-done | bytes 196640 | tf_op jit(solution)/shard_map/ppermute | solution.py:1045
  104.0 3.5 %collective-permute-start.38 = (bf16[192,768]{1,0:T(8,128)(2,1)S(1)}, bf16[192,768]{1,0:T(8,128)(2,1)S(1)}, u32[]{:S(2)}, u32[]{:S(2)}) collective-permute-start(bf16[192,768]{1,0:T(8,128)(2,1)S(1)} %get-tuple-element.158), channel_id=1, source_target_pairs={{0,3},{1,2},{2,1},{3,0},{4,7},{5,6},{6,5},{7,4},{8,11},{9,10},{10,... | collective-permute-start | bytes 884744 | tf_op jit(solution)/shard_map/ppermute | solution.py:1050
  108.4 1.6 collective-permute-start.35
  112.0 11.2 %collective-permute-done.37.refs_2_ = bf16[192,768]{1,0:T(8,128)(2,1)S(1)} collective-permute-done((bf16[192,768]{1,0:T(8,128)(2,1)S(1)}, bf16[192,768]{1,0:T(8,128)(2,1)S(1)}, u32[]{:S(2)}, u32[]{:S(2)}) %collective-permute-start.37) | collective-permute-done | bytes 294944 | tf_op jit(solution)/shard_map/ppermute | solution.py:1050
  125.4 1.9 %attend_back.1.mine = bf16[1024,640]{1,0:T(8,128)(2,1)S(1)} custom-call(bf16[512,192]{1,0:T(8,128)(2,1)S(1)} %context_back.1.own, bf16[512,192]{1,0:T(8,128)(2,1)S(1)} %collective-permute-done.39.other, bf16[3,512,128]{2,1,0:T(8,128)(2,1)S(1)} %get-tuple-element.122.pick, bf16[3,1024,64]{2,1,0:T(8,128)(2,1)S(1)} %get-tuple-element.123.place, ...), custom_call_target="tpu_custom_call" | custom-call | flops 1 | bytes 1 | tf_op jit(solution)/shard_map/attend_back/pallas_call | solution.py:381
  129.1 4.9 %collective-permute-start.53 = (bf16[2,64,768]{2,1,0:T(8,128)(2,1)S(1)}, bf16[2,64,768]{2,1,0:T(8,128)(2,1)S(1)}, u32[]{:S(2)}, u32[]{:S(2)}) collective-permute-start(bf16[2,64,768]{2,1,0:T(8,128)(2,1)S(1)} %get-tuple-element.185), channel_id=1, source_target_pairs={{0,1},{1,0},{2,3},{3,2},{4,5},{5,4},{6,7},{7,6},{8,9},{9,8},{10,11... | collective-permute-start | bytes 589832 | tf_op jit(solution)/shard_map/ppermute | solution.py:1050
  135.3 1.6 collective-permute-start.41
  136.9 1.6 project_grads.1
  139.2 3.5 %collective-permute-start.54 = (bf16[1,64,768]{2,1,0:T(8,128)(2,1)S(1)}, bf16[1,64,768]{2,1,0:T(8,128)(2,1)S(1)}, u32[]{:S(2)}, u32[]{:S(2)}) collective-permute-start(bf16[1,64,768]{2,1,0:T(8,128)(2,1)S(1)} %get-tuple-element.187), channel_id=1, source_target_pairs={{0,2},{1,3},{2,0},{3,1},{4,6},{5,7},{6,4},{7,5},{8,10},{9,11},{10,... | collective-permute-start | bytes 294920 | tf_op jit(solution)/shard_map/ppermute | solution.py:1050
  143.9 2.8 %collective-permute-done.54.refs_3_ = bf16[1,64,768]{2,1,0:T(8,128)(2,1)S(1)} collective-permute-done((bf16[1,64,768]{2,1,0:T(8,128)(2,1)S(1)}, bf16[1,64,768]{2,1,0:T(8,128)(2,1)S(1)}, u32[]{:S(2)}, u32[]{:S(2)}) %collective-permute-start.54) | collective-permute-done | bytes 98336 | tf_op jit(solution)/shard_map/ppermute | solution.py:1050
  146.7 1.6 collective-permute-start.43
  149.0 3.4 %collective-permute-start.52 = (bf16[1,80,768]{2,1,0:T(8,128)(2,1)S(1)}, bf16[1,80,768]{2,1,0:T(8,128)(2,1)S(1)}, u32[]{:S(2)}, u32[]{:S(2)}) collective-permute-start(bf16[1,80,768]{2,1,0:T(8,128)(2,1)S(1)} %get-tuple-element.183), channel_id=1, source_target_pairs={{0,2},{1,3},{2,0},{3,1},{4,6},{5,7},{6,4},{7,5},{8,10},{9,11},{10,... | collective-permute-start | bytes 368648 | tf_op jit(solution)/shard_map/ppermute | solution.py:1050
  152.5 2.5 %collective-permute-done.43.refs_4_ = bf16[128,768]{1,0:T(8,128)(2,1)S(1)} collective-permute-done((bf16[128,768]{1,0:T(8,128)(2,1)S(1)}, bf16[128,768]{1,0:T(8,128)(2,1)S(1)}, u32[]{:S(2)}, u32[]{:S(2)}) %collective-permute-start.43) | collective-permute-done | bytes 196640 | tf_op jit(solution)/shard_map/ppermute | solution.py:1045
  155.9 1.6 collective-permute-start.57
  159.5 6.5 %collective-permute-done.46.refs_3_ = bf16[192,768]{1,0:T(8,128)(2,1)S(1)} collective-permute-done((bf16[192,768]{1,0:T(8,128)(2,1)S(1)}, bf16[192,768]{1,0:T(8,128)(2,1)S(1)}, u32[]{:S(2)}, u32[]{:S(2)}) %collective-permute-start.46) | collective-permute-done | bytes 294944 | tf_op jit(solution)/shard_map/ppermute | solution.py:1045
  166.6 4.1 %collective-permute-done.56.refs_2_ = bf16[144,768]{1,0:T(8,128)(2,1)S(1)} collective-permute-done((bf16[144,768]{1,0:T(8,128)(2,1)S(1)}, bf16[144,768]{1,0:T(8,128)(2,1)S(1)}, u32[]{:S(2)}, u32[]{:S(2)}) %collective-permute-start.56) | collective-permute-done | bytes 221216 | tf_op jit(solution)/shard_map/ppermute | solution.py:1045
  171.2 3.9 %mlp_lay.1 = (f32[192,3072]{1,0:T(8,128)}, f32[768,768]{1,0:T(8,128)}) custom-call(s32[3]{0:T(128)S(1)} %pad_add_fusion.sc, bf16[192,768]{1,0:T(8,128)(2,1)S(1)} %mlp_sum.1.refs_0_, bf16[192,768]{1,0:T(8,128)(2,1)S(1)} %collective-permute-done.44.refs_1_, bf16[192,768]{1,0:T(8,128)(2,1)S(1)} %collective-permute-done.45.refs_2_, ...), custom_call_target="tpu_custom_call" | custom-call | flops 1 | bytes 1 | tf_op jit(solution)/shard_map/mlp_lay/pallas_call | solution.py:381
  175.2 3.3 %last_lay.1 = (f32[192,768]{1,0:T(8,128)}, f32[192,768]{1,0:T(8,128)}, f32[192,768]{1,0:T(8,128)}, f32[192]{0:T(256)}, f32[192]{0:T(256)}, /*index=5*/f32[192,76...) custom-call(s32[3]{0:T(128)S(1)} %pad_add_fusion.sc, ...), custom_call_target="tpu_custom_call" | custom-call | flops 1 | bytes 1 | tf_op jit(solution)/shard_map/last_lay/pallas_call | solution.py:381
  (113 shorter events, 35.3 us)
Async XLA Ops:
  2.8 13.9 %collective-permute-start = (bf16[128,768]{1,0:T(8,128)(2,1)}, bf16[128,768]{1,0:T(8,128)(2,1)S(1)}, u32[]{:S(2)}, u32[]{:S(2)}) collective-permute-start(bf16[128,768]{1,0:T(8,128)(2,1)} %bitcast.10), channel_id=1, source_target_pairs={{0,8},{4,12},{8,0},{12,4},{16,24},{20,28},{24,16},{28,20},{1,9},{5... | collective-permute-start | bytes 589832 | tf_op jit(solution)/shard_map/ppermute | solution.py:1045
  5.8 9.3 %collective-permute-start.8 = (bf16[112,576]{1,0:T(8,128)(2,1)S(1)}, bf16[112,576]{1,0:T(8,128)(2,1)S(1)}, u32[]{:S(2)}, u32[]{:S(2)}) collective-permute-start(bf16[112,576]{1,0:T(8,128)(2,1)S(1)} %get-tuple-element.110._), channel_id=1, source_target_pairs={{0,2},{1,3},{2,0},{3,1},{4,6},{5,7},{6,4},{7,5},{8,10},{9,11},{10,... | collective-permute-start | bytes 387080 | tf_op jit(solution)/shard_map/ppermute | solution.py:1050
  8.4 6.9 %collective-permute-start.7 = (bf16[112,576]{1,0:T(8,128)(2,1)S(1)}, bf16[112,576]{1,0:T(8,128)(2,1)S(1)}, u32[]{:S(2)}, u32[]{:S(2)}) collective-permute-start(bf16[112,576]{1,0:T(8,128)(2,1)S(1)} %get-tuple-element.110._), channel_id=1, source_target_pairs={{0,1},{1,0},{2,3},{3,2},{4,5},{5,4},{6,7},{7,6},{8,9},{9,8},{10,11... | collective-permute-start | bytes 387080 | tf_op jit(solution)/shard_map/ppermute | solution.py:1050
  10.0 9.1 %collective-permute-start.2 = (bf16[128,768]{1,0:T(8,128)(2,1)}, bf16[128,768]{1,0:T(8,128)(2,1)S(1)}, u32[]{:S(2)}, u32[]{:S(2)}) collective-permute-start(bf16[128,768]{1,0:T(8,128)(2,1)} %bitcast.11), channel_id=1, source_target_pairs={{0,24},{4,28},{8,16},{12,20},{16,8},{20,12},{24,0},{28,4},{1,25},{... | collective-permute-start | bytes 589832 | tf_op jit(solution)/shard_map/ppermute | solution.py:1045
  11.4 9.7 %collective-permute-start.1 = (bf16[128,768]{1,0:T(8,128)(2,1)}, bf16[128,768]{1,0:T(8,128)(2,1)S(1)}, u32[]{:S(2)}, u32[]{:S(2)}) collective-permute-start(bf16[128,768]{1,0:T(8,128)(2,1)} %bitcast.12), channel_id=1, source_target_pairs={{0,16},{4,20},{8,24},{12,28},{16,0},{20,4},{24,8},{28,12},{1,17},{... | collective-permute-start | bytes 589832 | tf_op jit(solution)/shard_map/ppermute | solution.py:1045
  16.7 23.0 %collective-permute-start.18 = (bf16[288,768]{1,0:T(8,128)(2,1)S(1)}, bf16[288,768]{1,0:T(8,128)(2,1)S(1)}, u32[]{:S(2)}, u32[]{:S(2)}) collective-permute-start(bf16[288,768]{1,0:T(8,128)(2,1)S(1)} %get-tuple-element.114), channel_id=1, source_target_pairs={{0,2},{1,3},{2,0},{3,1},{4,6},{5,7},{6,4},{7,5},{8,10},{9,11},{10,... | collective-permute-start | bytes 1327112 | tf_op jit(solution)/shard_map/ppermute | solution.py:1050
  19.1 20.6 %collective-permute-start.17 = (bf16[288,768]{1,0:T(8,128)(2,1)S(1)}, bf16[288,768]{1,0:T(8,128)(2,1)S(1)}, u32[]{:S(2)}, u32[]{:S(2)}) collective-permute-start(bf16[288,768]{1,0:T(8,128)(2,1)S(1)} %get-tuple-element.114), channel_id=1, source_target_pairs={{0,1},{1,0},{2,3},{3,2},{4,5},{5,4},{6,7},{7,6},{8,9},{9,8},{10,11... | collective-permute-start | bytes 1327112 | tf_op jit(solution)/shard_map/ppermute | solution.py:1050
  22.5 6.6 %collective-permute-start.3 = (bf16[128,768]{1,0:T(8,128)(2,1)S(1)}, bf16[128,768]{1,0:T(8,128)(2,1)S(1)}, u32[]{:S(2)}, u32[]{:S(2)}) collective-permute-start(bf16[128,768]{1,0:T(8,128)(2,1)S(1)} %bitcast.13), channel_id=1, source_target_pairs={{0,4},{4,0},{8,12},{12,8},{16,20},{20,16},{24,28},{28,24},{1,5},{5... | collective-permute-start | bytes 589832 | tf_op jit(solution)/shard_map/ppermute | solution.py:1040
  22.7 6.4 %collective-permute-start.5 = (bf16[128,768]{1,0:T(8,128)(2,1)S(1)}, bf16[128,768]{1,0:T(8,128)(2,1)S(1)}, u32[]{:S(2)}, u32[]{:S(2)}) collective-permute-start(bf16[128,768]{1,0:T(8,128)(2,1)S(1)} %collective-permute-done.1.refs_2_.refs_6_), channel_id=1, source_target_pairs={{0,4},{4,0},{8,12},{12,8},{16,20},{20,16},{24,28},{28,24},{1,5},{5... | collective-permute-start | bytes 589832 | tf_op jit(solution)/shard_map/ppermute | solution.py:1040
  23.0 6.1 %collective-permute-start.4 = (bf16[128,768]{1,0:T(8,128)(2,1)S(1)}, bf16[128,768]{1,0:T(8,128)(2,1)S(1)}, u32[]{:S(2)}, u32[]{:S(2)}) collective-permute-start(bf16[128,768]{1,0:T(8,128)(2,1)S(1)} %collective-permute-done.refs_1_.refs_5_), channel_id=1, source_target_pairs={{0,4},{4,0},{8,12},{12,8},{16,20},{20,16},{24,28},{28,24},{1,5},{5... | collective-permute-start | bytes 589832 | tf_op jit(solution)/shard_map/ppermute | solution.py:1040
  39.7 18.6 %collective-permute-start.19 = (bf16[288,768]{1,0:T(8,128)(2,1)S(1)}, bf16[288,768]{1,0:T(8,128)(2,1)S(1)}, u32[]{:S(2)}, u32[]{:S(2)}) collective-permute-start(bf16[288,768]{1,0:T(8,128)(2,1)S(1)} %collective-permute-done.18.refs_13_), channel_id=1, source_target_pairs={{0,1},{1,0},{2,3},{3,2},{4,5},{5,4},{6,7},{7,6},{8,9},{9,8},{10,11... | collective-permute-start | bytes 1327112 | tf_op jit(solution)/shard_map/ppermute | solution.py:1050
  42.7 10.2 %collective-permute-start.16 = (bf16[512,192]{1,0:T(8,128)(2,1)S(1)}, bf16[512,192]{1,0:T(8,128)(2,1)S(1)}, u32[]{:S(2)}, u32[]{:S(2)}) collective-permute-start(bf16[512,192]{1,0:T(8,128)(2,1)S(1)} %join_context.1.refs_0_.refs_4_), channel_id=1, source_target_pairs={{0,24},{4,28},{8,16},{12,20},{16,8},{20,12},{24,0},{28,4},{1,25},{... | collective-permute-start | bytes 589832 | tf_op jit(solution)/shard_map/ppermute | solution.py:1045
  44.3 13.4 %collective-permute-start.15 = (bf16[512,192]{1,0:T(8,128)(2,1)S(1)}, bf16[512,192]{1,0:T(8,128)(2,1)S(1)}, u32[]{:S(2)}, u32[]{:S(2)}) collective-permute-start(bf16[512,192]{1,0:T(8,128)(2,1)S(1)} %join_context.1.refs_0_.refs_4_), channel_id=1, source_target_pairs={{0,16},{4,20},{8,24},{12,28},{16,0},{20,4},{24,8},{28,12},{1,17},{... | collective-permute-start | bytes 589832 | tf_op jit(solution)/shard_map/ppermute | solution.py:1045
  44.8 13.0 %collective-permute-start.14 = (bf16[512,192]{1,0:T(8,128)(2,1)S(1)}, bf16[512,192]{1,0:T(8,128)(2,1)S(1)}, u32[]{:S(2)}, u32[]{:S(2)}) collective-permute-start(bf16[512,192]{1,0:T(8,128)(2,1)S(1)} %join_context.1.refs_0_.refs_4_), channel_id=1, source_target_pairs={{0,8},{4,12},{8,0},{12,4},{16,24},{20,28},{24,16},{28,20},{1,9},{5... | collective-permute-start | bytes 589832 | tf_op jit(solution)/shard_map/ppermute | solution.py:1045
  64.1 7.8 %collective-permute-start.23 = (bf16[128,768]{1,0:T(8,128)(2,1)S(1)}, bf16[128,768]{1,0:T(8,128)(2,1)S(1)}, u32[]{:S(2)}, u32[]{:S(2)}) collective-permute-start(bf16[128,768]{1,0:T(8,128)(2,1)S(1)} %get-tuple-element.136), channel_id=1, source_target_pairs={{0,8},{4,12},{8,0},{12,4},{16,24},{20,28},{24,16},{28,20},{1,9},{5... | collective-permute-start | bytes 589832 | tf_op jit(solution)/shard_map/ppermute | solution.py:1045
  64.6 7.5 %collective-permute-start.24 = (bf16[128,768]{1,0:T(8,128)(2,1)S(1)}, bf16[128,768]{1,0:T(8,128)(2,1)S(1)}, u32[]{:S(2)}, u32[]{:S(2)}) collective-permute-start(bf16[128,768]{1,0:T(8,128)(2,1)S(1)} %get-tuple-element.137), channel_id=1, source_target_pairs={{0,16},{4,20},{8,24},{12,28},{16,0},{20,4},{24,8},{28,12},{1,17},{... | collective-permute-start | bytes 589832 | tf_op jit(solution)/shard_map/ppermute | solution.py:1045
  66.0 9.4 %collective-permute-start.25 = (bf16[128,768]{1,0:T(8,128)(2,1)S(1)}, bf16[128,768]{1,0:T(8,128)(2,1)S(1)}, u32[]{:S(2)}, u32[]{:S(2)}) collective-permute-start(bf16[128,768]{1,0:T(8,128)(2,1)S(1)} %get-tuple-element.138), channel_id=1, source_target_pairs={{0,24},{4,28},{8,16},{12,20},{16,8},{20,12},{24,0},{28,4},{1,25},{... | collective-permute-start | bytes 589832 | tf_op jit(solution)/shard_map/ppermute | solution.py:1045
  76.5 9.3 %collective-permute-start.28 = (bf16[144,768]{1,0:T(8,128)(2,1)S(1)}, bf16[144,768]{1,0:T(8,128)(2,1)S(1)}, u32[]{:S(2)}, u32[]{:S(2)}) collective-permute-start(bf16[144,768]{1,0:T(8,128)(2,1)S(1)} %get-tuple-element.143.refs_0_), channel_id=1, source_target_pairs={{0,24},{4,28},{8,16},{12,20},{16,8},{20,12},{24,0},{28,4},{1,25},{... | collective-permute-start | bytes 663560 | tf_op jit(solution)/shard_map/ppermute | solution.py:1045
  78.1 10.6 %collective-permute-start.27 = (bf16[144,768]{1,0:T(8,128)(2,1)S(1)}, bf16[144,768]{1,0:T(8,128)(2,1)S(1)}, u32[]{:S(2)}, u32[]{:S(2)}) collective-permute-start(bf16[144,768]{1,0:T(8,128)(2,1)S(1)} %get-tuple-element.143.refs_0_), channel_id=1, source_target_pairs={{0,16},{4,20},{8,24},{12,28},{16,0},{20,4},{24,8},{28,12},{1,17},{... | collective-permute-start | bytes 663560 | tf_op jit(solution)/shard_map/ppermute | solution.py:1045
  79.5 9.2 %collective-permute-start.26 = (bf16[144,768]{1,0:T(8,128)(2,1)S(1)}, bf16[144,768]{1,0:T(8,128)(2,1)S(1)}, u32[]{:S(2)}, u32[]{:S(2)}) collective-permute-start(bf16[144,768]{1,0:T(8,128)(2,1)S(1)} %get-tuple-element.143.refs_0_), channel_id=1, source_target_pairs={{0,8},{4,12},{8,0},{12,4},{16,24},{20,28},{24,16},{28,20},{1,9},{5... | collective-permute-start | bytes 663560 | tf_op jit(solution)/shard_map/ppermute | solution.py:1045
  95.6 15.1 %collective-permute-start.36 = (bf16[192,768]{1,0:T(8,128)(2,1)S(1)}, bf16[192,768]{1,0:T(8,128)(2,1)S(1)}, u32[]{:S(2)}, u32[]{:S(2)}) collective-permute-start(bf16[192,768]{1,0:T(8,128)(2,1)S(1)} %get-tuple-element.156), channel_id=1, source_target_pairs={{0,1},{1,0},{2,3},{3,2},{4,5},{5,4},{6,7},{7,6},{8,9},{9,8},{10,11... | collective-permute-start | bytes 884744 | tf_op jit(solution)/shard_map/ppermute | solution.py:1050
  96.2 7.8 %collective-permute-start.29 = (bf16[128,768]{1,0:T(8,128)(2,1)S(1)}, bf16[128,768]{1,0:T(8,128)(2,1)S(1)}, u32[]{:S(2)}, u32[]{:S(2)}) collective-permute-start(bf16[128,768]{1,0:T(8,128)(2,1)S(1)} %get-tuple-element.147), channel_id=1, source_target_pairs={{0,8},{4,12},{8,0},{12,4},{16,24},{20,28},{24,16},{28,20},{1,9},{5... | collective-permute-start | bytes 589832 | tf_op jit(solution)/shard_map/ppermute | solution.py:1045
  97.5 10.6 %collective-permute-start.30 = (bf16[128,768]{1,0:T(8,128)(2,1)S(1)}, bf16[128,768]{1,0:T(8,128)(2,1)S(1)}, u32[]{:S(2)}, u32[]{:S(2)}) collective-permute-start(bf16[128,768]{1,0:T(8,128)(2,1)S(1)} %get-tuple-element.148), channel_id=1, source_target_pairs={{0,16},{4,20},{8,24},{12,28},{16,0},{20,4},{24,8},{28,12},{1,17},{... | collective-permute-start | bytes 589832 | tf_op jit(solution)/shard_map/ppermute | solution.py:1045
  98.1 10.0 %collective-permute-start.31 = (bf16[128,768]{1,0:T(8,128)(2,1)S(1)}, bf16[128,768]{1,0:T(8,128)(2,1)S(1)}, u32[]{:S(2)}, u32[]{:S(2)}) collective-permute-start(bf16[128,768]{1,0:T(8,128)(2,1)S(1)} %get-tuple-element.149), channel_id=1, source_target_pairs={{0,24},{4,28},{8,16},{12,20},{16,8},{20,12},{24,0},{28,4},{1,25},{... | collective-permute-start | bytes 589832 | tf_op jit(solution)/shard_map/ppermute | solution.py:1045
  99.7 23.5 %collective-permute-start.37 = (bf16[192,768]{1,0:T(8,128)(2,1)S(1)}, bf16[192,768]{1,0:T(8,128)(2,1)S(1)}, u32[]{:S(2)}, u32[]{:S(2)}) collective-permute-start(bf16[192,768]{1,0:T(8,128)(2,1)S(1)} %get-tuple-element.157), channel_id=1, source_target_pairs={{0,2},{1,3},{2,0},{3,1},{4,6},{5,7},{6,4},{7,5},{8,10},{9,11},{10,... | collective-permute-start | bytes 884744 | tf_op jit(solution)/shard_map/ppermute | solution.py:1050
  104.0 19.2 %collective-permute-start.38 = (bf16[192,768]{1,0:T(8,128)(2,1)S(1)}, bf16[192,768]{1,0:T(8,128)(2,1)S(1)}, u32[]{:S(2)}, u32[]{:S(2)}) collective-permute-start(bf16[192,768]{1,0:T(8,128)(2,1)S(1)} %get-tuple-element.158), channel_id=1, source_target_pairs={{0,3},{1,2},{2,1},{3,0},{4,7},{5,6},{6,5},{7,4},{8,11},{9,10},{10,... | collective-permute-start | bytes 884744 | tf_op jit(solution)/shard_map/ppermute | solution.py:1050
  108.4 14.9 %collective-permute-start.35 = (bf16[144,768]{1,0:T(8,128)(2,1)S(1)}, bf16[144,768]{1,0:T(8,128)(2,1)S(1)}, u32[]{:S(2)}, u32[]{:S(2)}) collective-permute-start(bf16[144,768]{1,0:T(8,128)(2,1)S(1)} %get-tuple-element.163.refs_0_), channel_id=1, source_target_pairs={{0,24},{4,28},{8,16},{12,20},{16,8},{20,12},{24,0},{28,4},{1,25},{... | collective-permute-start | bytes 663560 | tf_op jit(solution)/shard_map/ppermute | solution.py:1045
  110.1 13.3 %collective-permute-start.34 = (bf16[144,768]{1,0:T(8,128)(2,1)S(1)}, bf16[144,768]{1,0:T(8,128)(2,1)S(1)}, u32[]{:S(2)}, u32[]{:S(2)}) collective-permute-start(bf16[144,768]{1,0:T(8,128)(2,1)S(1)} %get-tuple-element.163.refs_0_), channel_id=1, source_target_pairs={{0,16},{4,20},{8,24},{12,28},{16,0},{20,4},{24,8},{28,12},{1,17},{... | collective-permute-start | bytes 663560 | tf_op jit(solution)/shard_map/ppermute | solution.py:1045
  110.7 12.6 %collective-permute-start.33 = (bf16[144,768]{1,0:T(8,128)(2,1)S(1)}, bf16[144,768]{1,0:T(8,128)(2,1)S(1)}, u32[]{:S(2)}, u32[]{:S(2)}) collective-permute-start(bf16[144,768]{1,0:T(8,128)(2,1)S(1)} %get-tuple-element.163.refs_0_), channel_id=1, source_target_pairs={{0,8},{4,12},{8,0},{12,4},{16,24},{20,28},{24,16},{28,20},{1,9},{5... | collective-permute-start | bytes 663560 | tf_op jit(solution)/shard_map/ppermute | solution.py:1045
  127.3 7.2 %collective-permute-start.40 = (bf16[1024,640]{1,0:T(8,128)(2,1)S(1)}, bf16[1024,640]{1,0:T(8,128)(2,1)S(1)}, u32[]{:S(2)}, u32[]{:S(2)}) collective-permute-start(bf16[1024,640]{1,0:T(8,128)(2,1)S(1)} %attend_back.1.mine), channel_id=1, source_target_pairs={{0,4},{4,0},{8,12},{12,8},{16,20},{20,16},{24,28},{28,24},{1,5},{5... | collective-permute-start | bytes 3932168 | tf_op jit(solution)/shard_map/ppermute | solution.py:1040
  127.7 15.0 %collective-permute-start.45 = (bf16[192,768]{1,0:T(8,128)(2,1)S(1)}, bf16[192,768]{1,0:T(8,128)(2,1)S(1)}, u32[]{:S(2)}, u32[]{:S(2)}) collective-permute-start(bf16[192,768]{1,0:T(8,128)(2,1)S(1)} %mlp_sum.1.refs_0_), channel_id=1, source_target_pairs={{0,16},{4,20},{8,24},{12,28},{16,0},{20,4},{24,8},{28,12},{1,17},{... | collective-permute-start | bytes 884744 | tf_op jit(solution)/shard_map/ppermute | solution.py:1045
  129.1 10.0 %collective-permute-start.53 = (bf16[2,64,768]{2,1,0:T(8,128)(2,1)S(1)}, bf16[2,64,768]{2,1,0:T(8,128)(2,1)S(1)}, u32[]{:S(2)}, u32[]{:S(2)}) collective-permute-start(bf16[2,64,768]{2,1,0:T(8,128)(2,1)S(1)} %get-tuple-element.185), channel_id=1, source_target_pairs={{0,1},{1,0},{2,3},{3,2},{4,5},{5,4},{6,7},{7,6},{8,9},{9,8},{10,11... | collective-permute-start | bytes 589832 | tf_op jit(solution)/shard_map/ppermute | solution.py:1050
  134.0 9.9 %collective-permute-start.44 = (bf16[192,768]{1,0:T(8,128)(2,1)S(1)}, bf16[192,768]{1,0:T(8,128)(2,1)S(1)}, u32[]{:S(2)}, u32[]{:S(2)}) collective-permute-start(bf16[192,768]{1,0:T(8,128)(2,1)S(1)} %mlp_sum.1.refs_0_), channel_id=1, source_target_pairs={{0,8},{4,12},{8,0},{12,4},{16,24},{20,28},{24,16},{28,20},{1,9},{5... | collective-permute-start | bytes 884744 | tf_op jit(solution)/shard_map/ppermute | solution.py:1045
  135.3 11.4 %collective-permute-start.41 = (bf16[128,768]{1,0:T(8,128)(2,1)S(1)}, bf16[128,768]{1,0:T(8,128)(2,1)S(1)}, u32[]{:S(2)}, u32[]{:S(2)}) collective-permute-start(bf16[128,768]{1,0:T(8,128)(2,1)S(1)} %get-tuple-element.174), channel_id=1, source_target_pairs={{0,8},{4,12},{8,0},{12,4},{16,24},{20,28},{24,16},{28,20},{1,9},{5... | collective-permute-start | bytes 589832 | tf_op jit(solution)/shard_map/ppermute | solution.py:1045
  138.5 9.8 %collective-permute-start.51 = (bf16[2,80,768]{2,1,0:T(8,128)(2,1)S(1)}, bf16[2,80,768]{2,1,0:T(8,128)(2,1)S(1)}, u32[]{:S(2)}, u32[]{:S(2)}) collective-permute-start(bf16[2,80,768]{2,1,0:T(8,128)(2,1)S(1)} %get-tuple-element.181), channel_id=1, source_target_pairs={{0,1},{1,0},{2,3},{3,2},{4,5},{5,4},{6,7},{7,6},{8,9},{9,8},{10,11... | collective-permute-start | bytes 737288 | tf_op jit(solution)/shard_map/ppermute | solution.py:1050
  139.2 7.5 %collective-permute-start.54 = (bf16[1,64,768]{2,1,0:T(8,128)(2,1)S(1)}, bf16[1,64,768]{2,1,0:T(8,128)(2,1)S(1)}, u32[]{:S(2)}, u32[]{:S(2)}) collective-permute-start(bf16[1,64,768]{2,1,0:T(8,128)(2,1)S(1)} %get-tuple-element.187), channel_id=1, source_target_pairs={{0,2},{1,3},{2,0},{3,1},{4,6},{5,7},{6,4},{7,5},{8,10},{9,11},{10,... | collective-permute-start | bytes 294920 | tf_op jit(solution)/shard_map/ppermute | solution.py:1050
  142.7 6.3 %collective-permute-start.42 = (bf16[128,768]{1,0:T(8,128)(2,1)S(1)}, bf16[128,768]{1,0:T(8,128)(2,1)S(1)}, u32[]{:S(2)}, u32[]{:S(2)}) collective-permute-start(bf16[128,768]{1,0:T(8,128)(2,1)S(1)} %get-tuple-element.175), channel_id=1, source_target_pairs={{0,16},{4,20},{8,24},{12,28},{16,0},{20,4},{24,8},{28,12},{1,17},{... | collective-permute-start | bytes 589832 | tf_op jit(solution)/shard_map/ppermute | solution.py:1045
  143.9 13.6 %collective-permute-start.47 = (bf16[192,768]{1,0:T(8,128)(2,1)S(1)}, bf16[192,768]{1,0:T(8,128)(2,1)S(1)}, u32[]{:S(2)}, u32[]{:S(2)}) collective-permute-start(bf16[192,768]{1,0:T(8,128)(2,1)S(1)} %mlp_sum.1.refs_0_), channel_id=1, source_target_pairs={{0,4},{4,0},{8,12},{12,8},{16,20},{20,16},{24,28},{28,24},{1,5},{5... | collective-permute-start | bytes 884744 | tf_op jit(solution)/shard_map/ppermute | solution.py:1040
  146.7 12.0 %collective-permute-start.49 = (bf16[192,768]{1,0:T(8,128)(2,1)S(1)}, bf16[192,768]{1,0:T(8,128)(2,1)S(1)}, u32[]{:S(2)}, u32[]{:S(2)}) collective-permute-start(bf16[192,768]{1,0:T(8,128)(2,1)S(1)} %collective-permute-done.45.refs_2_), channel_id=1, source_target_pairs={{0,4},{4,0},{8,12},{12,8},{16,20},{20,16},{24,28},{28,24},{1,5},{5... | collective-permute-start | bytes 884744 | tf_op jit(solution)/shard_map/ppermute | solution.py:1040
  146.7 8.3 %collective-permute-start.43 = (bf16[128,768]{1,0:T(8,128)(2,1)S(1)}, bf16[128,768]{1,0:T(8,128)(2,1)S(1)}, u32[]{:S(2)}, u32[]{:S(2)}) collective-permute-start(bf16[128,768]{1,0:T(8,128)(2,1)S(1)} %get-tuple-element.176), channel_id=1, source_target_pairs={{0,24},{4,28},{8,16},{12,20},{16,8},{20,12},{24,0},{28,4},{1,25},{... | collective-permute-start | bytes 589832 | tf_op jit(solution)/shard_map/ppermute | solution.py:1045
  148.3 17.8 %collective-permute-start.46 = (bf16[192,768]{1,0:T(8,128)(2,1)S(1)}, bf16[192,768]{1,0:T(8,128)(2,1)S(1)}, u32[]{:S(2)}, u32[]{:S(2)}) collective-permute-start(bf16[192,768]{1,0:T(8,128)(2,1)S(1)} %collective-permute-done.44.refs_1_), channel_id=1, source_target_pairs={{0,16},{4,20},{8,24},{12,28},{16,0},{20,4},{24,8},{28,12},{1,17},{... | collective-permute-start | bytes 884744 | tf_op jit(solution)/shard_map/ppermute | solution.py:1045
  149.0 6.9 %collective-permute-start.52 = (bf16[1,80,768]{2,1,0:T(8,128)(2,1)S(1)}, bf16[1,80,768]{2,1,0:T(8,128)(2,1)S(1)}, u32[]{:S(2)}, u32[]{:S(2)}) collective-permute-start(bf16[1,80,768]{2,1,0:T(8,128)(2,1)S(1)} %get-tuple-element.183), channel_id=1, source_target_pairs={{0,2},{1,3},{2,0},{3,1},{4,6},{5,7},{6,4},{7,5},{8,10},{9,11},{10,... | collective-permute-start | bytes 368648 | tf_op jit(solution)/shard_map/ppermute | solution.py:1050
  155.0 11.0 %collective-permute-start.48 = (bf16[192,768]{1,0:T(8,128)(2,1)S(1)}, bf16[192,768]{1,0:T(8,128)(2,1)S(1)}, u32[]{:S(2)}, u32[]{:S(2)}) collective-permute-start(bf16[192,768]{1,0:T(8,128)(2,1)S(1)} %collective-permute-done.44.refs_1_), channel_id=1, source_target_pairs={{0,4},{4,0},{8,12},{12,8},{16,20},{20,16},{24,28},{28,24},{1,5},{5... | collective-permute-start | bytes 884744 | tf_op jit(solution)/shard_map/ppermute | solution.py:1040
  155.9 10.6 %collective-permute-start.57 = (bf16[144,768]{1,0:T(8,128)(2,1)S(1)}, bf16[144,768]{1,0:T(8,128)(2,1)S(1)}, u32[]{:S(2)}, u32[]{:S(2)}) collective-permute-start(bf16[144,768]{1,0:T(8,128)(2,1)S(1)} %last_sum.1.refs_0_), channel_id=1, source_target_pairs={{0,24},{4,28},{8,16},{12,20},{16,8},{20,12},{24,0},{28,4},{1,25},{... | collective-permute-start | bytes 663560 | tf_op jit(solution)/shard_map/ppermute | solution.py:1045
  157.5 13.2 %collective-permute-start.56 = (bf16[144,768]{1,0:T(8,128)(2,1)S(1)}, bf16[144,768]{1,0:T(8,128)(2,1)S(1)}, u32[]{:S(2)}, u32[]{:S(2)}) collective-permute-start(bf16[144,768]{1,0:T(8,128)(2,1)S(1)} %last_sum.1.refs_0_), channel_id=1, source_target_pairs={{0,16},{4,20},{8,24},{12,28},{16,0},{20,4},{24,8},{28,12},{1,17},{... | collective-permute-start | bytes 663560 | tf_op jit(solution)/shard_map/ppermute | solution.py:1045
  158.7 12.0 %collective-permute-start.55 = (bf16[144,768]{1,0:T(8,128)(2,1)S(1)}, bf16[144,768]{1,0:T(8,128)(2,1)S(1)}, u32[]{:S(2)}, u32[]{:S(2)}) collective-permute-start(bf16[144,768]{1,0:T(8,128)(2,1)S(1)} %last_sum.1.refs_0_), channel_id=1, source_target_pairs={{0,8},{4,12},{8,0},{12,4},{16,24},{20,28},{24,16},{28,20},{1,9},{5... | collective-permute-start | bytes 663560 | tf_op jit(solution)/shard_map/ppermute | solution.py:1045
  166.0 9.1 %collective-permute-start.58 = (bf16[144,768]{1,0:T(8,128)(2,1)S(1)}, bf16[144,768]{1,0:T(8,128)(2,1)S(1)}, u32[]{:S(2)}, u32[]{:S(2)}) collective-permute-start(bf16[144,768]{1,0:T(8,128)(2,1)S(1)} %last_sum.1.refs_0_), channel_id=1, source_target_pairs={{0,4},{4,0},{8,12},{12,8},{16,20},{20,16},{24,28},{28,24},{1,5},{5... | collective-permute-start | bytes 663560 | tf_op jit(solution)/shard_map/ppermute | solution.py:1040
  166.5 8.6 %collective-permute-start.61 = (bf16[144,768]{1,0:T(8,128)(2,1)S(1)}, bf16[144,768]{1,0:T(8,128)(2,1)S(1)}, u32[]{:S(2)}, u32[]{:S(2)}) collective-permute-start(bf16[144,768]{1,0:T(8,128)(2,1)S(1)} %collective-permute-done.57.refs_3_), channel_id=1, source_target_pairs={{0,4},{4,0},{8,12},{12,8},{16,20},{20,16},{24,28},{28,24},{1,5},{5... | collective-permute-start | bytes 663560 | tf_op jit(solution)/shard_map/ppermute | solution.py:1040
  (18 other events, 113.9 us)

commit v5 on v4

--- a/solution.py
+++ b/solution.py
@@ -363,6 +363,7 @@
 FAR = pl.BlockSpec(memory_space=pltpu.HBM)
 SMEM = pl.BlockSpec(memory_space=pltpu.SMEM)
 VEC = 16
+STATS = 8
 SLAB = 64
 
 
@@ -729,8 +730,16 @@
 
 
 def seen(g, ref, j):
+    half = g.chips // 2
     return jnp.concatenate(
-        [ref[g.rows * (i ^ j) : g.rows * ((i ^ j) + 1)] for i in range(g.chips)], axis=0
+        [
+            ref[
+                g.rows * ((i ^ j) % half) : g.rows * ((i ^ j) % half + 1),
+                g.cols * ((i ^ j) // half) : g.cols * ((i ^ j) // half + 1),
+            ]
+            for i in range(g.chips)
+        ],
+        axis=0,
     )
 
 
@@ -809,8 +818,8 @@
     branch[0 : g.rows] = grad.astype(BF)
     one = jnp.sum(dy * z, axis=0, keepdims=True)
     two = jnp.sum(dy, axis=0, keepdims=True)
-    rest = jnp.zeros((VEC - 2, g.width), F32)
-    branch[g.rows : g.rows + VEC] = jnp.concatenate([one, two, rest], axis=0).astype(BF)
+    rest = jnp.zeros((STATS - 2, g.width), F32)
+    branch[g.rows : g.rows + STATS] = jnp.concatenate([one, two, rest], axis=0).astype(BF)
 
 
 def back_kernel(g, *refs):
@@ -845,9 +854,9 @@
     split_rows(g, sc, total, g.bhalf, own, other, g.half)
     total[...] = dot_tn(low[...], d_inner[...])
     split_rows(g, sc, total, g.half, own, other, 0)
-    stats = branches[0][g.rows : g.rows + VEC].astype(F32)
+    stats = branches[0][g.rows : g.rows + STATS].astype(F32)
     for j in range(1, c):
-        stats = stats + branches[j][g.rows : g.rows + VEC].astype(F32)
+        stats = stats + branches[j][g.rows : g.rows + STATS].astype(F32)
     down = jnp.sum(rows.astype(F32), axis=0, keepdims=True)
     up = jnp.sum(d_inner[...].astype(F32), axis=0, keepdims=True)
     sums[...] = jnp.concatenate([stats[0:2], down, up, jnp.zeros((4, g.width), F32)], axis=0)
@@ -866,8 +875,8 @@
     attended[0 : g.rows] = grad.astype(BF)
     one = jnp.sum(d_first * z, axis=0, keepdims=True)
     two = jnp.sum(d_first, axis=0, keepdims=True)
-    rest = jnp.zeros((VEC - 2, g.width), F32)
-    attended[g.rows : g.rows + VEC] = jnp.concatenate([one, two, rest], axis=0).astype(BF)
+    rest = jnp.zeros((STATS - 2, g.width), F32)
+    attended[g.rows : g.rows + STATS] = jnp.concatenate([one, two, rest], axis=0).astype(BF)
 
 
 def context_kernel(g, *refs):
@@ -885,11 +894,11 @@
     for j in range(c):
         q = jnp.bitwise_xor(p, j)
         total[pl.ds(pl.multiple_of(g.cols * q, 64), g.cols), :] = dot_tn(seen(g, ctxs[j], j), rows)
-    stats = grads[0][g.rows : g.rows + VEC].astype(F32)
+    stats = grads[0][g.rows : g.rows + STATS].astype(F32)
     for j in range(1, c):
-        stats = stats + grads[j][g.rows : g.rows + VEC].astype(F32)
+        stats = stats + grads[j][g.rows : g.rows + STATS].astype(F32)
     out = jnp.sum(rows.astype(F32), axis=0, keepdims=True)
-    rest = jnp.zeros((VEC - 7, g.width), F32)
+    rest = jnp.zeros((STATS - 7, g.width), F32)
     block = jnp.concatenate([sums[0:4], stats[0:2], out, rest], axis=0)
     size = g.shard // c
     for s in range(g.ring):
@@ -974,21 +983,35 @@
     return far if len(far) > 1 else [far[0].at[j] for j in range(g.chips)]
 
 
+def paired(g, sc, refs, body):
+    p, k = sc[0], sc[1]
+    mine, theirs = refs[: g.chips], others(g, refs)
+    for odd in range(2):
+
+        @pl.when(p & 1 == odd)
+        def _(odd=odd):
+            for j in range(0, g.chips, 2):
+                pair = jnp.bitwise_xor(over(p, 2), j // 2)
+                for found, core in ((mine, k), (theirs, 1 - k)):
+                    body(pair, core, found[j ^ odd], found[j ^ odd ^ 1])
+
+
 def mlp_final_kernel(g, sc, *refs):
     found, (g_in, g_down) = refs[:-2], refs[-2:]
-    for q, core, ref in sources(g, sc, found):
-        at = pl.multiple_of(g.block * q + g.bhalf * core, 8)
-        g_down[pl.ds(at, g.bhalf), :] = ref[g.half :, :].astype(F32)
+
+    def place(pair, core, even, odd):
         mine = pl.ds(pl.multiple_of(g.half * core, 8), g.half)
-        for chip in range(g.chips):
-
-            @pl.when(q == chip)
-            def _(chip=chip, ref=ref, mine=mine):
-                for r in range(g.ring):
-                    lane = g.hshard * r + g.block * chip
-                    g_in[mine, lane : lane + g.block] = ref[
-                        0 : g.half, g.block * r : g.block * (r + 1)
-                    ].astype(F32)
+        for i, ref in enumerate((even, odd)):
+            at = pl.multiple_of(g.block * (2 * pair + i) + g.bhalf * core, 8)
+            g_down[pl.ds(at, g.bhalf), :] = ref[g.half :, :].astype(F32)
+        for r in range(g.ring):
+            lane = pl.multiple_of(g.hshard * r + 2 * g.block * pair, 128)
+            lanes = slice(g.block * r, g.block * (r + 1))
+            g_in[mine, pl.ds(lane, 2 * g.block)] = jnp.concatenate(
+                [even[0 : g.half, lanes], odd[0 : g.half, lanes]], axis=1
+            ).astype(F32)
+
+    paired(g, sc, found, place)
 
 
 def last_kernel(g, sc, *refs):
@@ -1005,26 +1028,30 @@
             for dst, at in zip((g_bq, g_bv), (0, 2)):
                 dst[...] = row[:, g.cols * at : g.cols * (at + 1)].reshape(g.shard)
 
+    def place(pair, core, even, odd):
         base = pl.multiple_of(g.half * core, 8)
-        for chip in range(g.chips):
-
-            @pl.when(q == chip)
-            def _(chip=chip, ref=ref, base=base):
-                lane = g.cols * chip
-                for i, dst in enumerate((gq, gk, gv)):
-                    dst[pl.ds(base, g.packed), lane : lane + g.cols] = ref[
-                        0 : g.packed, g.cols * i : g.cols * (i + 1)
-                    ].astype(F32)
-                    dst[pl.ds(base + g.packed, step), lane : lane + g.cols] = ref[
-                        step * i : step * (i + 1), g.qkv :
-                    ].astype(F32)
-
+        lane = pl.ds(pl.multiple_of(2 * g.cols * pair, 128), 2 * g.cols)
+        for i, dst in enumerate((gq, gk, gv)):
+            for rows, at, lanes in (
+                (pl.ds(base, g.packed), slice(0, g.packed), slice(g.cols * i, g.cols * (i + 1))),
+                (
+                    pl.ds(base + g.packed, step),
+                    slice(step * i, step * (i + 1)),
+                    slice(g.qkv, g.width),
+                ),
+            ):
+                dst[rows, lane] = jnp.concatenate(
+                    [even[at, lanes], odd[at, lanes]], axis=1
+                ).astype(F32)
+
+    paired(g, sc, found, place)
+    far = others(g, found)
     for j in range(g.chips):
         q = jnp.bitwise_xor(p, j)
-        one, two = found[j], found[g.chips + j]
+        one, two = found[j], far[j]
         both = one[top:, :].astype(F32) + two[top:, :].astype(F32)
         g_out[pl.ds(pl.multiple_of(size * q, 8), size), :] = both[0:size]
-        back = pltpu.roll(both[size : size + VEC], lax.rem(g.width - g.shard * f, g.width), 1)
+        back = pltpu.roll(both[size : size + STATS], lax.rem(g.width - g.shard * f, g.width), 1)
         for chip in range(g.chips):
 
             @pl.when(q == chip)
@@ -1277,8 +1304,10 @@
         name="attend",
     )
     (ctx,) = mix(
-        lambda a, b: (a + b,),
-        [shaped((g.tokens, g.cols), BF)],
+        lambda a, b: (
+            jnp.concatenate([a[: g.tokens // 2] + b[: g.tokens // 2], a[g.tokens // 2 :] + b[g.tokens // 2 :]], axis=1),
+        ),
+        [shaped((g.tokens // 2, 2 * g.cols), BF)],
         ctx_own,
         to_core(ctx_other),
         name="join_context",
@@ -1328,7 +1357,7 @@
         [
             shaped((rows, width), BF),
             shaped((rows, width), F32),
-            shaped((rows + VEC, width), BF),
+            shaped((rows + STATS, width), BF),
         ],
         [VMEM] * (chips + 2),
         [*second, after(full, turned_x), out_grad.reshape(rows, width)],
@@ -1380,7 +1409,7 @@
     )
     d_sum, attended = call(
         bind(first_kernel, g),
-        [shaped((rows, width), F32), shaped((rows + VEC, width), BF)],
+        [shaped((rows, width), F32), shaped((rows + STATS, width), BF)],
         [VMEM] * (chips + 4),
         [*d_first, after(d_second, *m_away), z_own, s_own, full],
         name="norm_one",
@@ -1394,7 +1423,7 @@
         name="context_back",
     )
     d_ctx_other = to_core(d_ctx)
-    o_rows = g.shard // chips + VEC
+    o_rows = g.shard // chips + STATS
     o_own, o_away = call(
         bind(out_grads_kernel, g),
         [shaped((ring // 2, o_rows, width), F32), shaped((ring // 2, o_rows, width), BF)],

time: 180 us -> 176 us (0.978)
  waiting for transfers between devices: 74.8 us -> 70.2 us
    ppermute x27, waiting for transfers between devices: 43.1 us -> 38.7 us  [to_chip(): return lax.ppermute(x, 'ctx', [(i, i ^ 2 * j) for i in range(n)])]
  transfers between devices with their start and end apart: 62 -> 62, of which waited for: 30 -> 28; matrix products, arithmetic and copies ran while one was open for 0% -> 0% of each run, Pallas kernels for 13% -> 13%
where the time goes in v5:
time: 176 us; the launch traced here: 174 us
  waiting for transfers between devices  70.2 us (40%)
  starting transfers between devices  64.8 us (37%)
  Pallas kernels  37.6 us (21%)
    ppermute x27, waiting for transfers between devices, to_chip(): return lax.ppermute(x, 'ctx', [(i, i ^ 2 * j) for i in range(n)])  38.7 us
    pallas_call x27, Pallas kernels, call(): pl.pallas_call(kernel, out_shape=outs, in_specs=ins, out_specs=[VMEM] * l...  37.6 us
    ppermute x27, starting transfers between devices, to_chip(): return lax.ppermute(x, 'ctx', [(i, i ^ 2 * j) for i in range(n)])  33 us
    ppermute x13, starting transfers between devices, along(): return lax.ppermute(x, 'fsdp', [(i, i ^ mask) for i in range(n)])  28.3 us
    ppermute x13, waiting for transfers between devices, along(): return lax.ppermute(x, 'fsdp', [(i, i ^ mask) for i in range(n)])  23.7 us
    ppermute x22, waiting for transfers between devices, to_core(): return lax.ppermute(x, 'ctx', [(i, i ^ 1) for i in range(n)])  7.84 us
  transfers between devices with their start and end apart: 62, of which 28 were waited for; matrix products, arithmetic and copies ran while one was open for 0% of the time, Pallas kernels for 13%

profile of v5, /device:TPU:0, one launch (start us, length us, event | category | flops | bytes accessed | tf_op | source)
XLA Modules:
  0.0 173.9 jit_solution(15054158730799123866)
XLA Ops:
  0.7 2.0 %pick_weights.1 = (bf16[192,576]{1,0:T(8,128)(2,1)S(1)}, bf16[112,576]{1,0:T(8,128)(2,1)S(1)}, bf16[16,256]{1,0:T(8,128)(2,1)S(1)}) custom-call(s32[3]{0:T(128)S(1)} %pad_add_fusion.sc, bf16[192,768]{1,0:T(8,128)(2,1)} %refs_0_.1, bf16[192,768]{1,0:T(8,128)(2,1)} %refs_1_.1, bf16[192,768]{1,0:T(8,128)(2,1)} %refs_2_.1, bf16[192]{0:T(256)(128)(2,1)} %refs_3_.1, ...), custom_call_target="tpu_custom_call" | custom-call | flops 1 | bytes 1 | tf_op jit(solution)/shard_map/pick_weights/pallas_call | solution.py:382
  2.8 3.0 %collective-permute-start = (bf16[128,768]{1,0:T(8,128)(2,1)}, bf16[128,768]{1,0:T(8,128)(2,1)S(1)}, u32[]{:S(2)}, u32[]{:S(2)}) collective-permute-start(bf16[128,768]{1,0:T(8,128)(2,1)} %bitcast.10), channel_id=1, source_target_pairs={{0,8},{4,12},{8,0},{12,4},{16,24},{20,28},{24,16},{28,20},{1,9},{5... | collective-permute-start | bytes 589832 | tf_op jit(solution)/shard_map/ppermute | solution.py:1072
  5.8 2.6 %collective-permute-start.8 = (bf16[112,576]{1,0:T(8,128)(2,1)S(1)}, bf16[112,576]{1,0:T(8,128)(2,1)S(1)}, u32[]{:S(2)}, u32[]{:S(2)}) collective-permute-start(bf16[112,576]{1,0:T(8,128)(2,1)S(1)} %get-tuple-element.110._), channel_id=1, source_target_pairs={{0,2},{1,3},{2,0},{3,1},{4,6},{5,7},{6,4},{7,5},{8,10},{9,11},{10,... | collective-permute-start | bytes 387080 | tf_op jit(solution)/shard_map/ppermute | solution.py:1077
  8.4 1.6 collective-permute-start.7
  10.0 1.5 collective-permute-start.2
  11.9 2.0 %prepare_weights.1 = (bf16[192,768]{1,0:T(8,128)(2,1)S(1)}, bf16[192,768]{1,0:T(8,128)(2,1)S(1)}, bf16[192,768]{1,0:T(8,128)(2,1)S(1)}, bf16[288,768]{1,0:T(8,128)(2,1)S(1)}) custom-call(s32[3]{0:T(128)S(1)} %pad_add_fusion.sc, bf16[112,576]{1,0:T(8,128)(2,1)S(1)} %get-tuple-element.110._, bf16[192,3072]{1,0:T(8,128)(2,1)} %wi.1, bf16[768,768]{1,0:T(8,128)(2,1)} %wd.1, ...), custom_call_target="tpu_custom_call" | custom-call | flops 1 | bytes 1 | tf_op jit(solution)/shard_map/prepare_weights/pallas_call | solution.py:382
  16.7 2.4 %collective-permute-start.18 = (bf16[288,768]{1,0:T(8,128)(2,1)S(1)}, bf16[288,768]{1,0:T(8,128)(2,1)S(1)}, u32[]{:S(2)}, u32[]{:S(2)}) collective-permute-start(bf16[288,768]{1,0:T(8,128)(2,1)S(1)} %get-tuple-element.114), channel_id=1, source_target_pairs={{0,2},{1,3},{2,0},{3,1},{4,6},{5,7},{6,4},{7,5},{8,10},{9,11},{10,... | collective-permute-start | bytes 1327112 | tf_op jit(solution)/shard_map/ppermute | solution.py:1077
  23.2 4.9 %cluster_tables.1 = (bf16[3,512,128]{2,1,0:T(8,128)(2,1)S(1)}, bf16[3,1024,64]{2,1,0:T(8,128)(2,1)S(1)}, bf16[8,1024]{1,0:T(8,128)(2,1)S(1)}) custom-call(s32[3]{0:T(128)S(1)} %pad_add_fusion.sc, bf16[112,576]{1,0:T(8,128)(2,1)S(1)} %collective-permute-done.7.refs_10_._, s32[12,1024]{1,0:T(8,128)S(1)} %bitcast.17, s32[1,1024]{1,0:T(1,128)S(1)} %copy-done.2), custom_call_target="tpu_custom_call" | custom-call | flops 1 | bytes 1 | tf_op jit(solution)/shard_map/cluster_tables/pallas_call | solution.py:382
  29.1 2.1 %project.1 = (bf16[1024,768]{1,0:T(8,128)(2,1)S(1)}, bf16[768,576]{1,0:T(8,128)(2,1)S(1)}, f32[16,768]{1,0:T(8,128)S(1)}) custom-call(s32[3]{0:T(128)S(1)} %pad_add_fusion.sc, bf16[128,768]{1,0:T(8,128)(2,1)S(1)} %bitcast.14, bf16[128,768]{1,0:T(8,128)(2,1)S(1)} %collective-permute-done.refs_1_.refs_5_, ...), custom_call_target="tpu_custom_call" | custom-call | flops 1 | bytes 1 | tf_op jit(solution)/shard_map/project/pallas_call | solution.py:382
  32.6 7.1 %collective-permute-done.18.refs_13_ = bf16[288,768]{1,0:T(8,128)(2,1)S(1)} collective-permute-done((bf16[288,768]{1,0:T(8,128)(2,1)S(1)}, bf16[288,768]{1,0:T(8,128)(2,1)S(1)}, u32[]{:S(2)}, u32[]{:S(2)}) %collective-permute-start.18) | collective-permute-done | bytes 442400 | tf_op jit(solution)/shard_map/ppermute | solution.py:1077
  39.7 1.5 collective-permute-start.19
  41.2 1.5 collective-permute-done.13.refs_1_
  42.8 1.5 collective-permute-start.16
  44.9 1.5 collective-permute-start.14
  46.4 5.2 %collective-permute-done.16.refs_3_.refs_7_ = bf16[256,384]{1,0:T(8,128)(2,1)S(1)} collective-permute-done((bf16[256,384]{1,0:T(8,128)(2,1)S(1)}, bf16[256,384]{1,0:T(8,128)(2,1)S(1)}, u32[]{:S(2)}, u32[]{:S(2)}) %collective-permute-start.16) | collective-permute-done | bytes 196640 | tf_op jit(solution)/shard_map/ppermute | solution.py:1072
  51.6 3.4 %collective-permute-done.15.refs_2_.refs_6_ = bf16[256,384]{1,0:T(8,128)(2,1)S(1)} collective-permute-done((bf16[256,384]{1,0:T(8,128)(2,1)S(1)}, bf16[256,384]{1,0:T(8,128)(2,1)S(1)}, u32[]{:S(2)}, u32[]{:S(2)}) %collective-permute-start.15) | collective-permute-done | bytes 196640 | tf_op jit(solution)/shard_map/ppermute | solution.py:1072
  58.1 3.2 %mlp_forward.1 = (f32[128,768]{1,0:T(8,128)S(1)}, bf16[128,768]{1,0:T(8,128)(2,1)S(1)}, bf16[128,768]{1,0:T(8,128)(2,1)S(1)}, bf16[128,768]{1,0:T(8,128)(2,1)S(1...) custom-call(s32[3]{0:T(128)S(1)} %pad_add_fusion.sc, ...), custom_call_target="tpu_custom_call" | custom-call | flops 1 | bytes 1 | tf_op jit(solution)/shard_map/mlp_forward/pallas_call | solution.py:382
  63.4 1.6 collective-permute-start.25
  64.9 1.4 turn_rows.1.turned_x
  66.4 2.8 %collective-permute-done.23.refs_1_ = bf16[128,768]{1,0:T(8,128)(2,1)S(1)} collective-permute-done((bf16[128,768]{1,0:T(8,128)(2,1)S(1)}, bf16[128,768]{1,0:T(8,128)(2,1)S(1)}, u32[]{:S(2)}, u32[]{:S(2)}) %collective-permute-start.23) | collective-permute-done | bytes 196640 | tf_op jit(solution)/shard_map/ppermute | solution.py:1072
  69.4 3.4 %collective-permute-done.25.refs_3_ = bf16[128,768]{1,0:T(8,128)(2,1)S(1)} collective-permute-done((bf16[128,768]{1,0:T(8,128)(2,1)S(1)}, bf16[128,768]{1,0:T(8,128)(2,1)S(1)}, u32[]{:S(2)}, u32[]{:S(2)}) %collective-permute-start.25) | collective-permute-done | bytes 196640 | tf_op jit(solution)/shard_map/ppermute | solution.py:1072
  73.8 1.7 collective-permute-start.28
  77.9 5.0 %collective-permute-done.28.refs_3_ = bf16[136,768]{1,0:T(8,128)(2,1)S(1)} collective-permute-done((bf16[136,768]{1,0:T(8,128)(2,1)S(1)}, bf16[136,768]{1,0:T(8,128)(2,1)S(1)}, u32[]{:S(2)}, u32[]{:S(2)}) %collective-permute-start.28) | collective-permute-done | bytes 208928 | tf_op jit(solution)/shard_map/ppermute | solution.py:1072
  82.8 2.7 %collective-permute-done.27.refs_2_ = bf16[136,768]{1,0:T(8,128)(2,1)S(1)} collective-permute-done((bf16[136,768]{1,0:T(8,128)(2,1)S(1)}, bf16[136,768]{1,0:T(8,128)(2,1)S(1)}, u32[]{:S(2)}, u32[]{:S(2)}) %collective-permute-start.27) | collective-permute-done | bytes 208928 | tf_op jit(solution)/shard_map/ppermute | solution.py:1072
  85.5 1.6 mlp_back.1
  87.1 2.3 %mlp_grads.1 = (f32[4,192,768]{2,1,0:T(8,128)S(1)}, bf16[4,192,768]{2,1,0:T(8,128)(2,1)S(1)}, f32[8,768]{1,0:T(8,128)S(1)}) custom-call(s32[3]{0:T(128)S(1)} %pad_add_fusion.sc, bf16[136,768]{1,0:T(8,128)(2,1)S(1)} %get-tuple-element.143.refs_0_, bf16[136,768]{1,0:T(8,128)(2,1)S(1)} %collective-permute-done.26.refs_1_, ...), custom_call_target="tpu_custom_call" | custom-call | flops 1 | bytes 1 | tf_op jit(solution)/shard_map/mlp_grads/pallas_call | solution.py:382
  89.4 2.8 %collective-permute-done.32.refs_1_ = bf16[4,192,768]{2,1,0:T(8,128)(2,1)S(1)} collective-permute-done((bf16[4,192,768]{2,1,0:T(8,128)(2,1)S(1)}, bf16[4,192,768]{2,1,0:T(8,128)(2,1)S(1)}, u32[]{:S(2)}, u32[]{:S(2)}) %collective-permute-start.32) | collective-permute-done | bytes 1179680 | tf_op jit(solution)/shard_map/ppermute | solution.py:1067
  94.9 1.6 collective-permute-start.31
  96.5 2.3 %collective-permute-start.37 = (bf16[192,768]{1,0:T(8,128)(2,1)S(1)}, bf16[192,768]{1,0:T(8,128)(2,1)S(1)}, u32[]{:S(2)}, u32[]{:S(2)}) collective-permute-start(bf16[192,768]{1,0:T(8,128)(2,1)S(1)} %get-tuple-element.157), channel_id=1, source_target_pairs={{0,2},{1,3},{2,0},{3,1},{4,6},{5,7},{6,4},{7,5},{8,10},{9,11},{10,... | collective-permute-start | bytes 884744 | tf_op jit(solution)/shard_map/ppermute | solution.py:1077
  98.8 2.0 %collective-permute-done.29.refs_1_ = bf16[128,768]{1,0:T(8,128)(2,1)S(1)} collective-permute-done((bf16[128,768]{1,0:T(8,128)(2,1)S(1)}, bf16[128,768]{1,0:T(8,128)(2,1)S(1)}, u32[]{:S(2)}, u32[]{:S(2)}) %collective-permute-start.29) | collective-permute-done | bytes 196640 | tf_op jit(solution)/shard_map/ppermute | solution.py:1072
  100.8 3.4 %collective-permute-start.38 = (bf16[192,768]{1,0:T(8,128)(2,1)S(1)}, bf16[192,768]{1,0:T(8,128)(2,1)S(1)}, u32[]{:S(2)}, u32[]{:S(2)}) collective-permute-start(bf16[192,768]{1,0:T(8,128)(2,1)S(1)} %get-tuple-element.158), channel_id=1, source_target_pairs={{0,3},{1,2},{2,1},{3,0},{4,7},{5,6},{6,5},{7,4},{8,11},{9,10},{10,... | collective-permute-start | bytes 884744 | tf_op jit(solution)/shard_map/ppermute | solution.py:1077
  105.2 1.6 collective-permute-start.35
  108.8 11.2 %collective-permute-done.37.refs_2_ = bf16[192,768]{1,0:T(8,128)(2,1)S(1)} collective-permute-done((bf16[192,768]{1,0:T(8,128)(2,1)S(1)}, bf16[192,768]{1,0:T(8,128)(2,1)S(1)}, u32[]{:S(2)}, u32[]{:S(2)}) %collective-permute-start.37) | collective-permute-done | bytes 294944 | tf_op jit(solution)/shard_map/ppermute | solution.py:1077
  120.7 1.9 %out_grads.1 = (f32[2,56,768]{2,1,0:T(8,128)S(1)}, bf16[2,56,768]{2,1,0:T(8,128)(2,1)S(1)}) custom-call(s32[3]{0:T(128)S(1)} %pad_add_fusion.sc, bf16[136,768]{1,0:T(8,128)(2,1)S(1)} %get-tuple-element.163.refs_0_, bf16[136,768]{1,0:T(8,128)(2,1)S(1)} %collective-permute-done.33.refs_1_, bf16[136,768]{1,0:T(8,128)(2,1)S(1)} %collective-permute-done.34.refs_2_, ...), custom_call_target="tpu_custom_call" | custom-call | flops 1 | bytes 1 | tf_op jit(solution)/shard_map/out_grads/pallas_call | solution.py:382
  122.6 1.9 %attend_back.1.mine = bf16[1024,640]{1,0:T(8,128)(2,1)S(1)} custom-call(bf16[512,192]{1,0:T(8,128)(2,1)S(1)} %context_back.1.own, bf16[512,192]{1,0:T(8,128)(2,1)S(1)} %collective-permute-done.39.other, bf16[3,512,128]{2,1,0:T(8,128)(2,1)S(1)} %get-tuple-element.122.pick, bf16[3,1024,64]{2,1,0:T(8,128)(2,1)S(1)} %get-tuple-element.123.place, ...), custom_call_target="tpu_custom_call" | custom-call | flops 1 | bytes 1 | tf_op jit(solution)/shard_map/attend_back/pallas_call | solution.py:382
  126.9 4.9 %collective-permute-start.53 = (bf16[2,56,768]{2,1,0:T(8,128)(2,1)S(1)}, bf16[2,56,768]{2,1,0:T(8,128)(2,1)S(1)}, u32[]{:S(2)}, u32[]{:S(2)}) collective-permute-start(bf16[2,56,768]{2,1,0:T(8,128)(2,1)S(1)} %get-tuple-element.185), channel_id=1, source_target_pairs={{0,1},{1,0},{2,3},{3,2},{4,5},{5,4},{6,7},{7,6},{8,9},{9,8},{10,11... | collective-permute-start | bytes 516104 | tf_op jit(solution)/shard_map/ppermute | solution.py:1077
  132.6 1.6 collective-permute-start.41
  134.2 1.6 project_grads.1
  136.5 3.5 %collective-permute-start.54 = (bf16[1,56,768]{2,1,0:T(8,128)(2,1)S(1)}, bf16[1,56,768]{2,1,0:T(8,128)(2,1)S(1)}, u32[]{:S(2)}, u32[]{:S(2)}) collective-permute-start(bf16[1,56,768]{2,1,0:T(8,128)(2,1)S(1)} %get-tuple-element.187), channel_id=1, source_target_pairs={{0,2},{1,3},{2,0},{3,1},{4,6},{5,7},{6,4},{7,5},{8,10},{9,11},{10,... | collective-permute-start | bytes 258056 | tf_op jit(solution)/shard_map/ppermute | solution.py:1077
  141.0 2.7 %collective-permute-done.54.refs_3_ = bf16[1,56,768]{2,1,0:T(8,128)(2,1)S(1)} collective-permute-done((bf16[1,56,768]{2,1,0:T(8,128)(2,1)S(1)}, bf16[1,56,768]{2,1,0:T(8,128)(2,1)S(1)}, u32[]{:S(2)}, u32[]{:S(2)}) %collective-permute-start.54) | collective-permute-done | bytes 86048 | tf_op jit(solution)/shard_map/ppermute | solution.py:1077
  143.7 1.6 collective-permute-start.43
  146.0 3.4 %collective-permute-start.52 = (bf16[1,80,768]{2,1,0:T(8,128)(2,1)S(1)}, bf16[1,80,768]{2,1,0:T(8,128)(2,1)S(1)}, u32[]{:S(2)}, u32[]{:S(2)}) collective-permute-start(bf16[1,80,768]{2,1,0:T(8,128)(2,1)S(1)} %get-tuple-element.183), channel_id=1, source_target_pairs={{0,2},{1,3},{2,0},{3,1},{4,6},{5,7},{6,4},{7,5},{8,10},{9,11},{10,... | collective-permute-start | bytes 368648 | tf_op jit(solution)/shard_map/ppermute | solution.py:1077
  149.5 2.5 %collective-permute-done.43.refs_4_ = bf16[128,768]{1,0:T(8,128)(2,1)S(1)} collective-permute-done((bf16[128,768]{1,0:T(8,128)(2,1)S(1)}, bf16[128,768]{1,0:T(8,128)(2,1)S(1)}, u32[]{:S(2)}, u32[]{:S(2)}) %collective-permute-start.43) | collective-permute-done | bytes 196640 | tf_op jit(solution)/shard_map/ppermute | solution.py:1072
  153.0 1.6 collective-permute-start.57
  156.5 6.2 %collective-permute-done.46.refs_3_ = bf16[192,768]{1,0:T(8,128)(2,1)S(1)} collective-permute-done((bf16[192,768]{1,0:T(8,128)(2,1)S(1)}, bf16[192,768]{1,0:T(8,128)(2,1)S(1)}, u32[]{:S(2)}, u32[]{:S(2)}) %collective-permute-start.46) | collective-permute-done | bytes 294944 | tf_op jit(solution)/shard_map/ppermute | solution.py:1072
  163.4 3.8 %collective-permute-done.56.refs_2_ = bf16[136,768]{1,0:T(8,128)(2,1)S(1)} collective-permute-done((bf16[136,768]{1,0:T(8,128)(2,1)S(1)}, bf16[136,768]{1,0:T(8,128)(2,1)S(1)}, u32[]{:S(2)}, u32[]{:S(2)}) %collective-permute-start.56) | collective-permute-done | bytes 208928 | tf_op jit(solution)/shard_map/ppermute | solution.py:1072
  167.7 3.2 %mlp_lay.1 = (f32[192,3072]{1,0:T(8,128)}, f32[768,768]{1,0:T(8,128)}) custom-call(s32[3]{0:T(128)S(1)} %pad_add_fusion.sc, bf16[192,768]{1,0:T(8,128)(2,1)S(1)} %mlp_sum.1.refs_0_, bf16[192,768]{1,0:T(8,128)(2,1)S(1)} %collective-permute-done.44.refs_1_, bf16[192,768]{1,0:T(8,128)(2,1)S(1)} %collective-permute-done.45.refs_2_, ...), custom_call_target="tpu_custom_call" | custom-call | flops 1 | bytes 1 | tf_op jit(solution)/shard_map/mlp_lay/pallas_call | solution.py:382
  170.9 2.8 %last_lay.1 = (f32[192,768]{1,0:T(8,128)}, f32[192,768]{1,0:T(8,128)}, f32[192,768]{1,0:T(8,128)}, f32[192]{0:T(256)}, f32[192]{0:T(256)}, /*index=5*/f32[192,76...) custom-call(s32[3]{0:T(128)S(1)} %pad_add_fusion.sc, ...), custom_call_target="tpu_custom_call" | custom-call | flops 1 | bytes 1 | tf_op jit(solution)/shard_map/last_lay/pallas_call | solution.py:382
  (113 shorter events, 35.1 us)
Async XLA Ops:
  2.8 13.9 %collective-permute-start = (bf16[128,768]{1,0:T(8,128)(2,1)}, bf16[128,768]{1,0:T(8,128)(2,1)S(1)}, u32[]{:S(2)}, u32[]{:S(2)}) collective-permute-start(bf16[128,768]{1,0:T(8,128)(2,1)} %bitcast.10), channel_id=1, source_target_pairs={{0,8},{4,12},{8,0},{12,4},{16,24},{20,28},{24,16},{28,20},{1,9},{5... | collective-permute-start | bytes 589832 | tf_op jit(solution)/shard_map/ppermute | solution.py:1072
  5.8 9.3 %collective-permute-start.8 = (bf16[112,576]{1,0:T(8,128)(2,1)S(1)}, bf16[112,576]{1,0:T(8,128)(2,1)S(1)}, u32[]{:S(2)}, u32[]{:S(2)}) collective-permute-start(bf16[112,576]{1,0:T(8,128)(2,1)S(1)} %get-tuple-element.110._), channel_id=1, source_target_pairs={{0,2},{1,3},{2,0},{3,1},{4,6},{5,7},{6,4},{7,5},{8,10},{9,11},{10,... | collective-permute-start | bytes 387080 | tf_op jit(solution)/shard_map/ppermute | solution.py:1077
  8.4 6.9 %collective-permute-start.7 = (bf16[112,576]{1,0:T(8,128)(2,1)S(1)}, bf16[112,576]{1,0:T(8,128)(2,1)S(1)}, u32[]{:S(2)}, u32[]{:S(2)}) collective-permute-start(bf16[112,576]{1,0:T(8,128)(2,1)S(1)} %get-tuple-element.110._), channel_id=1, source_target_pairs={{0,1},{1,0},{2,3},{3,2},{4,5},{5,4},{6,7},{7,6},{8,9},{9,8},{10,11... | collective-permute-start | bytes 387080 | tf_op jit(solution)/shard_map/ppermute | solution.py:1077
  10.0 9.1 %collective-permute-start.2 = (bf16[128,768]{1,0:T(8,128)(2,1)}, bf16[128,768]{1,0:T(8,128)(2,1)S(1)}, u32[]{:S(2)}, u32[]{:S(2)}) collective-permute-start(bf16[128,768]{1,0:T(8,128)(2,1)} %bitcast.11), channel_id=1, source_target_pairs={{0,24},{4,28},{8,16},{12,20},{16,8},{20,12},{24,0},{28,4},{1,25},{... | collective-permute-start | bytes 589832 | tf_op jit(solution)/shard_map/ppermute | solution.py:1072
  11.4 9.7 %collective-permute-start.1 = (bf16[128,768]{1,0:T(8,128)(2,1)}, bf16[128,768]{1,0:T(8,128)(2,1)S(1)}, u32[]{:S(2)}, u32[]{:S(2)}) collective-permute-start(bf16[128,768]{1,0:T(8,128)(2,1)} %bitcast.12), channel_id=1, source_target_pairs={{0,16},{4,20},{8,24},{12,28},{16,0},{20,4},{24,8},{28,12},{1,17},{... | collective-permute-start | bytes 589832 | tf_op jit(solution)/shard_map/ppermute | solution.py:1072
  16.7 23.0 %collective-permute-start.18 = (bf16[288,768]{1,0:T(8,128)(2,1)S(1)}, bf16[288,768]{1,0:T(8,128)(2,1)S(1)}, u32[]{:S(2)}, u32[]{:S(2)}) collective-permute-start(bf16[288,768]{1,0:T(8,128)(2,1)S(1)} %get-tuple-element.114), channel_id=1, source_target_pairs={{0,2},{1,3},{2,0},{3,1},{4,6},{5,7},{6,4},{7,5},{8,10},{9,11},{10,... | collective-permute-start | bytes 1327112 | tf_op jit(solution)/shard_map/ppermute | solution.py:1077
  19.1 20.6 %collective-permute-start.17 = (bf16[288,768]{1,0:T(8,128)(2,1)S(1)}, bf16[288,768]{1,0:T(8,128)(2,1)S(1)}, u32[]{:S(2)}, u32[]{:S(2)}) collective-permute-start(bf16[288,768]{1,0:T(8,128)(2,1)S(1)} %get-tuple-element.114), channel_id=1, source_target_pairs={{0,1},{1,0},{2,3},{3,2},{4,5},{5,4},{6,7},{7,6},{8,9},{9,8},{10,11... | collective-permute-start | bytes 1327112 | tf_op jit(solution)/shard_map/ppermute | solution.py:1077
  22.5 6.6 %collective-permute-start.3 = (bf16[128,768]{1,0:T(8,128)(2,1)S(1)}, bf16[128,768]{1,0:T(8,128)(2,1)S(1)}, u32[]{:S(2)}, u32[]{:S(2)}) collective-permute-start(bf16[128,768]{1,0:T(8,128)(2,1)S(1)} %bitcast.13), channel_id=1, source_target_pairs={{0,4},{4,0},{8,12},{12,8},{16,20},{20,16},{24,28},{28,24},{1,5},{5... | collective-permute-start | bytes 589832 | tf_op jit(solution)/shard_map/ppermute | solution.py:1067
  22.7 6.4 %collective-permute-start.5 = (bf16[128,768]{1,0:T(8,128)(2,1)S(1)}, bf16[128,768]{1,0:T(8,128)(2,1)S(1)}, u32[]{:S(2)}, u32[]{:S(2)}) collective-permute-start(bf16[128,768]{1,0:T(8,128)(2,1)S(1)} %collective-permute-done.1.refs_2_.refs_6_), channel_id=1, source_target_pairs={{0,4},{4,0},{8,12},{12,8},{16,20},{20,16},{24,28},{28,24},{1,5},{5... | collective-permute-start | bytes 589832 | tf_op jit(solution)/shard_map/ppermute | solution.py:1067
  23.0 6.1 %collective-permute-start.4 = (bf16[128,768]{1,0:T(8,128)(2,1)S(1)}, bf16[128,768]{1,0:T(8,128)(2,1)S(1)}, u32[]{:S(2)}, u32[]{:S(2)}) collective-permute-start(bf16[128,768]{1,0:T(8,128)(2,1)S(1)} %collective-permute-done.refs_1_.refs_5_), channel_id=1, source_target_pairs={{0,4},{4,0},{8,12},{12,8},{16,20},{20,16},{24,28},{28,24},{1,5},{5... | collective-permute-start | bytes 589832 | tf_op jit(solution)/shard_map/ppermute | solution.py:1067
  39.7 15.9 %collective-permute-start.19 = (bf16[288,768]{1,0:T(8,128)(2,1)S(1)}, bf16[288,768]{1,0:T(8,128)(2,1)S(1)}, u32[]{:S(2)}, u32[]{:S(2)}) collective-permute-start(bf16[288,768]{1,0:T(8,128)(2,1)S(1)} %collective-permute-done.18.refs_13_), channel_id=1, source_target_pairs={{0,1},{1,0},{2,3},{3,2},{4,5},{5,4},{6,7},{7,6},{8,9},{9,8},{10,11... | collective-permute-start | bytes 1327112 | tf_op jit(solution)/shard_map/ppermute | solution.py:1077
  42.8 8.8 %collective-permute-start.16 = (bf16[256,384]{1,0:T(8,128)(2,1)S(1)}, bf16[256,384]{1,0:T(8,128)(2,1)S(1)}, u32[]{:S(2)}, u32[]{:S(2)}) collective-permute-start(bf16[256,384]{1,0:T(8,128)(2,1)S(1)} %join_context.1.refs_0_.refs_4_), channel_id=1, source_target_pairs={{0,24},{4,28},{8,16},{12,20},{16,8},{20,12},{24,0},{28,4},{1,25},{... | collective-permute-start | bytes 589832 | tf_op jit(solution)/shard_map/ppermute | solution.py:1072
  44.4 10.6 %collective-permute-start.15 = (bf16[256,384]{1,0:T(8,128)(2,1)S(1)}, bf16[256,384]{1,0:T(8,128)(2,1)S(1)}, u32[]{:S(2)}, u32[]{:S(2)}) collective-permute-start(bf16[256,384]{1,0:T(8,128)(2,1)S(1)} %join_context.1.refs_0_.refs_4_), channel_id=1, source_target_pairs={{0,16},{4,20},{8,24},{12,28},{16,0},{20,4},{24,8},{28,12},{1,17},{... | collective-permute-start | bytes 589832 | tf_op jit(solution)/shard_map/ppermute | solution.py:1072
  44.9 10.2 %collective-permute-start.14 = (bf16[256,384]{1,0:T(8,128)(2,1)S(1)}, bf16[256,384]{1,0:T(8,128)(2,1)S(1)}, u32[]{:S(2)}, u32[]{:S(2)}) collective-permute-start(bf16[256,384]{1,0:T(8,128)(2,1)S(1)} %join_context.1.refs_0_.refs_4_), channel_id=1, source_target_pairs={{0,8},{4,12},{8,0},{12,4},{16,24},{20,28},{24,16},{28,20},{1,9},{5... | collective-permute-start | bytes 589832 | tf_op jit(solution)/shard_map/ppermute | solution.py:1072
  61.4 7.8 %collective-permute-start.23 = (bf16[128,768]{1,0:T(8,128)(2,1)S(1)}, bf16[128,768]{1,0:T(8,128)(2,1)S(1)}, u32[]{:S(2)}, u32[]{:S(2)}) collective-permute-start(bf16[128,768]{1,0:T(8,128)(2,1)S(1)} %get-tuple-element.136), channel_id=1, source_target_pairs={{0,8},{4,12},{8,0},{12,4},{16,24},{20,28},{24,16},{28,20},{1,9},{5... | collective-permute-start | bytes 589832 | tf_op jit(solution)/shard_map/ppermute | solution.py:1072
  61.9 7.5 %collective-permute-start.24 = (bf16[128,768]{1,0:T(8,128)(2,1)S(1)}, bf16[128,768]{1,0:T(8,128)(2,1)S(1)}, u32[]{:S(2)}, u32[]{:S(2)}) collective-permute-start(bf16[128,768]{1,0:T(8,128)(2,1)S(1)} %get-tuple-element.137), channel_id=1, source_target_pairs={{0,16},{4,20},{8,24},{12,28},{16,0},{20,4},{24,8},{28,12},{1,17},{... | collective-permute-start | bytes 589832 | tf_op jit(solution)/shard_map/ppermute | solution.py:1072
  63.4 9.5 %collective-permute-start.25 = (bf16[128,768]{1,0:T(8,128)(2,1)S(1)}, bf16[128,768]{1,0:T(8,128)(2,1)S(1)}, u32[]{:S(2)}, u32[]{:S(2)}) collective-permute-start(bf16[128,768]{1,0:T(8,128)(2,1)S(1)} %get-tuple-element.138), channel_id=1, source_target_pairs={{0,24},{4,28},{8,16},{12,20},{16,8},{20,12},{24,0},{28,4},{1,25},{... | collective-permute-start | bytes 589832 | tf_op jit(solution)/shard_map/ppermute | solution.py:1072
  73.8 9.0 %collective-permute-start.28 = (bf16[136,768]{1,0:T(8,128)(2,1)S(1)}, bf16[136,768]{1,0:T(8,128)(2,1)S(1)}, u32[]{:S(2)}, u32[]{:S(2)}) collective-permute-start(bf16[136,768]{1,0:T(8,128)(2,1)S(1)} %get-tuple-element.143.refs_0_), channel_id=1, source_target_pairs={{0,24},{4,28},{8,16},{12,20},{16,8},{20,12},{24,0},{28,4},{1,25},{... | collective-permute-start | bytes 626696 | tf_op jit(solution)/shard_map/ppermute | solution.py:1072
  75.5 10.0 %collective-permute-start.27 = (bf16[136,768]{1,0:T(8,128)(2,1)S(1)}, bf16[136,768]{1,0:T(8,128)(2,1)S(1)}, u32[]{:S(2)}, u32[]{:S(2)}) collective-permute-start(bf16[136,768]{1,0:T(8,128)(2,1)S(1)} %get-tuple-element.143.refs_0_), channel_id=1, source_target_pairs={{0,16},{4,20},{8,24},{12,28},{16,0},{20,4},{24,8},{28,12},{1,17},{... | collective-permute-start | bytes 626696 | tf_op jit(solution)/shard_map/ppermute | solution.py:1072
  76.8 8.7 %collective-permute-start.26 = (bf16[136,768]{1,0:T(8,128)(2,1)S(1)}, bf16[136,768]{1,0:T(8,128)(2,1)S(1)}, u32[]{:S(2)}, u32[]{:S(2)}) collective-permute-start(bf16[136,768]{1,0:T(8,128)(2,1)S(1)} %get-tuple-element.143.refs_0_), channel_id=1, source_target_pairs={{0,8},{4,12},{8,0},{12,4},{16,24},{20,28},{24,16},{28,20},{1,9},{5... | collective-permute-start | bytes 626696 | tf_op jit(solution)/shard_map/ppermute | solution.py:1072
  92.4 15.1 %collective-permute-start.36 = (bf16[192,768]{1,0:T(8,128)(2,1)S(1)}, bf16[192,768]{1,0:T(8,128)(2,1)S(1)}, u32[]{:S(2)}, u32[]{:S(2)}) collective-permute-start(bf16[192,768]{1,0:T(8,128)(2,1)S(1)} %get-tuple-element.156), channel_id=1, source_target_pairs={{0,1},{1,0},{2,3},{3,2},{4,5},{5,4},{6,7},{7,6},{8,9},{9,8},{10,11... | collective-permute-start | bytes 884744 | tf_op jit(solution)/shard_map/ppermute | solution.py:1077
  93.0 7.8 %collective-permute-start.29 = (bf16[128,768]{1,0:T(8,128)(2,1)S(1)}, bf16[128,768]{1,0:T(8,128)(2,1)S(1)}, u32[]{:S(2)}, u32[]{:S(2)}) collective-permute-start(bf16[128,768]{1,0:T(8,128)(2,1)S(1)} %get-tuple-element.147), channel_id=1, source_target_pairs={{0,8},{4,12},{8,0},{12,4},{16,24},{20,28},{24,16},{28,20},{1,9},{5... | collective-permute-start | bytes 589832 | tf_op jit(solution)/shard_map/ppermute | solution.py:1072
  94.3 10.6 %collective-permute-start.30 = (bf16[128,768]{1,0:T(8,128)(2,1)S(1)}, bf16[128,768]{1,0:T(8,128)(2,1)S(1)}, u32[]{:S(2)}, u32[]{:S(2)}) collective-permute-start(bf16[128,768]{1,0:T(8,128)(2,1)S(1)} %get-tuple-element.148), channel_id=1, source_target_pairs={{0,16},{4,20},{8,24},{12,28},{16,0},{20,4},{24,8},{28,12},{1,17},{... | collective-permute-start | bytes 589832 | tf_op jit(solution)/shard_map/ppermute | solution.py:1072
  94.9 10.0 %collective-permute-start.31 = (bf16[128,768]{1,0:T(8,128)(2,1)S(1)}, bf16[128,768]{1,0:T(8,128)(2,1)S(1)}, u32[]{:S(2)}, u32[]{:S(2)}) collective-permute-start(bf16[128,768]{1,0:T(8,128)(2,1)S(1)} %get-tuple-element.149), channel_id=1, source_target_pairs={{0,24},{4,28},{8,16},{12,20},{16,8},{20,12},{24,0},{28,4},{1,25},{... | collective-permute-start | bytes 589832 | tf_op jit(solution)/shard_map/ppermute | solution.py:1072
  96.5 23.5 %collective-permute-start.37 = (bf16[192,768]{1,0:T(8,128)(2,1)S(1)}, bf16[192,768]{1,0:T(8,128)(2,1)S(1)}, u32[]{:S(2)}, u32[]{:S(2)}) collective-permute-start(bf16[192,768]{1,0:T(8,128)(2,1)S(1)} %get-tuple-element.157), channel_id=1, source_target_pairs={{0,2},{1,3},{2,0},{3,1},{4,6},{5,7},{6,4},{7,5},{8,10},{9,11},{10,... | collective-permute-start | bytes 884744 | tf_op jit(solution)/shard_map/ppermute | solution.py:1077
  100.8 19.2 %collective-permute-start.38 = (bf16[192,768]{1,0:T(8,128)(2,1)S(1)}, bf16[192,768]{1,0:T(8,128)(2,1)S(1)}, u32[]{:S(2)}, u32[]{:S(2)}) collective-permute-start(bf16[192,768]{1,0:T(8,128)(2,1)S(1)} %get-tuple-element.158), channel_id=1, source_target_pairs={{0,3},{1,2},{2,1},{3,0},{4,7},{5,6},{6,5},{7,4},{8,11},{9,10},{10,... | collective-permute-start | bytes 884744 | tf_op jit(solution)/shard_map/ppermute | solution.py:1077
  105.2 14.9 %collective-permute-start.35 = (bf16[136,768]{1,0:T(8,128)(2,1)S(1)}, bf16[136,768]{1,0:T(8,128)(2,1)S(1)}, u32[]{:S(2)}, u32[]{:S(2)}) collective-permute-start(bf16[136,768]{1,0:T(8,128)(2,1)S(1)} %get-tuple-element.163.refs_0_), channel_id=1, source_target_pairs={{0,24},{4,28},{8,16},{12,20},{16,8},{20,12},{24,0},{28,4},{1,25},{... | collective-permute-start | bytes 626696 | tf_op jit(solution)/shard_map/ppermute | solution.py:1072
  106.9 13.3 %collective-permute-start.34 = (bf16[136,768]{1,0:T(8,128)(2,1)S(1)}, bf16[136,768]{1,0:T(8,128)(2,1)S(1)}, u32[]{:S(2)}, u32[]{:S(2)}) collective-permute-start(bf16[136,768]{1,0:T(8,128)(2,1)S(1)} %get-tuple-element.163.refs_0_), channel_id=1, source_target_pairs={{0,16},{4,20},{8,24},{12,28},{16,0},{20,4},{24,8},{28,12},{1,17},{... | collective-permute-start | bytes 626696 | tf_op jit(solution)/shard_map/ppermute | solution.py:1072
  107.5 12.6 %collective-permute-start.33 = (bf16[136,768]{1,0:T(8,128)(2,1)S(1)}, bf16[136,768]{1,0:T(8,128)(2,1)S(1)}, u32[]{:S(2)}, u32[]{:S(2)}) collective-permute-start(bf16[136,768]{1,0:T(8,128)(2,1)S(1)} %get-tuple-element.163.refs_0_), channel_id=1, source_target_pairs={{0,8},{4,12},{8,0},{12,4},{16,24},{20,28},{24,16},{28,20},{1,9},{5... | collective-permute-start | bytes 626696 | tf_op jit(solution)/shard_map/ppermute | solution.py:1072
  124.5 7.3 %collective-permute-start.40 = (bf16[1024,640]{1,0:T(8,128)(2,1)S(1)}, bf16[1024,640]{1,0:T(8,128)(2,1)S(1)}, u32[]{:S(2)}, u32[]{:S(2)}) collective-permute-start(bf16[1024,640]{1,0:T(8,128)(2,1)S(1)} %attend_back.1.mine), channel_id=1, source_target_pairs={{0,4},{4,0},{8,12},{12,8},{16,20},{20,16},{24,28},{28,24},{1,5},{5... | collective-permute-start | bytes 3932168 | tf_op jit(solution)/shard_map/ppermute | solution.py:1067
  125.0 15.0 %collective-permute-start.45 = (bf16[192,768]{1,0:T(8,128)(2,1)S(1)}, bf16[192,768]{1,0:T(8,128)(2,1)S(1)}, u32[]{:S(2)}, u32[]{:S(2)}) collective-permute-start(bf16[192,768]{1,0:T(8,128)(2,1)S(1)} %mlp_sum.1.refs_0_), channel_id=1, source_target_pairs={{0,16},{4,20},{8,24},{12,28},{16,0},{20,4},{24,8},{28,12},{1,17},{... | collective-permute-start | bytes 884744 | tf_op jit(solution)/shard_map/ppermute | solution.py:1072
  126.4 14.7 %collective-permute-start.44 = (bf16[192,768]{1,0:T(8,128)(2,1)S(1)}, bf16[192,768]{1,0:T(8,128)(2,1)S(1)}, u32[]{:S(2)}, u32[]{:S(2)}) collective-permute-start(bf16[192,768]{1,0:T(8,128)(2,1)S(1)} %mlp_sum.1.refs_0_), channel_id=1, source_target_pairs={{0,8},{4,12},{8,0},{12,4},{16,24},{20,28},{24,16},{28,20},{1,9},{5... | collective-permute-start | bytes 884744 | tf_op jit(solution)/shard_map/ppermute | solution.py:1072
  126.9 9.5 %collective-permute-start.53 = (bf16[2,56,768]{2,1,0:T(8,128)(2,1)S(1)}, bf16[2,56,768]{2,1,0:T(8,128)(2,1)S(1)}, u32[]{:S(2)}, u32[]{:S(2)}) collective-permute-start(bf16[2,56,768]{2,1,0:T(8,128)(2,1)S(1)} %get-tuple-element.185), channel_id=1, source_target_pairs={{0,1},{1,0},{2,3},{3,2},{4,5},{5,4},{6,7},{7,6},{8,9},{9,8},{10,11... | collective-permute-start | bytes 516104 | tf_op jit(solution)/shard_map/ppermute | solution.py:1077
  132.6 11.1 %collective-permute-start.41 = (bf16[128,768]{1,0:T(8,128)(2,1)S(1)}, bf16[128,768]{1,0:T(8,128)(2,1)S(1)}, u32[]{:S(2)}, u32[]{:S(2)}) collective-permute-start(bf16[128,768]{1,0:T(8,128)(2,1)S(1)} %get-tuple-element.174), channel_id=1, source_target_pairs={{0,8},{4,12},{8,0},{12,4},{16,24},{20,28},{24,16},{28,20},{1,9},{5... | collective-permute-start | bytes 589832 | tf_op jit(solution)/shard_map/ppermute | solution.py:1072
  135.8 9.5 %collective-permute-start.51 = (bf16[2,80,768]{2,1,0:T(8,128)(2,1)S(1)}, bf16[2,80,768]{2,1,0:T(8,128)(2,1)S(1)}, u32[]{:S(2)}, u32[]{:S(2)}) collective-permute-start(bf16[2,80,768]{2,1,0:T(8,128)(2,1)S(1)} %get-tuple-element.181), channel_id=1, source_target_pairs={{0,1},{1,0},{2,3},{3,2},{4,5},{5,4},{6,7},{7,6},{8,9},{9,8},{10,11... | collective-permute-start | bytes 737288 | tf_op jit(solution)/shard_map/ppermute | solution.py:1077
  136.5 7.2 %collective-permute-start.54 = (bf16[1,56,768]{2,1,0:T(8,128)(2,1)S(1)}, bf16[1,56,768]{2,1,0:T(8,128)(2,1)S(1)}, u32[]{:S(2)}, u32[]{:S(2)}) collective-permute-start(bf16[1,56,768]{2,1,0:T(8,128)(2,1)S(1)} %get-tuple-element.187), channel_id=1, source_target_pairs={{0,2},{1,3},{2,0},{3,1},{4,6},{5,7},{6,4},{7,5},{8,10},{9,11},{10,... | collective-permute-start | bytes 258056 | tf_op jit(solution)/shard_map/ppermute | solution.py:1077
  140.0 6.1 %collective-permute-start.42 = (bf16[128,768]{1,0:T(8,128)(2,1)S(1)}, bf16[128,768]{1,0:T(8,128)(2,1)S(1)}, u32[]{:S(2)}, u32[]{:S(2)}) collective-permute-start(bf16[128,768]{1,0:T(8,128)(2,1)S(1)} %get-tuple-element.175), channel_id=1, source_target_pairs={{0,16},{4,20},{8,24},{12,28},{16,0},{20,4},{24,8},{28,12},{1,17},{... | collective-permute-start | bytes 589832 | tf_op jit(solution)/shard_map/ppermute | solution.py:1072
  141.0 13.5 %collective-permute-start.47 = (bf16[192,768]{1,0:T(8,128)(2,1)S(1)}, bf16[192,768]{1,0:T(8,128)(2,1)S(1)}, u32[]{:S(2)}, u32[]{:S(2)}) collective-permute-start(bf16[192,768]{1,0:T(8,128)(2,1)S(1)} %mlp_sum.1.refs_0_), channel_id=1, source_target_pairs={{0,4},{4,0},{8,12},{12,8},{16,20},{20,16},{24,28},{28,24},{1,5},{5... | collective-permute-start | bytes 884744 | tf_op jit(solution)/shard_map/ppermute | solution.py:1067
  143.7 12.0 %collective-permute-start.49 = (bf16[192,768]{1,0:T(8,128)(2,1)S(1)}, bf16[192,768]{1,0:T(8,128)(2,1)S(1)}, u32[]{:S(2)}, u32[]{:S(2)}) collective-permute-start(bf16[192,768]{1,0:T(8,128)(2,1)S(1)} %collective-permute-done.45.refs_2_), channel_id=1, source_target_pairs={{0,4},{4,0},{8,12},{12,8},{16,20},{20,16},{24,28},{28,24},{1,5},{5... | collective-permute-start | bytes 884744 | tf_op jit(solution)/shard_map/ppermute | solution.py:1067
  143.7 8.3 %collective-permute-start.43 = (bf16[128,768]{1,0:T(8,128)(2,1)S(1)}, bf16[128,768]{1,0:T(8,128)(2,1)S(1)}, u32[]{:S(2)}, u32[]{:S(2)}) collective-permute-start(bf16[128,768]{1,0:T(8,128)(2,1)S(1)} %get-tuple-element.176), channel_id=1, source_target_pairs={{0,24},{4,28},{8,16},{12,20},{16,8},{20,12},{24,0},{28,4},{1,25},{... | collective-permute-start | bytes 589832 | tf_op jit(solution)/shard_map/ppermute | solution.py:1072
  145.3 17.5 %collective-permute-start.46 = (bf16[192,768]{1,0:T(8,128)(2,1)S(1)}, bf16[192,768]{1,0:T(8,128)(2,1)S(1)}, u32[]{:S(2)}, u32[]{:S(2)}) collective-permute-start(bf16[192,768]{1,0:T(8,128)(2,1)S(1)} %collective-permute-done.44.refs_1_), channel_id=1, source_target_pairs={{0,16},{4,20},{8,24},{12,28},{16,0},{20,4},{24,8},{28,12},{1,17},{... | collective-permute-start | bytes 884744 | tf_op jit(solution)/shard_map/ppermute | solution.py:1072
  146.0 6.9 %collective-permute-start.52 = (bf16[1,80,768]{2,1,0:T(8,128)(2,1)S(1)}, bf16[1,80,768]{2,1,0:T(8,128)(2,1)S(1)}, u32[]{:S(2)}, u32[]{:S(2)}) collective-permute-start(bf16[1,80,768]{2,1,0:T(8,128)(2,1)S(1)} %get-tuple-element.183), channel_id=1, source_target_pairs={{0,2},{1,3},{2,0},{3,1},{4,6},{5,7},{6,4},{7,5},{8,10},{9,11},{10,... | collective-permute-start | bytes 368648 | tf_op jit(solution)/shard_map/ppermute | solution.py:1077
  152.0 10.8 %collective-permute-start.48 = (bf16[192,768]{1,0:T(8,128)(2,1)S(1)}, bf16[192,768]{1,0:T(8,128)(2,1)S(1)}, u32[]{:S(2)}, u32[]{:S(2)}) collective-permute-start(bf16[192,768]{1,0:T(8,128)(2,1)S(1)} %collective-permute-done.44.refs_1_), channel_id=1, source_target_pairs={{0,4},{4,0},{8,12},{12,8},{16,20},{20,16},{24,28},{28,24},{1,5},{5... | collective-permute-start | bytes 884744 | tf_op jit(solution)/shard_map/ppermute | solution.py:1067
  153.0 10.3 %collective-permute-start.57 = (bf16[136,768]{1,0:T(8,128)(2,1)S(1)}, bf16[136,768]{1,0:T(8,128)(2,1)S(1)}, u32[]{:S(2)}, u32[]{:S(2)}) collective-permute-start(bf16[136,768]{1,0:T(8,128)(2,1)S(1)} %last_sum.1.refs_0_), channel_id=1, source_target_pairs={{0,24},{4,28},{8,16},{12,20},{16,8},{20,12},{24,0},{28,4},{1,25},{... | collective-permute-start | bytes 626696 | tf_op jit(solution)/shard_map/ppermute | solution.py:1072
  154.6 12.6 %collective-permute-start.56 = (bf16[136,768]{1,0:T(8,128)(2,1)S(1)}, bf16[136,768]{1,0:T(8,128)(2,1)S(1)}, u32[]{:S(2)}, u32[]{:S(2)}) collective-permute-start(bf16[136,768]{1,0:T(8,128)(2,1)S(1)} %last_sum.1.refs_0_), channel_id=1, source_target_pairs={{0,16},{4,20},{8,24},{12,28},{16,0},{20,4},{24,8},{28,12},{1,17},{... | collective-permute-start | bytes 626696 | tf_op jit(solution)/shard_map/ppermute | solution.py:1072
  155.7 11.5 %collective-permute-start.55 = (bf16[136,768]{1,0:T(8,128)(2,1)S(1)}, bf16[136,768]{1,0:T(8,128)(2,1)S(1)}, u32[]{:S(2)}, u32[]{:S(2)}) collective-permute-start(bf16[136,768]{1,0:T(8,128)(2,1)S(1)} %last_sum.1.refs_0_), channel_id=1, source_target_pairs={{0,8},{4,12},{8,0},{12,4},{16,24},{20,28},{24,16},{28,20},{1,9},{5... | collective-permute-start | bytes 626696 | tf_op jit(solution)/shard_map/ppermute | solution.py:1072
  162.8 8.1 %collective-permute-start.58 = (bf16[136,768]{1,0:T(8,128)(2,1)S(1)}, bf16[136,768]{1,0:T(8,128)(2,1)S(1)}, u32[]{:S(2)}, u32[]{:S(2)}) collective-permute-start(bf16[136,768]{1,0:T(8,128)(2,1)S(1)} %last_sum.1.refs_0_), channel_id=1, source_target_pairs={{0,4},{4,0},{8,12},{12,8},{16,20},{20,16},{24,28},{28,24},{1,5},{5... | collective-permute-start | bytes 626696 | tf_op jit(solution)/shard_map/ppermute | solution.py:1067
  163.3 7.6 %collective-permute-start.61 = (bf16[136,768]{1,0:T(8,128)(2,1)S(1)}, bf16[136,768]{1,0:T(8,128)(2,1)S(1)}, u32[]{:S(2)}, u32[]{:S(2)}) collective-permute-start(bf16[136,768]{1,0:T(8,128)(2,1)S(1)} %collective-permute-done.57.refs_3_), channel_id=1, source_target_pairs={{0,4},{4,0},{8,12},{12,8},{16,20},{20,16},{24,28},{28,24},{1,5},{5... | collective-permute-start | bytes 626696 | tf_op jit(solution)/shard_map/ppermute | solution.py:1067
  (18 other events, 112.5 us)

commit v6 on v5

--- a/solution.py
+++ b/solution.py
@@ -1458,7 +1458,7 @@
         bind(input_kernel, g),
         [shaped((rows, width), F32)] + [shaped((rows, width), BF)] * (chips - 1),
         [VMEM] * 3,
-        [dq_mine, dq_theirs, w_qkv],
+        [after(dq_mine, q_away), dq_theirs, w_qkv],
         name="project_back",
     )
     d_in = swap(d_in)
@@ -1470,7 +1470,7 @@
         o_own, o_away = ring_step(o_own, o_away, mask_at // 2)
         mask_at *= 2
     near = pass_on(m_piece, chips, dq_theirs)
-    m_pieces = near + [to_core(part) for part in near]
+    m_pieces = near + [to_core(after(part, q_away)) for part in near]
     (input_grad,) = mix(
         lambda kept, *parts: (sum((part.astype(F32) for part in parts), kept).astype(BF),),
         [shaped((rows, width), BF)],
@@ -1498,7 +1498,7 @@
         name="last_sum",
     )
     near = spread(after(piece, input_grad), chips)
-    pieces = near + [to_core(part) for part in near]
+    pieces = near + [to_core(after(part, g_down)) for part in near]
     found = call(
         bind(last_kernel, g),
         [shaped((g.shard, width), F32)] * 3
@@ -1506,7 +1506,7 @@
         + [shaped((g.shard, width), F32), shaped((g.hshard,), F32)]
         + [vector] * 6,
         [SMEM] + [VMEM] * (2 * chips),
-        [after(sc, g_down), *pieces],
+        [sc, *pieces],
         name="last_lay",
     )
     gq, gk, gv, g_bq, g_bv, g_out, g_bin, g_gain2, g_bias2, g_bdown, g_gain1, g_bias1, g_bout = found

time: 176 us -> 174 us (0.989); the launches traced: 174 us -> 174 us
    ppermute x27, waiting for transfers between devices: 38.7 us -> 36.4 us  [to_chip(): return lax.ppermute(x, 'ctx', [(i, i ^ 2 * j) for i in range(n)])]
  transfers between devices with their start and end apart: 62 -> 62, of which waited for: 28 -> 31; matrix products, arithmetic and copies ran while one was open for 0% -> 0% of each run, Pallas kernels for 13% -> 13%
where the time goes in v6:
time: 174 us
  waiting for transfers between devices  69.7 us (40%)
  starting transfers between devices  65.4 us (38%)
  Pallas kernels  37.6 us (22%)
    pallas_call x27, Pallas kernels, call(): pl.pallas_call(kernel, out_shape=outs, in_specs=ins, out_specs=[VMEM] * l...  37.6 us
    ppermute x27, waiting for transfers between devices, to_chip(): return lax.ppermute(x, 'ctx', [(i, i ^ 2 * j) for i in range(n)])  36.4 us
    ppermute x27, starting transfers between devices, to_chip(): return lax.ppermute(x, 'ctx', [(i, i ^ 2 * j) for i in range(n)])  31.3 us
    ppermute x13, starting transfers between devices, along(): return lax.ppermute(x, 'fsdp', [(i, i ^ mask) for i in range(n)])  29.6 us
    ppermute x13, waiting for transfers between devices, along(): return lax.ppermute(x, 'fsdp', [(i, i ^ mask) for i in range(n)])  24.2 us
    ppermute x22, waiting for transfers between devices, to_core(): return lax.ppermute(x, 'ctx', [(i, i ^ 1) for i in range(n)])  9.16 us
    ppermute x22, starting transfers between devices, to_core(): return lax.ppermute(x, 'ctx', [(i, i ^ 1) for i in range(n)])  4.5 us
  transfers between devices with their start and end apart: 62, of which 31 were waited for; matrix products, arithmetic and copies ran while one was open for 0% of the time, Pallas kernels for 13%

profile of v6, /device:TPU:0, one launch (start us, length us, event | category | flops | bytes accessed | tf_op | source)
XLA Modules:
  0.0 174.0 jit_solution(14322487998342629778)
XLA Ops:
  0.7 2.0 %pick_weights.1 = (bf16[192,576]{1,0:T(8,128)(2,1)S(1)}, bf16[112,576]{1,0:T(8,128)(2,1)S(1)}, bf16[16,256]{1,0:T(8,128)(2,1)S(1)}) custom-call(s32[3]{0:T(128)S(1)} %pad_add_fusion.sc, bf16[192,768]{1,0:T(8,128)(2,1)} %refs_0_.1, bf16[192,768]{1,0:T(8,128)(2,1)} %refs_1_.1, bf16[192,768]{1,0:T(8,128)(2,1)} %refs_2_.1, bf16[192]{0:T(256)(128)(2,1)} %refs_3_.1, ...), custom_call_target="tpu_custom_call" | custom-call | flops 1 | bytes 1 | tf_op jit(solution)/shard_map/pick_weights/pallas_call | solution.py:382
  2.8 3.0 %collective-permute-start = (bf16[128,768]{1,0:T(8,128)(2,1)}, bf16[128,768]{1,0:T(8,128)(2,1)S(1)}, u32[]{:S(2)}, u32[]{:S(2)}) collective-permute-start(bf16[128,768]{1,0:T(8,128)(2,1)} %bitcast.10), channel_id=1, source_target_pairs={{0,8},{4,12},{8,0},{12,4},{16,24},{20,28},{24,16},{28,20},{1,9},{5... | collective-permute-start | bytes 589832 | tf_op jit(solution)/shard_map/ppermute | solution.py:1072
  5.8 2.6 %collective-permute-start.8 = (bf16[112,576]{1,0:T(8,128)(2,1)S(1)}, bf16[112,576]{1,0:T(8,128)(2,1)S(1)}, u32[]{:S(2)}, u32[]{:S(2)}) collective-permute-start(bf16[112,576]{1,0:T(8,128)(2,1)S(1)} %get-tuple-element.118._), channel_id=1, source_target_pairs={{0,2},{1,3},{2,0},{3,1},{4,6},{5,7},{6,4},{7,5},{8,10},{9,11},{10,... | collective-permute-start | bytes 387080 | tf_op jit(solution)/shard_map/ppermute | solution.py:1077
  8.4 1.6 collective-permute-start.7
  10.0 1.5 collective-permute-start.2
  11.9 2.0 %prepare_weights.1 = (bf16[192,768]{1,0:T(8,128)(2,1)S(1)}, bf16[192,768]{1,0:T(8,128)(2,1)S(1)}, bf16[192,768]{1,0:T(8,128)(2,1)S(1)}, bf16[288,768]{1,0:T(8,128)(2,1)S(1)}) custom-call(s32[3]{0:T(128)S(1)} %pad_add_fusion.sc, bf16[112,576]{1,0:T(8,128)(2,1)S(1)} %get-tuple-element.118._, bf16[192,3072]{1,0:T(8,128)(2,1)} %wi.1, bf16[768,768]{1,0:T(8,128)(2,1)} %wd.1, ...), custom_call_target="tpu_custom_call" | custom-call | flops 1 | bytes 1 | tf_op jit(solution)/shard_map/prepare_weights/pallas_call | solution.py:382
  16.7 2.4 %collective-permute-start.18 = (bf16[288,768]{1,0:T(8,128)(2,1)S(1)}, bf16[288,768]{1,0:T(8,128)(2,1)S(1)}, u32[]{:S(2)}, u32[]{:S(2)}) collective-permute-start(bf16[288,768]{1,0:T(8,128)(2,1)S(1)} %get-tuple-element.122), channel_id=1, source_target_pairs={{0,2},{1,3},{2,0},{3,1},{4,6},{5,7},{6,4},{7,5},{8,10},{9,11},{10,... | collective-permute-start | bytes 1327112 | tf_op jit(solution)/shard_map/ppermute | solution.py:1077
  23.2 4.9 %cluster_tables.1 = (bf16[3,512,128]{2,1,0:T(8,128)(2,1)S(1)}, bf16[3,1024,64]{2,1,0:T(8,128)(2,1)S(1)}, bf16[8,1024]{1,0:T(8,128)(2,1)S(1)}) custom-call(s32[3]{0:T(128)S(1)} %pad_add_fusion.sc, bf16[112,576]{1,0:T(8,128)(2,1)S(1)} %collective-permute-done.7.refs_10_._, s32[12,1024]{1,0:T(8,128)S(1)} %bitcast.17, s32[1,1024]{1,0:T(1,128)S(1)} %copy-done.2), custom_call_target="tpu_custom_call" | custom-call | flops 1 | bytes 1 | tf_op jit(solution)/shard_map/cluster_tables/pallas_call | solution.py:382
  29.1 2.1 %project.1 = (bf16[1024,768]{1,0:T(8,128)(2,1)S(1)}, bf16[768,576]{1,0:T(8,128)(2,1)S(1)}, f32[16,768]{1,0:T(8,128)S(1)}) custom-call(s32[3]{0:T(128)S(1)} %pad_add_fusion.sc, bf16[128,768]{1,0:T(8,128)(2,1)S(1)} %bitcast.14, bf16[128,768]{1,0:T(8,128)(2,1)S(1)} %collective-permute-done.refs_1_.refs_5_, ...), custom_call_target="tpu_custom_call" | custom-call | flops 1 | bytes 1 | tf_op jit(solution)/shard_map/project/pallas_call | solution.py:382
  32.6 7.1 %collective-permute-done.18.refs_13_ = bf16[288,768]{1,0:T(8,128)(2,1)S(1)} collective-permute-done((bf16[288,768]{1,0:T(8,128)(2,1)S(1)}, bf16[288,768]{1,0:T(8,128)(2,1)S(1)}, u32[]{:S(2)}, u32[]{:S(2)}) %collective-permute-start.18) | collective-permute-done | bytes 442400 | tf_op jit(solution)/shard_map/ppermute | solution.py:1077
  39.7 1.5 collective-permute-start.19
  41.2 1.5 collective-permute-done.13.refs_1_
  42.8 1.5 collective-permute-start.16
  44.9 1.5 collective-permute-start.14
  46.4 5.2 %collective-permute-done.16.refs_3_.refs_7_ = bf16[256,384]{1,0:T(8,128)(2,1)S(1)} collective-permute-done((bf16[256,384]{1,0:T(8,128)(2,1)S(1)}, bf16[256,384]{1,0:T(8,128)(2,1)S(1)}, u32[]{:S(2)}, u32[]{:S(2)}) %collective-permute-start.16) | collective-permute-done | bytes 196640 | tf_op jit(solution)/shard_map/ppermute | solution.py:1072
  51.6 3.4 %collective-permute-done.15.refs_2_.refs_6_ = bf16[256,384]{1,0:T(8,128)(2,1)S(1)} collective-permute-done((bf16[256,384]{1,0:T(8,128)(2,1)S(1)}, bf16[256,384]{1,0:T(8,128)(2,1)S(1)}, u32[]{:S(2)}, u32[]{:S(2)}) %collective-permute-start.15) | collective-permute-done | bytes 196640 | tf_op jit(solution)/shard_map/ppermute | solution.py:1072
  58.1 3.2 %mlp_forward.1 = (f32[128,768]{1,0:T(8,128)S(1)}, bf16[128,768]{1,0:T(8,128)(2,1)S(1)}, bf16[128,768]{1,0:T(8,128)(2,1)S(1)}, bf16[128,768]{1,0:T(8,128)(2,1)S(1...) custom-call(s32[3]{0:T(128)S(1)} %pad_add_fusion.sc, ...), custom_call_target="tpu_custom_call" | custom-call | flops 1 | bytes 1 | tf_op jit(solution)/shard_map/mlp_forward/pallas_call | solution.py:382
  61.9 1.4 collective-permute-start.24
  63.4 1.6 collective-permute-start.25
  64.9 1.4 turn_rows.1.turned_x
  66.4 2.8 %collective-permute-done.23.refs_1_ = bf16[128,768]{1,0:T(8,128)(2,1)S(1)} collective-permute-done((bf16[128,768]{1,0:T(8,128)(2,1)S(1)}, bf16[128,768]{1,0:T(8,128)(2,1)S(1)}, u32[]{:S(2)}, u32[]{:S(2)}) %collective-permute-start.23) | collective-permute-done | bytes 196640 | tf_op jit(solution)/shard_map/ppermute | solution.py:1072
  69.4 3.4 %collective-permute-done.25.refs_3_ = bf16[128,768]{1,0:T(8,128)(2,1)S(1)} collective-permute-done((bf16[128,768]{1,0:T(8,128)(2,1)S(1)}, bf16[128,768]{1,0:T(8,128)(2,1)S(1)}, u32[]{:S(2)}, u32[]{:S(2)}) %collective-permute-start.25) | collective-permute-done | bytes 196640 | tf_op jit(solution)/shard_map/ppermute | solution.py:1072
  73.8 1.7 collective-permute-start.28
  77.9 5.0 %collective-permute-done.28.refs_3_ = bf16[136,768]{1,0:T(8,128)(2,1)S(1)} collective-permute-done((bf16[136,768]{1,0:T(8,128)(2,1)S(1)}, bf16[136,768]{1,0:T(8,128)(2,1)S(1)}, u32[]{:S(2)}, u32[]{:S(2)}) %collective-permute-start.28) | collective-permute-done | bytes 208928 | tf_op jit(solution)/shard_map/ppermute | solution.py:1072
  82.8 2.7 %collective-permute-done.27.refs_2_ = bf16[136,768]{1,0:T(8,128)(2,1)S(1)} collective-permute-done((bf16[136,768]{1,0:T(8,128)(2,1)S(1)}, bf16[136,768]{1,0:T(8,128)(2,1)S(1)}, u32[]{:S(2)}, u32[]{:S(2)}) %collective-permute-start.27) | collective-permute-done | bytes 208928 | tf_op jit(solution)/shard_map/ppermute | solution.py:1072
  85.5 1.6 mlp_back.1
  87.1 2.3 %mlp_grads.1 = (f32[4,192,768]{2,1,0:T(8,128)S(1)}, bf16[4,192,768]{2,1,0:T(8,128)(2,1)S(1)}, f32[8,768]{1,0:T(8,128)S(1)}) custom-call(s32[3]{0:T(128)S(1)} %pad_add_fusion.sc, bf16[136,768]{1,0:T(8,128)(2,1)S(1)} %get-tuple-element.151.refs_0_, bf16[136,768]{1,0:T(8,128)(2,1)S(1)} %collective-permute-done.26.refs_1_, ...), custom_call_target="tpu_custom_call" | custom-call | flops 1 | bytes 1 | tf_op jit(solution)/shard_map/mlp_grads/pallas_call | solution.py:382
  89.4 2.8 %collective-permute-done.32.refs_1_ = bf16[4,192,768]{2,1,0:T(8,128)(2,1)S(1)} collective-permute-done((bf16[4,192,768]{2,1,0:T(8,128)(2,1)S(1)}, bf16[4,192,768]{2,1,0:T(8,128)(2,1)S(1)}, u32[]{:S(2)}, u32[]{:S(2)}) %collective-permute-start.32) | collective-permute-done | bytes 1179680 | tf_op jit(solution)/shard_map/ppermute | solution.py:1067
  94.9 1.6 collective-permute-start.31
  96.5 2.3 %collective-permute-start.37 = (bf16[192,768]{1,0:T(8,128)(2,1)S(1)}, bf16[192,768]{1,0:T(8,128)(2,1)S(1)}, u32[]{:S(2)}, u32[]{:S(2)}) collective-permute-start(bf16[192,768]{1,0:T(8,128)(2,1)S(1)} %get-tuple-element.165), channel_id=1, source_target_pairs={{0,2},{1,3},{2,0},{3,1},{4,6},{5,7},{6,4},{7,5},{8,10},{9,11},{10,... | collective-permute-start | bytes 884744 | tf_op jit(solution)/shard_map/ppermute | solution.py:1077
  98.8 2.0 %collective-permute-done.29.refs_1_ = bf16[128,768]{1,0:T(8,128)(2,1)S(1)} collective-permute-done((bf16[128,768]{1,0:T(8,128)(2,1)S(1)}, bf16[128,768]{1,0:T(8,128)(2,1)S(1)}, u32[]{:S(2)}, u32[]{:S(2)}) %collective-permute-start.29) | collective-permute-done | bytes 196640 | tf_op jit(solution)/shard_map/ppermute | solution.py:1072
  100.8 3.4 %collective-permute-start.38 = (bf16[192,768]{1,0:T(8,128)(2,1)S(1)}, bf16[192,768]{1,0:T(8,128)(2,1)S(1)}, u32[]{:S(2)}, u32[]{:S(2)}) collective-permute-start(bf16[192,768]{1,0:T(8,128)(2,1)S(1)} %get-tuple-element.166), channel_id=1, source_target_pairs={{0,3},{1,2},{2,1},{3,0},{4,7},{5,6},{6,5},{7,4},{8,11},{9,10},{10,... | collective-permute-start | bytes 884744 | tf_op jit(solution)/shard_map/ppermute | solution.py:1077
  105.2 1.6 collective-permute-start.35
  108.8 11.2 %collective-permute-done.37.refs_2_ = bf16[192,768]{1,0:T(8,128)(2,1)S(1)} collective-permute-done((bf16[192,768]{1,0:T(8,128)(2,1)S(1)}, bf16[192,768]{1,0:T(8,128)(2,1)S(1)}, u32[]{:S(2)}, u32[]{:S(2)}) %collective-permute-start.37) | collective-permute-done | bytes 294944 | tf_op jit(solution)/shard_map/ppermute | solution.py:1077
  120.7 1.9 %out_grads.1 = (f32[2,56,768]{2,1,0:T(8,128)S(1)}, bf16[2,56,768]{2,1,0:T(8,128)(2,1)S(1)}) custom-call(s32[3]{0:T(128)S(1)} %pad_add_fusion.sc, bf16[136,768]{1,0:T(8,128)(2,1)S(1)} %get-tuple-element.171.refs_0_, bf16[136,768]{1,0:T(8,128)(2,1)S(1)} %collective-permute-done.33.refs_1_, bf16[136,768]{1,0:T(8,128)(2,1)S(1)} %collective-permute-done.34.refs_2_, ...), custom_call_target="tpu_custom_call" | custom-call | flops 1 | bytes 1 | tf_op jit(solution)/shard_map/out_grads/pallas_call | solution.py:382
  122.6 1.9 %attend_back.1.mine = bf16[1024,640]{1,0:T(8,128)(2,1)S(1)} custom-call(bf16[512,192]{1,0:T(8,128)(2,1)S(1)} %context_back.1.own, bf16[512,192]{1,0:T(8,128)(2,1)S(1)} %collective-permute-done.39.other, bf16[3,512,128]{2,1,0:T(8,128)(2,1)S(1)} %get-tuple-element.130.pick, bf16[3,1024,64]{2,1,0:T(8,128)(2,1)S(1)} %get-tuple-element.131.place, ...), custom_call_target="tpu_custom_call" | custom-call | flops 1 | bytes 1 | tf_op jit(solution)/shard_map/attend_back/pallas_call | solution.py:382
  126.9 4.9 %collective-permute-start.46 = (bf16[2,56,768]{2,1,0:T(8,128)(2,1)S(1)}, bf16[2,56,768]{2,1,0:T(8,128)(2,1)S(1)}, u32[]{:S(2)}, u32[]{:S(2)}) collective-permute-start(bf16[2,56,768]{2,1,0:T(8,128)(2,1)S(1)} %get-tuple-element.191), channel_id=1, source_target_pairs={{0,1},{1,0},{2,3},{3,2},{4,5},{5,4},{6,7},{7,6},{8,9},{9,8},{10,11... | collective-permute-start | bytes 516104 | tf_op jit(solution)/shard_map/ppermute | solution.py:1077
  131.8 1.6 project_grads.1
  137.1 6.0 %collective-permute-start.47 = (bf16[1,56,768]{2,1,0:T(8,128)(2,1)S(1)}, bf16[1,56,768]{2,1,0:T(8,128)(2,1)S(1)}, u32[]{:S(2)}, u32[]{:S(2)}) collective-permute-start(bf16[1,56,768]{2,1,0:T(8,128)(2,1)S(1)} %get-tuple-element.193), channel_id=1, source_target_pairs={{0,2},{1,3},{2,0},{3,1},{4,6},{5,7},{6,4},{7,5},{8,10},{9,11},{10,... | collective-permute-start | bytes 258056 | tf_op jit(solution)/shard_map/ppermute | solution.py:1077
  143.7 3.3 %collective-permute-done.47.refs_3_ = bf16[1,56,768]{2,1,0:T(8,128)(2,1)S(1)} collective-permute-done((bf16[1,56,768]{2,1,0:T(8,128)(2,1)S(1)}, bf16[1,56,768]{2,1,0:T(8,128)(2,1)S(1)}, u32[]{:S(2)}, u32[]{:S(2)}) %collective-permute-start.47) | collective-permute-done | bytes 86048 | tf_op jit(solution)/shard_map/ppermute | solution.py:1077
  148.3 1.9 %collective-permute-start.45 = (bf16[1,80,768]{2,1,0:T(8,128)(2,1)S(1)}, bf16[1,80,768]{2,1,0:T(8,128)(2,1)S(1)}, u32[]{:S(2)}, u32[]{:S(2)}) collective-permute-start(bf16[1,80,768]{2,1,0:T(8,128)(2,1)S(1)} %get-tuple-element.189), channel_id=1, source_target_pairs={{0,2},{1,3},{2,0},{3,1},{4,6},{5,7},{6,4},{7,5},{8,10},{9,11},{10,... | collective-permute-start | bytes 368648 | tf_op jit(solution)/shard_map/ppermute | solution.py:1077
  150.2 4.6 %collective-permute-done.42.refs_3_ = bf16[128,768]{1,0:T(8,128)(2,1)S(1)} collective-permute-done((bf16[128,768]{1,0:T(8,128)(2,1)S(1)}, bf16[128,768]{1,0:T(8,128)(2,1)S(1)}, u32[]{:S(2)}, u32[]{:S(2)}) %collective-permute-start.42) | collective-permute-done | bytes 196640 | tf_op jit(solution)/shard_map/ppermute | solution.py:1072
  156.2 1.5 collective-permute-start.50
  158.3 1.4 collective-permute-start.48
  159.7 3.2 %mlp_lay.1 = (f32[192,3072]{1,0:T(8,128)}, f32[768,768]{1,0:T(8,128)}) custom-call(s32[3]{0:T(128)S(1)} %pad_add_fusion.sc, bf16[192,768]{1,0:T(8,128)(2,1)S(1)} %mlp_sum.1.refs_0_, bf16[192,768]{1,0:T(8,128)(2,1)S(1)} %collective-permute-done.51.refs_1_, bf16[192,768]{1,0:T(8,128)(2,1)S(1)} %collective-permute-done.52.refs_2_, ...), custom_call_target="tpu_custom_call" | custom-call | flops 1 | bytes 1 | tf_op jit(solution)/shard_map/mlp_lay/pallas_call | solution.py:382
  162.9 2.3 %collective-permute-done.50.refs_3_ = bf16[136,768]{1,0:T(8,128)(2,1)S(1)} collective-permute-done((bf16[136,768]{1,0:T(8,128)(2,1)S(1)}, bf16[136,768]{1,0:T(8,128)(2,1)S(1)}, u32[]{:S(2)}, u32[]{:S(2)}) %collective-permute-start.50) | collective-permute-done | bytes 208928 | tf_op jit(solution)/shard_map/ppermute | solution.py:1072
  165.2 3.5 %collective-permute-done.49.refs_2_ = bf16[136,768]{1,0:T(8,128)(2,1)S(1)} collective-permute-done((bf16[136,768]{1,0:T(8,128)(2,1)S(1)}, bf16[136,768]{1,0:T(8,128)(2,1)S(1)}, u32[]{:S(2)}, u32[]{:S(2)}) %collective-permute-start.49) | collective-permute-done | bytes 208928 | tf_op jit(solution)/shard_map/ppermute | solution.py:1072
  171.0 2.8 %last_lay.1 = (f32[192,768]{1,0:T(8,128)}, f32[192,768]{1,0:T(8,128)}, f32[192,768]{1,0:T(8,128)}, f32[192]{0:T(256)}, f32[192]{0:T(256)}, /*index=5*/f32[192,76...) custom-call(s32[3]{0:T(128)S(1)} %pad_add_fusion.sc, ...), custom_call_target="tpu_custom_call" | custom-call | flops 1 | bytes 1 | tf_op jit(solution)/shard_map/last_lay/pallas_call | solution.py:382
  (113 shorter events, 36.4 us)
Async XLA Ops:
  2.8 13.9 %collective-permute-start = (bf16[128,768]{1,0:T(8,128)(2,1)}, bf16[128,768]{1,0:T(8,128)(2,1)S(1)}, u32[]{:S(2)}, u32[]{:S(2)}) collective-permute-start(bf16[128,768]{1,0:T(8,128)(2,1)} %bitcast.10), channel_id=1, source_target_pairs={{0,8},{4,12},{8,0},{12,4},{16,24},{20,28},{24,16},{28,20},{1,9},{5... | collective-permute-start | bytes 589832 | tf_op jit(solution)/shard_map/ppermute | solution.py:1072
  5.8 9.3 %collective-permute-start.8 = (bf16[112,576]{1,0:T(8,128)(2,1)S(1)}, bf16[112,576]{1,0:T(8,128)(2,1)S(1)}, u32[]{:S(2)}, u32[]{:S(2)}) collective-permute-start(bf16[112,576]{1,0:T(8,128)(2,1)S(1)} %get-tuple-element.118._), channel_id=1, source_target_pairs={{0,2},{1,3},{2,0},{3,1},{4,6},{5,7},{6,4},{7,5},{8,10},{9,11},{10,... | collective-permute-start | bytes 387080 | tf_op jit(solution)/shard_map/ppermute | solution.py:1077
  8.4 6.9 %collective-permute-start.7 = (bf16[112,576]{1,0:T(8,128)(2,1)S(1)}, bf16[112,576]{1,0:T(8,128)(2,1)S(1)}, u32[]{:S(2)}, u32[]{:S(2)}) collective-permute-start(bf16[112,576]{1,0:T(8,128)(2,1)S(1)} %get-tuple-element.118._), channel_id=1, source_target_pairs={{0,1},{1,0},{2,3},{3,2},{4,5},{5,4},{6,7},{7,6},{8,9},{9,8},{10,11... | collective-permute-start | bytes 387080 | tf_op jit(solution)/shard_map/ppermute | solution.py:1077
  10.0 9.1 %collective-permute-start.2 = (bf16[128,768]{1,0:T(8,128)(2,1)}, bf16[128,768]{1,0:T(8,128)(2,1)S(1)}, u32[]{:S(2)}, u32[]{:S(2)}) collective-permute-start(bf16[128,768]{1,0:T(8,128)(2,1)} %bitcast.11), channel_id=1, source_target_pairs={{0,24},{4,28},{8,16},{12,20},{16,8},{20,12},{24,0},{28,4},{1,25},{... | collective-permute-start | bytes 589832 | tf_op jit(solution)/shard_map/ppermute | solution.py:1072
  11.4 9.7 %collective-permute-start.1 = (bf16[128,768]{1,0:T(8,128)(2,1)}, bf16[128,768]{1,0:T(8,128)(2,1)S(1)}, u32[]{:S(2)}, u32[]{:S(2)}) collective-permute-start(bf16[128,768]{1,0:T(8,128)(2,1)} %bitcast.12), channel_id=1, source_target_pairs={{0,16},{4,20},{8,24},{12,28},{16,0},{20,4},{24,8},{28,12},{1,17},{... | collective-permute-start | bytes 589832 | tf_op jit(solution)/shard_map/ppermute | solution.py:1072
  15.3 5.1 %collective-permute-start.9 = (bf16[112,576]{1,0:T(8,128)(2,1)S(1)}, bf16[112,576]{1,0:T(8,128)(2,1)S(1)}, u32[]{:S(2)}, u32[]{:S(2)}) collective-permute-start(bf16[112,576]{1,0:T(8,128)(2,1)S(1)} %collective-permute-done.8.refs_11_), channel_id=1, source_target_pairs={{0,1},{1,0},{2,3},{3,2},{4,5},{5,4},{6,7},{7,6},{8,9},{9,8},{10,11... | collective-permute-start | bytes 387080 | tf_op jit(solution)/shard_map/ppermute | solution.py:1077
  16.7 23.0 %collective-permute-start.18 = (bf16[288,768]{1,0:T(8,128)(2,1)S(1)}, bf16[288,768]{1,0:T(8,128)(2,1)S(1)}, u32[]{:S(2)}, u32[]{:S(2)}) collective-permute-start(bf16[288,768]{1,0:T(8,128)(2,1)S(1)} %get-tuple-element.122), channel_id=1, source_target_pairs={{0,2},{1,3},{2,0},{3,1},{4,6},{5,7},{6,4},{7,5},{8,10},{9,11},{10,... | collective-permute-start | bytes 1327112 | tf_op jit(solution)/shard_map/ppermute | solution.py:1077
  19.1 20.6 %collective-permute-start.17 = (bf16[288,768]{1,0:T(8,128)(2,1)S(1)}, bf16[288,768]{1,0:T(8,128)(2,1)S(1)}, u32[]{:S(2)}, u32[]{:S(2)}) collective-permute-start(bf16[288,768]{1,0:T(8,128)(2,1)S(1)} %get-tuple-element.122), channel_id=1, source_target_pairs={{0,1},{1,0},{2,3},{3,2},{4,5},{5,4},{6,7},{7,6},{8,9},{9,8},{10,11... | collective-permute-start | bytes 1327112 | tf_op jit(solution)/shard_map/ppermute | solution.py:1077
  22.5 6.6 %collective-permute-start.3 = (bf16[128,768]{1,0:T(8,128)(2,1)S(1)}, bf16[128,768]{1,0:T(8,128)(2,1)S(1)}, u32[]{:S(2)}, u32[]{:S(2)}) collective-permute-start(bf16[128,768]{1,0:T(8,128)(2,1)S(1)} %bitcast.13), channel_id=1, source_target_pairs={{0,4},{4,0},{8,12},{12,8},{16,20},{20,16},{24,28},{28,24},{1,5},{5... | collective-permute-start | bytes 589832 | tf_op jit(solution)/shard_map/ppermute | solution.py:1067
  22.7 6.4 %collective-permute-start.5 = (bf16[128,768]{1,0:T(8,128)(2,1)S(1)}, bf16[128,768]{1,0:T(8,128)(2,1)S(1)}, u32[]{:S(2)}, u32[]{:S(2)}) collective-permute-start(bf16[128,768]{1,0:T(8,128)(2,1)S(1)} %collective-permute-done.1.refs_2_.refs_6_), channel_id=1, source_target_pairs={{0,4},{4,0},{8,12},{12,8},{16,20},{20,16},{24,28},{28,24},{1,5},{5... | collective-permute-start | bytes 589832 | tf_op jit(solution)/shard_map/ppermute | solution.py:1067
  23.0 6.1 %collective-permute-start.4 = (bf16[128,768]{1,0:T(8,128)(2,1)S(1)}, bf16[128,768]{1,0:T(8,128)(2,1)S(1)}, u32[]{:S(2)}, u32[]{:S(2)}) collective-permute-start(bf16[128,768]{1,0:T(8,128)(2,1)S(1)} %collective-permute-done.refs_1_.refs_5_), channel_id=1, source_target_pairs={{0,4},{4,0},{8,12},{12,8},{16,20},{20,16},{24,28},{28,24},{1,5},{5... | collective-permute-start | bytes 589832 | tf_op jit(solution)/shard_map/ppermute | solution.py:1067
  39.7 15.9 %collective-permute-start.19 = (bf16[288,768]{1,0:T(8,128)(2,1)S(1)}, bf16[288,768]{1,0:T(8,128)(2,1)S(1)}, u32[]{:S(2)}, u32[]{:S(2)}) collective-permute-start(bf16[288,768]{1,0:T(8,128)(2,1)S(1)} %collective-permute-done.18.refs_13_), channel_id=1, source_target_pairs={{0,1},{1,0},{2,3},{3,2},{4,5},{5,4},{6,7},{7,6},{8,9},{9,8},{10,11... | collective-permute-start | bytes 1327112 | tf_op jit(solution)/shard_map/ppermute | solution.py:1077
  42.8 8.8 %collective-permute-start.16 = (bf16[256,384]{1,0:T(8,128)(2,1)S(1)}, bf16[256,384]{1,0:T(8,128)(2,1)S(1)}, u32[]{:S(2)}, u32[]{:S(2)}) collective-permute-start(bf16[256,384]{1,0:T(8,128)(2,1)S(1)} %join_context.1.refs_0_.refs_4_), channel_id=1, source_target_pairs={{0,24},{4,28},{8,16},{12,20},{16,8},{20,12},{24,0},{28,4},{1,25},{... | collective-permute-start | bytes 589832 | tf_op jit(solution)/shard_map/ppermute | solution.py:1072
  44.4 10.6 %collective-permute-start.15 = (bf16[256,384]{1,0:T(8,128)(2,1)S(1)}, bf16[256,384]{1,0:T(8,128)(2,1)S(1)}, u32[]{:S(2)}, u32[]{:S(2)}) collective-permute-start(bf16[256,384]{1,0:T(8,128)(2,1)S(1)} %join_context.1.refs_0_.refs_4_), channel_id=1, source_target_pairs={{0,16},{4,20},{8,24},{12,28},{16,0},{20,4},{24,8},{28,12},{1,17},{... | collective-permute-start | bytes 589832 | tf_op jit(solution)/shard_map/ppermute | solution.py:1072
  44.9 10.2 %collective-permute-start.14 = (bf16[256,384]{1,0:T(8,128)(2,1)S(1)}, bf16[256,384]{1,0:T(8,128)(2,1)S(1)}, u32[]{:S(2)}, u32[]{:S(2)}) collective-permute-start(bf16[256,384]{1,0:T(8,128)(2,1)S(1)} %join_context.1.refs_0_.refs_4_), channel_id=1, source_target_pairs={{0,8},{4,12},{8,0},{12,4},{16,24},{20,28},{24,16},{28,20},{1,9},{5... | collective-permute-start | bytes 589832 | tf_op jit(solution)/shard_map/ppermute | solution.py:1072
  61.4 7.8 %collective-permute-start.23 = (bf16[128,768]{1,0:T(8,128)(2,1)S(1)}, bf16[128,768]{1,0:T(8,128)(2,1)S(1)}, u32[]{:S(2)}, u32[]{:S(2)}) collective-permute-start(bf16[128,768]{1,0:T(8,128)(2,1)S(1)} %get-tuple-element.144), channel_id=1, source_target_pairs={{0,8},{4,12},{8,0},{12,4},{16,24},{20,28},{24,16},{28,20},{1,9},{5... | collective-permute-start | bytes 589832 | tf_op jit(solution)/shard_map/ppermute | solution.py:1072
  61.9 7.5 %collective-permute-start.24 = (bf16[128,768]{1,0:T(8,128)(2,1)S(1)}, bf16[128,768]{1,0:T(8,128)(2,1)S(1)}, u32[]{:S(2)}, u32[]{:S(2)}) collective-permute-start(bf16[128,768]{1,0:T(8,128)(2,1)S(1)} %get-tuple-element.145), channel_id=1, source_target_pairs={{0,16},{4,20},{8,24},{12,28},{16,0},{20,4},{24,8},{28,12},{1,17},{... | collective-permute-start | bytes 589832 | tf_op jit(solution)/shard_map/ppermute | solution.py:1072
  63.4 9.5 %collective-permute-start.25 = (bf16[128,768]{1,0:T(8,128)(2,1)S(1)}, bf16[128,768]{1,0:T(8,128)(2,1)S(1)}, u32[]{:S(2)}, u32[]{:S(2)}) collective-permute-start(bf16[128,768]{1,0:T(8,128)(2,1)S(1)} %get-tuple-element.146), channel_id=1, source_target_pairs={{0,24},{4,28},{8,16},{12,20},{16,8},{20,12},{24,0},{28,4},{1,25},{... | collective-permute-start | bytes 589832 | tf_op jit(solution)/shard_map/ppermute | solution.py:1072
  73.8 9.0 %collective-permute-start.28 = (bf16[136,768]{1,0:T(8,128)(2,1)S(1)}, bf16[136,768]{1,0:T(8,128)(2,1)S(1)}, u32[]{:S(2)}, u32[]{:S(2)}) collective-permute-start(bf16[136,768]{1,0:T(8,128)(2,1)S(1)} %get-tuple-element.151.refs_0_), channel_id=1, source_target_pairs={{0,24},{4,28},{8,16},{12,20},{16,8},{20,12},{24,0},{28,4},{1,25},{... | collective-permute-start | bytes 626696 | tf_op jit(solution)/shard_map/ppermute | solution.py:1072
  75.5 10.0 %collective-permute-start.27 = (bf16[136,768]{1,0:T(8,128)(2,1)S(1)}, bf16[136,768]{1,0:T(8,128)(2,1)S(1)}, u32[]{:S(2)}, u32[]{:S(2)}) collective-permute-start(bf16[136,768]{1,0:T(8,128)(2,1)S(1)} %get-tuple-element.151.refs_0_), channel_id=1, source_target_pairs={{0,16},{4,20},{8,24},{12,28},{16,0},{20,4},{24,8},{28,12},{1,17},{... | collective-permute-start | bytes 626696 | tf_op jit(solution)/shard_map/ppermute | solution.py:1072
  76.8 8.7 %collective-permute-start.26 = (bf16[136,768]{1,0:T(8,128)(2,1)S(1)}, bf16[136,768]{1,0:T(8,128)(2,1)S(1)}, u32[]{:S(2)}, u32[]{:S(2)}) collective-permute-start(bf16[136,768]{1,0:T(8,128)(2,1)S(1)} %get-tuple-element.151.refs_0_), channel_id=1, source_target_pairs={{0,8},{4,12},{8,0},{12,4},{16,24},{20,28},{24,16},{28,20},{1,9},{5... | collective-permute-start | bytes 626696 | tf_op jit(solution)/shard_map/ppermute | solution.py:1072
  92.4 15.1 %collective-permute-start.36 = (bf16[192,768]{1,0:T(8,128)(2,1)S(1)}, bf16[192,768]{1,0:T(8,128)(2,1)S(1)}, u32[]{:S(2)}, u32[]{:S(2)}) collective-permute-start(bf16[192,768]{1,0:T(8,128)(2,1)S(1)} %get-tuple-element.164), channel_id=1, source_target_pairs={{0,1},{1,0},{2,3},{3,2},{4,5},{5,4},{6,7},{7,6},{8,9},{9,8},{10,11... | collective-permute-start | bytes 884744 | tf_op jit(solution)/shard_map/ppermute | solution.py:1077
  93.0 7.8 %collective-permute-start.29 = (bf16[128,768]{1,0:T(8,128)(2,1)S(1)}, bf16[128,768]{1,0:T(8,128)(2,1)S(1)}, u32[]{:S(2)}, u32[]{:S(2)}) collective-permute-start(bf16[128,768]{1,0:T(8,128)(2,1)S(1)} %get-tuple-element.155), channel_id=1, source_target_pairs={{0,8},{4,12},{8,0},{12,4},{16,24},{20,28},{24,16},{28,20},{1,9},{5... | collective-permute-start | bytes 589832 | tf_op jit(solution)/shard_map/ppermute | solution.py:1072
  94.3 10.6 %collective-permute-start.30 = (bf16[128,768]{1,0:T(8,128)(2,1)S(1)}, bf16[128,768]{1,0:T(8,128)(2,1)S(1)}, u32[]{:S(2)}, u32[]{:S(2)}) collective-permute-start(bf16[128,768]{1,0:T(8,128)(2,1)S(1)} %get-tuple-element.156), channel_id=1, source_target_pairs={{0,16},{4,20},{8,24},{12,28},{16,0},{20,4},{24,8},{28,12},{1,17},{... | collective-permute-start | bytes 589832 | tf_op jit(solution)/shard_map/ppermute | solution.py:1072
  94.9 10.0 %collective-permute-start.31 = (bf16[128,768]{1,0:T(8,128)(2,1)S(1)}, bf16[128,768]{1,0:T(8,128)(2,1)S(1)}, u32[]{:S(2)}, u32[]{:S(2)}) collective-permute-start(bf16[128,768]{1,0:T(8,128)(2,1)S(1)} %get-tuple-element.157), channel_id=1, source_target_pairs={{0,24},{4,28},{8,16},{12,20},{16,8},{20,12},{24,0},{28,4},{1,25},{... | collective-permute-start | bytes 589832 | tf_op jit(solution)/shard_map/ppermute | solution.py:1072
  96.5 23.5 %collective-permute-start.37 = (bf16[192,768]{1,0:T(8,128)(2,1)S(1)}, bf16[192,768]{1,0:T(8,128)(2,1)S(1)}, u32[]{:S(2)}, u32[]{:S(2)}) collective-permute-start(bf16[192,768]{1,0:T(8,128)(2,1)S(1)} %get-tuple-element.165), channel_id=1, source_target_pairs={{0,2},{1,3},{2,0},{3,1},{4,6},{5,7},{6,4},{7,5},{8,10},{9,11},{10,... | collective-permute-start | bytes 884744 | tf_op jit(solution)/shard_map/ppermute | solution.py:1077
  100.8 19.2 %collective-permute-start.38 = (bf16[192,768]{1,0:T(8,128)(2,1)S(1)}, bf16[192,768]{1,0:T(8,128)(2,1)S(1)}, u32[]{:S(2)}, u32[]{:S(2)}) collective-permute-start(bf16[192,768]{1,0:T(8,128)(2,1)S(1)} %get-tuple-element.166), channel_id=1, source_target_pairs={{0,3},{1,2},{2,1},{3,0},{4,7},{5,6},{6,5},{7,4},{8,11},{9,10},{10,... | collective-permute-start | bytes 884744 | tf_op jit(solution)/shard_map/ppermute | solution.py:1077
  105.2 14.9 %collective-permute-start.35 = (bf16[136,768]{1,0:T(8,128)(2,1)S(1)}, bf16[136,768]{1,0:T(8,128)(2,1)S(1)}, u32[]{:S(2)}, u32[]{:S(2)}) collective-permute-start(bf16[136,768]{1,0:T(8,128)(2,1)S(1)} %get-tuple-element.171.refs_0_), channel_id=1, source_target_pairs={{0,24},{4,28},{8,16},{12,20},{16,8},{20,12},{24,0},{28,4},{1,25},{... | collective-permute-start | bytes 626696 | tf_op jit(solution)/shard_map/ppermute | solution.py:1072
  106.9 13.3 %collective-permute-start.34 = (bf16[136,768]{1,0:T(8,128)(2,1)S(1)}, bf16[136,768]{1,0:T(8,128)(2,1)S(1)}, u32[]{:S(2)}, u32[]{:S(2)}) collective-permute-start(bf16[136,768]{1,0:T(8,128)(2,1)S(1)} %get-tuple-element.171.refs_0_), channel_id=1, source_target_pairs={{0,16},{4,20},{8,24},{12,28},{16,0},{20,4},{24,8},{28,12},{1,17},{... | collective-permute-start | bytes 626696 | tf_op jit(solution)/shard_map/ppermute | solution.py:1072
  107.5 12.6 %collective-permute-start.33 = (bf16[136,768]{1,0:T(8,128)(2,1)S(1)}, bf16[136,768]{1,0:T(8,128)(2,1)S(1)}, u32[]{:S(2)}, u32[]{:S(2)}) collective-permute-start(bf16[136,768]{1,0:T(8,128)(2,1)S(1)} %get-tuple-element.171.refs_0_), channel_id=1, source_target_pairs={{0,8},{4,12},{8,0},{12,4},{16,24},{20,28},{24,16},{28,20},{1,9},{5... | collective-permute-start | bytes 626696 | tf_op jit(solution)/shard_map/ppermute | solution.py:1072
  124.5 7.3 %collective-permute-start.40 = (bf16[1024,640]{1,0:T(8,128)(2,1)S(1)}, bf16[1024,640]{1,0:T(8,128)(2,1)S(1)}, u32[]{:S(2)}, u32[]{:S(2)}) collective-permute-start(bf16[1024,640]{1,0:T(8,128)(2,1)S(1)} %attend_back.1.mine), channel_id=1, source_target_pairs={{0,4},{4,0},{8,12},{12,8},{16,20},{20,16},{24,28},{28,24},{1,5},{5... | collective-permute-start | bytes 3932168 | tf_op jit(solution)/shard_map/ppermute | solution.py:1067
  125.0 11.4 %collective-permute-start.51 = (bf16[192,768]{1,0:T(8,128)(2,1)S(1)}, bf16[192,768]{1,0:T(8,128)(2,1)S(1)}, u32[]{:S(2)}, u32[]{:S(2)}) collective-permute-start(bf16[192,768]{1,0:T(8,128)(2,1)S(1)} %mlp_sum.1.refs_0_), channel_id=1, source_target_pairs={{0,8},{4,12},{8,0},{12,4},{16,24},{20,28},{24,16},{28,20},{1,9},{5... | collective-permute-start | bytes 884744 | tf_op jit(solution)/shard_map/ppermute | solution.py:1072
  126.3 16.9 %collective-permute-start.52 = (bf16[192,768]{1,0:T(8,128)(2,1)S(1)}, bf16[192,768]{1,0:T(8,128)(2,1)S(1)}, u32[]{:S(2)}, u32[]{:S(2)}) collective-permute-start(bf16[192,768]{1,0:T(8,128)(2,1)S(1)} %mlp_sum.1.refs_0_), channel_id=1, source_target_pairs={{0,16},{4,20},{8,24},{12,28},{16,0},{20,4},{24,8},{28,12},{1,17},{... | collective-permute-start | bytes 884744 | tf_op jit(solution)/shard_map/ppermute | solution.py:1072
  126.9 10.1 %collective-permute-start.46 = (bf16[2,56,768]{2,1,0:T(8,128)(2,1)S(1)}, bf16[2,56,768]{2,1,0:T(8,128)(2,1)S(1)}, u32[]{:S(2)}, u32[]{:S(2)}) collective-permute-start(bf16[2,56,768]{2,1,0:T(8,128)(2,1)S(1)} %get-tuple-element.191), channel_id=1, source_target_pairs={{0,1},{1,0},{2,3},{3,2},{4,5},{5,4},{6,7},{7,6},{8,9},{9,8},{10,11... | collective-permute-start | bytes 516104 | tf_op jit(solution)/shard_map/ppermute | solution.py:1077
  133.4 9.7 %collective-permute-start.44 = (bf16[2,80,768]{2,1,0:T(8,128)(2,1)S(1)}, bf16[2,80,768]{2,1,0:T(8,128)(2,1)S(1)}, u32[]{:S(2)}, u32[]{:S(2)}) collective-permute-start(bf16[2,80,768]{2,1,0:T(8,128)(2,1)S(1)} %get-tuple-element.180), channel_id=1, source_target_pairs={{0,1},{1,0},{2,3},{3,2},{4,5},{5,4},{6,7},{7,6},{8,9},{9,8},{10,11... | collective-permute-start | bytes 737288 | tf_op jit(solution)/shard_map/ppermute | solution.py:1077
  135.1 12.9 %collective-permute-start.41 = (bf16[128,768]{1,0:T(8,128)(2,1)S(1)}, bf16[128,768]{1,0:T(8,128)(2,1)S(1)}, u32[]{:S(2)}, u32[]{:S(2)}) collective-permute-start(bf16[128,768]{1,0:T(8,128)(2,1)S(1)} %get-tuple-element.184), channel_id=1, source_target_pairs={{0,8},{4,12},{8,0},{12,4},{16,24},{20,28},{24,16},{28,20},{1,9},{5... | collective-permute-start | bytes 589832 | tf_op jit(solution)/shard_map/ppermute | solution.py:1072
  136.4 11.9 %collective-permute-start.53 = (bf16[192,768]{1,0:T(8,128)(2,1)S(1)}, bf16[192,768]{1,0:T(8,128)(2,1)S(1)}, u32[]{:S(2)}, u32[]{:S(2)}) collective-permute-start(bf16[192,768]{1,0:T(8,128)(2,1)S(1)} %collective-permute-done.51.refs_1_), channel_id=1, source_target_pairs={{0,16},{4,20},{8,24},{12,28},{16,0},{20,4},{24,8},{28,12},{1,17},{... | collective-permute-start | bytes 884744 | tf_op jit(solution)/shard_map/ppermute | solution.py:1072
  137.1 9.9 %collective-permute-start.47 = (bf16[1,56,768]{2,1,0:T(8,128)(2,1)S(1)}, bf16[1,56,768]{2,1,0:T(8,128)(2,1)S(1)}, u32[]{:S(2)}, u32[]{:S(2)}) collective-permute-start(bf16[1,56,768]{2,1,0:T(8,128)(2,1)S(1)} %get-tuple-element.193), channel_id=1, source_target_pairs={{0,2},{1,3},{2,0},{3,1},{4,6},{5,7},{6,4},{7,5},{8,10},{9,11},{10,... | collective-permute-start | bytes 258056 | tf_op jit(solution)/shard_map/ppermute | solution.py:1077
  143.1 14.6 %collective-permute-start.54 = (bf16[192,768]{1,0:T(8,128)(2,1)S(1)}, bf16[192,768]{1,0:T(8,128)(2,1)S(1)}, u32[]{:S(2)}, u32[]{:S(2)}) collective-permute-start(bf16[192,768]{1,0:T(8,128)(2,1)S(1)} %mlp_sum.1.refs_0_), channel_id=1, source_target_pairs={{0,4},{4,0},{8,12},{12,8},{16,20},{20,16},{24,28},{28,24},{1,5},{5... | collective-permute-start | bytes 884744 | tf_op jit(solution)/shard_map/ppermute | solution.py:1067
  143.2 15.1 %collective-permute-start.55 = (bf16[192,768]{1,0:T(8,128)(2,1)S(1)}, bf16[192,768]{1,0:T(8,128)(2,1)S(1)}, u32[]{:S(2)}, u32[]{:S(2)}) collective-permute-start(bf16[192,768]{1,0:T(8,128)(2,1)S(1)} %collective-permute-done.51.refs_1_), channel_id=1, source_target_pairs={{0,4},{4,0},{8,12},{12,8},{16,20},{20,16},{24,28},{28,24},{1,5},{5... | collective-permute-start | bytes 884744 | tf_op jit(solution)/shard_map/ppermute | solution.py:1067
  147.0 7.8 %collective-permute-start.42 = (bf16[128,768]{1,0:T(8,128)(2,1)S(1)}, bf16[128,768]{1,0:T(8,128)(2,1)S(1)}, u32[]{:S(2)}, u32[]{:S(2)}) collective-permute-start(bf16[128,768]{1,0:T(8,128)(2,1)S(1)} %get-tuple-element.185), channel_id=1, source_target_pairs={{0,16},{4,20},{8,24},{12,28},{16,0},{20,4},{24,8},{28,12},{1,17},{... | collective-permute-start | bytes 589832 | tf_op jit(solution)/shard_map/ppermute | solution.py:1072
  148.0 6.8 %collective-permute-start.43 = (bf16[128,768]{1,0:T(8,128)(2,1)S(1)}, bf16[128,768]{1,0:T(8,128)(2,1)S(1)}, u32[]{:S(2)}, u32[]{:S(2)}) collective-permute-start(bf16[128,768]{1,0:T(8,128)(2,1)S(1)} %get-tuple-element.186), channel_id=1, source_target_pairs={{0,24},{4,28},{8,16},{12,20},{16,8},{20,12},{24,0},{28,4},{1,25},{... | collective-permute-start | bytes 589832 | tf_op jit(solution)/shard_map/ppermute | solution.py:1072
  148.3 7.8 %collective-permute-start.45 = (bf16[1,80,768]{2,1,0:T(8,128)(2,1)S(1)}, bf16[1,80,768]{2,1,0:T(8,128)(2,1)S(1)}, u32[]{:S(2)}, u32[]{:S(2)}) collective-permute-start(bf16[1,80,768]{2,1,0:T(8,128)(2,1)S(1)} %get-tuple-element.189), channel_id=1, source_target_pairs={{0,2},{1,3},{2,0},{3,1},{4,6},{5,7},{6,4},{7,5},{8,10},{9,11},{10,... | collective-permute-start | bytes 368648 | tf_op jit(solution)/shard_map/ppermute | solution.py:1077
  154.8 4.9 %collective-permute-start.56 = (bf16[192,768]{1,0:T(8,128)(2,1)S(1)}, bf16[192,768]{1,0:T(8,128)(2,1)S(1)}, u32[]{:S(2)}, u32[]{:S(2)}) collective-permute-start(bf16[192,768]{1,0:T(8,128)(2,1)S(1)} %collective-permute-done.52.refs_2_), channel_id=1, source_target_pairs={{0,4},{4,0},{8,12},{12,8},{16,20},{20,16},{24,28},{28,24},{1,5},{5... | collective-permute-start | bytes 884744 | tf_op jit(solution)/shard_map/ppermute | solution.py:1067
  154.8 4.9 %collective-permute-start.57 = (bf16[192,768]{1,0:T(8,128)(2,1)S(1)}, bf16[192,768]{1,0:T(8,128)(2,1)S(1)}, u32[]{:S(2)}, u32[]{:S(2)}) collective-permute-start(bf16[192,768]{1,0:T(8,128)(2,1)S(1)} %collective-permute-done.53.refs_3_), channel_id=1, source_target_pairs={{0,4},{4,0},{8,12},{12,8},{16,20},{20,16},{24,28},{28,24},{1,5},{5... | collective-permute-start | bytes 884744 | tf_op jit(solution)/shard_map/ppermute | solution.py:1067
  156.2 9.0 %collective-permute-start.50 = (bf16[136,768]{1,0:T(8,128)(2,1)S(1)}, bf16[136,768]{1,0:T(8,128)(2,1)S(1)}, u32[]{:S(2)}, u32[]{:S(2)}) collective-permute-start(bf16[136,768]{1,0:T(8,128)(2,1)S(1)} %last_sum.1.refs_0_), channel_id=1, source_target_pairs={{0,24},{4,28},{8,16},{12,20},{16,8},{20,12},{24,0},{28,4},{1,25},{... | collective-permute-start | bytes 626696 | tf_op jit(solution)/shard_map/ppermute | solution.py:1072
  157.7 11.0 %collective-permute-start.49 = (bf16[136,768]{1,0:T(8,128)(2,1)S(1)}, bf16[136,768]{1,0:T(8,128)(2,1)S(1)}, u32[]{:S(2)}, u32[]{:S(2)}) collective-permute-start(bf16[136,768]{1,0:T(8,128)(2,1)S(1)} %last_sum.1.refs_0_), channel_id=1, source_target_pairs={{0,16},{4,20},{8,24},{12,28},{16,0},{20,4},{24,8},{28,12},{1,17},{... | collective-permute-start | bytes 626696 | tf_op jit(solution)/shard_map/ppermute | solution.py:1072
  158.3 10.4 %collective-permute-start.48 = (bf16[136,768]{1,0:T(8,128)(2,1)S(1)}, bf16[136,768]{1,0:T(8,128)(2,1)S(1)}, u32[]{:S(2)}, u32[]{:S(2)}) collective-permute-start(bf16[136,768]{1,0:T(8,128)(2,1)S(1)} %last_sum.1.refs_0_), channel_id=1, source_target_pairs={{0,8},{4,12},{8,0},{12,4},{16,24},{20,28},{24,16},{28,20},{1,9},{5... | collective-permute-start | bytes 626696 | tf_op jit(solution)/shard_map/ppermute | solution.py:1072
  (18 other events, 101.7 us)

commit v7 on v6

--- a/solution.py
+++ b/solution.py
@@ -827,12 +827,14 @@
     branches, slope, wd, wi = refs[:c], refs[c], refs[c + 1], refs[c + 2]
     parts, d_inner = refs[c + 3 : 2 * c + 3], refs[2 * c + 3]
     rows = jnp.concatenate([b[0 : g.rows] for b in branches], axis=0)
-    d_active = dot_nt(rows, wd[...])
-    d_inner[...] = (d_active * slope[...]).astype(BF)
-    total = dot_nt(d_inner[...], wi[...])
-    parts[0][...] = total[: g.rows]
-    for j in range(1, c):
-        parts[j][...] = total[g.rows * j : g.rows * (j + 1)].astype(BF)
+    halves = [slice(i, i + g.tokens // 2) for i in range(0, g.tokens, g.tokens // 2)]
+    for half in halves:
+        d_inner[half] = (dot_nt(rows[half], wd[...]) * slope[half]).astype(BF)
+    for half in halves:
+        total = dot_nt(d_inner[half], wi[...])
+        for i in range(half.start, half.stop, g.rows):
+            block = total[i - half.start : i - half.start + g.rows]
+            parts[i // g.rows][...] = block if i == 0 else block.astype(BF)
 
 
 def split_rows(g, sc, total, size, own, other, at):

time: 174 us -> 174 us (level)
  no operation moved by 1% of the time
where the time goes in v7:
time: 174 us
  waiting for transfers between devices  69.7 us (40%)
  starting transfers between devices  65.4 us (38%)
  Pallas kernels  37.5 us (22%)
    pallas_call x27, Pallas kernels, call(): pl.pallas_call(kernel, out_shape=outs, in_specs=ins, out_specs=[VMEM] * l...  37.5 us
    ppermute x27, waiting for transfers between devices, to_chip(): return lax.ppermute(x, 'ctx', [(i, i ^ 2 * j) for i in range(n)])  36.4 us
    ppermute x27, starting transfers between devices, to_chip(): return lax.ppermute(x, 'ctx', [(i, i ^ 2 * j) for i in range(n)])  31.3 us
    ppermute x13, starting transfers between devices, along(): return lax.ppermute(x, 'fsdp', [(i, i ^ mask) for i in range(n)])  29.6 us
    ppermute x13, waiting for transfers between devices, along(): return lax.ppermute(x, 'fsdp', [(i, i ^ mask) for i in range(n)])  24.2 us
    ppermute x22, waiting for transfers between devices, to_core(): return lax.ppermute(x, 'ctx', [(i, i ^ 1) for i in range(n)])  9.16 us
    ppermute x22, starting transfers between devices, to_core(): return lax.ppermute(x, 'ctx', [(i, i ^ 1) for i in range(n)])  4.5 us
  transfers between devices with their start and end apart: 62, of which 31 were waited for; matrix products, arithmetic and copies ran while one was open for 0% of the time, Pallas kernels for 13%

profile of v7, /device:TPU:0, one launch (start us, length us, event | category | flops | bytes accessed | tf_op | source)
XLA Modules:
  0.0 173.9 jit_solution(17433867870140563687)
XLA Ops:
  0.7 2.0 %pick_weights.1 = (bf16[192,576]{1,0:T(8,128)(2,1)S(1)}, bf16[112,576]{1,0:T(8,128)(2,1)S(1)}, bf16[16,256]{1,0:T(8,128)(2,1)S(1)}) custom-call(s32[3]{0:T(128)S(1)} %pad_add_fusion.sc, bf16[192,768]{1,0:T(8,128)(2,1)} %refs_0_.1, bf16[192,768]{1,0:T(8,128)(2,1)} %refs_1_.1, bf16[192,768]{1,0:T(8,128)(2,1)} %refs_2_.1, bf16[192]{0:T(256)(128)(2,1)} %refs_3_.1, ...), custom_call_target="tpu_custom_call" | custom-call | flops 1 | bytes 1 | tf_op jit(solution)/shard_map/pick_weights/pallas_call | solution.py:382
  2.8 3.0 %collective-permute-start = (bf16[128,768]{1,0:T(8,128)(2,1)}, bf16[128,768]{1,0:T(8,128)(2,1)S(1)}, u32[]{:S(2)}, u32[]{:S(2)}) collective-permute-start(bf16[128,768]{1,0:T(8,128)(2,1)} %bitcast.10), channel_id=1, source_target_pairs={{0,8},{4,12},{8,0},{12,4},{16,24},{20,28},{24,16},{28,20},{1,9},{5... | collective-permute-start | bytes 589832 | tf_op jit(solution)/shard_map/ppermute | solution.py:1074
  5.8 2.6 %collective-permute-start.8 = (bf16[112,576]{1,0:T(8,128)(2,1)S(1)}, bf16[112,576]{1,0:T(8,128)(2,1)S(1)}, u32[]{:S(2)}, u32[]{:S(2)}) collective-permute-start(bf16[112,576]{1,0:T(8,128)(2,1)S(1)} %get-tuple-element.118._), channel_id=1, source_target_pairs={{0,2},{1,3},{2,0},{3,1},{4,6},{5,7},{6,4},{7,5},{8,10},{9,11},{10,... | collective-permute-start | bytes 387080 | tf_op jit(solution)/shard_map/ppermute | solution.py:1079
  8.4 1.6 collective-permute-start.7
  10.0 1.5 collective-permute-start.2
  11.9 2.0 %prepare_weights.1 = (bf16[192,768]{1,0:T(8,128)(2,1)S(1)}, bf16[192,768]{1,0:T(8,128)(2,1)S(1)}, bf16[192,768]{1,0:T(8,128)(2,1)S(1)}, bf16[288,768]{1,0:T(8,128)(2,1)S(1)}) custom-call(s32[3]{0:T(128)S(1)} %pad_add_fusion.sc, bf16[112,576]{1,0:T(8,128)(2,1)S(1)} %get-tuple-element.118._, bf16[192,3072]{1,0:T(8,128)(2,1)} %wi.1, bf16[768,768]{1,0:T(8,128)(2,1)} %wd.1, ...), custom_call_target="tpu_custom_call" | custom-call | flops 1 | bytes 1 | tf_op jit(solution)/shard_map/prepare_weights/pallas_call | solution.py:382
  16.7 2.4 %collective-permute-start.18 = (bf16[288,768]{1,0:T(8,128)(2,1)S(1)}, bf16[288,768]{1,0:T(8,128)(2,1)S(1)}, u32[]{:S(2)}, u32[]{:S(2)}) collective-permute-start(bf16[288,768]{1,0:T(8,128)(2,1)S(1)} %get-tuple-element.122), channel_id=1, source_target_pairs={{0,2},{1,3},{2,0},{3,1},{4,6},{5,7},{6,4},{7,5},{8,10},{9,11},{10,... | collective-permute-start | bytes 1327112 | tf_op jit(solution)/shard_map/ppermute | solution.py:1079
  23.2 4.9 %cluster_tables.1 = (bf16[3,512,128]{2,1,0:T(8,128)(2,1)S(1)}, bf16[3,1024,64]{2,1,0:T(8,128)(2,1)S(1)}, bf16[8,1024]{1,0:T(8,128)(2,1)S(1)}) custom-call(s32[3]{0:T(128)S(1)} %pad_add_fusion.sc, bf16[112,576]{1,0:T(8,128)(2,1)S(1)} %collective-permute-done.7.refs_10_._, s32[12,1024]{1,0:T(8,128)S(1)} %bitcast.17, s32[1,1024]{1,0:T(1,128)S(1)} %copy-done.2), custom_call_target="tpu_custom_call" | custom-call | flops 1 | bytes 1 | tf_op jit(solution)/shard_map/cluster_tables/pallas_call | solution.py:382
  29.1 2.1 %project.1 = (bf16[1024,768]{1,0:T(8,128)(2,1)S(1)}, bf16[768,576]{1,0:T(8,128)(2,1)S(1)}, f32[16,768]{1,0:T(8,128)S(1)}) custom-call(s32[3]{0:T(128)S(1)} %pad_add_fusion.sc, bf16[128,768]{1,0:T(8,128)(2,1)S(1)} %bitcast.14, bf16[128,768]{1,0:T(8,128)(2,1)S(1)} %collective-permute-done.refs_1_.refs_5_, ...), custom_call_target="tpu_custom_call" | custom-call | flops 1 | bytes 1 | tf_op jit(solution)/shard_map/project/pallas_call | solution.py:382
  32.6 7.1 %collective-permute-done.18.refs_13_ = bf16[288,768]{1,0:T(8,128)(2,1)S(1)} collective-permute-done((bf16[288,768]{1,0:T(8,128)(2,1)S(1)}, bf16[288,768]{1,0:T(8,128)(2,1)S(1)}, u32[]{:S(2)}, u32[]{:S(2)}) %collective-permute-start.18) | collective-permute-done | bytes 442400 | tf_op jit(solution)/shard_map/ppermute | solution.py:1079
  39.7 1.5 collective-permute-start.19
  41.2 1.5 collective-permute-done.13.refs_1_
  42.8 1.5 collective-permute-start.16
  44.9 1.5 collective-permute-start.14
  46.4 5.2 %collective-permute-done.16.refs_3_.refs_7_ = bf16[256,384]{1,0:T(8,128)(2,1)S(1)} collective-permute-done((bf16[256,384]{1,0:T(8,128)(2,1)S(1)}, bf16[256,384]{1,0:T(8,128)(2,1)S(1)}, u32[]{:S(2)}, u32[]{:S(2)}) %collective-permute-start.16) | collective-permute-done | bytes 196640 | tf_op jit(solution)/shard_map/ppermute | solution.py:1074
  51.6 3.4 %collective-permute-done.15.refs_2_.refs_6_ = bf16[256,384]{1,0:T(8,128)(2,1)S(1)} collective-permute-done((bf16[256,384]{1,0:T(8,128)(2,1)S(1)}, bf16[256,384]{1,0:T(8,128)(2,1)S(1)}, u32[]{:S(2)}, u32[]{:S(2)}) %collective-permute-start.15) | collective-permute-done | bytes 196640 | tf_op jit(solution)/shard_map/ppermute | solution.py:1074
  58.1 3.2 %mlp_forward.1 = (f32[128,768]{1,0:T(8,128)S(1)}, bf16[128,768]{1,0:T(8,128)(2,1)S(1)}, bf16[128,768]{1,0:T(8,128)(2,1)S(1)}, bf16[128,768]{1,0:T(8,128)(2,1)S(1...) custom-call(s32[3]{0:T(128)S(1)} %pad_add_fusion.sc, ...), custom_call_target="tpu_custom_call" | custom-call | flops 1 | bytes 1 | tf_op jit(solution)/shard_map/mlp_forward/pallas_call | solution.py:382
  61.9 1.4 collective-permute-start.24
  63.4 1.6 collective-permute-start.25
  64.9 1.4 turn_rows.1.turned_x
  66.4 2.8 %collective-permute-done.23.refs_1_ = bf16[128,768]{1,0:T(8,128)(2,1)S(1)} collective-permute-done((bf16[128,768]{1,0:T(8,128)(2,1)S(1)}, bf16[128,768]{1,0:T(8,128)(2,1)S(1)}, u32[]{:S(2)}, u32[]{:S(2)}) %collective-permute-start.23) | collective-permute-done | bytes 196640 | tf_op jit(solution)/shard_map/ppermute | solution.py:1074
  69.4 3.4 %collective-permute-done.25.refs_3_ = bf16[128,768]{1,0:T(8,128)(2,1)S(1)} collective-permute-done((bf16[128,768]{1,0:T(8,128)(2,1)S(1)}, bf16[128,768]{1,0:T(8,128)(2,1)S(1)}, u32[]{:S(2)}, u32[]{:S(2)}) %collective-permute-start.25) | collective-permute-done | bytes 196640 | tf_op jit(solution)/shard_map/ppermute | solution.py:1074
  73.8 1.7 collective-permute-start.28
  77.9 5.0 %collective-permute-done.28.refs_3_ = bf16[136,768]{1,0:T(8,128)(2,1)S(1)} collective-permute-done((bf16[136,768]{1,0:T(8,128)(2,1)S(1)}, bf16[136,768]{1,0:T(8,128)(2,1)S(1)}, u32[]{:S(2)}, u32[]{:S(2)}) %collective-permute-start.28) | collective-permute-done | bytes 208928 | tf_op jit(solution)/shard_map/ppermute | solution.py:1074
  82.8 2.7 %collective-permute-done.27.refs_2_ = bf16[136,768]{1,0:T(8,128)(2,1)S(1)} collective-permute-done((bf16[136,768]{1,0:T(8,128)(2,1)S(1)}, bf16[136,768]{1,0:T(8,128)(2,1)S(1)}, u32[]{:S(2)}, u32[]{:S(2)}) %collective-permute-start.27) | collective-permute-done | bytes 208928 | tf_op jit(solution)/shard_map/ppermute | solution.py:1074
  85.5 1.5 mlp_back.1
  87.0 2.3 %mlp_grads.1 = (f32[4,192,768]{2,1,0:T(8,128)S(1)}, bf16[4,192,768]{2,1,0:T(8,128)(2,1)S(1)}, f32[8,768]{1,0:T(8,128)S(1)}) custom-call(s32[3]{0:T(128)S(1)} %pad_add_fusion.sc, bf16[136,768]{1,0:T(8,128)(2,1)S(1)} %get-tuple-element.151.refs_0_, bf16[136,768]{1,0:T(8,128)(2,1)S(1)} %collective-permute-done.26.refs_1_, ...), custom_call_target="tpu_custom_call" | custom-call | flops 1 | bytes 1 | tf_op jit(solution)/shard_map/mlp_grads/pallas_call | solution.py:382
  89.3 2.8 %collective-permute-done.32.refs_1_ = bf16[4,192,768]{2,1,0:T(8,128)(2,1)S(1)} collective-permute-done((bf16[4,192,768]{2,1,0:T(8,128)(2,1)S(1)}, bf16[4,192,768]{2,1,0:T(8,128)(2,1)S(1)}, u32[]{:S(2)}, u32[]{:S(2)}) %collective-permute-start.32) | collective-permute-done | bytes 1179680 | tf_op jit(solution)/shard_map/ppermute | solution.py:1069
  94.8 1.6 collective-permute-start.31
  96.4 2.3 %collective-permute-start.37 = (bf16[192,768]{1,0:T(8,128)(2,1)S(1)}, bf16[192,768]{1,0:T(8,128)(2,1)S(1)}, u32[]{:S(2)}, u32[]{:S(2)}) collective-permute-start(bf16[192,768]{1,0:T(8,128)(2,1)S(1)} %get-tuple-element.165), channel_id=1, source_target_pairs={{0,2},{1,3},{2,0},{3,1},{4,6},{5,7},{6,4},{7,5},{8,10},{9,11},{10,... | collective-permute-start | bytes 884744 | tf_op jit(solution)/shard_map/ppermute | solution.py:1079
  98.8 2.0 %collective-permute-done.29.refs_1_ = bf16[128,768]{1,0:T(8,128)(2,1)S(1)} collective-permute-done((bf16[128,768]{1,0:T(8,128)(2,1)S(1)}, bf16[128,768]{1,0:T(8,128)(2,1)S(1)}, u32[]{:S(2)}, u32[]{:S(2)}) %collective-permute-start.29) | collective-permute-done | bytes 196640 | tf_op jit(solution)/shard_map/ppermute | solution.py:1074
  100.7 3.4 %collective-permute-start.38 = (bf16[192,768]{1,0:T(8,128)(2,1)S(1)}, bf16[192,768]{1,0:T(8,128)(2,1)S(1)}, u32[]{:S(2)}, u32[]{:S(2)}) collective-permute-start(bf16[192,768]{1,0:T(8,128)(2,1)S(1)} %get-tuple-element.166), channel_id=1, source_target_pairs={{0,3},{1,2},{2,1},{3,0},{4,7},{5,6},{6,5},{7,4},{8,11},{9,10},{10,... | collective-permute-start | bytes 884744 | tf_op jit(solution)/shard_map/ppermute | solution.py:1079
  105.2 1.6 collective-permute-start.35
  108.7 11.2 %collective-permute-done.37.refs_2_ = bf16[192,768]{1,0:T(8,128)(2,1)S(1)} collective-permute-done((bf16[192,768]{1,0:T(8,128)(2,1)S(1)}, bf16[192,768]{1,0:T(8,128)(2,1)S(1)}, u32[]{:S(2)}, u32[]{:S(2)}) %collective-permute-start.37) | collective-permute-done | bytes 294944 | tf_op jit(solution)/shard_map/ppermute | solution.py:1079
  120.6 1.9 %out_grads.1 = (f32[2,56,768]{2,1,0:T(8,128)S(1)}, bf16[2,56,768]{2,1,0:T(8,128)(2,1)S(1)}) custom-call(s32[3]{0:T(128)S(1)} %pad_add_fusion.sc, bf16[136,768]{1,0:T(8,128)(2,1)S(1)} %get-tuple-element.171.refs_0_, bf16[136,768]{1,0:T(8,128)(2,1)S(1)} %collective-permute-done.33.refs_1_, bf16[136,768]{1,0:T(8,128)(2,1)S(1)} %collective-permute-done.34.refs_2_, ...), custom_call_target="tpu_custom_call" | custom-call | flops 1 | bytes 1 | tf_op jit(solution)/shard_map/out_grads/pallas_call | solution.py:382
  122.5 1.9 %attend_back.1.mine = bf16[1024,640]{1,0:T(8,128)(2,1)S(1)} custom-call(bf16[512,192]{1,0:T(8,128)(2,1)S(1)} %context_back.1.own, bf16[512,192]{1,0:T(8,128)(2,1)S(1)} %collective-permute-done.39.other, bf16[3,512,128]{2,1,0:T(8,128)(2,1)S(1)} %get-tuple-element.130.pick, bf16[3,1024,64]{2,1,0:T(8,128)(2,1)S(1)} %get-tuple-element.131.place, ...), custom_call_target="tpu_custom_call" | custom-call | flops 1 | bytes 1 | tf_op jit(solution)/shard_map/attend_back/pallas_call | solution.py:382
  126.8 4.9 %collective-permute-start.46 = (bf16[2,56,768]{2,1,0:T(8,128)(2,1)S(1)}, bf16[2,56,768]{2,1,0:T(8,128)(2,1)S(1)}, u32[]{:S(2)}, u32[]{:S(2)}) collective-permute-start(bf16[2,56,768]{2,1,0:T(8,128)(2,1)S(1)} %get-tuple-element.191), channel_id=1, source_target_pairs={{0,1},{1,0},{2,3},{3,2},{4,5},{5,4},{6,7},{7,6},{8,9},{9,8},{10,11... | collective-permute-start | bytes 516104 | tf_op jit(solution)/shard_map/ppermute | solution.py:1079
  131.7 1.6 project_grads.1
  137.0 6.0 %collective-permute-start.47 = (bf16[1,56,768]{2,1,0:T(8,128)(2,1)S(1)}, bf16[1,56,768]{2,1,0:T(8,128)(2,1)S(1)}, u32[]{:S(2)}, u32[]{:S(2)}) collective-permute-start(bf16[1,56,768]{2,1,0:T(8,128)(2,1)S(1)} %get-tuple-element.193), channel_id=1, source_target_pairs={{0,2},{1,3},{2,0},{3,1},{4,6},{5,7},{6,4},{7,5},{8,10},{9,11},{10,... | collective-permute-start | bytes 258056 | tf_op jit(solution)/shard_map/ppermute | solution.py:1079
  143.6 3.3 %collective-permute-done.47.refs_3_ = bf16[1,56,768]{2,1,0:T(8,128)(2,1)S(1)} collective-permute-done((bf16[1,56,768]{2,1,0:T(8,128)(2,1)S(1)}, bf16[1,56,768]{2,1,0:T(8,128)(2,1)S(1)}, u32[]{:S(2)}, u32[]{:S(2)}) %collective-permute-start.47) | collective-permute-done | bytes 86048 | tf_op jit(solution)/shard_map/ppermute | solution.py:1079
  148.2 2.0 %collective-permute-start.45 = (bf16[1,80,768]{2,1,0:T(8,128)(2,1)S(1)}, bf16[1,80,768]{2,1,0:T(8,128)(2,1)S(1)}, u32[]{:S(2)}, u32[]{:S(2)}) collective-permute-start(bf16[1,80,768]{2,1,0:T(8,128)(2,1)S(1)} %get-tuple-element.189), channel_id=1, source_target_pairs={{0,2},{1,3},{2,0},{3,1},{4,6},{5,7},{6,4},{7,5},{8,10},{9,11},{10,... | collective-permute-start | bytes 368648 | tf_op jit(solution)/shard_map/ppermute | solution.py:1079
  150.2 4.6 %collective-permute-done.42.refs_3_ = bf16[128,768]{1,0:T(8,128)(2,1)S(1)} collective-permute-done((bf16[128,768]{1,0:T(8,128)(2,1)S(1)}, bf16[128,768]{1,0:T(8,128)(2,1)S(1)}, u32[]{:S(2)}, u32[]{:S(2)}) %collective-permute-start.42) | collective-permute-done | bytes 196640 | tf_op jit(solution)/shard_map/ppermute | solution.py:1074
  156.1 1.5 collective-permute-start.50
  158.2 1.4 collective-permute-start.48
  159.7 3.2 %mlp_lay.1 = (f32[192,3072]{1,0:T(8,128)}, f32[768,768]{1,0:T(8,128)}) custom-call(s32[3]{0:T(128)S(1)} %pad_add_fusion.sc, bf16[192,768]{1,0:T(8,128)(2,1)S(1)} %mlp_sum.1.refs_0_, bf16[192,768]{1,0:T(8,128)(2,1)S(1)} %collective-permute-done.51.refs_1_, bf16[192,768]{1,0:T(8,128)(2,1)S(1)} %collective-permute-done.52.refs_2_, ...), custom_call_target="tpu_custom_call" | custom-call | flops 1 | bytes 1 | tf_op jit(solution)/shard_map/mlp_lay/pallas_call | solution.py:382
  162.8 2.3 %collective-permute-done.50.refs_3_ = bf16[136,768]{1,0:T(8,128)(2,1)S(1)} collective-permute-done((bf16[136,768]{1,0:T(8,128)(2,1)S(1)}, bf16[136,768]{1,0:T(8,128)(2,1)S(1)}, u32[]{:S(2)}, u32[]{:S(2)}) %collective-permute-start.50) | collective-permute-done | bytes 208928 | tf_op jit(solution)/shard_map/ppermute | solution.py:1074
  165.1 3.5 %collective-permute-done.49.refs_2_ = bf16[136,768]{1,0:T(8,128)(2,1)S(1)} collective-permute-done((bf16[136,768]{1,0:T(8,128)(2,1)S(1)}, bf16[136,768]{1,0:T(8,128)(2,1)S(1)}, u32[]{:S(2)}, u32[]{:S(2)}) %collective-permute-start.49) | collective-permute-done | bytes 208928 | tf_op jit(solution)/shard_map/ppermute | solution.py:1074
  171.0 2.8 %last_lay.1 = (f32[192,768]{1,0:T(8,128)}, f32[192,768]{1,0:T(8,128)}, f32[192,768]{1,0:T(8,128)}, f32[192]{0:T(256)}, f32[192]{0:T(256)}, /*index=5*/f32[192,76...) custom-call(s32[3]{0:T(128)S(1)} %pad_add_fusion.sc, ...), custom_call_target="tpu_custom_call" | custom-call | flops 1 | bytes 1 | tf_op jit(solution)/shard_map/last_lay/pallas_call | solution.py:382
  (113 shorter events, 36.4 us)
Async XLA Ops:
  2.8 13.9 %collective-permute-start = (bf16[128,768]{1,0:T(8,128)(2,1)}, bf16[128,768]{1,0:T(8,128)(2,1)S(1)}, u32[]{:S(2)}, u32[]{:S(2)}) collective-permute-start(bf16[128,768]{1,0:T(8,128)(2,1)} %bitcast.10), channel_id=1, source_target_pairs={{0,8},{4,12},{8,0},{12,4},{16,24},{20,28},{24,16},{28,20},{1,9},{5... | collective-permute-start | bytes 589832 | tf_op jit(solution)/shard_map/ppermute | solution.py:1074
  5.8 9.3 %collective-permute-start.8 = (bf16[112,576]{1,0:T(8,128)(2,1)S(1)}, bf16[112,576]{1,0:T(8,128)(2,1)S(1)}, u32[]{:S(2)}, u32[]{:S(2)}) collective-permute-start(bf16[112,576]{1,0:T(8,128)(2,1)S(1)} %get-tuple-element.118._), channel_id=1, source_target_pairs={{0,2},{1,3},{2,0},{3,1},{4,6},{5,7},{6,4},{7,5},{8,10},{9,11},{10,... | collective-permute-start | bytes 387080 | tf_op jit(solution)/shard_map/ppermute | solution.py:1079
  8.4 6.9 %collective-permute-start.7 = (bf16[112,576]{1,0:T(8,128)(2,1)S(1)}, bf16[112,576]{1,0:T(8,128)(2,1)S(1)}, u32[]{:S(2)}, u32[]{:S(2)}) collective-permute-start(bf16[112,576]{1,0:T(8,128)(2,1)S(1)} %get-tuple-element.118._), channel_id=1, source_target_pairs={{0,1},{1,0},{2,3},{3,2},{4,5},{5,4},{6,7},{7,6},{8,9},{9,8},{10,11... | collective-permute-start | bytes 387080 | tf_op jit(solution)/shard_map/ppermute | solution.py:1079
  10.0 9.1 %collective-permute-start.2 = (bf16[128,768]{1,0:T(8,128)(2,1)}, bf16[128,768]{1,0:T(8,128)(2,1)S(1)}, u32[]{:S(2)}, u32[]{:S(2)}) collective-permute-start(bf16[128,768]{1,0:T(8,128)(2,1)} %bitcast.11), channel_id=1, source_target_pairs={{0,24},{4,28},{8,16},{12,20},{16,8},{20,12},{24,0},{28,4},{1,25},{... | collective-permute-start | bytes 589832 | tf_op jit(solution)/shard_map/ppermute | solution.py:1074
  11.4 9.7 %collective-permute-start.1 = (bf16[128,768]{1,0:T(8,128)(2,1)}, bf16[128,768]{1,0:T(8,128)(2,1)S(1)}, u32[]{:S(2)}, u32[]{:S(2)}) collective-permute-start(bf16[128,768]{1,0:T(8,128)(2,1)} %bitcast.12), channel_id=1, source_target_pairs={{0,16},{4,20},{8,24},{12,28},{16,0},{20,4},{24,8},{28,12},{1,17},{... | collective-permute-start | bytes 589832 | tf_op jit(solution)/shard_map/ppermute | solution.py:1074
  15.3 5.1 %collective-permute-start.9 = (bf16[112,576]{1,0:T(8,128)(2,1)S(1)}, bf16[112,576]{1,0:T(8,128)(2,1)S(1)}, u32[]{:S(2)}, u32[]{:S(2)}) collective-permute-start(bf16[112,576]{1,0:T(8,128)(2,1)S(1)} %collective-permute-done.8.refs_11_), channel_id=1, source_target_pairs={{0,1},{1,0},{2,3},{3,2},{4,5},{5,4},{6,7},{7,6},{8,9},{9,8},{10,11... | collective-permute-start | bytes 387080 | tf_op jit(solution)/shard_map/ppermute | solution.py:1079
  16.7 23.0 %collective-permute-start.18 = (bf16[288,768]{1,0:T(8,128)(2,1)S(1)}, bf16[288,768]{1,0:T(8,128)(2,1)S(1)}, u32[]{:S(2)}, u32[]{:S(2)}) collective-permute-start(bf16[288,768]{1,0:T(8,128)(2,1)S(1)} %get-tuple-element.122), channel_id=1, source_target_pairs={{0,2},{1,3},{2,0},{3,1},{4,6},{5,7},{6,4},{7,5},{8,10},{9,11},{10,... | collective-permute-start | bytes 1327112 | tf_op jit(solution)/shard_map/ppermute | solution.py:1079
  19.1 20.6 %collective-permute-start.17 = (bf16[288,768]{1,0:T(8,128)(2,1)S(1)}, bf16[288,768]{1,0:T(8,128)(2,1)S(1)}, u32[]{:S(2)}, u32[]{:S(2)}) collective-permute-start(bf16[288,768]{1,0:T(8,128)(2,1)S(1)} %get-tuple-element.122), channel_id=1, source_target_pairs={{0,1},{1,0},{2,3},{3,2},{4,5},{5,4},{6,7},{7,6},{8,9},{9,8},{10,11... | collective-permute-start | bytes 1327112 | tf_op jit(solution)/shard_map/ppermute | solution.py:1079
  22.5 6.6 %collective-permute-start.3 = (bf16[128,768]{1,0:T(8,128)(2,1)S(1)}, bf16[128,768]{1,0:T(8,128)(2,1)S(1)}, u32[]{:S(2)}, u32[]{:S(2)}) collective-permute-start(bf16[128,768]{1,0:T(8,128)(2,1)S(1)} %bitcast.13), channel_id=1, source_target_pairs={{0,4},{4,0},{8,12},{12,8},{16,20},{20,16},{24,28},{28,24},{1,5},{5... | collective-permute-start | bytes 589832 | tf_op jit(solution)/shard_map/ppermute | solution.py:1069
  22.7 6.4 %collective-permute-start.5 = (bf16[128,768]{1,0:T(8,128)(2,1)S(1)}, bf16[128,768]{1,0:T(8,128)(2,1)S(1)}, u32[]{:S(2)}, u32[]{:S(2)}) collective-permute-start(bf16[128,768]{1,0:T(8,128)(2,1)S(1)} %collective-permute-done.1.refs_2_.refs_6_), channel_id=1, source_target_pairs={{0,4},{4,0},{8,12},{12,8},{16,20},{20,16},{24,28},{28,24},{1,5},{5... | collective-permute-start | bytes 589832 | tf_op jit(solution)/shard_map/ppermute | solution.py:1069
  23.0 6.1 %collective-permute-start.4 = (bf16[128,768]{1,0:T(8,128)(2,1)S(1)}, bf16[128,768]{1,0:T(8,128)(2,1)S(1)}, u32[]{:S(2)}, u32[]{:S(2)}) collective-permute-start(bf16[128,768]{1,0:T(8,128)(2,1)S(1)} %collective-permute-done.refs_1_.refs_5_), channel_id=1, source_target_pairs={{0,4},{4,0},{8,12},{12,8},{16,20},{20,16},{24,28},{28,24},{1,5},{5... | collective-permute-start | bytes 589832 | tf_op jit(solution)/shard_map/ppermute | solution.py:1069
  39.7 15.9 %collective-permute-start.19 = (bf16[288,768]{1,0:T(8,128)(2,1)S(1)}, bf16[288,768]{1,0:T(8,128)(2,1)S(1)}, u32[]{:S(2)}, u32[]{:S(2)}) collective-permute-start(bf16[288,768]{1,0:T(8,128)(2,1)S(1)} %collective-permute-done.18.refs_13_), channel_id=1, source_target_pairs={{0,1},{1,0},{2,3},{3,2},{4,5},{5,4},{6,7},{7,6},{8,9},{9,8},{10,11... | collective-permute-start | bytes 1327112 | tf_op jit(solution)/shard_map/ppermute | solution.py:1079
  42.8 8.8 %collective-permute-start.16 = (bf16[256,384]{1,0:T(8,128)(2,1)S(1)}, bf16[256,384]{1,0:T(8,128)(2,1)S(1)}, u32[]{:S(2)}, u32[]{:S(2)}) collective-permute-start(bf16[256,384]{1,0:T(8,128)(2,1)S(1)} %join_context.1.refs_0_.refs_4_), channel_id=1, source_target_pairs={{0,24},{4,28},{8,16},{12,20},{16,8},{20,12},{24,0},{28,4},{1,25},{... | collective-permute-start | bytes 589832 | tf_op jit(solution)/shard_map/ppermute | solution.py:1074
  44.4 10.6 %collective-permute-start.15 = (bf16[256,384]{1,0:T(8,128)(2,1)S(1)}, bf16[256,384]{1,0:T(8,128)(2,1)S(1)}, u32[]{:S(2)}, u32[]{:S(2)}) collective-permute-start(bf16[256,384]{1,0:T(8,128)(2,1)S(1)} %join_context.1.refs_0_.refs_4_), channel_id=1, source_target_pairs={{0,16},{4,20},{8,24},{12,28},{16,0},{20,4},{24,8},{28,12},{1,17},{... | collective-permute-start | bytes 589832 | tf_op jit(solution)/shard_map/ppermute | solution.py:1074
  44.9 10.2 %collective-permute-start.14 = (bf16[256,384]{1,0:T(8,128)(2,1)S(1)}, bf16[256,384]{1,0:T(8,128)(2,1)S(1)}, u32[]{:S(2)}, u32[]{:S(2)}) collective-permute-start(bf16[256,384]{1,0:T(8,128)(2,1)S(1)} %join_context.1.refs_0_.refs_4_), channel_id=1, source_target_pairs={{0,8},{4,12},{8,0},{12,4},{16,24},{20,28},{24,16},{28,20},{1,9},{5... | collective-permute-start | bytes 589832 | tf_op jit(solution)/shard_map/ppermute | solution.py:1074
  61.4 7.8 %collective-permute-start.23 = (bf16[128,768]{1,0:T(8,128)(2,1)S(1)}, bf16[128,768]{1,0:T(8,128)(2,1)S(1)}, u32[]{:S(2)}, u32[]{:S(2)}) collective-permute-start(bf16[128,768]{1,0:T(8,128)(2,1)S(1)} %get-tuple-element.144), channel_id=1, source_target_pairs={{0,8},{4,12},{8,0},{12,4},{16,24},{20,28},{24,16},{28,20},{1,9},{5... | collective-permute-start | bytes 589832 | tf_op jit(solution)/shard_map/ppermute | solution.py:1074
  61.9 7.5 %collective-permute-start.24 = (bf16[128,768]{1,0:T(8,128)(2,1)S(1)}, bf16[128,768]{1,0:T(8,128)(2,1)S(1)}, u32[]{:S(2)}, u32[]{:S(2)}) collective-permute-start(bf16[128,768]{1,0:T(8,128)(2,1)S(1)} %get-tuple-element.145), channel_id=1, source_target_pairs={{0,16},{4,20},{8,24},{12,28},{16,0},{20,4},{24,8},{28,12},{1,17},{... | collective-permute-start | bytes 589832 | tf_op jit(solution)/shard_map/ppermute | solution.py:1074
  63.4 9.5 %collective-permute-start.25 = (bf16[128,768]{1,0:T(8,128)(2,1)S(1)}, bf16[128,768]{1,0:T(8,128)(2,1)S(1)}, u32[]{:S(2)}, u32[]{:S(2)}) collective-permute-start(bf16[128,768]{1,0:T(8,128)(2,1)S(1)} %get-tuple-element.146), channel_id=1, source_target_pairs={{0,24},{4,28},{8,16},{12,20},{16,8},{20,12},{24,0},{28,4},{1,25},{... | collective-permute-start | bytes 589832 | tf_op jit(solution)/shard_map/ppermute | solution.py:1074
  73.8 9.0 %collective-permute-start.28 = (bf16[136,768]{1,0:T(8,128)(2,1)S(1)}, bf16[136,768]{1,0:T(8,128)(2,1)S(1)}, u32[]{:S(2)}, u32[]{:S(2)}) collective-permute-start(bf16[136,768]{1,0:T(8,128)(2,1)S(1)} %get-tuple-element.151.refs_0_), channel_id=1, source_target_pairs={{0,24},{4,28},{8,16},{12,20},{16,8},{20,12},{24,0},{28,4},{1,25},{... | collective-permute-start | bytes 626696 | tf_op jit(solution)/shard_map/ppermute | solution.py:1074
  75.5 10.0 %collective-permute-start.27 = (bf16[136,768]{1,0:T(8,128)(2,1)S(1)}, bf16[136,768]{1,0:T(8,128)(2,1)S(1)}, u32[]{:S(2)}, u32[]{:S(2)}) collective-permute-start(bf16[136,768]{1,0:T(8,128)(2,1)S(1)} %get-tuple-element.151.refs_0_), channel_id=1, source_target_pairs={{0,16},{4,20},{8,24},{12,28},{16,0},{20,4},{24,8},{28,12},{1,17},{... | collective-permute-start | bytes 626696 | tf_op jit(solution)/shard_map/ppermute | solution.py:1074
  76.8 8.7 %collective-permute-start.26 = (bf16[136,768]{1,0:T(8,128)(2,1)S(1)}, bf16[136,768]{1,0:T(8,128)(2,1)S(1)}, u32[]{:S(2)}, u32[]{:S(2)}) collective-permute-start(bf16[136,768]{1,0:T(8,128)(2,1)S(1)} %get-tuple-element.151.refs_0_), channel_id=1, source_target_pairs={{0,8},{4,12},{8,0},{12,4},{16,24},{20,28},{24,16},{28,20},{1,9},{5... | collective-permute-start | bytes 626696 | tf_op jit(solution)/shard_map/ppermute | solution.py:1074
  92.4 15.1 %collective-permute-start.36 = (bf16[192,768]{1,0:T(8,128)(2,1)S(1)}, bf16[192,768]{1,0:T(8,128)(2,1)S(1)}, u32[]{:S(2)}, u32[]{:S(2)}) collective-permute-start(bf16[192,768]{1,0:T(8,128)(2,1)S(1)} %get-tuple-element.164), channel_id=1, source_target_pairs={{0,1},{1,0},{2,3},{3,2},{4,5},{5,4},{6,7},{7,6},{8,9},{9,8},{10,11... | collective-permute-start | bytes 884744 | tf_op jit(solution)/shard_map/ppermute | solution.py:1079
  93.0 7.8 %collective-permute-start.29 = (bf16[128,768]{1,0:T(8,128)(2,1)S(1)}, bf16[128,768]{1,0:T(8,128)(2,1)S(1)}, u32[]{:S(2)}, u32[]{:S(2)}) collective-permute-start(bf16[128,768]{1,0:T(8,128)(2,1)S(1)} %get-tuple-element.155), channel_id=1, source_target_pairs={{0,8},{4,12},{8,0},{12,4},{16,24},{20,28},{24,16},{28,20},{1,9},{5... | collective-permute-start | bytes 589832 | tf_op jit(solution)/shard_map/ppermute | solution.py:1074
  94.2 10.6 %collective-permute-start.30 = (bf16[128,768]{1,0:T(8,128)(2,1)S(1)}, bf16[128,768]{1,0:T(8,128)(2,1)S(1)}, u32[]{:S(2)}, u32[]{:S(2)}) collective-permute-start(bf16[128,768]{1,0:T(8,128)(2,1)S(1)} %get-tuple-element.156), channel_id=1, source_target_pairs={{0,16},{4,20},{8,24},{12,28},{16,0},{20,4},{24,8},{28,12},{1,17},{... | collective-permute-start | bytes 589832 | tf_op jit(solution)/shard_map/ppermute | solution.py:1074
  94.8 10.0 %collective-permute-start.31 = (bf16[128,768]{1,0:T(8,128)(2,1)S(1)}, bf16[128,768]{1,0:T(8,128)(2,1)S(1)}, u32[]{:S(2)}, u32[]{:S(2)}) collective-permute-start(bf16[128,768]{1,0:T(8,128)(2,1)S(1)} %get-tuple-element.157), channel_id=1, source_target_pairs={{0,24},{4,28},{8,16},{12,20},{16,8},{20,12},{24,0},{28,4},{1,25},{... | collective-permute-start | bytes 589832 | tf_op jit(solution)/shard_map/ppermute | solution.py:1074
  96.4 23.5 %collective-permute-start.37 = (bf16[192,768]{1,0:T(8,128)(2,1)S(1)}, bf16[192,768]{1,0:T(8,128)(2,1)S(1)}, u32[]{:S(2)}, u32[]{:S(2)}) collective-permute-start(bf16[192,768]{1,0:T(8,128)(2,1)S(1)} %get-tuple-element.165), channel_id=1, source_target_pairs={{0,2},{1,3},{2,0},{3,1},{4,6},{5,7},{6,4},{7,5},{8,10},{9,11},{10,... | collective-permute-start | bytes 884744 | tf_op jit(solution)/shard_map/ppermute | solution.py:1079
  100.7 19.2 %collective-permute-start.38 = (bf16[192,768]{1,0:T(8,128)(2,1)S(1)}, bf16[192,768]{1,0:T(8,128)(2,1)S(1)}, u32[]{:S(2)}, u32[]{:S(2)}) collective-permute-start(bf16[192,768]{1,0:T(8,128)(2,1)S(1)} %get-tuple-element.166), channel_id=1, source_target_pairs={{0,3},{1,2},{2,1},{3,0},{4,7},{5,6},{6,5},{7,4},{8,11},{9,10},{10,... | collective-permute-start | bytes 884744 | tf_op jit(solution)/shard_map/ppermute | solution.py:1079
  105.2 14.9 %collective-permute-start.35 = (bf16[136,768]{1,0:T(8,128)(2,1)S(1)}, bf16[136,768]{1,0:T(8,128)(2,1)S(1)}, u32[]{:S(2)}, u32[]{:S(2)}) collective-permute-start(bf16[136,768]{1,0:T(8,128)(2,1)S(1)} %get-tuple-element.171.refs_0_), channel_id=1, source_target_pairs={{0,24},{4,28},{8,16},{12,20},{16,8},{20,12},{24,0},{28,4},{1,25},{... | collective-permute-start | bytes 626696 | tf_op jit(solution)/shard_map/ppermute | solution.py:1074
  106.8 13.3 %collective-permute-start.34 = (bf16[136,768]{1,0:T(8,128)(2,1)S(1)}, bf16[136,768]{1,0:T(8,128)(2,1)S(1)}, u32[]{:S(2)}, u32[]{:S(2)}) collective-permute-start(bf16[136,768]{1,0:T(8,128)(2,1)S(1)} %get-tuple-element.171.refs_0_), channel_id=1, source_target_pairs={{0,16},{4,20},{8,24},{12,28},{16,0},{20,4},{24,8},{28,12},{1,17},{... | collective-permute-start | bytes 626696 | tf_op jit(solution)/shard_map/ppermute | solution.py:1074
  107.5 12.6 %collective-permute-start.33 = (bf16[136,768]{1,0:T(8,128)(2,1)S(1)}, bf16[136,768]{1,0:T(8,128)(2,1)S(1)}, u32[]{:S(2)}, u32[]{:S(2)}) collective-permute-start(bf16[136,768]{1,0:T(8,128)(2,1)S(1)} %get-tuple-element.171.refs_0_), channel_id=1, source_target_pairs={{0,8},{4,12},{8,0},{12,4},{16,24},{20,28},{24,16},{28,20},{1,9},{5... | collective-permute-start | bytes 626696 | tf_op jit(solution)/shard_map/ppermute | solution.py:1074
  124.4 7.3 %collective-permute-start.40 = (bf16[1024,640]{1,0:T(8,128)(2,1)S(1)}, bf16[1024,640]{1,0:T(8,128)(2,1)S(1)}, u32[]{:S(2)}, u32[]{:S(2)}) collective-permute-start(bf16[1024,640]{1,0:T(8,128)(2,1)S(1)} %attend_back.1.mine), channel_id=1, source_target_pairs={{0,4},{4,0},{8,12},{12,8},{16,20},{20,16},{24,28},{28,24},{1,5},{5... | collective-permute-start | bytes 3932168 | tf_op jit(solution)/shard_map/ppermute | solution.py:1069
  124.9 11.4 %collective-permute-start.51 = (bf16[192,768]{1,0:T(8,128)(2,1)S(1)}, bf16[192,768]{1,0:T(8,128)(2,1)S(1)}, u32[]{:S(2)}, u32[]{:S(2)}) collective-permute-start(bf16[192,768]{1,0:T(8,128)(2,1)S(1)} %mlp_sum.1.refs_0_), channel_id=1, source_target_pairs={{0,8},{4,12},{8,0},{12,4},{16,24},{20,28},{24,16},{28,20},{1,9},{5... | collective-permute-start | bytes 884744 | tf_op jit(solution)/shard_map/ppermute | solution.py:1074
  126.2 16.9 %collective-permute-start.52 = (bf16[192,768]{1,0:T(8,128)(2,1)S(1)}, bf16[192,768]{1,0:T(8,128)(2,1)S(1)}, u32[]{:S(2)}, u32[]{:S(2)}) collective-permute-start(bf16[192,768]{1,0:T(8,128)(2,1)S(1)} %mlp_sum.1.refs_0_), channel_id=1, source_target_pairs={{0,16},{4,20},{8,24},{12,28},{16,0},{20,4},{24,8},{28,12},{1,17},{... | collective-permute-start | bytes 884744 | tf_op jit(solution)/shard_map/ppermute | solution.py:1074
  126.8 10.2 %collective-permute-start.46 = (bf16[2,56,768]{2,1,0:T(8,128)(2,1)S(1)}, bf16[2,56,768]{2,1,0:T(8,128)(2,1)S(1)}, u32[]{:S(2)}, u32[]{:S(2)}) collective-permute-start(bf16[2,56,768]{2,1,0:T(8,128)(2,1)S(1)} %get-tuple-element.191), channel_id=1, source_target_pairs={{0,1},{1,0},{2,3},{3,2},{4,5},{5,4},{6,7},{7,6},{8,9},{9,8},{10,11... | collective-permute-start | bytes 516104 | tf_op jit(solution)/shard_map/ppermute | solution.py:1079
  133.3 9.7 %collective-permute-start.44 = (bf16[2,80,768]{2,1,0:T(8,128)(2,1)S(1)}, bf16[2,80,768]{2,1,0:T(8,128)(2,1)S(1)}, u32[]{:S(2)}, u32[]{:S(2)}) collective-permute-start(bf16[2,80,768]{2,1,0:T(8,128)(2,1)S(1)} %get-tuple-element.180), channel_id=1, source_target_pairs={{0,1},{1,0},{2,3},{3,2},{4,5},{5,4},{6,7},{7,6},{8,9},{9,8},{10,11... | collective-permute-start | bytes 737288 | tf_op jit(solution)/shard_map/ppermute | solution.py:1079
  135.1 12.9 %collective-permute-start.41 = (bf16[128,768]{1,0:T(8,128)(2,1)S(1)}, bf16[128,768]{1,0:T(8,128)(2,1)S(1)}, u32[]{:S(2)}, u32[]{:S(2)}) collective-permute-start(bf16[128,768]{1,0:T(8,128)(2,1)S(1)} %get-tuple-element.184), channel_id=1, source_target_pairs={{0,8},{4,12},{8,0},{12,4},{16,24},{20,28},{24,16},{28,20},{1,9},{5... | collective-permute-start | bytes 589832 | tf_op jit(solution)/shard_map/ppermute | solution.py:1074
  136.3 11.9 %collective-permute-start.53 = (bf16[192,768]{1,0:T(8,128)(2,1)S(1)}, bf16[192,768]{1,0:T(8,128)(2,1)S(1)}, u32[]{:S(2)}, u32[]{:S(2)}) collective-permute-start(bf16[192,768]{1,0:T(8,128)(2,1)S(1)} %collective-permute-done.51.refs_1_), channel_id=1, source_target_pairs={{0,16},{4,20},{8,24},{12,28},{16,0},{20,4},{24,8},{28,12},{1,17},{... | collective-permute-start | bytes 884744 | tf_op jit(solution)/shard_map/ppermute | solution.py:1074
  137.0 9.9 %collective-permute-start.47 = (bf16[1,56,768]{2,1,0:T(8,128)(2,1)S(1)}, bf16[1,56,768]{2,1,0:T(8,128)(2,1)S(1)}, u32[]{:S(2)}, u32[]{:S(2)}) collective-permute-start(bf16[1,56,768]{2,1,0:T(8,128)(2,1)S(1)} %get-tuple-element.193), channel_id=1, source_target_pairs={{0,2},{1,3},{2,0},{3,1},{4,6},{5,7},{6,4},{7,5},{8,10},{9,11},{10,... | collective-permute-start | bytes 258056 | tf_op jit(solution)/shard_map/ppermute | solution.py:1079
  143.1 14.6 %collective-permute-start.54 = (bf16[192,768]{1,0:T(8,128)(2,1)S(1)}, bf16[192,768]{1,0:T(8,128)(2,1)S(1)}, u32[]{:S(2)}, u32[]{:S(2)}) collective-permute-start(bf16[192,768]{1,0:T(8,128)(2,1)S(1)} %mlp_sum.1.refs_0_), channel_id=1, source_target_pairs={{0,4},{4,0},{8,12},{12,8},{16,20},{20,16},{24,28},{28,24},{1,5},{5... | collective-permute-start | bytes 884744 | tf_op jit(solution)/shard_map/ppermute | solution.py:1069
  143.1 15.1 %collective-permute-start.55 = (bf16[192,768]{1,0:T(8,128)(2,1)S(1)}, bf16[192,768]{1,0:T(8,128)(2,1)S(1)}, u32[]{:S(2)}, u32[]{:S(2)}) collective-permute-start(bf16[192,768]{1,0:T(8,128)(2,1)S(1)} %collective-permute-done.51.refs_1_), channel_id=1, source_target_pairs={{0,4},{4,0},{8,12},{12,8},{16,20},{20,16},{24,28},{28,24},{1,5},{5... | collective-permute-start | bytes 884744 | tf_op jit(solution)/shard_map/ppermute | solution.py:1069
  146.9 7.9 %collective-permute-start.42 = (bf16[128,768]{1,0:T(8,128)(2,1)S(1)}, bf16[128,768]{1,0:T(8,128)(2,1)S(1)}, u32[]{:S(2)}, u32[]{:S(2)}) collective-permute-start(bf16[128,768]{1,0:T(8,128)(2,1)S(1)} %get-tuple-element.185), channel_id=1, source_target_pairs={{0,16},{4,20},{8,24},{12,28},{16,0},{20,4},{24,8},{28,12},{1,17},{... | collective-permute-start | bytes 589832 | tf_op jit(solution)/shard_map/ppermute | solution.py:1074
  148.0 6.8 %collective-permute-start.43 = (bf16[128,768]{1,0:T(8,128)(2,1)S(1)}, bf16[128,768]{1,0:T(8,128)(2,1)S(1)}, u32[]{:S(2)}, u32[]{:S(2)}) collective-permute-start(bf16[128,768]{1,0:T(8,128)(2,1)S(1)} %get-tuple-element.186), channel_id=1, source_target_pairs={{0,24},{4,28},{8,16},{12,20},{16,8},{20,12},{24,0},{28,4},{1,25},{... | collective-permute-start | bytes 589832 | tf_op jit(solution)/shard_map/ppermute | solution.py:1074
  148.2 7.8 %collective-permute-start.45 = (bf16[1,80,768]{2,1,0:T(8,128)(2,1)S(1)}, bf16[1,80,768]{2,1,0:T(8,128)(2,1)S(1)}, u32[]{:S(2)}, u32[]{:S(2)}) collective-permute-start(bf16[1,80,768]{2,1,0:T(8,128)(2,1)S(1)} %get-tuple-element.189), channel_id=1, source_target_pairs={{0,2},{1,3},{2,0},{3,1},{4,6},{5,7},{6,4},{7,5},{8,10},{9,11},{10,... | collective-permute-start | bytes 368648 | tf_op jit(solution)/shard_map/ppermute | solution.py:1079
  154.7 4.9 %collective-permute-start.56 = (bf16[192,768]{1,0:T(8,128)(2,1)S(1)}, bf16[192,768]{1,0:T(8,128)(2,1)S(1)}, u32[]{:S(2)}, u32[]{:S(2)}) collective-permute-start(bf16[192,768]{1,0:T(8,128)(2,1)S(1)} %collective-permute-done.52.refs_2_), channel_id=1, source_target_pairs={{0,4},{4,0},{8,12},{12,8},{16,20},{20,16},{24,28},{28,24},{1,5},{5... | collective-permute-start | bytes 884744 | tf_op jit(solution)/shard_map/ppermute | solution.py:1069
  154.8 4.9 %collective-permute-start.57 = (bf16[192,768]{1,0:T(8,128)(2,1)S(1)}, bf16[192,768]{1,0:T(8,128)(2,1)S(1)}, u32[]{:S(2)}, u32[]{:S(2)}) collective-permute-start(bf16[192,768]{1,0:T(8,128)(2,1)S(1)} %collective-permute-done.53.refs_3_), channel_id=1, source_target_pairs={{0,4},{4,0},{8,12},{12,8},{16,20},{20,16},{24,28},{28,24},{1,5},{5... | collective-permute-start | bytes 884744 | tf_op jit(solution)/shard_map/ppermute | solution.py:1069
  156.1 9.0 %collective-permute-start.50 = (bf16[136,768]{1,0:T(8,128)(2,1)S(1)}, bf16[136,768]{1,0:T(8,128)(2,1)S(1)}, u32[]{:S(2)}, u32[]{:S(2)}) collective-permute-start(bf16[136,768]{1,0:T(8,128)(2,1)S(1)} %last_sum.1.refs_0_), channel_id=1, source_target_pairs={{0,24},{4,28},{8,16},{12,20},{16,8},{20,12},{24,0},{28,4},{1,25},{... | collective-permute-start | bytes 626696 | tf_op jit(solution)/shard_map/ppermute | solution.py:1074
  157.6 11.0 %collective-permute-start.49 = (bf16[136,768]{1,0:T(8,128)(2,1)S(1)}, bf16[136,768]{1,0:T(8,128)(2,1)S(1)}, u32[]{:S(2)}, u32[]{:S(2)}) collective-permute-start(bf16[136,768]{1,0:T(8,128)(2,1)S(1)} %last_sum.1.refs_0_), channel_id=1, source_target_pairs={{0,16},{4,20},{8,24},{12,28},{16,0},{20,4},{24,8},{28,12},{1,17},{... | collective-permute-start | bytes 626696 | tf_op jit(solution)/shard_map/ppermute | solution.py:1074
  158.2 10.4 %collective-permute-start.48 = (bf16[136,768]{1,0:T(8,128)(2,1)S(1)}, bf16[136,768]{1,0:T(8,128)(2,1)S(1)}, u32[]{:S(2)}, u32[]{:S(2)}) collective-permute-start(bf16[136,768]{1,0:T(8,128)(2,1)S(1)} %last_sum.1.refs_0_), channel_id=1, source_target_pairs={{0,8},{4,12},{8,0},{12,4},{16,24},{20,28},{24,16},{28,20},{1,9},{5... | collective-permute-start | bytes 626696 | tf_op jit(solution)/shard_map/ppermute | solution.py:1074
  (18 other events, 101.7 us)
